TPU v7x, 32 devices: a whole 2x2x4 slice. The times are simulated.
32 devices in a mesh: dp: 8 (over z, y), tensor: 4 (over x, core).
Axes of the slice: x: 2, y: 2, z: 4, core: 2. Of those that a mesh axis runs over, the one named last changes fastest.
Arguments:
- tokens: bfloat16 [16384, 768], P(('dp', 'tensor')), may hold values from -6 to 6
- segments: int32 [8, 2048], P('dp', 'tensor'), may hold values from 0 to 3, never falling along the last dimension, each value on 1 to 1024 neighbouring positions
- query_proj: bfloat16 [768, 768], P('dp', 'tensor'), may hold values from -0.3125 to 0.3125
- query_bias: float32 [768], P(('dp', 'tensor')), may hold values from -3 to 3
- key_proj: bfloat16 [768, 768], P('dp', 'tensor'), may hold values from -0.21875 to 0.21875
- value_proj: bfloat16 [768, 768], P('dp', 'tensor'), may hold values from -0.21875 to 0.21875
- value_bias: float32 [768], P(('dp', 'tensor')), may hold values from -3 to 3
- merge_proj: bfloat16 [768, 768], P('tensor', 'dp'), may hold values from -1.75 to 1.75
- merge_bias: float32 [768], P(('dp', 'tensor')), may hold values from -3 to 3
- first_gain: float32 [768], P(('dp', 'tensor')), may hold values from 0.5 to 1.5
- first_shift: float32 [768], P(('dp', 'tensor')), may hold values from -3 to 3
- expand_proj: bfloat16 [768, 3072], P('dp', 'tensor'), may hold values from -0.21875 to 0.21875
- expand_bias: float32 [3072], P(('dp', 'tensor')), may hold values from -3 to 3
- shrink_proj: bfloat16 [3072, 768], P('tensor', 'dp'), may hold values from -0.15625 to 0.15625
- shrink_bias: float32 [768], P(('dp', 'tensor')), may hold values from -3 to 3
- second_gain: float32 [768], P(('dp', 'tensor')), may hold values from 0.5 to 1.5
- second_shift: float32 [768], P(('dp', 'tensor')), may hold values from -3 to 3
- cotangent: bfloat16 [16384, 768], P(('dp', 'tensor')), may hold values from -6 to 6
Outputs:
- output: bfloat16 [16384, 768], P(('dp', 'tensor'))
- tokens_grad: bfloat16 [16384, 768], P(('dp', 'tensor'))
- querygrad: float32 [768, 768], P('dp', 'tensor')
- qbiasgrad: float32 [768], P(('dp', 'tensor'))
- keygrad: float32 [768, 768], P('dp', 'tensor')
- valuegrad: float32 [768, 768], P('dp', 'tensor')
- vbiasgrad: float32 [768], P(('dp', 'tensor'))
- mergegrad: float32 [768, 768], P('tensor', 'dp')
- mbiasgrad: float32 [768], P(('dp', 'tensor'))
- fgaingrad: float32 [768], P(('dp', 'tensor'))
- fshiftgrad: float32 [768], P(('dp', 'tensor'))
- expandgrad: float32 [768, 3072], P('dp', 'tensor')
- ebiasgrad: float32 [3072], P(('dp', 'tensor'))
- shrinkgrad: float32 [3072, 768], P('tensor', 'dp')
- sbiasgrad: float32 [768], P(('dp', 'tensor'))
- sgaingrad: float32 [768], P(('dp', 'tensor'))
- sshiftgrad: float32 [768], P(('dp', 'tensor'))
Inputs may be any that keep to these rules, and one draw needn't show every extreme that they name: `segments`: along each sequence the segment numbers never fall; each of the 4 numbers marks 1 to 1024 positions of every sequence.
All inputs are finite; a program needn't handle non-finite values.
Results may differ from a plain program's by a relative error of at most 0.023.
Values may be sent and summed in bfloat16 or wider, within the bound.
No kernel may reach another device: no remote copies, remote signals or barrier semaphores. Data moves between devices by JAX's collectives and lax.ppermute only.
A program may use at most 128 MiB of HBM per device.

v0:
```python
import jax
import jax.numpy as jnp
from jax import lax
from jax.sharding import PartitionSpec as P

HD = 64


EPSILON = 1e-12
CONTRACT_ROWS = (((0,), (0,)), ((), ()))
CONTRACT_COLUMNS = (((1,), (1,)), ((), ()))


def normalize(values, gain, shift):
    centre = jnp.mean(values, axis=-1, keepdims=True)
    centred = values - centre
    spread = jnp.mean(centred * centred, axis=-1, keepdims=True)
    return centred * lax.rsqrt(spread + EPSILON) * gain + shift


def gelu_exact(values):
    return jax.nn.gelu(values, approximate=False)


def assemble(pieces, count, heads):
    block = pieces.shape[1]
    depth = pieces.shape[2]
    return (
        pieces.reshape(count, heads, block, depth)
        .transpose(0, 2, 1, 3)
        .reshape(count * block, heads * depth)
    )


def attend(query, keys, values, seg_row, depth):
    length, width = query.shape
    heads = width // depth
    block = min(512, length)
    count = length // block
    scale = depth ** (-0.5)

    def one(index):
        start = index // heads * block
        column = index % heads * depth
        query_rows = lax.dynamic_slice(query, (start, column), (block, depth))
        key_head = lax.dynamic_slice(keys, (0, column), (length, depth))
        value_head = lax.dynamic_slice(values, (0, column), (length, depth))
        seg_rows = lax.dynamic_slice_in_dim(seg_row, start, block)
        scores = (
            lax.dot_general(
                query_rows, key_head, CONTRACT_COLUMNS, preferred_element_type=jnp.float32
            )
            * scale
        )
        scores = jnp.where(seg_rows[:, None] == seg_row[None, :], scores, -1e30)
        peak = jnp.max(scores, axis=1, keepdims=True)
        raised = jnp.exp(scores - peak)
        total = jnp.sum(raised, axis=1, keepdims=True)
        chance = (raised / total).astype(jnp.bfloat16)
        context = jnp.dot(chance, value_head, preferred_element_type=jnp.float32)
        return (context, (peak + jnp.log(total))[:, 0])

    contexts, logsum = lax.map(one, jnp.arange(count * heads))
    return (assemble(contexts, count, heads), logsum)


def attend_back(query, keys, values, grad_context, logsum, seg_row, depth):
    length, width = query.shape
    heads = width // depth
    block = min(512, length)
    count = length // block
    scale = depth ** (-0.5)

    def one(carry, index):
        grad_keys, grad_values = carry
        start = index // heads * block
        column = index % heads * depth
        query_rows = lax.dynamic_slice(query, (start, column), (block, depth))
        grad_rows = lax.dynamic_slice(grad_context, (start, column), (block, depth))
        key_head = lax.dynamic_slice(keys, (0, column), (length, depth))
        value_head = lax.dynamic_slice(values, (0, column), (length, depth))
        seg_rows = lax.dynamic_slice_in_dim(seg_row, start, block)
        scores = (
            lax.dot_general(
                query_rows, key_head, CONTRACT_COLUMNS, preferred_element_type=jnp.float32
            )
            * scale
        )
        scores = jnp.where(seg_rows[:, None] == seg_row[None, :], scores, -1e30)
        chance = jnp.exp(scores - logsum[index][:, None])
        grad_chance = lax.dot_general(
            grad_rows, value_head, CONTRACT_COLUMNS, preferred_element_type=jnp.float32
        )
        inner = jnp.sum(chance * grad_chance, axis=1, keepdims=True)
        grad_scores = (chance * (grad_chance - inner) * scale).astype(jnp.bfloat16)
        grad_query = jnp.dot(grad_scores, key_head, preferred_element_type=jnp.float32)
        key_part = lax.dot_general(
            grad_scores, query_rows, CONTRACT_ROWS, preferred_element_type=jnp.float32
        )
        value_part = lax.dot_general(
            chance.astype(jnp.bfloat16),
            grad_rows,
            CONTRACT_ROWS,
            preferred_element_type=jnp.float32,
        )
        old_keys = lax.dynamic_slice(grad_keys, (0, column), (length, depth))
        old_values = lax.dynamic_slice(grad_values, (0, column), (length, depth))
        grad_keys = lax.dynamic_update_slice(grad_keys, old_keys + key_part, (0, column))
        grad_values = lax.dynamic_update_slice(grad_values, old_values + value_part, (0, column))
        return ((grad_keys, grad_values), grad_query)

    empty = jnp.zeros((length, width), jnp.float32)
    (grad_keys, grad_values), grad_queries = lax.scan(
        one, (empty, empty), jnp.arange(count * heads)
    )
    return (assemble(grad_queries, count, heads), grad_keys, grad_values)


def widen(local, full_size, offset):
    return lax.dynamic_update_slice_in_dim(jnp.zeros((full_size,), jnp.float32), local, offset, 0)


def on_device(
    tokens,
    segments,
    query_proj,
    query_bias,
    key_proj,
    value_proj,
    value_bias,
    merge_proj,
    merge_bias,
    first_gain,
    first_shift,
    expand_proj,
    expand_bias,
    shrink_proj,
    shrink_bias,
    second_gain,
    second_shift,
    cotangent,
):
    part = lax.axis_index("tensor")
    query_full, key_full, value_full, merge_full, expand_full, shrink_full = (
        lax.all_gather(query_proj, "dp", axis=0, tiled=True),
        lax.all_gather(key_proj, "dp", axis=0, tiled=True),
        lax.all_gather(value_proj, "dp", axis=0, tiled=True),
        lax.all_gather(merge_proj, "dp", axis=1, tiled=True),
        lax.all_gather(expand_proj, "dp", axis=0, tiled=True),
        lax.all_gather(shrink_proj, "dp", axis=1, tiled=True),
    )
    (
        bias_query,
        bias_value,
        bias_merge,
        gain_first,
        shift_first,
        bias_expand,
        bias_shrink,
        gain_second,
        shift_second,
    ) = (
        lax.all_gather(query_bias, ("dp", "tensor"), axis=0, tiled=True),
        lax.all_gather(value_bias, ("dp", "tensor"), axis=0, tiled=True),
        lax.all_gather(merge_bias, ("dp", "tensor"), axis=0, tiled=True),
        lax.all_gather(first_gain, ("dp", "tensor"), axis=0, tiled=True),
        lax.all_gather(first_shift, ("dp", "tensor"), axis=0, tiled=True),
        lax.all_gather(expand_bias, ("dp", "tensor"), axis=0, tiled=True),
        lax.all_gather(shrink_bias, ("dp", "tensor"), axis=0, tiled=True),
        lax.all_gather(second_gain, ("dp", "tensor"), axis=0, tiled=True),
        lax.all_gather(second_shift, ("dp", "tensor"), axis=0, tiled=True),
    )
    width = query_full.shape[1]
    units = expand_full.shape[1]
    model_width = bias_query.shape[0]
    unit_count = bias_expand.shape[0]
    local_query_bias = lax.dynamic_slice_in_dim(bias_query, part * width, width)
    local_value_bias = lax.dynamic_slice_in_dim(bias_value, part * width, width)
    local_expand_bias = lax.dynamic_slice_in_dim(bias_expand, part * units, units)
    full_tokens, full_segments = (
        lax.all_gather(tokens, "tensor", axis=0, tiled=True),
        lax.all_gather(segments, "tensor", axis=1, tiled=True),
    )
    seg_row = full_segments[0]
    query = (
        jnp.dot(full_tokens, query_full, preferred_element_type=jnp.float32) + local_query_bias
    ).astype(jnp.bfloat16)
    keys = jnp.dot(full_tokens, key_full, preferred_element_type=jnp.float32).astype(jnp.bfloat16)
    values = (
        jnp.dot(full_tokens, value_full, preferred_element_type=jnp.float32) + local_value_bias
    ).astype(jnp.bfloat16)
    context, logsum = attend(query, keys, values, seg_row, HD)
    context_low = context.astype(jnp.bfloat16)
    attended = lax.psum_scatter(
        jnp.dot(context_low, merge_full, preferred_element_type=jnp.float32).astype(jnp.bfloat16),
        "tensor",
        scatter_dimension=0,
        tiled=True,
    ).astype(jnp.float32)
    mixed = tokens.astype(jnp.float32) + attended + bias_merge
    hidden = normalize(mixed, gain_first, shift_first)
    full_hidden = lax.all_gather(hidden.astype(jnp.bfloat16), "tensor", axis=0, tiled=True)
    inner = (
        jnp.dot(full_hidden, expand_full, preferred_element_type=jnp.float32) + local_expand_bias
    )
    active = gelu_exact(inner).astype(jnp.bfloat16)
    summed = (
        hidden
        + lax.psum_scatter(
            jnp.dot(active, shrink_full, preferred_element_type=jnp.float32).astype(jnp.bfloat16),
            "tensor",
            scatter_dimension=0,
            tiled=True,
        ).astype(jnp.float32)
        + bias_shrink
    )
    result, pull_second = jax.vjp(normalize, summed, gain_second, shift_second)
    output = result.astype(jnp.bfloat16)
    grad_summed, grad_gain_second, grad_shift_second = pull_second(cotangent.astype(jnp.float32))
    grad_bias_shrink = jnp.sum(grad_summed, axis=0)
    full_grad_summed = lax.all_gather(
        grad_summed.astype(jnp.bfloat16), "tensor", axis=0, tiled=True
    )
    shrink_local = lax.dot_general(
        active, full_grad_summed, CONTRACT_ROWS, preferred_element_type=jnp.float32
    )
    grad_active = lax.dot_general(
        full_grad_summed, shrink_full, CONTRACT_COLUMNS, preferred_element_type=jnp.float32
    )
    grad_inner = jax.vjp(gelu_exact, inner)[1](grad_active)[0]
    expand_bias_term = widen(jnp.sum(grad_inner, axis=0), unit_count, part * units)
    inner_low = grad_inner.astype(jnp.bfloat16)
    expand_local = lax.dot_general(
        full_hidden, inner_low, CONTRACT_ROWS, preferred_element_type=jnp.float32
    )
    grad_hidden = grad_summed + lax.psum_scatter(
        lax.dot_general(
            inner_low, expand_full, CONTRACT_COLUMNS, preferred_element_type=jnp.float32
        ).astype(jnp.bfloat16),
        "tensor",
        scatter_dimension=0,
        tiled=True,
    ).astype(jnp.float32)
    grad_mixed, grad_gain_first, grad_shift_first = jax.vjp(
        normalize, mixed, gain_first, shift_first
    )[1](grad_hidden)
    grad_bias_merge = jnp.sum(grad_mixed, axis=0)
    full_grad_mixed = lax.all_gather(grad_mixed.astype(jnp.bfloat16), "tensor", axis=0, tiled=True)
    merge_local = lax.dot_general(
        context_low, full_grad_mixed, CONTRACT_ROWS, preferred_element_type=jnp.float32
    )
    grad_context = lax.dot_general(
        full_grad_mixed, merge_full, CONTRACT_COLUMNS, preferred_element_type=jnp.float32
    ).astype(jnp.bfloat16)
    grad_query, grad_keys, grad_values = attend_back(
        query, keys, values, grad_context, logsum, seg_row, HD
    )
    grad_bias_query = jnp.sum(grad_query, axis=0)
    grad_bias_value = jnp.sum(grad_values, axis=0)
    query_low = grad_query.astype(jnp.bfloat16)
    key_low = grad_keys.astype(jnp.bfloat16)
    value_low = grad_values.astype(jnp.bfloat16)
    query_local = lax.dot_general(
        full_tokens, query_low, CONTRACT_ROWS, preferred_element_type=jnp.float32
    )
    key_local = lax.dot_general(
        full_tokens, key_low, CONTRACT_ROWS, preferred_element_type=jnp.float32
    )
    value_local = lax.dot_general(
        full_tokens, value_low, CONTRACT_ROWS, preferred_element_type=jnp.float32
    )
    total = lax.dot_general(
        query_low, query_full, CONTRACT_COLUMNS, preferred_element_type=jnp.float32
    )
    total = total + lax.dot_general(
        key_low, key_full, CONTRACT_COLUMNS, preferred_element_type=jnp.float32
    )
    tokens_grad = (
        grad_mixed
        + lax.psum_scatter(
            (
                total
                + lax.dot_general(
                    value_low, value_full, CONTRACT_COLUMNS, preferred_element_type=jnp.float32
                )
            ).astype(jnp.bfloat16),
            "tensor",
            scatter_dimension=0,
            tiled=True,
        ).astype(jnp.float32)
    ).astype(jnp.bfloat16)
    (
        qbiasgrad,
        vbiasgrad,
        mbiasgrad,
        fgaingrad,
        fshiftgrad,
        ebiasgrad,
        sbiasgrad,
        sgaingrad,
        sshiftgrad,
    ) = (
        lax.psum_scatter(
            widen(grad_bias_query, model_width, part * width),
            ("dp", "tensor"),
            scatter_dimension=0,
            tiled=True,
        ),
        lax.psum_scatter(
            widen(grad_bias_value, model_width, part * width),
            ("dp", "tensor"),
            scatter_dimension=0,
            tiled=True,
        ),
        lax.psum_scatter(grad_bias_merge, ("dp", "tensor"), scatter_dimension=0, tiled=True),
        lax.psum_scatter(grad_gain_first, ("dp", "tensor"), scatter_dimension=0, tiled=True),
        lax.psum_scatter(grad_shift_first, ("dp", "tensor"), scatter_dimension=0, tiled=True),
        lax.psum_scatter(expand_bias_term, ("dp", "tensor"), scatter_dimension=0, tiled=True),
        lax.psum_scatter(grad_bias_shrink, ("dp", "tensor"), scatter_dimension=0, tiled=True),
        lax.psum_scatter(grad_gain_second, ("dp", "tensor"), scatter_dimension=0, tiled=True),
        lax.psum_scatter(grad_shift_second, ("dp", "tensor"), scatter_dimension=0, tiled=True),
    )
    querygrad, keygrad, valuegrad, mergegrad, expandgrad, shrinkgrad = (
        lax.psum_scatter(query_local, "dp", scatter_dimension=0, tiled=True),
        lax.psum_scatter(key_local, "dp", scatter_dimension=0, tiled=True),
        lax.psum_scatter(value_local, "dp", scatter_dimension=0, tiled=True),
        lax.psum_scatter(merge_local, "dp", scatter_dimension=1, tiled=True),
        lax.psum_scatter(expand_local, "dp", scatter_dimension=0, tiled=True),
        lax.psum_scatter(shrink_local, "dp", scatter_dimension=1, tiled=True),
    )
    return (
        output,
        tokens_grad,
        querygrad,
        qbiasgrad,
        keygrad,
        valuegrad,
        vbiasgrad,
        mergegrad,
        mbiasgrad,
        fgaingrad,
        fshiftgrad,
        expandgrad,
        ebiasgrad,
        shrinkgrad,
        sbiasgrad,
        sgaingrad,
        sshiftgrad,
    )


def solution(mesh):
    return jax.shard_map(
        on_device,
        mesh=mesh,
        in_specs=(
            P(("dp", "tensor"), None),
            P("dp", "tensor"),
            P("dp", "tensor"),
            P(("dp", "tensor")),
            P("dp", "tensor"),
            P("dp", "tensor"),
            P(("dp", "tensor")),
            P("tensor", "dp"),
            P(("dp", "tensor")),
            P(("dp", "tensor")),
            P(("dp", "tensor")),
            P("dp", "tensor"),
            P(("dp", "tensor")),
            P("tensor", "dp"),
            P(("dp", "tensor")),
            P(("dp", "tensor")),
            P(("dp", "tensor")),
            P(("dp", "tensor"), None),
        ),
        out_specs=(
            P(("dp", "tensor"), None),
            P(("dp", "tensor"), None),
            P("dp", "tensor"),
            P(("dp", "tensor")),
            P("dp", "tensor"),
            P("dp", "tensor"),
            P(("dp", "tensor")),
            P("tensor", "dp"),
            P(("dp", "tensor")),
            P(("dp", "tensor")),
            P(("dp", "tensor")),
            P("dp", "tensor"),
            P(("dp", "tensor")),
            P("tensor", "dp"),
            P(("dp", "tensor")),
            P(("dp", "tensor")),
            P(("dp", "tensor")),
        ),
        check_vma=False,
    )
```

profile of v0, /device:TPU:0, one launch (start us, length us, event | category | flops | bytes accessed | tf_op | source)
XLA Modules:
  0.0 1345.1 jit_solution(11370294428568450697)
XLA Ops:
  15.5 43.1 %all-reduce.19 = (f32[768]{0:T(1024)}, f32[768]{0:T(1024)}, f32[768]{0:T(1024)S(1)}, f32[768]{0:T(1024)S(1)}, f32[768]{0:T(1024)S(1)}, /*index=5*/f32[3072]{0:T(1024)}, f32[768]{0:T(1024)}, f32[768]{0:T(1024)}) all-reduce(f32[768]{0:T(1024)S(1)} %dynamic-update-slice.4, ...), channel_id=1, replica_groups=mesh['dp'=8,'tensor'=4] {'dp','tensor'}, use_global_device_ids=true, to_apply=%add.4 | all-reduce | flops 8448 | bytes 67584
  60.3 5.6 all_gather.60
  65.9 33.4 %all_gather.62 = bf16[768,192]{1,0:T(8,128)(2,1)} all-gather(bf16[96,192]{1,0:T(8,128)(2,1)} %param.24), channel_id=1, replica_groups=mesh['dp'=8,'tensor'=4] {'dp'}, dimensions={0}, use_global_device_ids=true | all-gather | bytes 331776 | tf_op jit(solution)/shard_map/all_gather | solution.py:145
  99.2 33.3 %all_gather.65 = bf16[768,192]{1,0:T(8,128)(2,1)} all-gather(bf16[96,192]{1,0:T(8,128)(2,1)} %param.27), channel_id=1, replica_groups=mesh['dp'=8,'tensor'=4] {'dp'}, dimensions={0}, use_global_device_ids=true | all-gather | bytes 331776 | tf_op jit(solution)/shard_map/all_gather | solution.py:147
  132.5 31.3 %all_gather.64 = bf16[768,192]{1,0:T(8,128)(2,1)S(1)} all-gather(bf16[96,192]{1,0:T(8,128)(2,1)} %param.26), channel_id=1, replica_groups=mesh['dp'=8,'tensor'=4] {'dp'}, dimensions={0}, use_global_device_ids=true | all-gather | bytes 331776 | tf_op jit(solution)/shard_map/all_gather | solution.py:146
  163.8 33.0 %all_gather.67 = bf16[192,768]{0,1:T(8,128)(2,1)} all-gather(bf16[192,96]{0,1:T(8,128)(2,1)S(1)} %copy.61), channel_id=1, replica_groups=mesh['dp'=8,'tensor'=4] {'dp'}, dimensions={1}, use_global_device_ids=true | all-gather | bytes 331776 | tf_op jit(solution)/shard_map/all_gather | solution.py:148
  197.7 4.2 fusion.30
  213.0 150.0 %while.32 = (s32[]{:T(128)}, bf16[12,512,64]{1,2,0:T(8,128)(2,1)}, f32[12,512]{1,0:T(8,128)}, s32[12]{0:T(128)S(1)}, s32[2048]{0:T(1024)S(1)}, /*index=5*/s32[1,...) while((s32[]{:T(128)}, bf16[12,512,64]{1,2,0:T(8,128)(2,1)}, ...), condition=%wide.region_3.4_spmd.clone, body=%wide.region_0.3_spmd.sunk.clone | while | flops 277872128 | bytes 33853836 | solution.py:63
  221.6 3.9 fusion.127
  234.1 3.9 fusion.127
  246.6 3.9 fusion.127
  259.1 3.9 fusion.127
  271.6 3.9 fusion.127
  284.1 3.9 fusion.127
  296.6 3.9 fusion.127
  321.6 3.9 fusion.127
  346.6 3.9 fusion.127
  369.3 37.0 %reduce-scatter.19.cloned.1.call-done = bf16[512,768]{1,0:T(8,128)(2,1)} async-done(((bf16[2048,768]{1,0:T(8,128)(2,1)}), bf16[512,768]{1,0:T(8,128)(2,1)}) %reduce-scatter.19.cloned.1.call-update) | async-done | bytes 786448 | tf_op jit(solution)/shard_map/reduce_scatter | solution.py:194
  412.4 29.0 %all-gather.9.cloned.1.call-done = bf16[2048,768]{1,0:T(8,128)(2,1)} async-done(((bf16[512,768]{1,0:T(8,128)(2,1)}), bf16[2048,768]{1,0:T(8,128)(2,1)}) %all-gather.9.cloned.1.call-update) | async-done | bytes 3145744 | tf_op jit(solution)/shard_map/all_gather | solution.py:202
  441.3 19.0 %multiply_convert_fusion.1 = (bf16[2048,768]{1,0:T(8,128)(2,1)}, f32[2048,768]{1,0:T(8,128)}, f32[2048,768]{1,0:T(8,128)}) fusion(f32[768]{0:T(1024)S(1)} %dynamic_slice.96, bf16[2048,768]{1,0:T(8,128)(2,1)} %all-gather.9.cloned.1.call-done, bf16[768,768]{1,0:T(8,128)(2,1)} %all-gather.11.cloned.1.call-done), kind=kOutput, calls=%fused_computation.39 | convolution fusion | flops 2519728128 | bytes 20057088 | tf_op jit(solution)/shard_map/dot_general | solution.py:204
  460.3 24.9 %all-gather.13.cloned.1.call-done = bf16[768,768]{0,1:T(8,128)(2,1)} async-done(((bf16[768,96]{0,1:T(8,128)(2,1)}), bf16[768,768]{0,1:T(8,128)(2,1)}) %all-gather.13.cloned.1.call-update) | async-done | bytes 1179664 | tf_op jit(solution)/shard_map/all_gather | solution.py:150
  485.2 6.5 convolution_convert_fusion.1
  491.8 36.3 %reduce-scatter.21.cloned.1.call-done = bf16[512,768]{1,0:T(8,128)(2,1)} async-done(((bf16[2048,768]{1,0:T(8,128)(2,1)}), bf16[512,768]{1,0:T(8,128)(2,1)}) %reduce-scatter.21.cloned.1.call-update) | async-done | bytes 786448 | tf_op jit(solution)/shard_map/reduce_scatter | solution.py:209
  534.3 28.5 %all-gather.15.cloned.1.call-done = bf16[2048,768]{1,0:T(8,128)(2,1)} async-done(((bf16[512,768]{1,0:T(8,128)(2,1)}), bf16[2048,768]{1,0:T(8,128)(2,1)}) %all-gather.15.cloned.1.call-update) | async-done | bytes 3145744 | tf_op jit(solution)/shard_map/all_gather | solution.py:221
  562.8 11.1 fusion.50
  575.5 4.1 convolution_convert_fusion
  579.7 37.9 %reduce-scatter.23.cloned.1.call-done = bf16[512,768]{1,0:T(8,128)(2,1)} async-done(((bf16[2048,768]{1,0:T(8,128)(2,1)}), bf16[512,768]{1,0:T(8,128)(2,1)}) %reduce-scatter.23.cloned.1.call-update) | async-done | bytes 786448 | tf_op jit(solution)/shard_map/reduce_scatter | solution.py:236
  625.4 28.4 %all-gather.17.cloned.1.call-done = bf16[2048,768]{1,0:T(8,128)(2,1)} async-done(((bf16[512,768]{1,0:T(8,128)(2,1)}), bf16[2048,768]{1,0:T(8,128)(2,1)}) %all-gather.17.cloned.1.call-update) | async-done | bytes 3145744 | tf_op jit(solution)/shard_map/all_gather | solution.py:248
  653.8 4.0 convolution_convert_fusion.3
  658.1 228.1 %while.33 = (s32[]{:T(128)}, f32[2048,192]{0,1:T(8,128)S(1)}, f32[2048,192]{0,1:T(8,128)S(1)}, f32[12,512,64]{1,2,0:T(8,128)}, s32[12]{0:T(128)S(1)}, /*index=5*...) while((s32[]{:T(128)}, f32[2048,192]{0,1:T(8,128)S(1)}, ...), condition=%wide.region_17.18_spmd.clone, body=%wide.region_15.17_spmd.sunk.clone | while | flops 682884608 | bytes 55606196 | solution.py:113
  660.7 3.9 fusion.136
  667.3 4.0 multiply_reduce_fusion.7
  679.7 3.9 fusion.136
  686.3 4.0 multiply_reduce_fusion.7
  698.7 3.9 fusion.136
  705.4 4.0 multiply_reduce_fusion.7
  717.7 3.9 fusion.136
  724.4 4.0 multiply_reduce_fusion.7
  736.7 3.9 fusion.136
  743.4 4.0 multiply_reduce_fusion.7
  755.7 3.9 fusion.136
  762.4 4.0 multiply_reduce_fusion.7
  774.7 3.9 fusion.136
  781.4 4.0 multiply_reduce_fusion.7
  793.7 3.9 fusion.136
  800.4 4.0 multiply_reduce_fusion.7
  812.7 3.9 fusion.136
  819.4 4.0 multiply_reduce_fusion.7
  831.7 3.9 fusion.136
  838.4 4.0 multiply_reduce_fusion.7
  850.7 3.9 fusion.136
  857.4 4.0 multiply_reduce_fusion.7
  869.8 3.9 fusion.136
  876.4 4.0 multiply_reduce_fusion.7
  898.7 6.9 fusion.57
  905.7 6.9 fusion.36
  932.5 22.4 %reduce-scatter.37.cloned.1.call-done = f32[96,192]{1,0:T(8,128)} async-done(((f32[768,192]{1,0:T(8,128)}), f32[96,192]{1,0:T(8,128)}) %reduce-scatter.37.cloned.1.call-update) | async-done | bytes 73744
  956.6 37.7 %reduce-scatter.25.cloned.1.call-done = bf16[512,768]{1,0:T(8,128)(2,1)} async-done(((bf16[2048,768]{1,0:T(8,128)(2,1)}), bf16[512,768]{1,0:T(8,128)(2,1)}) %reduce-scatter.25.cloned.1.call-update) | async-done | bytes 786448 | tf_op jit(solution)/shard_map/reduce_scatter | solution.py:280
  997.1 41.4 %all-reduce.18 = (f32[768]{0:T(1024)S(1)}, f32[768]{0:T(1024)S(1)}, f32[768]{0:T(1024)S(1)}, f32[768]{0:T(1024)S(1)}, f32[768]{0:T(1024)S(1)}, /*index=5*/f32[76...) all-reduce(f32[768]{0:T(1024)S(1)} %dynamic-update-slice.8, ...), channel_id=1, replica_groups=mesh['dp'=8,'tensor'=4] {'dp','tensor'}, use_global_device_ids=true, to_apply=%add.8 | all-reduce | flops 9984 | bytes 79872
  1045.0 23.0 %reduce-scatter.29.cloned.1.call-done = f32[768,96]{0,1:T(8,128)} async-done(((f32[768,768]{0,1:T(8,128)}), f32[768,96]{0,1:T(8,128)}) %reduce-scatter.29.cloned.1.call-update) | async-done | bytes 294928 | tf_op jit(solution)/shard_map/reduce_scatter | solution.py:329
  1068.0 72.3 %reduce-scatter.27.cloned.1.call-done = f32[96,768]{1,0:T(8,128)} async-done(((f32[768,768]{1,0:T(8,128)}), f32[96,768]{1,0:T(8,128)}) %reduce-scatter.27.cloned.1.call-update) | async-done | bytes 294928 | tf_op jit(solution)/shard_map/reduce_scatter | solution.py:328
  1140.3 65.9 %reduce-scatter.31.cloned.1.call-done = f32[96,192]{1,0:T(8,128)} async-done(((f32[768,192]{1,0:T(8,128)}), f32[96,192]{1,0:T(8,128)}) %reduce-scatter.31.cloned.1.call-update) | async-done | bytes 73744
  1206.3 65.5 %reduce-scatter.33.cloned.1.call-done = f32[96,192]{1,0:T(8,128)} async-done(((f32[768,192]{1,0:T(8,128)}), f32[96,192]{1,0:T(8,128)}) %reduce-scatter.33.cloned.1.call-update) | async-done | bytes 73744
  1271.7 65.8 %reduce-scatter.35.cloned.1.call-done = f32[96,192]{1,0:T(8,128)} async-done(((f32[768,192]{1,0:T(8,128)}), f32[96,192]{1,0:T(8,128)}) %reduce-scatter.35.cloned.1.call-update) | async-done | bytes 73744
  (462 shorter events, 268.1 us)
Async XLA Ops:
  8.0 189.7 %all-gather.7.cloned.1.call-start = ((), (), s32[]{:S(2)}) async-start(), calls=%async_computation.10 | async-start | bytes 3932160 | tf_op jit(solution)/shard_map/all_gather | solution.py:181
  8.8 397.5 %reduce-scatter.19.cloned.1.call-start = ((), (), s32[]{:S(2)}) async-start(), calls=%async_computation.11 | async-start | bytes 3932160 | tf_op jit(solution)/shard_map/reduce_scatter | solution.py:194
  163.8 45.6 %copy-start.11 = (bf16[768,192]{1,0:T(8,128)(2,1)}, bf16[768,192]{1,0:T(8,128)(2,1)S(1)}, u32[]{:S(2)}) copy-start(bf16[768,192]{1,0:T(8,128)(2,1)S(1)} %all_gather.64) | copy-start | bytes 884740
  197.7 6.4 copy-start.2
  217.5 4.1 copy-start.10
  230.0 4.1 copy-start.10
  242.5 4.1 copy-start.10
  255.0 4.1 copy-start.10
  267.5 4.1 copy-start.10
  280.0 4.1 copy-start.10
  292.5 4.1 copy-start.10
  305.0 4.1 copy-start.10
  317.5 4.1 copy-start.10
  330.0 4.1 copy-start.10
  342.5 4.1 copy-start.10
  355.0 4.1 copy-start.10
  365.4 40.9 %copy-start.5 = (bf16[512,768]{1,0:T(8,128)(2,1)S(1)}, bf16[512,768]{1,0:T(8,128)(2,1)}, u32[]{:S(2)}) copy-start(bf16[512,768]{1,0:T(8,128)(2,1)} %param.22) | copy-start | bytes 2359300
  368.1 41.3 %copy-start.22 = (f32[768]{0:T(1024)S(1)}, f32[768]{0:T(1024)}, u32[]{:S(2)}) copy-start(f32[768]{0:T(1024)} %get-tuple-element.467) | copy-start | bytes 9220
  368.1 41.3 %copy-start.39 = (f32[768]{0:T(1024)S(1)}, f32[768]{0:T(1024)}, u32[]{:S(2)}) copy-start(f32[768]{0:T(1024)} %get-tuple-element.466) | copy-start | bytes 9220
  368.2 44.2 %all-gather.11.cloned.1.call-start = ((), (), s32[]{:S(2)}) async-start(), calls=%async_computation.13 | async-start | bytes 1327104 | tf_op jit(solution)/shard_map/all_gather | solution.py:149
  368.8 72.6 %all-gather.9.cloned.1.call-start = ((), (), s32[]{:S(2)}) async-start(), calls=%async_computation.12 | async-start | bytes 3932160 | tf_op jit(solution)/shard_map/all_gather | solution.py:202
  409.4 50.9 %copy-start.33 = (f32[512]{0:T(512)}, f32[512]{0:T(512)S(1)}, u32[]{:S(2)}) copy-start(f32[512]{0:T(512)S(1)} %multiply_reduce_fusion.4) | copy-start | bytes 6148
  409.4 118.7 %copy-start.24 = (f32[512]{0:T(512)}, f32[512]{0:T(512)S(1)}, u32[]{:S(2)}) copy-start(f32[512]{0:T(512)S(1)} %fusion.47) | copy-start | bytes 6148
  410.8 74.3 %all-gather.13.cloned.1.call-start = ((), (), s32[]{:S(2)}) async-start(), calls=%async_computation.14 | async-start | bytes 1327104 | tf_op jit(solution)/shard_map/all_gather | solution.py:150
  411.4 116.7 %reduce-scatter.21.cloned.1.call-start = ((), (), s32[]{:S(2)}) async-start(), calls=%async_computation.15 | async-start | bytes 3932160 | tf_op jit(solution)/shard_map/reduce_scatter | solution.py:209
  412.3 48.0 %copy-start.41 = (f32[768]{0:T(1024)}, f32[768]{0:T(1024)S(1)}, u32[]{:S(2)}) copy-start(f32[768]{0:T(1024)S(1)} %dynamic_slice.96) | copy-start | bytes 9220
  491.7 36.4 %copy-start.42 = (f32[768]{0:T(1024)S(1)}, f32[768]{0:T(1024)}, u32[]{:S(2)}) copy-start(f32[768]{0:T(1024)} %get-tuple-element.472) | copy-start | bytes 9220
  491.7 38.8 %copy-start.16 = (bf16[512,768]{1,0:T(8,128)(2,1)S(1)}, bf16[512,768]{1,0:T(8,128)(2,1)}, u32[]{:S(2)}) copy-start(bf16[512,768]{1,0:T(8,128)(2,1)} %param.39) | copy-start | bytes 2359300
  491.7 38.8 %copy-start.27 = (f32[768]{0:T(1024)S(1)}, f32[768]{0:T(1024)}, u32[]{:S(2)}) copy-start(f32[768]{0:T(1024)} %get-tuple-element.473) | copy-start | bytes 9220
  491.7 71.0 %all-gather.15.cloned.1.call-start = ((), (), s32[]{:S(2)}) async-start(), calls=%async_computation.16 | async-start | bytes 3932160 | tf_op jit(solution)/shard_map/all_gather | solution.py:221
  534.1 83.5 %reduce-scatter.23.cloned.1.call-start = ((), (), s32[]{:S(2)}) async-start(), calls=%async_computation.17 | async-start | bytes 3932160 | tf_op jit(solution)/shard_map/reduce_scatter | solution.py:236
  562.8 12.8 copy-start.43
  579.7 74.1 %all-gather.17.cloned.1.call-start = ((), (), s32[]{:S(2)}) async-start(), calls=%async_computation.18 | async-start | bytes 3932160 | tf_op jit(solution)/shard_map/all_gather | solution.py:248
  625.1 329.8 %reduce-scatter.37.cloned.1.call-start = ((), (), s32[]{:S(2)}) async-start(), calls=%async_computation.25 | async-start | bytes 884736
  667.3 4.0 copy-start
  686.3 4.0 copy-start
  705.4 4.0 copy-start
  724.4 4.0 copy-start
  743.4 4.0 copy-start
  762.4 4.0 copy-start
  781.4 4.0 copy-start
  800.4 4.0 copy-start
  819.4 4.0 copy-start
  838.4 4.0 copy-start
  857.4 4.0 copy-start
  876.4 4.0 copy-start
  886.2 3.7 copy-start.15
  892.2 102.1 %reduce-scatter.25.cloned.1.call-start = ((), (), s32[]{:S(2)}) async-start(), calls=%async_computation.19 | async-start | bytes 3932160 | tf_op jit(solution)/shard_map/reduce_scatter | solution.py:280
  898.4 169.6 %reduce-scatter.29.cloned.1.call-start = ((), (), s32[]{:S(2)}) async-start(), calls=%async_computation.21 | async-start | bytes 2654208 | tf_op jit(solution)/shard_map/reduce_scatter | solution.py:329
  905.6 234.7 %reduce-scatter.27.cloned.1.call-start = ((), (), s32[]{:S(2)}) async-start(), calls=%async_computation.20 | async-start | bytes 2654208 | tf_op jit(solution)/shard_map/reduce_scatter | solution.py:328
  912.6 293.6 %reduce-scatter.31.cloned.1.call-start = ((), (), s32[]{:S(2)}) async-start(), calls=%async_computation.22 | async-start | bytes 884736
  918.7 353.0 %reduce-scatter.33.cloned.1.call-start = ((), (), s32[]{:S(2)}) async-start(), calls=%async_computation.23 | async-start | bytes 884736
  924.5 4.0 copy-start.44
  924.6 4.2 copy-start.40
  924.6 412.9 %reduce-scatter.35.cloned.1.call-start = ((), (), s32[]{:S(2)}) async-start(), calls=%async_computation.24 | async-start | bytes 884736
  929.0 68.0 %copy-start.34 = (f32[768]{0:T(1024)S(1)}, f32[768]{0:T(1024)}, u32[]{:S(2)}) copy-start(f32[768]{0:T(1024)} %get-tuple-element.409) | copy-start | bytes 9220
  929.0 68.0 %copy-start.35 = (f32[768]{0:T(1024)S(1)}, f32[768]{0:T(1024)}, u32[]{:S(2)}) copy-start(f32[768]{0:T(1024)} %get-tuple-element.413) | copy-start | bytes 9220
  929.0 68.0 %copy-start.36 = (f32[768]{0:T(1024)S(1)}, f32[768]{0:T(1024)}, u32[]{:S(2)}) copy-start(f32[768]{0:T(1024)} %get-tuple-element.407) | copy-start | bytes 9220
  929.0 68.0 %copy-start.37 = (f32[768]{0:T(1024)S(1)}, f32[768]{0:T(1024)}, u32[]{:S(2)}) copy-start(f32[768]{0:T(1024)} %get-tuple-element.411) | copy-start | bytes 9220
  929.1 68.0 %copy-start.38 = (f32[768]{0:T(1024)S(1)}, f32[768]{0:T(1024)}, u32[]{:S(2)}) copy-start(f32[768]{0:T(1024)} %get-tuple-element.412) | copy-start | bytes 9220
  929.1 114.7 %copy-start.4 = (f32[512,768]{1,0:T(8,128)S(1)}, f32[512,768]{1,0:T(8,128)}, u32[]{:S(2)}) copy-start(f32[512,768]{1,0:T(8,128)} %copy-done.3) | copy-start | bytes 4718596
  929.1 114.7 %copy-start.26 = (f32[512]{0:T(512)S(1)}, f32[512]{0:T(512)}, u32[]{:S(2)}) copy-start(f32[512]{0:T(512)} %copy-done.25) | copy-start | bytes 6148
  929.1 114.7 %copy-start.29 = (f32[768]{0:T(1024)S(1)}, f32[768]{0:T(1024)}, u32[]{:S(2)}) copy-start(f32[768]{0:T(1024)} %get-tuple-element.473) | copy-start | bytes 9220
  929.1 114.7 %copy-start.32 = (f32[512]{0:T(512)S(1)}, f32[512]{0:T(512)}, u32[]{:S(2)}) copy-start(f32[512]{0:T(512)} %copy-done.31) | copy-start | bytes 6148
  (42 other events, 83.7 us)
Sparse Core Ops, SparseCore 0:
  10.4 31.9 all-gather.6
  368.3 37.9 reduce-scatter.18
  534.2 28.5 all-gather.14
  625.2 28.5 all-gather.16
Sparse Core Ops, SparseCore 1:
  370.8 41.5 all-gather.10
  414.5 26.8 all-gather.8
  443.6 41.5 all-gather.12
  491.8 36.3 reduce-scatter.20
  579.7 37.8 reduce-scatter.22
  892.3 62.6 reduce-scatter.36
  957.3 36.9 reduce-scatter.24
  998.6 69.4 reduce-scatter.28
  1072.4 67.9 reduce-scatter.26
  1144.6 61.6 reduce-scatter.30
  1210.0 61.7 reduce-scatter.32
  1276.0 61.5 reduce-scatter.34
where the time goes:
time: 1360 us; the launch traced here: 1350 us
  waiting for transfers between devices  577 us (42%)
  matrix products  307 us (23%)
  blocking collectives  221 us (16%)
  local copies, waits for them, and re-layouts  112 us (8%)
  loops' own time  71.6 us (5%)
  other arithmetic  38.9 us (3%)
  between operations  16.4 us (1%)
    unnamed x20, waiting for transfers between devices  222 us
    unnamed x2, blocking collectives  84.6 us
    reduce_scatter x1, waiting for transfers between devices, on_device(): lax.psum_scatter(expand_local, 'dp', scatter_dimension=0, tiled=True)  72.3 us
    dot_general x24, matrix products, one(): lax.dot_general(query_rows, key_head, CONTRACT_COLUMNS, preferred_element...  70.4 us
    another operation x1, loops' own time, attend_back(): lax.scan(one, (empty, empty), jnp.arange(count * heads))  47.7 us
    dot_general x12, matrix products, one(): lax.dot_general(grad_rows, value_head, CONTRACT_COLUMNS, preferred_elemen...  47.1 us
    dot_general x12, matrix products, one(): context = jnp.dot(chance, value_head, preferred_element_type=jnp.float32)  46.9 us
    reduce_scatter x1, waiting for transfers between devices, on_device(): lax.psum_scatter(lax.dot_general(inner_low, expand_full, CONTRACT_COLUMNS...  37.9 us
  transfers between devices with their start and end apart: 16, of which 15 were waited for; matrix products, arithmetic and copies ran while one was open for 6% of the time, Pallas kernels for 0%

commit v1 on v0

v1 whole, which is shorter than its diff:
```python
import jax, jax.numpy as jnp
from jax import lax
from jax.sharding import PartitionSpec as P
from jax.experimental import pallas as pl
from jax.experimental.pallas import tpu as pltpu

HD=64
BQ=256
BK=256
LOG2E=1.4426950408889634
NN=(((1,),(0,)),((),()))
NT=(((1,),(1,)),((),()))
TN=(((0,),(0,)),((),()))
f32=jnp.float32; bf16=jnp.bfloat16

def head_cols(h, heads):
    start=(h//2)*128
    stop=min(start+128, heads*HD)
    return start, stop

def padded(ref, h, heads, rows):
    start, stop = head_cols(h, heads)
    piece = ref[h*HD:(h+1)*HD, rows]
    if stop-start == HD: return piece
    zero = jnp.zeros_like(piece)
    return jnp.concatenate([piece, zero] if h%2==0 else [zero, piece], axis=0)

def fwd_kernel(lo_ref, hi_ref, flip_ref, q_ref, k_ref, v_ref, segc_ref, segr_ref, o_ref, lse_ref, s_ref):
    heads = q_ref.shape[0]//HD
    i = pl.program_id(0)
    lo = lo_ref[i]; hi = hi_ref[i]; flip = flip_ref[0]
    c = LOG2E * HD**-0.5
    qz = [padded(q_ref, h, heads, slice(None)) for h in range(heads)]
    segq = segr_ref[...]
    def one(kb, peaks):
        start = pl.multiple_of(jnp.bitwise_xor(kb, flip)*BK, BK)
        same = segc_ref[pl.ds(start,BK),:] == segq
        new=[]
        for h in range(heads):
            a,b = head_cols(h, heads)
            s = lax.dot_general(k_ref[pl.ds(start,BK), a:b], qz[h], NN, preferred_element_type=f32)
            s = jnp.where(same, s, -1e30)
            s_ref[h, kb-lo] = s
            new.append(jnp.maximum(peaks[h], jnp.max(s.reshape(BK//8,8,BQ),axis=0)))
        return tuple(new)
    peaks = lax.fori_loop(lo, hi, one, tuple(jnp.full((8,BQ),-1e30,f32) for _ in range(heads)))
    peaks = [jnp.max(p,axis=0,keepdims=True)*c for p in peaks]
    def two(kb, carry):
        sums, outs = carry
        start = pl.multiple_of(jnp.bitwise_xor(kb, flip)*BK, BK)
        ns=[];no=[]
        for h in range(heads):
            p = jnp.exp2(s_ref[h, kb-lo]*c - peaks[h])
            ns.append(sums[h]+jnp.sum(p.reshape(BK//8,8,BQ),axis=0))
            no.append(outs[h]+lax.dot_general(v_ref[h*HD:(h+1)*HD, pl.ds(start,BK)], p.astype(bf16), NN, preferred_element_type=f32))
        return tuple(ns),tuple(no)
    sums, outs = lax.fori_loop(lo, hi, two, (tuple(jnp.zeros((8,BQ),f32) for _ in range(heads)), tuple(jnp.zeros((HD,BQ),f32) for _ in range(heads))))
    for h in range(heads):
        total = jnp.sum(sums[h],axis=0,keepdims=True)
        o_ref[h*HD:(h+1)*HD,:] = (outs[h]/total).astype(bf16)
        lse_ref[h:h+1,:] = peaks[h]+jnp.log2(total)

def attn_fwd(qT,k,vT,segc,segr,lo,hi,flip):
    width,length=qT.shape
    heads=width//HD
    blocks=length//BQ
    return pl.pallas_call(
        fwd_kernel,
        out_shape=(jax.ShapeDtypeStruct((width,length),bf16), jax.ShapeDtypeStruct((heads,length),f32)),
        grid_spec=pltpu.PrefetchScalarGridSpec(num_scalar_prefetch=3, grid=(blocks,),
            in_specs=[pl.BlockSpec((width,BQ),lambda i,*_:(0,i)),
                      pl.BlockSpec((length,width),lambda i,*_:(0,0)),
                      pl.BlockSpec((width,length),lambda i,*_:(0,0)),
                      pl.BlockSpec((length,1),lambda i,*_:(0,0)),
                      pl.BlockSpec((1,BQ),lambda i,*_:(0,i))],
            out_specs=[pl.BlockSpec((width,BQ),lambda i,*_:(0,i)),pl.BlockSpec((heads,BQ),lambda i,*_:(0,i))],
            scratch_shapes=[pltpu.VMEM((heads,length//BK,BK,BQ),f32)]),
        compiler_params=pltpu.CompilerParams(dimension_semantics=("arbitrary",),vmem_limit_bytes=40<<20),
        cost_estimate=pl.CostEstimate(flops=4*length*length//2*width,bytes_accessed=8*length*width,transcendentals=heads*length*length//2),
        name="attention",
    )(lo,hi,flip,qT,k,vT,segc,segr)

def bwd_kernel(lo_ref, hi_ref, flip_ref, q_ref, k_ref, kT_ref, v_ref, do_ref, o_ref, lse_ref, segc_ref, segr_ref,
               dq_ref, dk_ref, dv_ref, qb_ref, vb_ref, dk_acc, dv_acc):
    heads = q_ref.shape[0]//HD
    width = q_ref.shape[0]
    i = pl.program_id(0)
    @pl.when(i==0)
    def _():
        dk_acc[...]=jnp.zeros_like(dk_acc); dv_acc[...]=jnp.zeros_like(dv_acc)
        qb_ref[...]=jnp.zeros_like(qb_ref)
    lo = lo_ref[i]; hi = hi_ref[i]; flip = flip_ref[0]
    scale = HD**-0.5
    c = LOG2E*scale
    qz = [padded(q_ref, h, heads, slice(None)) for h in range(heads)]
    dz = [padded(do_ref, h, heads, slice(None)) for h in range(heads)]
    deltas = [jnp.sum(do_ref[h*HD:(h+1)*HD,:].astype(f32)*o_ref[h*HD:(h+1)*HD,:].astype(f32),axis=0,keepdims=True) for h in range(heads)]
    segq = segr_ref[...]
    def one(kb, dqs):
        start = pl.multiple_of(jnp.bitwise_xor(kb, flip)*BK, BK)
        rows = pl.ds(start,BK)
        same = segc_ref[rows,:] == segq
        out=[]
        parts={}
        for h in range(heads):
            a,b = head_cols(h, heads)
            s = lax.dot_general(k_ref[rows, a:b], qz[h], NN, preferred_element_type=f32)
            p = jnp.exp2(jnp.where(same, s*c - lse_ref[h:h+1,:], -1e30))
            dp = lax.dot_general(v_ref[rows, a:b], dz[h], NN, preferred_element_type=f32)
            ds = (p*((dp-deltas[h])*scale)).astype(bf16)
            dvp = lax.dot_general(p.astype(bf16), dz[h], NT, preferred_element_type=f32)
            dkp = lax.dot_general(ds, qz[h], NT, preferred_element_type=f32)
            if (a,b) in parts: parts[a,b]=(parts[a,b][0]+dkp,parts[a,b][1]+dvp)
            else: parts[a,b]=(dkp,dvp)
            out.append(dqs[h]+lax.dot_general(kT_ref[h*HD:(h+1)*HD, rows], ds, NN, preferred_element_type=f32))
        for (a,b),(dkp,dvp) in parts.items():
            dk_acc[rows,a:b]+=dkp
            dv_acc[rows,a:b]+=dvp
        return tuple(out)
    dqs = lax.fori_loop(lo,hi,one,tuple(jnp.zeros((HD,BQ),f32) for _ in range(heads)))
    for h in range(heads):
        dq_ref[h*HD:(h+1)*HD,:]=dqs[h].astype(bf16)
        part = dqs[h][:,:128]
        for n in range(128,BQ,128): part=part+dqs[h][:,n:n+128]
        qb_ref[h*HD:(h+1)*HD,:]+=part
    @pl.when(i==pl.num_programs(0)-1)
    def _():
        dk_ref[...]=dk_acc[...].astype(bf16)
        dv_ref[...]=dv_acc[...].astype(bf16)
        vb_ref[...]=jnp.sum(dv_acc[...].reshape(dv_acc.shape[0]//8,8,width),axis=0)

def attn_bwd(qT,k,kT,v,doT,oT,lse,segc,segr,lo,hi,flip):
    width,length=qT.shape
    heads=width//HD
    blocks=length//BQ
    col=pl.BlockSpec((width,BQ),lambda i,*_:(0,i))
    row=pl.BlockSpec((length,width),lambda i,*_:(0,0))
    return pl.pallas_call(
        bwd_kernel,
        out_shape=(jax.ShapeDtypeStruct((width,length),bf16), jax.ShapeDtypeStruct((length,width),bf16), jax.ShapeDtypeStruct((length,width),bf16), jax.ShapeDtypeStruct((width,128),f32), jax.ShapeDtypeStruct((8,width),f32)),
        grid_spec=pltpu.PrefetchScalarGridSpec(num_scalar_prefetch=3, grid=(blocks,),
            in_specs=[col,row,pl.BlockSpec((width,length),lambda i,*_:(0,0)),row,col,col,
                      pl.BlockSpec((heads,BQ),lambda i,*_:(0,i)),
                      pl.BlockSpec((length,1),lambda i,*_:(0,0)),
                      pl.BlockSpec((1,BQ),lambda i,*_:(0,i))],
            out_specs=[col,row,row,pl.BlockSpec((width,128),lambda i,*_:(0,0)),pl.BlockSpec((8,width),lambda i,*_:(0,0))],
            scratch_shapes=[pltpu.VMEM((length,width),f32),pltpu.VMEM((length,width),f32)]),
        compiler_params=pltpu.CompilerParams(dimension_semantics=("arbitrary",),vmem_limit_bytes=40<<20),
        cost_estimate=pl.CostEstimate(flops=10*length*length//2*width,bytes_accessed=20*length*width,transcendentals=heads*length*length//2),
        name="attention_back",
    )(lo,hi,flip,qT,k,kT,v,doT,oT,lse,segc,segr)

def spans(seg_row):
    length=seg_row.shape[0]
    first=seg_row[::BQ]; last=seg_row[BQ-1::BQ]
    lo=jnp.sum(seg_row[None,:]<first[:,None],axis=1,dtype=jnp.int32)//BK
    hi=(jnp.sum(seg_row[None,:]<=last[:,None],axis=1,dtype=jnp.int32)+BK-1)//BK
    return lo,hi

EPSILON=1e-12
T=256
RC=32

def row_stats(values):
    centre=jnp.mean(values,axis=1,keepdims=True)
    centred=values-centre
    spread=jnp.mean(centred*centred,axis=1,keepdims=True)
    scale=lax.rsqrt(spread+EPSILON)
    return centred*scale, scale

def fold(values):
    return jnp.sum(values.reshape(values.shape[0]//8,8,values.shape[1]),axis=0)

def ffn_kernel(tok_ref, a0_ref, a1_ref, a2_ref, cot_ref, vec_ref, be_ref,
               e0,e1,e2,e3,
               out_ref, gm_ref, gml_ref, vg_ref, eb_ref, d0,d1,d2,d3,
               we, ws, hl, hlT, hid, xhat, rs1, act, gp, acc, sl, slT, gsum, il, de, dt, wsem, osem):
    es=(e0,e1,e2,e3); ds=(d0,d1,d2,d3)
    rows, width = tok_ref.shape
    blocks=len(es); units=we.shape[2]
    for r in range(blocks):
        pltpu.make_async_copy(es[r].at[:,0:units],we.at[r],wsem.at[0,r]).start()
        pltpu.make_async_copy(es[r].at[:,units:],ws.at[r],wsem.at[1,r]).start()
    mb=vec_ref[0:1,:]; g1=vec_ref[1:2,:]; b1=vec_ref[2:3,:]; sb=vec_ref[3:4,:]; g2=vec_ref[4:5,:]; b2=vec_ref[5:6,:]
    def first(i,_):
        at=pl.ds(pl.multiple_of(i*RC,RC),RC)
        mixed=tok_ref[at,:].astype(f32)+(a0_ref[at,:].astype(f32)+a1_ref[at,:].astype(f32)+a2_ref[at,:].astype(f32))+mb
        z,scale=row_stats(mixed)
        xhat[at,:]=z
        rs1[at,:]=jnp.broadcast_to(scale,(RC,128))
        h=z*g1+b1
        hid[at,:]=h
        hl[at,:]=h.astype(bf16)
        acc[at,:]=jnp.zeros((RC,width),f32)
        return 0
    lax.fori_loop(0,rows//RC,first,0)
    def turn(src,dst):
        def go(i,_):
            at=pl.multiple_of(i*T,T)
            dst[:,pl.ds(at,T)]=jnp.transpose(src[pl.ds(at,T),:].astype(f32)).astype(bf16)
            return 0
        lax.fori_loop(0,rows//T,go,0)
    turn(hl,hlT)
    per=units//T; mt=rows//T
    def forward(r,_):
        for k in range(blocks):
            @pl.when(r==k)
            def _():
                pltpu.make_async_copy(es[k].at[:,0:units],we.at[k],wsem.at[0,k]).wait()
        def tile(j,_):
            n=pl.multiple_of((j//mt)*T,T); m=pl.multiple_of((j%mt)*T,T)
            u=lax.dot_general(hl[pl.ds(m,T),:],we[r,:,pl.ds(n,T)],NN,preferred_element_type=f32)+be_ref[pl.ds(r,1),pl.ds(n,T)]
            cdf=0.5+0.5*lax.erf(u*(0.5**0.5))
            act[r,pl.ds(m,T),pl.ds(n,T)]=(u*cdf).astype(bf16)
            gp[r,pl.ds(m,T),pl.ds(n,T)]=cdf+u*(jnp.exp(-0.5*u*u)*0.3989422804014327)
            return 0
        lax.fori_loop(0,per*mt,tile,0)
        for k in range(blocks):
            @pl.when(r==k)
            def _():
                pltpu.make_async_copy(es[k].at[:,units:],ws.at[k],wsem.at[1,k]).wait()
        def shrink(j,_):
            n=pl.multiple_of((j//mt)*T,T); m=pl.multiple_of((j%mt)*T,T)
            acc[pl.ds(m,T),pl.ds(n,T)]+=lax.dot_general(act[r,pl.ds(m,T),:],ws[r,pl.ds(n,T),:],NT,preferred_element_type=f32)
            return 0
        lax.fori_loop(0,(width//T)*mt,shrink,0)
        return 0
    lax.fori_loop(0,blocks,forward,0)
    def second(i,sums):
        at=pl.ds(pl.multiple_of(i*RC,RC),RC)
        summed=hid[at,:]+acc[at,:]+sb
        z,scale=row_stats(summed)
        out_ref[at,:]=(z*g2+b2).astype(bf16)
        cot=cot_ref[at,:].astype(f32)
        e=cot*g2
        g=(e-jnp.mean(e,axis=1,keepdims=True)-z*jnp.mean(e*z,axis=1,keepdims=True))*scale
        gsum[at,:]=g
        sl[at,:]=g.astype(bf16)
        acc[at,:]=g
        return (sums[0]+fold(cot*z),sums[1]+fold(cot),sums[2]+fold(g))
    zero=jnp.zeros((8,width),f32)
    sg,sh,sbg=lax.fori_loop(0,rows//RC,second,(zero,zero,zero))
    turn(sl,slT)
    def sent(r,slot,k):
        return (pltpu.make_async_copy(de.at[slot],ds[k].at[:,0:units],osem.at[0,slot]),pltpu.make_async_copy(dt.at[slot],ds[k].at[:,units:],osem.at[1,slot]))
    def backward(r,_):
        slot=r%2
        def tile(j,_):
            n=pl.multiple_of((j//mt)*T,T); m=pl.multiple_of((j%mt)*T,T)
            ga=lax.dot_general(sl[pl.ds(m,T),:],ws[r,:,pl.ds(n,T)],NN,preferred_element_type=f32)
            gi=ga*gp[r,pl.ds(m,T),pl.ds(n,T)]
            il[pl.ds(m,T),pl.ds(n,T)]=gi.astype(bf16)
            part=fold(gi)
            eb_ref[r,:,pl.ds(n,T)]=jnp.where(m==0,part,eb_ref[r,:,pl.ds(n,T)]+part)
            return 0
        lax.fori_loop(0,per*mt,tile,0)
        def back(j,_):
            n=pl.multiple_of((j//mt)*T,T); m=pl.multiple_of((j%mt)*T,T)
            acc[pl.ds(m,T),pl.ds(n,T)]+=lax.dot_general(il[pl.ds(m,T),:],we[r,pl.ds(n,T),:],NT,preferred_element_type=f32)
            return 0
        lax.fori_loop(0,(width//T)*mt,back,0)
        for k in range(2,blocks):
            @pl.when(r==k)
            def _():
                for c in sent(r,k%2,k-2): c.wait()
        def grads(j,_):
            n=pl.multiple_of((j//(width//T))*T,T); m=pl.multiple_of((j%(width//T))*T,T)
            dt[slot,pl.ds(m,T),pl.ds(n,T)]=lax.dot_general(slT[pl.ds(m,T),:],act[r,:,pl.ds(n,T)],NN,preferred_element_type=f32).astype(bf16)
            de[slot,pl.ds(m,T),pl.ds(n,T)]=lax.dot_general(hlT[pl.ds(m,T),:],il[:,pl.ds(n,T)],NN,preferred_element_type=f32).astype(bf16)
            return 0
        lax.fori_loop(0,(width//T)*per,grads,0)
        for k in range(blocks):
            @pl.when(r==k)
            def _():
                for c in sent(r,k%2,k): c.start()
        return 0
    lax.fori_loop(0,blocks,backward,0)
    def last(i,sums):
        at=pl.ds(pl.multiple_of(i*RC,RC),RC)
        g=acc[at,:]
        z=xhat[at,:]
        e=g*g1
        gm=(e-jnp.mean(e,axis=1,keepdims=True)-z*jnp.mean(e*z,axis=1,keepdims=True))*rs1[at,0:1]
        gm_ref[at,:]=gm
        gml_ref[at,:]=gm.astype(bf16)
        return (sums[0]+fold(g*z),sums[1]+fold(g),sums[2]+fold(gm))
    fg,fs,mbg=lax.fori_loop(0,rows//RC,last,(zero,zero,zero))
    for n,v in enumerate((mbg,fg,fs,sbg,sg,sh)):
        vg_ref[n]=v
    for k in range(max(0,blocks-2),blocks):
        for c in sent(k,k%2,k): c.wait()

def ffn(tok,a0,a1,a2,cot,vec,be,es):
    rows,width=tok.shape; blocks=len(es); units=es[0].shape[1]//2
    v=pl.BlockSpec(memory_space=pltpu.VMEM); h=pl.BlockSpec(memory_space=pltpu.HBM)
    g=jax.ShapeDtypeStruct((width,2*units),bf16)
    V=pltpu.VMEM
    return pl.pallas_call(
        ffn_kernel,
        out_shape=(jax.ShapeDtypeStruct((rows,width),bf16),jax.ShapeDtypeStruct((rows,width),f32),jax.ShapeDtypeStruct((rows,width),bf16),
                   jax.ShapeDtypeStruct((6,8,width),f32),jax.ShapeDtypeStruct((blocks,8,units),f32))+(g,)*blocks,
        in_specs=[v]*7+[h]*blocks,
        out_specs=[v]*5+[h]*blocks,
        scratch_shapes=[V((blocks,width,units),bf16),V((blocks,width,units),bf16),
            V((rows,width),bf16),V((width,rows),bf16),V((rows,width),f32),V((rows,width),f32),V((rows,128),f32),
            V((blocks,rows,units),bf16),V((blocks,rows,units),f32),V((rows,width),f32),V((rows,width),bf16),V((width,rows),bf16),V((rows,width),f32),
            V((rows,units),bf16),V((2,width,units),bf16),V((2,width,units),bf16),
            pltpu.SemaphoreType.DMA((2,blocks)),pltpu.SemaphoreType.DMA((2,2))],
        compiler_params=pltpu.CompilerParams(vmem_limit_bytes=60<<20),
        cost_estimate=pl.CostEstimate(flops=12*rows*width*units*blocks,bytes_accessed=8*blocks*width*units,transcendentals=2*rows*units*blocks),
        name="feed_forward",
    )(tok,a0,a1,a2,cot,vec,be,*es)

def exchange(value, bit):
    return lax.ppermute(value, "tensor", [(i, i ^ bit) for i in range(4)])


def gather_rows(own):
    across = exchange(own, 2)
    return jnp.concatenate([own, exchange(own, 1), across, exchange(across, 1)], axis=0)


def scatter_rows(partial):
    rows = partial.shape[0] // 4
    low = partial.astype(bf16)
    piece = lambda r: low[r * rows : (r + 1) * rows]
    beside = exchange(jnp.concatenate([piece(1), piece(3)], axis=0), 1)
    ahead = (piece(2).astype(f32) + beside[rows:].astype(f32)).astype(bf16)
    return piece(0), beside[:rows], exchange(ahead, 2)


def on_device(
    tokens,
    segments,
    query_proj,
    query_bias,
    key_proj,
    value_proj,
    value_bias,
    merge_proj,
    merge_bias,
    first_gain,
    first_shift,
    expand_proj,
    expand_bias,
    shrink_proj,
    shrink_bias,
    second_gain,
    second_shift,
    cotangent,
):
    everyone = ("dp", "tensor")
    part = lax.axis_index("tensor")
    dp = lax.axis_size("dp")
    world = dp * 4
    width = query_proj.shape[1]
    units = expand_proj.shape[1]
    model = width * 4
    share = model // world
    unit_share = units * 4 // world

    shard = jnp.concatenate([query_proj, key_proj, value_proj, merge_proj.T], axis=1)
    attn_w = lax.all_gather(shard, "dp", axis=0, tiled=True)
    wide = jnp.concatenate([expand_proj, shrink_proj.T], axis=1)
    w0 = lax.all_gather(wide, "dp", axis=0, tiled=True)
    w2 = lax.all_gather(exchange(wide, 2), "dp", axis=0, tiled=True)
    w1 = exchange(w0, 1)
    w3 = exchange(w2, 1)
    own = jnp.concatenate(
        [query_bias, value_bias, merge_bias, first_gain, first_shift, shrink_bias, second_gain, second_shift, expand_bias]
    )
    slots = -(-own.shape[0] // 1024) * 8
    own = jnp.pad(own, (0, slots * 128 - own.shape[0])).reshape(1, slots, 128)
    vectors = lax.all_to_all(jnp.broadcast_to(own, (world, slots, 128)), everyone, 0, 0, tiled=True)
    vectors = vectors.reshape(world, slots * 128)
    whole = [vectors[:, n * share : (n + 1) * share].reshape(model) for n in range(8)]
    unit_bias = vectors[:, 8 * share : 8 * share + unit_share].reshape(4, units)
    flips = jnp.bitwise_xor(jnp.arange(4), part)
    unit_bias = jnp.take(unit_bias, flips, axis=0)
    query_b = lax.dynamic_slice_in_dim(whole[0], part * width, width)
    value_b = lax.dynamic_slice_in_dim(whole[1], part * width, width)
    rows_b = jnp.stack(whole[2:8])

    full = gather_rows(tokens)
    seg = gather_rows(segments.reshape(-1))
    segc, segr = seg[:, None], seg[None, :]
    lo, hi = spans(seg)
    flip = (part * (tokens.shape[0] // BK)).astype(jnp.int32).reshape(1)
    wq, wk, wv, wm = (attn_w[:, n * width : (n + 1) * width] for n in range(4))
    dot = lambda a, b, dims: lax.dot_general(a, b, dims, preferred_element_type=f32)
    query_t = (dot(wq, full, (((0,), (1,)), ((), ()))) + query_b[:, None]).astype(bf16)
    key_t = dot(wk, full, (((0,), (1,)), ((), ()))).astype(bf16)
    value_t = (dot(wv, full, (((0,), (1,)), ((), ()))) + value_b[:, None]).astype(bf16)
    keys = dot(full, wk, NN).astype(bf16)
    values = (dot(full, wv, NN) + value_b).astype(bf16)
    context_t, logsum = attn_fwd(query_t, keys, value_t, segc, segr, lo, hi, flip)
    a0, a1, a2 = scatter_rows(dot(context_t, wm, (((0,), (1,)), ((), ()))))

    out = ffn(tokens, a0, a1, a2, cotangent, rows_b, unit_bias, [w0, w1, w2, w3])
    output, grad_mixed, mixed_low, row_sums, unit_sums = out[:5]
    g0, g1, g2, g3 = out[5:]

    full_mixed = gather_rows(mixed_low)
    grad_context_t = dot(wm, full_mixed, (((0,), (1,)), ((), ()))).astype(bf16)
    dq_t, dk, dv, q_sums, v_sums = attn_bwd(
        query_t, keys, key_t, values, grad_context_t, context_t, logsum, segc, segr, lo, hi, flip
    )
    total = dot(dq_t, wq, (((0,), (1,)), ((), ()))) + dot(dk, wk, NT) + dot(dv, wv, NT)
    b0, b1, b2 = scatter_rows(total)
    tokens_grad = (grad_mixed + (b0.astype(f32) + b1.astype(f32) + b2.astype(f32))).astype(bf16)

    merge_local = dot(full_mixed, context_t, (((0,), (1,)), ((), ())))
    query_local = dot(full, dq_t, (((0,), (1,)), ((), ())))
    key_local = dot(full, dk, TN)
    value_local = dot(full, dv, TN)
    attn_local = jnp.concatenate([query_local, key_local, value_local, merge_local], axis=1).astype(bf16)
    swapped = lax.all_to_all(attn_local, "dp", 0, 0, tiled=True)
    attn_grad = jnp.sum(swapped.reshape(dp, -1, model).astype(f32), axis=0)
    querygrad, keygrad, valuegrad, mergegrad = (attn_grad[:, n * width : (n + 1) * width] for n in range(4))

    near = (g0.astype(f32) + exchange(g1, 1).astype(f32)).astype(bf16)
    far = (g2.astype(f32) + exchange(g3, 1).astype(f32)).astype(bf16)
    wide_local = (near.astype(f32) + exchange(far, 2).astype(f32)).astype(bf16)
    wide_grad = lax.psum_scatter(wide_local, "dp", scatter_dimension=0, tiled=True).astype(f32)
    expandgrad = wide_grad[:, :units]
    shrinkgrad = wide_grad[:, units:].T

    zero = jnp.zeros((4, width), f32)
    q_all = lax.dynamic_update_slice(zero, jnp.sum(q_sums, axis=1)[None], (part, 0)).reshape(world, share)
    v_all = lax.dynamic_update_slice(zero, jnp.sum(v_sums, axis=0)[None], (part, 0)).reshape(world, share)
    u_all = jnp.take(jnp.sum(unit_sums, axis=1), flips, axis=0).reshape(world, unit_share)
    row_all = [v.reshape(world, share) for v in jnp.sum(row_sums, axis=1)]
    send = jnp.concatenate([q_all, v_all] + row_all + [u_all], axis=1)
    send = jnp.pad(send, ((0, 0), (0, slots * 128 - send.shape[1]))).reshape(world, slots, 128)
    got = jnp.sum(lax.all_to_all(send, everyone, 0, 0, tiled=True).reshape(world, slots * 128), axis=0)
    small = [got[n * share : (n + 1) * share] for n in range(8)]
    qbiasgrad, vbiasgrad, mbiasgrad, fgaingrad, fshiftgrad, sbiasgrad, sgaingrad, sshiftgrad = small
    ebiasgrad = got[8 * share : 8 * share + unit_share]
    return (
        output,
        tokens_grad,
        querygrad,
        qbiasgrad,
        keygrad,
        valuegrad,
        vbiasgrad,
        mergegrad.T,
        mbiasgrad,
        fgaingrad,
        fshiftgrad,
        expandgrad,
        ebiasgrad,
        shrinkgrad,
        sbiasgrad,
        sgaingrad,
        sshiftgrad,
    )


def solution(mesh):
    return jax.shard_map(
        on_device,
        mesh=mesh,
        in_specs=(
            P(("dp", "tensor"), None),
            P("dp", "tensor"),
            P("dp", "tensor"),
            P(("dp", "tensor")),
            P("dp", "tensor"),
            P("dp", "tensor"),
            P(("dp", "tensor")),
            P("tensor", "dp"),
            P(("dp", "tensor")),
            P(("dp", "tensor")),
            P(("dp", "tensor")),
            P("dp", "tensor"),
            P(("dp", "tensor")),
            P("tensor", "dp"),
            P(("dp", "tensor")),
            P(("dp", "tensor")),
            P(("dp", "tensor")),
            P(("dp", "tensor"), None),
        ),
        out_specs=(
            P(("dp", "tensor"), None),
            P(("dp", "tensor"), None),
            P("dp", "tensor"),
            P(("dp", "tensor")),
            P("dp", "tensor"),
            P("dp", "tensor"),
            P(("dp", "tensor")),
            P("tensor", "dp"),
            P(("dp", "tensor")),
            P(("dp", "tensor")),
            P(("dp", "tensor")),
            P("dp", "tensor"),
            P(("dp", "tensor")),
            P("tensor", "dp"),
            P(("dp", "tensor")),
            P(("dp", "tensor")),
            P(("dp", "tensor")),
        ),
        check_vma=False,
    )
```

time: 1360 us -> 422 us (0.31); the launches traced: 1350 us -> 423 us
  waiting for transfers between devices: 577 us -> 172 us
  matrix products: 307 us -> 25.7 us
  blocking collectives: 221 us -> 0 us
  Pallas kernels: 0 us -> 107 us
  loops' own time: 71.6 us -> 0 us
  local copies, waits for them, and re-layouts: 112 us -> 42.3 us
  starting transfers between devices: 1.78 us -> 31.6 us
    dot_general x101 -> x14, matrix products: 305 us -> 25.7 us  [on_device(): lax.dot_general(a, b, dims, preferred_element_type=f32)]
    reduce_scatter x6 -> x1, waiting for transfers between devices: 244 us -> 22.5 us  [on_device(): lax.psum_scatter(wide_local, 'dp', scatter_dimension=0, tiled=True)]
    unnamed x20 -> x4, waiting for transfers between devices: 222 us -> 0.07 us
    all_gather x5 -> x0, blocking collectives: 137 us -> none  [the longest x1 33.4 us: on_device(): lax.all_gather(query_proj, 'dp', axis=0, tiled=True)]
    pallas_call x0 -> x3, Pallas kernels: none -> 107 us  [the longest x1 55.7 us: ffn(): pl.pallas_call(ffn_kernel, out_shape=(jax.ShapeDtypeStruct((rows, width),...]
    unnamed x2 -> x0, blocking collectives: 84.6 us -> none
    another operation x2 -> x0, loops' own time: 71.6 us -> none  [the longest x1 47.7 us: attend_back(): lax.scan(one, (empty, empty), jnp.arange(count * heads))]
    ppermute x0 -> x19, waiting for transfers between devices: none -> 42.6 us  [exchange(): return lax.ppermute(value, 'tensor', [(i, i ^ bit) for i in range(4)])]
  transfers between devices with their start and end apart: 16 -> 26, of which waited for: 15 -> 10; matrix products, arithmetic and copies ran while one was open for 6% -> 20% of each run, Pallas kernels for 0% -> 12%
where the time goes in v1:
time: 422 us; the launch traced here: 423 us
  waiting for transfers between devices  172 us (41%)
  Pallas kernels  107 us (25%)
  local copies, waits for them, and re-layouts  42.3 us (10%)
  starting transfers between devices  31.6 us (7%)
  other arithmetic  29.8 us (7%)
  matrix products  25.7 us (6%)
  between operations  14.5 us (3%)
    pallas_call x1, Pallas kernels, ffn(): pl.pallas_call(ffn_kernel, out_shape=(jax.ShapeDtypeStruct((rows, width),...  55.7 us
    all_gather x1, waiting for transfers between devices, on_device(): w2 = lax.all_gather(exchange(wide, 2), 'dp', axis=0, tiled=True)  53.4 us
    ppermute x19, waiting for transfers between devices, exchange(): return lax.ppermute(value, 'tensor', [(i, i ^ bit) for i in range(4)])  42.6 us
    pallas_call x1, Pallas kernels, attn_bwd(): pl.pallas_call(bwd_kernel, out_shape=(jax.ShapeDtypeStruct((width, length...  32.2 us
    all_to_all x1, waiting for transfers between devices, on_device(): swapped = lax.all_to_all(attn_local, 'dp', 0, 0, tiled=True)  31.9 us
    dot_general x14, matrix products, on_device(): lax.dot_general(a, b, dims, preferred_element_type=f32)  25.7 us
    reduce_scatter x1, waiting for transfers between devices, on_device(): lax.psum_scatter(wide_local, 'dp', scatter_dimension=0, tiled=True)  22.5 us
    all_gather x1, waiting for transfers between devices, on_device(): w0 = lax.all_gather(wide, 'dp', axis=0, tiled=True)  21.3 us
  transfers between devices with their start and end apart: 26, of which 10 were waited for; matrix products, arithmetic and copies ran while one was open for 20% of the time, Pallas kernels for 12%

profile of v1, /device:TPU:0, one launch (start us, length us, event | category | flops | bytes accessed | tf_op | source)
XLA Modules:
  0.0 422.8 jit_solution(11602317528436004700)
XLA Ops:
  7.3 0.9 copy.85
  8.2 1.6 pad_maximum_fusion.4
  9.9 1.7 pad_maximum_fusion.3
  11.7 3.0 collective-permute-start.9
  14.7 7.2 %collective-permute-done.9 = bf16[96,1536]{1,0:T(8,128)(2,1)S(1)} collective-permute-done((bf16[96,1536]{1,0:T(8,128)(2,1)}, bf16[96,1536]{1,0:T(8,128)(2,1)S(1)}, u32[]{:S(2)}, u32[]{:S(2)}) %collective-permute-start.9) | collective-permute-done | bytes 294944 | tf_op jit(solution)/shard_map/ppermute | solution.py:315
  22.7 1.8 collective-permute-start.4
  26.8 6.1 %all-to-all-start = ((f32[32,8,128]{2,1,0:T(8,128)}), f32[32,8,128]{2,1,0:T(8,128)S(1)}, u32[]{:S(2)}, u32[]{:S(2)}) async-start(f32[32,8,128]{2,1,0:T(8,128)} %broadcast_in_dim.39), calls=%async_computation | async-start | bytes 262144 | tf_op jit(solution)/shard_map/all_to_all | solution.py:374
  32.9 10.0 %collective-permute-done.1 = s32[512]{0:T(512)S(1)} collective-permute-done((s32[512]{0:T(512)}, s32[512]{0:T(512)S(1)}, u32[]{:S(2)}, u32[]{:S(2)}) %collective-permute-start.1) | collective-permute-done | bytes 2080 | tf_op jit(solution)/shard_map/ppermute | solution.py:315
  42.9 0.9 constant_dynamic-update-slice_fusion.3
  47.2 0.9 copy.105
  48.8 1.4 reshape.95
  50.2 1.4 reshape.94
  51.6 1.3 dynamic_slice.7
  53.0 1.3 dynamic_slice.6
  54.3 1.0 constant_dynamic-update-slice_fusion.2
  55.3 1.0 constant_dynamic-update-slice_fusion.1
  56.3 1.0 constant_dynamic-update-slice_fusion
  57.2 3.3 fusion.2.v_ref
  60.6 1.2 fusion.1.q_ref
  61.8 1.1 convolution_convert_fusion.1.k_ref
  62.9 19.3 %attention.1 = (bf16[192,2048]{1,0:T(8,128)(2,1)S(1)}, f32[3,2048]{1,0:T(4,128)S(1)}) custom-call(s32[8]{0:T(128)S(1)} %get-tuple-element.186.lo_ref, s32[8]{0:T(128)S(1)} %get-tuple-element.185.hi_ref, s32[1]{0:T(128)} %bitcast.1.flip_ref, bf16[192,2048]{1,0:T(8,128)(2,1)S(1)} %fusion.1.q_ref, bf16[2048,192]{1,0:T(8,128)(2,1)S(1)} %convolution_convert_fusion.1.k_ref, ...), custom_call_target="tpu_custom_call" | custom-call | flops 1610612736 | bytes 3145728 | tf_op jit(solution)/shard_map/attention/pallas_call | solution.py:67
  82.3 1.2 convolution_convert_fusion
  83.6 1.2 fusion.16
  85.5 1.3 pad_maximum_fusion
  87.0 21.3 %all-gather.6.cloned.1.call-done.e0 = bf16[768,1536]{1,0:T(8,128)(2,1)} async-done(((bf16[96,1536]{1,0:T(8,128)(2,1)}), bf16[768,1536]{1,0:T(8,128)(2,1)}) %all-gather.6.cloned.1.call-update) | async-done | bytes 2359312 | tf_op jit(solution)/shard_map/all_gather | solution.py:365
  108.3 53.4 %all-gather.8.cloned.1.call-done.e2 = bf16[768,1536]{1,0:T(8,128)(2,1)} async-done(((bf16[96,1536]{1,0:T(8,128)(2,1)}), bf16[768,1536]{1,0:T(8,128)(2,1)}) %all-gather.8.cloned.1.call-update) | async-done | bytes 2359312 | tf_op jit(solution)/shard_map/all_gather | solution.py:366
  161.8 1.6 add_convert_fusion.6
  163.3 1.5 collective-permute-start.7
  167.5 2.1 slice.181.a1_ref
  169.6 13.8 %collective-permute-done.7.a2_ref = bf16[512,768]{1,0:T(8,128)(2,1)} collective-permute-done((bf16[512,768]{1,0:T(8,128)(2,1)S(1)}, bf16[512,768]{1,0:T(8,128)(2,1)}, u32[]{:S(2)}, u32[]{:S(2)}) %collective-permute-start.7) | collective-permute-done | bytes 786464 | tf_op jit(solution)/shard_map/ppermute | solution.py:315
  183.5 55.7 %feed_forward.1 = (bf16[512,768]{1,0:T(8,128)(2,1)}, f32[512,768]{1,0:T(8,128)}, bf16[512,768]{1,0:T(8,128)(2,1)}, f32[6,8,768]{2,1,0:T(8,128)}, f32[4,8,768]{2,...) custom-call(bf16[512,768]{1,0:T(8,128)(2,1)} %tok_ref.1, ...), custom_call_target="tpu_custom_call" | custom-call | flops 14495514624 | bytes 18874368 | tf_op jit(solution)/shard_map/feed_forward/pallas_call | solution.py:298
  239.3 4.0 fusion.v_ref
  243.9 1.5 collective-permute-start.12
  245.3 2.5 convolution_convert_fusion.3.kT_ref
  253.2 10.2 %collective-permute-done.12 = bf16[512,768]{1,0:T(8,128)(2,1)S(1)} collective-permute-done((bf16[512,768]{1,0:T(8,128)(2,1)S(1)}, bf16[512,768]{1,0:T(8,128)(2,1)S(1)}, u32[]{:S(2)}, u32[]{:S(2)}) %collective-permute-start.12) | collective-permute-done | bytes 786464 | tf_op jit(solution)/shard_map/ppermute | solution.py:315
  263.4 1.2 constant_dynamic-update-slice_fusion.6
  264.7 3.6 add_convert_fusion.2
  268.3 1.5 collective-permute-start.18
  269.9 3.0 convolution_convert_fusion.2.do_ref
  273.2 32.2 %attention_back.1 = (bf16[192,2048]{1,0:T(8,128)(2,1)S(1)}, bf16[2048,192]{1,0:T(8,128)(2,1)S(1)}, bf16[2048,192]{1,0:T(8,128)(2,1)S(1)}, f32[192,128]{1,0:T(8,128)S(1)}, f32[8,192]{1,0:T(8,128)S(1)}) custom-call(s32[8]{0:T(128)S(1)} %get-tuple-element.186.lo_ref, s32[8]{0:T(128)S(1)} %get-tuple-element.185.hi_ref, s32[1]{0:T(128)} %bitcast.1.flip_ref, ...), custom_call_target="tpu_custom_call" | custom-call | flops 4026531840 | bytes 7864320 | tf_op jit(solution)/shard_map/attention_back/pallas_call | solution.py:138
  305.4 1.0 copy-done
  308.4 7.6 %all-to-all-start.2 = ((f32[32,8,128]{2,1,0:T(8,128)}), f32[32,8,128]{2,1,0:T(8,128)}, u32[]{:S(2)}, u32[]{:S(2)}) async-start(f32[32,8,128]{2,1,0:T(8,128)} %bitcast.19), calls=%async_computation.2 | async-start | bytes 262144 | tf_op jit(solution)/shard_map/all_to_all | solution.py:435
  316.3 2.1 fusion.5
  318.5 1.1 fusion.11
  319.7 2.7 add_convert_fusion
  322.4 1.1 collective-permute-done.18
  323.5 4.7 %add_convert_fusion.1 = bf16[768,1536]{1,0:T(8,128)(2,1)} fusion(bf16[768,1536]{1,0:T(8,128)(2,1)} %collective-permute-done.18, bf16[768,1536]{1,0:T(8,128)(2,1)} %collective-permute-done.16, bf16[768,1536]{1,0:T(8,128)(2,1)S(1)} %copy-done.22), kind=kLoop, calls=%fused_computation.3 | loop fusion | flops 9437184 | bytes 9437184 | tf_op jit(solution)/shard_map/convert_element_type | solution.py:423
  328.2 1.5 fusion.15
  329.7 1.2 pad_maximum_fusion.1
  331.0 1.2 copy-done.16
  336.4 0.9 copy.98
  337.3 0.9 copy.99
  338.2 0.9 copy.100
  339.1 2.9 pad_maximum_fusion.2
  342.0 4.7 %all-to-all-start.1 = ((bf16[8,96,768]{2,1,0:T(8,128)(2,1)}), bf16[8,96,768]{2,1,0:T(8,128)(2,1)}, u32[]{:S(2)}, u32[]{:S(2)}) async-start(bf16[8,96,768]{2,1,0:T(8,128)(2,1)} %pad_maximum_fusion.2), calls=%async_computation.1 | async-start | bytes 2359296 | tf_op jit(solution)/shard_map/all_to_all | solution.py:417
  346.7 2.2 add_convert_fusion.5
  348.9 1.5 collective-permute-start.15
  350.4 0.9 reduce_sum.81
  352.6 31.9 %all-to-all-done.1 = bf16[8,96,768]{2,1,0:T(8,128)(2,1)} async-done(((bf16[8,96,768]{2,1,0:T(8,128)(2,1)}), bf16[8,96,768]{2,1,0:T(8,128)(2,1)}, u32[]{:S(2)}, u32[]{:S(2)}) %all-to-all-start.1) | async-done | bytes 1179680 | tf_op jit(solution)/shard_map/all_to_all | solution.py:417
  384.4 1.5 convert_reduce_fusion
  387.4 3.1 add_convert_fusion.4
  390.5 22.5 %reduce-scatter.2.cloned.1.call-done = bf16[96,1536]{1,0:T(8,128)(2,1)} async-done(((bf16[768,1536]{1,0:T(8,128)(2,1)}), bf16[96,1536]{1,0:T(8,128)(2,1)}) %reduce-scatter.2.cloned.1.call-update) | async-done | bytes 294928 | tf_op jit(solution)/shard_map/reduce_scatter | solution.py:424
  412.9 1.0 convert_element_type.129
  414.7 1.6 slice.201
  (178 shorter events, 27.1 us)
Async XLA Ops:
  7.2 35.7 %copy-start.23 = (bf16[512,768]{1,0:T(8,128)(2,1)S(1)}, bf16[512,768]{1,0:T(8,128)(2,1)}, u32[]{:S(2)}) copy-start(bf16[512,768]{1,0:T(8,128)(2,1)} %tok_ref.1) | copy-start | bytes 2359300
  7.2 36.9 %copy-start.38 = (s32[1,512]{1,0:T(1,128)S(1)}, s32[1,512]{1,0:T(1,128)}, u32[]{:S(2)}) copy-start(s32[1,512]{1,0:T(1,128)} %param.21) | copy-start | bytes 6148
  7.2 50.0 %all-gather.4.cloned.1.call-start = ((), (), s32[]{:S(2)}) async-start(), calls=%async_computation.4 | async-start | bytes 1327104 | tf_op jit(solution)/shard_map/all_gather | solution.py:363
  9.9 98.5 %all-gather.6.cloned.1.call-start = ((), (), s32[]{:S(2)}) async-start(), calls=%async_computation.5 | async-start | bytes 2654208 | tf_op jit(solution)/shard_map/all_gather | solution.py:365
  11.6 150.1 %all-gather.8.cloned.1.call-start = ((), (), s32[]{:S(2)}) async-start(), calls=%async_computation.6 | async-start | bytes 2654208 | tf_op jit(solution)/shard_map/all_gather | solution.py:366
  11.7 10.2 %collective-permute-start.9 = (bf16[96,1536]{1,0:T(8,128)(2,1)}, bf16[96,1536]{1,0:T(8,128)(2,1)S(1)}, u32[]{:S(2)}, u32[]{:S(2)}) collective-permute-start(bf16[96,1536]{1,0:T(8,128)(2,1)} %pad_maximum_fusion.3), channel_id=1, source_target_pairs={{0,2},{1,3},{2,0},{3,1},{4,6},{5,7},{6,4},{7,5},{8,10},{9,11},{10,... | collective-permute-start | bytes 884744 | tf_op jit(solution)/shard_map/ppermute | solution.py:315
  22.7 21.6 %collective-permute-start.4 = (bf16[512,768]{1,0:T(8,128)(2,1)}, bf16[512,768]{1,0:T(8,128)(2,1)S(1)}, u32[]{:S(2)}, u32[]{:S(2)}) collective-permute-start(bf16[512,768]{1,0:T(8,128)(2,1)} %tok_ref.1), channel_id=1, source_target_pairs={{0,2},{1,3},{2,0},{3,1},{4,6},{5,7},{6,4},{7,5},{8,10},{9,11},{10,... | collective-permute-start | bytes 2359304 | tf_op jit(solution)/shard_map/ppermute | solution.py:315
  24.5 18.5 %collective-permute-start.1 = (s32[512]{0:T(512)}, s32[512]{0:T(512)S(1)}, u32[]{:S(2)}, u32[]{:S(2)}) collective-permute-start(s32[512]{0:T(512)} %bitcast.60), channel_id=1, source_target_pairs={{0,2},{1,3},{2,0},{3,1},{4,6},{5,7},{6,4},{7,5},{8,10},{9,11},{10,... | collective-permute-start | bytes 6152 | tf_op jit(solution)/shard_map/ppermute | solution.py:315
  24.7 19.1 %collective-permute-start = (s32[512]{0:T(512)}, s32[512]{0:T(512)S(1)}, u32[]{:S(2)}, u32[]{:S(2)}) collective-permute-start(s32[512]{0:T(512)} %bitcast.61), channel_id=1, source_target_pairs={{0,1},{1,0},{2,3},{3,2},{4,5},{5,4},{6,7},{7,6},{8,9},{9,8},{10,11... | collective-permute-start | bytes 6152 | tf_op jit(solution)/shard_map/ppermute | solution.py:315
  24.7 29.5 %collective-permute-start.3 = (bf16[512,768]{1,0:T(8,128)(2,1)}, bf16[512,768]{1,0:T(8,128)(2,1)S(1)}, u32[]{:S(2)}, u32[]{:S(2)}) collective-permute-start(bf16[512,768]{1,0:T(8,128)(2,1)} %tok_ref.1), channel_id=1, source_target_pairs={{0,1},{1,0},{2,3},{3,2},{4,5},{5,4},{6,7},{7,6},{8,9},{9,8},{10,11... | collective-permute-start | bytes 2359304 | tf_op jit(solution)/shard_map/ppermute | solution.py:315
  26.8 19.7 %all-to-all-start = ((f32[32,8,128]{2,1,0:T(8,128)}), f32[32,8,128]{2,1,0:T(8,128)S(1)}, u32[]{:S(2)}, u32[]{:S(2)}) async-start(f32[32,8,128]{2,1,0:T(8,128)} %broadcast_in_dim.39), calls=%async_computation | async-start | bytes 262144 | tf_op jit(solution)/shard_map/all_to_all | solution.py:374
  42.9 1.2 collective-permute-start.2
  44.3 12.0 %collective-permute-start.5 = (bf16[512,768]{1,0:T(8,128)(2,1)S(1)}, bf16[512,768]{1,0:T(8,128)(2,1)S(1)}, u32[]{:S(2)}, u32[]{:S(2)}) collective-permute-start(bf16[512,768]{1,0:T(8,128)(2,1)S(1)} %collective-permute-done.4), channel_id=1, source_target_pairs={{0,1},{1,0},{2,3},{3,2},{4,5},{5,4},{6,7},{7,6},{8,9},{9,8},{10,11... | collective-permute-start | bytes 2359304 | tf_op jit(solution)/shard_map/ppermute | solution.py:315
  45.8 17.2 %copy-start.3 = (s32[2048,1]{1,0:T(8,128)}, s32[2048,1]{1,0:T(8,128)S(1)}, u32[]{:S(2)}) copy-start(s32[2048,1]{1,0:T(8,128)S(1)} %copy.87.segc_ref) | copy-start | bytes 24580
  57.2 3.3 copy-start.40
  57.2 3.3 copy-start.12
  57.2 3.3 copy-start.19
  61.8 1.1 copy-start.5
  62.9 19.4 %copy-start.7 = (bf16[2048,192]{1,0:T(8,128)(2,1)}, bf16[2048,192]{1,0:T(8,128)(2,1)S(1)}, u32[]{:S(2)}) copy-start(bf16[2048,192]{1,0:T(8,128)(2,1)S(1)} %convolution_convert_fusion.1.k_ref) | copy-start | bytes 2359300
  82.3 2.5 copy-start.10
  83.5 1.9 copy-start.18
  85.4 79.5 %copy-start.34 = (f32[32,24]{1,0:T(8,128)S(1)}, f32[32,24]{1,0:T(8,128)}, u32[]{:S(2)}) copy-start(f32[32,24]{1,0:T(8,128)} %get-tuple-element.174) | copy-start | bytes 9220
  85.4 79.6 %copy-start.33 = (f32[32,24]{1,0:T(8,128)S(1)}, f32[32,24]{1,0:T(8,128)}, u32[]{:S(2)}) copy-start(f32[32,24]{1,0:T(8,128)} %get-tuple-element.173) | copy-start | bytes 9220
  85.4 79.7 %copy-start.32 = (f32[32,24]{1,0:T(8,128)S(1)}, f32[32,24]{1,0:T(8,128)}, u32[]{:S(2)}) copy-start(f32[32,24]{1,0:T(8,128)} %get-tuple-element.172) | copy-start | bytes 9220
  85.5 79.8 %copy-start.31 = (f32[32,24]{1,0:T(8,128)S(1)}, f32[32,24]{1,0:T(8,128)}, u32[]{:S(2)}) copy-start(f32[32,24]{1,0:T(8,128)} %get-tuple-element.171) | copy-start | bytes 9220
  85.5 79.9 %copy-start.30 = (f32[32,24]{1,0:T(8,128)S(1)}, f32[32,24]{1,0:T(8,128)}, u32[]{:S(2)}) copy-start(f32[32,24]{1,0:T(8,128)} %get-tuple-element.170) | copy-start | bytes 9220
  85.5 80.0 %copy-start.29 = (f32[32,24]{1,0:T(8,128)S(1)}, f32[32,24]{1,0:T(8,128)}, u32[]{:S(2)}) copy-start(f32[32,24]{1,0:T(8,128)} %get-tuple-element.169) | copy-start | bytes 9220
  86.8 75.0 %collective-permute-start.6 = (bf16[1024,768]{1,0:T(8,128)(2,1)}, bf16[1024,768]{1,0:T(8,128)(2,1)}, u32[]{:S(2)}, u32[]{:S(2)}) collective-permute-start(bf16[1024,768]{1,0:T(8,128)(2,1)} %pad_maximum_fusion), channel_id=1, source_target_pairs={{0,1},{1,0},{2,3},{3,2},{4,5},{5,4},{6,7},{7,6},{8,9},{9,8},{10,11... | collective-permute-start | bytes 4718600 | tf_op jit(solution)/shard_map/ppermute | solution.py:315
  108.3 75.1 %collective-permute-start.8 = (bf16[768,1536]{1,0:T(8,128)(2,1)}, bf16[768,1536]{1,0:T(8,128)(2,1)}, u32[]{:S(2)}, u32[]{:S(2)}) collective-permute-start(bf16[768,1536]{1,0:T(8,128)(2,1)} %all-gather.6.cloned.1.call-done.e0), channel_id=1, source_target_pairs={{0,1},{1,0},{2,3},{3,2},{4,5},{5,4},{6,7},{7,6},{8,9},{9,8},{10,11... | collective-permute-start | bytes 7077896 | tf_op jit(solution)/shard_map/ppermute | solution.py:315
  161.8 21.7 %collective-permute-start.10 = (bf16[768,1536]{1,0:T(8,128)(2,1)}, bf16[768,1536]{1,0:T(8,128)(2,1)}, u32[]{:S(2)}, u32[]{:S(2)}) collective-permute-start(bf16[768,1536]{1,0:T(8,128)(2,1)} %all-gather.8.cloned.1.call-done.e2), channel_id=1, source_target_pairs={{0,1},{1,0},{2,3},{3,2},{4,5},{5,4},{6,7},{7,6},{8,9},{9,8},{10,11... | collective-permute-start | bytes 7077896 | tf_op jit(solution)/shard_map/ppermute | solution.py:315
  163.3 20.1 %collective-permute-start.7 = (bf16[512,768]{1,0:T(8,128)(2,1)S(1)}, bf16[512,768]{1,0:T(8,128)(2,1)}, u32[]{:S(2)}, u32[]{:S(2)}) collective-permute-start(bf16[512,768]{1,0:T(8,128)(2,1)S(1)} %add_convert_fusion.6), channel_id=1, source_target_pairs={{0,2},{1,3},{2,0},{3,1},{4,6},{5,7},{6,4},{7,5},{8,10},{9,11},{10,... | collective-permute-start | bytes 2359304 | tf_op jit(solution)/shard_map/ppermute | solution.py:315
  164.9 74.3 %copy-start.36 = (pred[4]{0:T(512)(128)(4,1)}, pred[4]{0:T(512)(128)(4,1)S(1)}, u32[]{:S(2)}) copy-start(pred[4]{0:T(512)(128)(4,1)S(1)} %compare_and_fusion) | copy-start | bytes 16
  164.9 74.2 %copy-start.35 = (s32[1024]{0:T(1024)}, s32[1024]{0:T(1024)S(1)}, u32[]{:S(2)}) copy-start(s32[1024]{0:T(1024)S(1)} %pad_clamp_fusion) | copy-start | bytes 12292
  183.5 55.8 %copy-start.39 = (f32[192]{0:T(256)S(1)}, f32[192]{0:T(256)}, u32[]{:S(2)}) copy-start(f32[192]{0:T(256)} %dynamic_slice.7) | copy-start | bytes 2308
  239.2 25.5 %collective-permute-start.17 = (bf16[768,1536]{1,0:T(8,128)(2,1)}, bf16[768,1536]{1,0:T(8,128)(2,1)}, u32[]{:S(2)}, u32[]{:S(2)}) collective-permute-start(bf16[768,1536]{1,0:T(8,128)(2,1)} %get-tuple-element.49), channel_id=1, source_target_pairs={{0,1},{1,0},{2,3},{3,2},{4,5},{5,4},{6,7},{7,6},{8,9},{9,8},{10,11... | collective-permute-start | bytes 7077896 | tf_op jit(solution)/shard_map/ppermute | solution.py:315
  239.3 4.1 copy-start.24
  239.3 6.1 %copy-start.13 = (bf16[2048,768]{1,0:T(8,128)(2,1)S(1)}, bf16[2048,768]{1,0:T(8,128)(2,1)}, u32[]{:S(2)}) copy-start(bf16[2048,768]{1,0:T(8,128)(2,1)} %constant_dynamic-update-slice_fusion) | copy-start | bytes 9437188
  243.3 4.6 %copy-start.27 = (f32[6,8,768]{2,1,0:T(8,128)S(1)}, f32[6,8,768]{2,1,0:T(8,128)}, u32[]{:S(2)}) copy-start(f32[6,8,768]{2,1,0:T(8,128)} %get-tuple-element.44) | copy-start | bytes 442372
  243.3 8.3 %copy-start.28 = (f32[4,8,768]{2,1,0:T(8,128)S(1)}, f32[4,8,768]{2,1,0:T(8,128)}, u32[]{:S(2)}) copy-start(f32[4,8,768]{2,1,0:T(8,128)} %get-tuple-element.45) | copy-start | bytes 294916
  243.3 9.0 %copy-start.37 = (pred[4]{0:T(512)(128)(4,1)S(1)}, pred[4]{0:T(512)(128)(4,1)}, u32[]{:S(2)}) copy-start(pred[4]{0:T(512)(128)(4,1)} %copy-done.36) | copy-start | bytes 16
  243.3 20.1 %collective-permute-start.11 = (bf16[512,768]{1,0:T(8,128)(2,1)S(1)}, bf16[512,768]{1,0:T(8,128)(2,1)}, u32[]{:S(2)}, u32[]{:S(2)}) collective-permute-start(bf16[512,768]{1,0:T(8,128)(2,1)S(1)} %copy-done.24), channel_id=1, source_target_pairs={{0,1},{1,0},{2,3},{3,2},{4,5},{5,4},{6,7},{7,6},{8,9},{9,8},{10,11... | collective-permute-start | bytes 2359304 | tf_op jit(solution)/shard_map/ppermute | solution.py:315
  243.9 19.5 %collective-permute-start.12 = (bf16[512,768]{1,0:T(8,128)(2,1)S(1)}, bf16[512,768]{1,0:T(8,128)(2,1)S(1)}, u32[]{:S(2)}, u32[]{:S(2)}) collective-permute-start(bf16[512,768]{1,0:T(8,128)(2,1)S(1)} %copy-done.24), channel_id=1, source_target_pairs={{0,2},{1,3},{2,0},{3,1},{4,6},{5,7},{6,4},{7,5},{8,10},{9,11},{10,... | collective-permute-start | bytes 2359304 | tf_op jit(solution)/shard_map/ppermute | solution.py:315
  247.9 74.6 %collective-permute-start.16 = (bf16[768,1536]{1,0:T(8,128)(2,1)}, bf16[768,1536]{1,0:T(8,128)(2,1)}, u32[]{:S(2)}, u32[]{:S(2)}) collective-permute-start(bf16[768,1536]{1,0:T(8,128)(2,1)} %get-tuple-element.47), channel_id=1, source_target_pairs={{0,1},{1,0},{2,3},{3,2},{4,5},{5,4},{6,7},{7,6},{8,9},{9,8},{10,11... | collective-permute-start | bytes 7077896 | tf_op jit(solution)/shard_map/ppermute | solution.py:315
  253.1 11.6 %copy-start.21 = (bf16[768,1536]{1,0:T(8,128)(2,1)S(1)}, bf16[768,1536]{1,0:T(8,128)(2,1)}, u32[]{:S(2)}) copy-start(bf16[768,1536]{1,0:T(8,128)(2,1)} %get-tuple-element.48) | copy-start | bytes 7077892
  263.4 6.4 %collective-permute-start.13 = (bf16[512,768]{1,0:T(8,128)(2,1)S(1)}, bf16[512,768]{1,0:T(8,128)(2,1)S(1)}, u32[]{:S(2)}, u32[]{:S(2)}) collective-permute-start(bf16[512,768]{1,0:T(8,128)(2,1)S(1)} %collective-permute-done.12), channel_id=1, source_target_pairs={{0,1},{1,0},{2,3},{3,2},{4,5},{5,4},{6,7},{7,6},{8,9},{9,8},{10,11... | collective-permute-start | bytes 2359304 | tf_op jit(solution)/shard_map/ppermute | solution.py:315
  268.3 55.2 %collective-permute-start.18 = (bf16[768,1536]{1,0:T(8,128)(2,1)}, bf16[768,1536]{1,0:T(8,128)(2,1)}, u32[]{:S(2)}, u32[]{:S(2)}) collective-permute-start(bf16[768,1536]{1,0:T(8,128)(2,1)} %add_convert_fusion.2), channel_id=1, source_target_pairs={{0,2},{1,3},{2,0},{3,1},{4,6},{5,7},{6,4},{7,5},{8,10},{9,11},{10,... | collective-permute-start | bytes 7077896 | tf_op jit(solution)/shard_map/ppermute | solution.py:315
  269.8 3.0 copy-start.15
  269.9 3.0 copy-start.4
  269.9 3.0 copy-start.6
  269.9 3.0 copy-start.8
  269.9 3.3 copy-start.9
  269.9 3.3 copy-start.11
  308.4 33.6 %all-to-all-start.2 = ((f32[32,8,128]{2,1,0:T(8,128)}), f32[32,8,128]{2,1,0:T(8,128)}, u32[]{:S(2)}, u32[]{:S(2)}) async-start(f32[32,8,128]{2,1,0:T(8,128)} %bitcast.19), calls=%async_computation.2 | async-start | bytes 262144 | tf_op jit(solution)/shard_map/all_to_all | solution.py:435
  316.0 96.9 %reduce-scatter.2.cloned.1.call-start = ((), (), s32[]{:S(2)}) async-start(), calls=%async_computation.7 | async-start | bytes 2654208 | tf_op jit(solution)/shard_map/reduce_scatter | solution.py:424
  316.3 2.2 copy-start.20
  318.5 1.2 copy-start.1
  319.7 3.8 copy-start.22
  329.7 2.5 copy-start.16
  331.0 2.3 copy-start.14
  331.0 15.8 %collective-permute-start.14 = (bf16[1024,768]{1,0:T(8,128)(2,1)}, bf16[1024,768]{1,0:T(8,128)(2,1)}, u32[]{:S(2)}, u32[]{:S(2)}) collective-permute-start(bf16[1024,768]{1,0:T(8,128)(2,1)} %pad_maximum_fusion.1), channel_id=1, source_target_pairs={{0,1},{1,0},{2,3},{3,2},{4,5},{5,4},{6,7},{7,6},{8,9},{9,8},{10,11... | collective-permute-start | bytes 4718600 | tf_op jit(solution)/shard_map/ppermute | solution.py:315
  333.3 1.2 copy-start.2
  339.1 7.6 %copy-start.17 = (bf16[2048,768]{1,0:T(8,128)(2,1)S(1)}, bf16[2048,768]{1,0:T(8,128)(2,1)}, u32[]{:S(2)}) copy-start(bf16[2048,768]{1,0:T(8,128)(2,1)} %add_convert_fusion) | copy-start | bytes 9437188
  342.0 42.4 %all-to-all-start.1 = ((bf16[8,96,768]{2,1,0:T(8,128)(2,1)}), bf16[8,96,768]{2,1,0:T(8,128)(2,1)}, u32[]{:S(2)}, u32[]{:S(2)}) async-start(bf16[8,96,768]{2,1,0:T(8,128)(2,1)} %pad_maximum_fusion.2), calls=%async_computation.1 | async-start | bytes 2359296 | tf_op jit(solution)/shard_map/all_to_all | solution.py:417
  348.9 38.5 %collective-permute-start.15 = (bf16[512,768]{1,0:T(8,128)(2,1)}, bf16[512,768]{1,0:T(8,128)(2,1)}, u32[]{:S(2)}, u32[]{:S(2)}) collective-permute-start(bf16[512,768]{1,0:T(8,128)(2,1)} %add_convert_fusion.5), channel_id=1, source_target_pairs={{0,2},{1,3},{2,0},{3,1},{4,6},{5,7},{6,4},{7,5},{8,10},{9,11},{10,... | collective-permute-start | bytes 2359304 | tf_op jit(solution)/shard_map/ppermute | solution.py:315
  (3 other events, 2.4 us)
Sparse Core Ops, SparseCore 0:
  10.8 43.9 all-gather.3
  57.5 50.7 all-gather.5
  111.1 50.6 all-gather.7
  328.4 84.5 reduce-scatter.1

commit v2 on v1

--- a/solution.py
+++ b/solution.py
@@ -75,13 +75,13 @@
                       pl.BlockSpec((1,BQ),lambda i,*_:(0,i))],
             out_specs=[pl.BlockSpec((width,BQ),lambda i,*_:(0,i)),pl.BlockSpec((heads,BQ),lambda i,*_:(0,i))],
             scratch_shapes=[pltpu.VMEM((heads,length//BK,BK,BQ),f32)]),
-        compiler_params=pltpu.CompilerParams(dimension_semantics=("arbitrary",),vmem_limit_bytes=40<<20),
-        cost_estimate=pl.CostEstimate(flops=4*length*length//2*width,bytes_accessed=8*length*width,transcendentals=heads*length*length//2),
+        compiler_params=pltpu.CompilerParams(dimension_semantics=("arbitrary",),vmem_limit_bytes=60<<20),
+        cost_estimate=pl.CostEstimate(flops=30*length*length*width,bytes_accessed=8*length*width,transcendentals=heads*length*length//2),
         name="attention",
     )(lo,hi,flip,qT,k,vT,segc,segr)
 
-def bwd_kernel(lo_ref, hi_ref, flip_ref, q_ref, k_ref, kT_ref, v_ref, do_ref, o_ref, lse_ref, segc_ref, segr_ref,
-               dq_ref, dk_ref, dv_ref, qb_ref, vb_ref, dk_acc, dv_acc):
+def bwd_kernel(lo_ref, hi_ref, flip_ref, q_ref, k_ref, kT_ref, v_ref, wT_ref, g0, g1, g2, g3, o_ref, lse_ref, segc_ref, segr_ref,
+               dq_ref, dk_ref, dv_ref, qb_ref, vb_ref, dk_acc, dv_acc, do_ref):
     heads = q_ref.shape[0]//HD
     width = q_ref.shape[0]
     i = pl.program_id(0)
@@ -91,6 +91,12 @@
         qb_ref[...]=jnp.zeros_like(qb_ref)
     lo = lo_ref[i]; hi = hi_ref[i]; flip = flip_ref[0]
     scale = HD**-0.5
+    per = g0.shape[0]//BQ
+    for n, g_ref in enumerate((g0, g1, g2, g3)):
+        @pl.when(i//per==n)
+        def _():
+            at = pl.multiple_of((i%per)*BQ, BQ)
+            do_ref[...] = lax.dot_general(wT_ref[3*width:,:], g_ref[pl.ds(at,BQ),:], NT, preferred_element_type=f32).astype(bf16)
     c = LOG2E*scale
     qz = [padded(q_ref, h, heads, slice(None)) for h in range(heads)]
     dz = [padded(do_ref, h, heads, slice(None)) for h in range(heads)]
@@ -129,7 +135,7 @@
         dv_ref[...]=dv_acc[...].astype(bf16)
         vb_ref[...]=jnp.sum(dv_acc[...].reshape(dv_acc.shape[0]//8,8,width),axis=0)
 
-def attn_bwd(qT,k,kT,v,doT,oT,lse,segc,segr,lo,hi,flip):
+def attn_bwd(qT,k,kT,v,wT,grads,oT,lse,segc,segr,lo,hi,flip):
     width,length=qT.shape
     heads=width//HD
     blocks=length//BQ
@@ -139,16 +145,16 @@
         bwd_kernel,
         out_shape=(jax.ShapeDtypeStruct((width,length),bf16), jax.ShapeDtypeStruct((length,width),bf16), jax.ShapeDtypeStruct((length,width),bf16), jax.ShapeDtypeStruct((width,128),f32), jax.ShapeDtypeStruct((8,width),f32)),
         grid_spec=pltpu.PrefetchScalarGridSpec(num_scalar_prefetch=3, grid=(blocks,),
-            in_specs=[col,row,pl.BlockSpec((width,length),lambda i,*_:(0,0)),row,col,col,
+            in_specs=[col,row,pl.BlockSpec((width,length),lambda i,*_:(0,0)),row,pl.BlockSpec(wT.shape,lambda i,*_:(0,0))]+[pl.BlockSpec(g.shape,lambda i,*_:(0,0)) for g in grads]+[col,
                       pl.BlockSpec((heads,BQ),lambda i,*_:(0,i)),
                       pl.BlockSpec((length,1),lambda i,*_:(0,0)),
                       pl.BlockSpec((1,BQ),lambda i,*_:(0,i))],
             out_specs=[col,row,row,pl.BlockSpec((width,128),lambda i,*_:(0,0)),pl.BlockSpec((8,width),lambda i,*_:(0,0))],
-            scratch_shapes=[pltpu.VMEM((length,width),f32),pltpu.VMEM((length,width),f32)]),
-        compiler_params=pltpu.CompilerParams(dimension_semantics=("arbitrary",),vmem_limit_bytes=40<<20),
-        cost_estimate=pl.CostEstimate(flops=10*length*length//2*width,bytes_accessed=20*length*width,transcendentals=heads*length*length//2),
+            scratch_shapes=[pltpu.VMEM((length,width),f32),pltpu.VMEM((length,width),f32),pltpu.VMEM((width,BQ),bf16)]),
+        compiler_params=pltpu.CompilerParams(dimension_semantics=("arbitrary",),vmem_limit_bytes=60<<20),
+        cost_estimate=pl.CostEstimate(flops=60*length*length*width,bytes_accessed=20*length*width,transcendentals=heads*length*length//2),
         name="attention_back",
-    )(lo,hi,flip,qT,k,kT,v,doT,oT,lse,segc,segr)
+    )(lo,hi,flip,qT,k,kT,v,wT,*grads,oT,lse,segc,segr)
 
 def spans(seg_row):
     length=seg_row.shape[0]
@@ -172,12 +178,13 @@
     return jnp.sum(values.reshape(values.shape[0]//8,8,values.shape[1]),axis=0)
 
 def ffn_kernel(tok_ref, a0_ref, a1_ref, a2_ref, cot_ref, vec_ref, be_ref,
-               e0,e1,e2,e3,
-               out_ref, gm_ref, gml_ref, vg_ref, eb_ref, d0,d1,d2,d3,
+               wa_ref,wb_ref,
+               out_ref, gm_ref, gml_ref, vg_ref, eb_ref, ga_ref,gb_ref,
                we, ws, hl, hlT, hid, xhat, rs1, act, gp, acc, sl, slT, gsum, il, de, dt, wsem, osem):
-    es=(e0,e1,e2,e3); ds=(d0,d1,d2,d3)
     rows, width = tok_ref.shape
-    blocks=len(es); units=we.shape[2]
+    blocks,_,units=we.shape
+    es=[(wa_ref,wb_ref)[r%2].at[:,(r//2)*2*units:(r//2+1)*2*units] for r in range(blocks)]
+    ds=[(ga_ref,gb_ref)[r%2].at[:,(r//2)*2*units:(r//2+1)*2*units] for r in range(blocks)]
     for r in range(blocks):
         pltpu.make_async_copy(es[r].at[:,0:units],we.at[r],wsem.at[0,r]).start()
         pltpu.make_async_copy(es[r].at[:,units:],ws.at[r],wsem.at[1,r]).start()
@@ -193,7 +200,7 @@
         hl[at,:]=h.astype(bf16)
         acc[at,:]=jnp.zeros((RC,width),f32)
         return 0
-    lax.fori_loop(0,rows//RC,first,0)
+    lax.fori_loop(0,rows//RC,first,0,unroll=4)
     def turn(src,dst):
         def go(i,_):
             at=pl.multiple_of(i*T,T)
@@ -201,29 +208,29 @@
             return 0
         lax.fori_loop(0,rows//T,go,0)
     turn(hl,hlT)
-    per=units//T; mt=rows//T
+    TG=768; TM=min(512,rows); per=units//T; mt=rows//TM
     def forward(r,_):
         for k in range(blocks):
             @pl.when(r==k)
             def _():
                 pltpu.make_async_copy(es[k].at[:,0:units],we.at[k],wsem.at[0,k]).wait()
         def tile(j,_):
-            n=pl.multiple_of((j//mt)*T,T); m=pl.multiple_of((j%mt)*T,T)
-            u=lax.dot_general(hl[pl.ds(m,T),:],we[r,:,pl.ds(n,T)],NN,preferred_element_type=f32)+be_ref[pl.ds(r,1),pl.ds(n,T)]
+            n=pl.multiple_of((j//mt)*T,T); m=pl.multiple_of((j%mt)*TM,TM)
+            u=lax.dot_general(hl[pl.ds(m,TM),:],we[r,:,pl.ds(n,T)],NN,preferred_element_type=f32)+be_ref[pl.ds(r,1),pl.ds(n,T)]
             cdf=0.5+0.5*lax.erf(u*(0.5**0.5))
-            act[r,pl.ds(m,T),pl.ds(n,T)]=(u*cdf).astype(bf16)
-            gp[r,pl.ds(m,T),pl.ds(n,T)]=cdf+u*(jnp.exp(-0.5*u*u)*0.3989422804014327)
-            return 0
-        lax.fori_loop(0,per*mt,tile,0)
+            act[r,pl.ds(m,TM),pl.ds(n,T)]=(u*cdf).astype(bf16)
+            gp[r,pl.ds(m,TM),pl.ds(n,T)]=cdf+u*(jnp.exp(-0.5*u*u)*0.3989422804014327)
+            return 0
+        lax.fori_loop(0,per*mt,tile,0,unroll=3)
         for k in range(blocks):
             @pl.when(r==k)
             def _():
                 pltpu.make_async_copy(es[k].at[:,units:],ws.at[k],wsem.at[1,k]).wait()
         def shrink(j,_):
-            n=pl.multiple_of((j//mt)*T,T); m=pl.multiple_of((j%mt)*T,T)
-            acc[pl.ds(m,T),pl.ds(n,T)]+=lax.dot_general(act[r,pl.ds(m,T),:],ws[r,pl.ds(n,T),:],NT,preferred_element_type=f32)
-            return 0
-        lax.fori_loop(0,(width//T)*mt,shrink,0)
+            n=pl.multiple_of((j//mt)*T,T); m=pl.multiple_of((j%mt)*TM,TM)
+            acc[pl.ds(m,TM),pl.ds(n,T)]+=lax.dot_general(act[r,pl.ds(m,TM),:],ws[r,pl.ds(n,T),:],NT,preferred_element_type=f32)
+            return 0
+        lax.fori_loop(0,(width//T)*mt,shrink,0,unroll=3)
         return 0
     lax.fori_loop(0,blocks,forward,0)
     def second(i,sums):
@@ -239,36 +246,36 @@
         acc[at,:]=g
         return (sums[0]+fold(cot*z),sums[1]+fold(cot),sums[2]+fold(g))
     zero=jnp.zeros((8,width),f32)
-    sg,sh,sbg=lax.fori_loop(0,rows//RC,second,(zero,zero,zero))
+    sg,sh,sbg=lax.fori_loop(0,rows//RC,second,(zero,zero,zero),unroll=4)
     turn(sl,slT)
     def sent(r,slot,k):
         return (pltpu.make_async_copy(de.at[slot],ds[k].at[:,0:units],osem.at[0,slot]),pltpu.make_async_copy(dt.at[slot],ds[k].at[:,units:],osem.at[1,slot]))
     def backward(r,_):
         slot=r%2
         def tile(j,_):
-            n=pl.multiple_of((j//mt)*T,T); m=pl.multiple_of((j%mt)*T,T)
-            ga=lax.dot_general(sl[pl.ds(m,T),:],ws[r,:,pl.ds(n,T)],NN,preferred_element_type=f32)
-            gi=ga*gp[r,pl.ds(m,T),pl.ds(n,T)]
-            il[pl.ds(m,T),pl.ds(n,T)]=gi.astype(bf16)
+            n=pl.multiple_of((j//mt)*T,T); m=pl.multiple_of((j%mt)*TM,TM)
+            ga=lax.dot_general(sl[pl.ds(m,TM),:],ws[r,:,pl.ds(n,T)],NN,preferred_element_type=f32)
+            gi=ga*gp[r,pl.ds(m,TM),pl.ds(n,T)]
+            il[pl.ds(m,TM),pl.ds(n,T)]=gi.astype(bf16)
             part=fold(gi)
             eb_ref[r,:,pl.ds(n,T)]=jnp.where(m==0,part,eb_ref[r,:,pl.ds(n,T)]+part)
             return 0
-        lax.fori_loop(0,per*mt,tile,0)
+        lax.fori_loop(0,per*mt,tile,0,unroll=3)
         def back(j,_):
-            n=pl.multiple_of((j//mt)*T,T); m=pl.multiple_of((j%mt)*T,T)
-            acc[pl.ds(m,T),pl.ds(n,T)]+=lax.dot_general(il[pl.ds(m,T),:],we[r,pl.ds(n,T),:],NT,preferred_element_type=f32)
-            return 0
-        lax.fori_loop(0,(width//T)*mt,back,0)
+            n=pl.multiple_of((j//mt)*T,T); m=pl.multiple_of((j%mt)*TM,TM)
+            acc[pl.ds(m,TM),pl.ds(n,T)]+=lax.dot_general(il[pl.ds(m,TM),:],we[r,pl.ds(n,T),:],NT,preferred_element_type=f32)
+            return 0
+        lax.fori_loop(0,(width//T)*mt,back,0,unroll=3)
         for k in range(2,blocks):
             @pl.when(r==k)
             def _():
                 for c in sent(r,k%2,k-2): c.wait()
         def grads(j,_):
-            n=pl.multiple_of((j//(width//T))*T,T); m=pl.multiple_of((j%(width//T))*T,T)
-            dt[slot,pl.ds(m,T),pl.ds(n,T)]=lax.dot_general(slT[pl.ds(m,T),:],act[r,:,pl.ds(n,T)],NN,preferred_element_type=f32).astype(bf16)
-            de[slot,pl.ds(m,T),pl.ds(n,T)]=lax.dot_general(hlT[pl.ds(m,T),:],il[:,pl.ds(n,T)],NN,preferred_element_type=f32).astype(bf16)
-            return 0
-        lax.fori_loop(0,(width//T)*per,grads,0)
+            n=pl.multiple_of((j//(width//TG))*T,T); m=pl.multiple_of((j%(width//TG))*TG,TG)
+            dt[slot,pl.ds(m,TG),pl.ds(n,T)]=lax.dot_general(slT[pl.ds(m,TG),:],act[r,:,pl.ds(n,T)],NN,preferred_element_type=f32).astype(bf16)
+            de[slot,pl.ds(m,TG),pl.ds(n,T)]=lax.dot_general(hlT[pl.ds(m,TG),:],il[:,pl.ds(n,T)],NN,preferred_element_type=f32).astype(bf16)
+            return 0
+        lax.fori_loop(0,(width//TG)*per,grads,0,unroll=3)
         for k in range(blocks):
             @pl.when(r==k)
             def _():
@@ -284,40 +291,177 @@
         gm_ref[at,:]=gm
         gml_ref[at,:]=gm.astype(bf16)
         return (sums[0]+fold(g*z),sums[1]+fold(g),sums[2]+fold(gm))
-    fg,fs,mbg=lax.fori_loop(0,rows//RC,last,(zero,zero,zero))
+    fg,fs,mbg=lax.fori_loop(0,rows//RC,last,(zero,zero,zero),unroll=4)
     for n,v in enumerate((mbg,fg,fs,sbg,sg,sh)):
         vg_ref[n]=v
     for k in range(max(0,blocks-2),blocks):
         for c in sent(k,k%2,k): c.wait()
 
-def ffn(tok,a0,a1,a2,cot,vec,be,es):
-    rows,width=tok.shape; blocks=len(es); units=es[0].shape[1]//2
+def ffn(tok,a0,a1,a2,cot,vec,be,w_own,w_other):
+    rows,width=tok.shape; blocks,units=be.shape
     v=pl.BlockSpec(memory_space=pltpu.VMEM); h=pl.BlockSpec(memory_space=pltpu.HBM)
-    g=jax.ShapeDtypeStruct((width,2*units),bf16)
+    g=jax.ShapeDtypeStruct((width,blocks*units),bf16)
     V=pltpu.VMEM
     return pl.pallas_call(
         ffn_kernel,
         out_shape=(jax.ShapeDtypeStruct((rows,width),bf16),jax.ShapeDtypeStruct((rows,width),f32),jax.ShapeDtypeStruct((rows,width),bf16),
-                   jax.ShapeDtypeStruct((6,8,width),f32),jax.ShapeDtypeStruct((blocks,8,units),f32))+(g,)*blocks,
-        in_specs=[v]*7+[h]*blocks,
-        out_specs=[v]*5+[h]*blocks,
+                   jax.ShapeDtypeStruct((6,8,width),f32),jax.ShapeDtypeStruct((blocks,8,units),f32))+(g,g),
+        in_specs=[v]*7+[h]*2,
+        out_specs=[v]*5+[h]*2,
         scratch_shapes=[V((blocks,width,units),bf16),V((blocks,width,units),bf16),
             V((rows,width),bf16),V((width,rows),bf16),V((rows,width),f32),V((rows,width),f32),V((rows,128),f32),
             V((blocks,rows,units),bf16),V((blocks,rows,units),f32),V((rows,width),f32),V((rows,width),bf16),V((width,rows),bf16),V((rows,width),f32),
             V((rows,units),bf16),V((2,width,units),bf16),V((2,width,units),bf16),
             pltpu.SemaphoreType.DMA((2,blocks)),pltpu.SemaphoreType.DMA((2,2))],
         compiler_params=pltpu.CompilerParams(vmem_limit_bytes=60<<20),
-        cost_estimate=pl.CostEstimate(flops=12*rows*width*units*blocks,bytes_accessed=8*blocks*width*units,transcendentals=2*rows*units*blocks),
+        cost_estimate=pl.CostEstimate(flops=30*rows*width*units*blocks,bytes_accessed=8*blocks*width*units,transcendentals=2*rows*units*blocks),
         name="feed_forward",
-    )(tok,a0,a1,a2,cot,vec,be,*es)
+    )(tok,a0,a1,a2,cot,vec,be,w_own,w_other)
+
+
+def proj_kernel(home_ref, x0, x1, x2, x3, wa_ref, wb_ref, bq_ref, bvc_ref, bvr_ref,
+                q_ref, kT_ref, vT_ref, k_ref, v_ref, wT, w_ref, sem):
+    model = w_ref.shape[0]
+    count, rows = sem.shape[0], model // sem.shape[0]
+    width = q_ref.shape[0]
+    home = home_ref[0]
+    def copy(r):
+        src = (wa_ref, wb_ref)[r % 2].at[(r // 2) * rows : (r // 2 + 1) * rows]
+        at = pl.multiple_of(jnp.bitwise_xor(home, r) * rows, rows)
+        return pltpu.make_async_copy(src, w_ref.at[pl.ds(at, rows)], sem.at[r])
+    if wa_ref.shape[0] == model:
+        count = 1
+        copy = lambda r: pltpu.make_async_copy(wa_ref, w_ref, sem.at[r])
+    for r in range(count):
+        copy(r).start()
+    for r in range(count):
+        copy(r).wait()
+    def turn(i, _):
+        at = pl.multiple_of(i * 256, 256)
+        wT[:, pl.ds(at, 256)] = jnp.transpose(w_ref[pl.ds(at, 256), :].astype(f32)).astype(bf16)
+        return 0
+    lax.fori_loop(0, model // 256, turn, 0)
+    for n, x_ref in enumerate((x0, x1, x2, x3)):
+        size = x_ref.shape[0]
+        def part(i, _):
+            at = pl.multiple_of(i * 256, 256)
+            to = pl.multiple_of(n * size + at, 256)
+            x = x_ref[pl.ds(at, 256), :]
+            kv = jnp.dot(x, w_ref[:, width : 3 * width], preferred_element_type=f32)
+            k_ref[pl.ds(to, 256), :] = kv[:, 0:width].astype(bf16)
+            v_ref[pl.ds(to, 256), :] = (kv[:, width:] + bvr_ref[...]).astype(bf16)
+            t = lax.dot_general(wT[0 : 3 * width], x, NT, preferred_element_type=f32)
+            q_ref[:, pl.ds(to, 256)] = (t[0:width] + bq_ref[...]).astype(bf16)
+            kT_ref[:, pl.ds(to, 256)] = t[width : 2 * width].astype(bf16)
+            vT_ref[:, pl.ds(to, 256)] = (t[2 * width :] + bvc_ref[...]).astype(bf16)
+            return 0
+        lax.fori_loop(0, size // 256, part, 0)
+
+
+def project(home, tokens, wa, wb, count, bq, bv):
+    length = 4 * tokens[0].shape[0]
+    model = tokens[0].shape[1]
+    width = bq.shape[0]
+    v = pl.BlockSpec(memory_space=pltpu.VMEM)
+    tall = jax.ShapeDtypeStruct((length, width), bf16)
+    flat = jax.ShapeDtypeStruct((width, length), bf16)
+    return pl.pallas_call(
+        proj_kernel,
+        out_shape=(flat, flat, flat, tall, tall, jax.ShapeDtypeStruct((model, model), bf16)),
+        in_specs=[pl.BlockSpec(memory_space=pltpu.SMEM)] + [v] * 9,
+        out_specs=[v] * 6,
+        scratch_shapes=[pltpu.VMEM((model, model), bf16), pltpu.SemaphoreType.DMA((count,))],
+        compiler_params=pltpu.CompilerParams(vmem_limit_bytes=60 << 20),
+        cost_estimate=pl.CostEstimate(flops=30 * length * model * width, bytes_accessed=4 * length * model, transcendentals=0),
+        name="projection",
+    )(home, *tokens, wa, wb, bq[:, None], bv[:, None], bv[None, :])
+
+
+def grads_kernel(x0, x1, x2, x3, g0, g1, g2, g3, c_ref, q_ref, k_ref, v_ref, o_ref, acc, xT, gT):
+    width = q_ref.shape[0]
+    model = x0.shape[1]
+    for n, (x_ref, g_ref) in enumerate(zip((x0, x1, x2, x3), (g0, g1, g2, g3))):
+        size = x_ref.shape[0]
+        rows = slice(n * size, (n + 1) * size)
+        def turn(i, _):
+            at = pl.multiple_of(i * 256, 256)
+            xT[:, pl.ds(at, 256)] = jnp.transpose(x_ref[pl.ds(at, 256), :].astype(f32)).astype(bf16)
+            gT[:, pl.ds(at, 256)] = jnp.transpose(g_ref[pl.ds(at, 256), :].astype(f32)).astype(bf16)
+            return 0
+        lax.fori_loop(0, size // 256, turn, 0)
+        def part(i, _):
+            at = pl.ds(pl.multiple_of(i * 256, 256), 256)
+            x = xT[at, :]
+            pieces = (
+                lax.dot_general(x, q_ref[:, rows], NT, preferred_element_type=f32),
+                jnp.dot(x, k_ref[rows, :], preferred_element_type=f32),
+                jnp.dot(x, v_ref[rows, :], preferred_element_type=f32),
+                lax.dot_general(gT[at, :], c_ref[:, rows], NT, preferred_element_type=f32),
+            )
+            for m, piece in enumerate(pieces):
+                total = piece if n == 0 else acc[m, at, :] + piece
+                if n == 3:
+                    o_ref[at, m * width : (m + 1) * width] = total.astype(bf16)
+                else:
+                    acc[m, at, :] = total
+            return 0
+        lax.fori_loop(0, model // 256, part, 0)
+
+
+def attn_grads(tokens, grads, contextT, dqT, dk, dv):
+    size, model = tokens[0].shape
+    width = dqT.shape[0]
+    v = pl.BlockSpec(memory_space=pltpu.VMEM)
+    return pl.pallas_call(
+        grads_kernel,
+        out_shape=jax.ShapeDtypeStruct((model, 4 * width), bf16),
+        in_specs=[v] * 12,
+        out_specs=v,
+        scratch_shapes=[pltpu.VMEM((4, model, width), f32), pltpu.VMEM((model, size), bf16), pltpu.VMEM((model, size), bf16)],
+        compiler_params=pltpu.CompilerParams(vmem_limit_bytes=60 << 20),
+        cost_estimate=pl.CostEstimate(flops=120 * size * model * width, bytes_accessed=24 * size * model, transcendentals=0),
+        name="projection_grads",
+    )(*tokens, *grads, contextT, dqT, dk, dv)
+
+
+def hop(value, bit):
+    count = lax.axis_size("dp")
+    return lax.ppermute(value, "dp", [(i, i ^ bit) for i in range(count)])
+
+
+def gather_shards(own):
+    count = lax.axis_size("dp")
+    if count != 8:
+        every = lax.all_gather(own, "dp", axis=0, tiled=True)
+        return every, every
+    even = jnp.concatenate([own] + [hop(own, bit) for bit in (2, 4, 6)], axis=0)
+    return even, hop(even, 1)
+
+
+def later(value, *markers):
+    anywhere = pl.BlockSpec(memory_space=pl.ANY)
+    return pl.pallas_call(
+        lambda *refs: None,
+        out_shape=jax.ShapeDtypeStruct(value.shape, value.dtype),
+        in_specs=[anywhere] * (1 + len(markers)),
+        out_specs=anywhere,
+        input_output_aliases={0: 0},
+        cost_estimate=pl.CostEstimate(flops=0, bytes_accessed=0, transcendentals=0),
+        name="later",
+    )(value, *markers)
+
 
 def exchange(value, bit):
     return lax.ppermute(value, "tensor", [(i, i ^ bit) for i in range(4)])
 
 
+def row_blocks(own):
+    across = exchange(own, 2)
+    return [own, exchange(own, 1), across, exchange(across, 1)]
+
+
 def gather_rows(own):
-    across = exchange(own, 2)
-    return jnp.concatenate([own, exchange(own, 1), across, exchange(across, 1)], axis=0)
+    return jnp.concatenate(row_blocks(own), axis=0)
 
 
 def scatter_rows(partial):
@@ -326,7 +470,7 @@
     piece = lambda r: low[r * rows : (r + 1) * rows]
     beside = exchange(jnp.concatenate([piece(1), piece(3)], axis=0), 1)
     ahead = (piece(2).astype(f32) + beside[rows:].astype(f32)).astype(bf16)
-    return piece(0), beside[:rows], exchange(ahead, 2)
+    return (piece(0), beside[:rows], exchange(ahead, 2)), ahead
 
 
 def on_device(
@@ -360,12 +504,10 @@
     unit_share = units * 4 // world
 
     shard = jnp.concatenate([query_proj, key_proj, value_proj, merge_proj.T], axis=1)
-    attn_w = lax.all_gather(shard, "dp", axis=0, tiled=True)
+    shards = gather_shards(shard)
     wide = jnp.concatenate([expand_proj, shrink_proj.T], axis=1)
-    w0 = lax.all_gather(wide, "dp", axis=0, tiled=True)
-    w2 = lax.all_gather(exchange(wide, 2), "dp", axis=0, tiled=True)
-    w1 = exchange(w0, 1)
-    w3 = exchange(w2, 1)
+    wide = jnp.concatenate([wide, exchange(wide, 2)], axis=1)
+    w_own = lax.all_gather(wide, "dp", axis=0, tiled=True)
     own = jnp.concatenate(
         [query_bias, value_bias, merge_bias, first_gain, first_shift, shrink_bias, second_gain, second_shift, expand_bias]
     )
@@ -381,47 +523,39 @@
     value_b = lax.dynamic_slice_in_dim(whole[1], part * width, width)
     rows_b = jnp.stack(whole[2:8])
 
-    full = gather_rows(tokens)
-    seg = gather_rows(segments.reshape(-1))
+    blocks = row_blocks(tokens)
+    seg = jnp.concatenate(row_blocks(segments.reshape(-1)), axis=0)
     segc, segr = seg[:, None], seg[None, :]
     lo, hi = spans(seg)
     flip = (part * (tokens.shape[0] // BK)).astype(jnp.int32).reshape(1)
-    wq, wk, wv, wm = (attn_w[:, n * width : (n + 1) * width] for n in range(4))
+    home = lax.axis_index("dp").astype(jnp.int32).reshape(1)
+    query_t, key_t, value_t, keys, values, attn_wt = project(home, blocks, *shards, dp, query_b, value_b)
+    wq, wk, wv, wm = (attn_wt[n * width : (n + 1) * width] for n in range(4))
     dot = lambda a, b, dims: lax.dot_general(a, b, dims, preferred_element_type=f32)
-    query_t = (dot(wq, full, (((0,), (1,)), ((), ()))) + query_b[:, None]).astype(bf16)
-    key_t = dot(wk, full, (((0,), (1,)), ((), ()))).astype(bf16)
-    value_t = (dot(wv, full, (((0,), (1,)), ((), ()))) + value_b[:, None]).astype(bf16)
-    keys = dot(full, wk, NN).astype(bf16)
-    values = (dot(full, wv, NN) + value_b).astype(bf16)
     context_t, logsum = attn_fwd(query_t, keys, value_t, segc, segr, lo, hi, flip)
-    a0, a1, a2 = scatter_rows(dot(context_t, wm, (((0,), (1,)), ((), ()))))
-
-    out = ffn(tokens, a0, a1, a2, cotangent, rows_b, unit_bias, [w0, w1, w2, w3])
+    (a0, a1, a2), ahead = scatter_rows(dot(context_t, wm, TN))
+
+    w_own = later(w_own, ahead)
+    w_other = exchange(w_own, 1)
+    out = ffn(tokens, a0, a1, a2, cotangent, rows_b, unit_bias, w_own, w_other)
     output, grad_mixed, mixed_low, row_sums, unit_sums = out[:5]
-    g0, g1, g2, g3 = out[5:]
-
-    full_mixed = gather_rows(mixed_low)
-    grad_context_t = dot(wm, full_mixed, (((0,), (1,)), ((), ()))).astype(bf16)
+    g_own, g_other = out[5:]
+
+    mixed_blocks = row_blocks(mixed_low)
+    wide_local = (g_own.astype(f32) + exchange(g_other, 1).astype(f32)).astype(bf16)
+    wide_local = lax.psum_scatter(wide_local, "dp", scatter_dimension=0, tiled=True)
     dq_t, dk, dv, q_sums, v_sums = attn_bwd(
-        query_t, keys, key_t, values, grad_context_t, context_t, logsum, segc, segr, lo, hi, flip
+        query_t, keys, key_t, values, attn_wt, mixed_blocks, context_t, logsum, segc, segr, lo, hi, flip
     )
-    total = dot(dq_t, wq, (((0,), (1,)), ((), ()))) + dot(dk, wk, NT) + dot(dv, wv, NT)
-    b0, b1, b2 = scatter_rows(total)
+    attn_local = attn_grads(blocks, mixed_blocks, context_t, dq_t, dk, dv)
+    swapped = lax.all_to_all(attn_local, "dp", 0, 0, tiled=True)
+    dq_late = later(dq_t, attn_local)
+    total = dot(dq_late, wq, TN) + dot(dk, wk, NN) + dot(dv, wv, NN)
+    (b0, b1, b2), _ = scatter_rows(total)
     tokens_grad = (grad_mixed + (b0.astype(f32) + b1.astype(f32) + b2.astype(f32))).astype(bf16)
-
-    merge_local = dot(full_mixed, context_t, (((0,), (1,)), ((), ())))
-    query_local = dot(full, dq_t, (((0,), (1,)), ((), ())))
-    key_local = dot(full, dk, TN)
-    value_local = dot(full, dv, TN)
-    attn_local = jnp.concatenate([query_local, key_local, value_local, merge_local], axis=1).astype(bf16)
-    swapped = lax.all_to_all(attn_local, "dp", 0, 0, tiled=True)
     attn_grad = jnp.sum(swapped.reshape(dp, -1, model).astype(f32), axis=0)
     querygrad, keygrad, valuegrad, mergegrad = (attn_grad[:, n * width : (n + 1) * width] for n in range(4))
-
-    near = (g0.astype(f32) + exchange(g1, 1).astype(f32)).astype(bf16)
-    far = (g2.astype(f32) + exchange(g3, 1).astype(f32)).astype(bf16)
-    wide_local = (near.astype(f32) + exchange(far, 2).astype(f32)).astype(bf16)
-    wide_grad = lax.psum_scatter(wide_local, "dp", scatter_dimension=0, tiled=True).astype(f32)
+    wide_grad = wide_local[:, : 2 * units].astype(f32) + exchange(wide_local[:, 2 * units :], 2).astype(f32)
     expandgrad = wide_grad[:, :units]
     shrinkgrad = wide_grad[:, units:].T
 

time: 422 us -> 332 us (0.79)
  waiting for transfers between devices: 172 us -> 106 us
  local copies, waits for them, and re-layouts: 42.3 us -> 18.8 us
  matrix products: 25.7 us -> 7.41 us
  Pallas kernels: 107 us -> 122 us
  starting transfers between devices: 31.6 us -> 36.6 us
    all_gather x3 -> x1, waiting for transfers between devices: 74.8 us -> 6.32 us  [on_device(): w_own = lax.all_gather(wide, 'dp', axis=0, tiled=True)]
    pallas_call x0 -> x4, Pallas kernels: none -> 25.1 us  [the longest x1 12.8 us: attn_grads(): pl.pallas_call(grads_kernel, out_shape=jax.ShapeDtypeStruct((model, 4 * w...]
    pallas_call x1, Pallas kernels: 55.7 us -> 32.3 us  [ffn(): pl.pallas_call(ffn_kernel, out_shape=(jax.ShapeDtypeStruct((rows, width),...]
    reduce_scatter x1, waiting for transfers between devices: 22.5 us -> 0.01 us  [on_device(): lax.psum_scatter(wide_local, 'dp', scatter_dimension=0, tiled=True)]
    dot_general x14 -> x4, matrix products: 25.7 us -> 7.41 us  [on_device(): lax.dot_general(a, b, dims, preferred_element_type=f32)]
    pallas_call x1, Pallas kernels: 32.2 us -> 41.4 us  [attn_bwd(): pl.pallas_call(bwd_kernel, out_shape=(jax.ShapeDtypeStruct((width, length...]
    ppermute x19 -> x17, waiting for transfers between devices: 42.6 us -> 50.6 us  [exchange(): return lax.ppermute(value, 'tensor', [(i, i ^ bit) for i in range(4)])]
    unnamed x93 -> x61, local copies, waits for them, and re-layouts: 13 us -> 5.21 us
  transfers between devices with their start and end apart: 26 -> 26, of which waited for: 10 -> 11; matrix products, arithmetic and copies ran while one was open for 20% -> 13% of each run, Pallas kernels for 12% -> 27%
where the time goes in v2:
time: 332 us; the launch traced here: 331 us
  Pallas kernels  122 us (37%)
  waiting for transfers between devices  106 us (32%)
  starting transfers between devices  36.6 us (11%)
  other arithmetic  25.8 us (8%)
  local copies, waits for them, and re-layouts  18.8 us (6%)
  between operations  14.7 us (4%)
  matrix products  7.41 us (2%)
    ppermute x17, waiting for transfers between devices, exchange(): return lax.ppermute(value, 'tensor', [(i, i ^ bit) for i in range(4)])  50.6 us
    pallas_call x1, Pallas kernels, attn_bwd(): pl.pallas_call(bwd_kernel, out_shape=(jax.ShapeDtypeStruct((width, length...  41.4 us
    all_to_all x1, waiting for transfers between devices, on_device(): swapped = lax.all_to_all(attn_local, 'dp', 0, 0, tiled=True)  36.4 us
    pallas_call x1, Pallas kernels, ffn(): pl.pallas_call(ffn_kernel, out_shape=(jax.ShapeDtypeStruct((rows, width),...  32.3 us
    pallas_call x1, Pallas kernels, attn_fwd(): pl.pallas_call(fwd_kernel, out_shape=(jax.ShapeDtypeStruct((width, length...  23 us
    pallas_call x1, Pallas kernels, attn_grads(): pl.pallas_call(grads_kernel, out_shape=jax.ShapeDtypeStruct((model, 4 * w...  12.8 us
    ppermute x17, starting transfers between devices, exchange(): return lax.ppermute(value, 'tensor', [(i, i ^ bit) for i in range(4)])  12.7 us
    pallas_call x1, Pallas kernels, project(): pl.pallas_call(proj_kernel, out_shape=(flat, flat, flat, tall, tall, jax....  12.3 us
  transfers between devices with their start and end apart: 26, of which 11 were waited for; matrix products, arithmetic and copies ran while one was open for 13% of the time, Pallas kernels for 27%

profile of v2, /device:TPU:0, one launch (start us, length us, event | category | flops | bytes accessed | tf_op | source)
XLA Modules:
  0.0 331.5 jit_solution(1060407631835695364)
XLA Ops:
  7.4 1.1 pad_maximum_fusion.4
  8.5 3.0 collective-permute-start.12
  11.5 7.0 %collective-permute-done.12 = bf16[96,1536]{1,0:T(8,128)(2,1)S(1)} collective-permute-done((bf16[96,1536]{1,0:T(8,128)(2,1)S(1)}, bf16[96,1536]{1,0:T(8,128)(2,1)S(1)}, u32[]{:S(2)}, u32[]{:S(2)}) %collective-permute-start.12) | collective-permute-done | bytes 294944 | tf_op jit(solution)/shard_map/ppermute | solution.py:455
  18.5 1.9 pad_maximum_fusion.3
  20.4 1.8 collective-permute-start.4
  22.5 1.7 collective-permute-start.6
  24.1 2.6 collective-permute-start.7
  27.4 0.7 broadcast_in_dim.45
  28.1 6.1 %all-to-all-start = ((f32[32,8,128]{2,1,0:T(8,128)}), f32[32,8,128]{2,1,0:T(8,128)S(1)}, u32[]{:S(2)}, u32[]{:S(2)}) async-start(f32[32,8,128]{2,1,0:T(8,128)} %broadcast_in_dim.45), calls=%async_computation | async-start | bytes 262144 | tf_op jit(solution)/shard_map/all_to_all | solution.py:516
  34.2 5.5 %collective-permute-done.1 = s32[512]{0:T(512)S(1)} collective-permute-done((s32[512]{0:T(512)S(1)}, s32[512]{0:T(512)S(1)}, u32[]{:S(2)}, u32[]{:S(2)}) %collective-permute-start.1) | collective-permute-done | bytes 2080 | tf_op jit(solution)/shard_map/ppermute | solution.py:455
  40.2 3.3 collective-permute-done.7
  44.1 1.6 collective-permute-start.9
  46.1 1.4 copy.58.segc_ref
  48.0 7.6 %all-to-all-done = f32[32,8,128]{2,1,0:T(8,128)S(1)} async-done(((f32[32,8,128]{2,1,0:T(8,128)}), f32[32,8,128]{2,1,0:T(8,128)S(1)}, u32[]{:S(2)}, u32[]{:S(2)}) %all-to-all-start) | async-done | bytes 131104 | tf_op jit(solution)/shard_map/all_to_all | solution.py:516
  56.0 0.8 copy.57.bvc_ref
  56.9 0.8 copy.56.bq_ref
  57.7 2.1 collective-permute-done.9.wb_ref
  59.8 12.3 %projection.1 = (bf16[192,2048]{1,0:T(8,128)(2,1)}, bf16[192,2048]{1,0:T(8,128)(2,1)}, bf16[192,2048]{1,0:T(8,128)(2,1)}, bf16[2048,192]{1,0:T(8,128)(2,1)}, bf1...) custom-call(s32[1]{0:T(128)} %bitcast.2.home_ref, bf16[512,768]{1,0:T(8,128)(2,1)} %x0.3, ...), custom_call_target="tpu_custom_call" | custom-call | flops 9059696640 | bytes 6291456 | tf_op jit(solution)/shard_map/projection/pallas_call | solution.py:368
  72.1 23.0 %attention.1 = (bf16[192,2048]{1,0:T(8,128)(2,1)}, f32[3,2048]{1,0:T(4,128)}) custom-call(s32[8]{0:T(128)} %get-tuple-element.162.lo_ref, s32[8]{0:T(128)} %get-tuple-element.161.hi_ref, s32[1]{0:T(128)} %bitcast.1.flip_ref, bf16[192,2048]{1,0:T(8,128)(2,1)} %get-tuple-element.38.q_ref, bf16[2048,192]{1,0:T(8,128)(2,1)} %get-tuple-element.39.k_ref, ...), custom_call_target="tpu_custom_call" | custom-call | flops 24159191040 | bytes 3145728 | tf_op jit(solution)/shard_map/attention/pallas_call | solution.py:67
  95.2 2.2 convolution_convert_fusion
  97.4 1.1 fusion.10
  98.7 3.4 %collective-permute-done.10 = bf16[1024,768]{1,0:T(8,128)(2,1)S(1)} collective-permute-done((bf16[1024,768]{1,0:T(8,128)(2,1)S(1)}, bf16[1024,768]{1,0:T(8,128)(2,1)S(1)}, u32[]{:S(2)}, u32[]{:S(2)}) %collective-permute-start.10) | collective-permute-done | bytes 1572896 | tf_op jit(solution)/shard_map/ppermute | solution.py:455
  102.1 1.1 add_convert_fusion.4.refs_1_
  103.2 6.3 %all-gather.2.cloned.1.call-done.refs_0_ = bf16[768,3072]{1,0:T(8,128)(2,1)} async-done(((bf16[96,3072]{1,0:T(8,128)(2,1)}), bf16[768,3072]{1,0:T(8,128)(2,1)}) %all-gather.2.cloned.1.call-update) | async-done | bytes 4718608 | tf_op jit(solution)/shard_map/all_gather | solution.py:510
  109.5 1.4 collective-permute-start.11
  111.6 0.6 gather_fusion
  112.2 0.6 stack.3.vec_ref
  112.9 0.7 broadcast_select_fusion.1.be_ref
  113.5 0.9 slice.185.a1_ref
  114.5 15.0 %collective-permute-done.11.a2_ref = bf16[512,768]{1,0:T(8,128)(2,1)S(1)} collective-permute-done((bf16[512,768]{1,0:T(8,128)(2,1)S(1)}, bf16[512,768]{1,0:T(8,128)(2,1)S(1)}, u32[]{:S(2)}, u32[]{:S(2)}) %collective-permute-start.11) | collective-permute-done | bytes 786464 | tf_op jit(solution)/shard_map/ppermute | solution.py:455
  129.4 0.9 copy-done.27
  130.3 32.3 %feed_forward.1 = (bf16[512,768]{1,0:T(8,128)(2,1)}, f32[512,768]{1,0:T(8,128)}, bf16[512,768]{1,0:T(8,128)(2,1)}, f32[6,8,768]{2,1,0:T(8,128)}, f32[4,8,768]{2,...) custom-call(bf16[512,768]{1,0:T(8,128)(2,1)} %x0.3, bf16[512,768]{1,0:T(8,128)(2,1)} %get-tuple-element.138.a0_ref, ...), custom_call_target="tpu_custom_call" | custom-call | flops 36238786560 | bytes 18874368 | tf_op jit(solution)/shard_map/feed_forward/pallas_call | solution.py:305
  162.7 1.5 collective-permute-start.15
  164.4 0.9 reduce_sum.79
  165.9 0.9 reduce_sum.80
  166.8 0.6 gather_fusion.1
  167.6 15.3 %collective-permute-done.15.g2 = bf16[512,768]{1,0:T(8,128)(2,1)S(1)} collective-permute-done((bf16[512,768]{1,0:T(8,128)(2,1)}, bf16[512,768]{1,0:T(8,128)(2,1)S(1)}, u32[]{:S(2)}, u32[]{:S(2)}) %collective-permute-start.15) | collective-permute-done | bytes 786464 | tf_op jit(solution)/shard_map/ppermute | solution.py:455
  182.9 8.1 %add_convert_fusion = bf16[768,3072]{1,0:T(8,128)(2,1)} fusion(bf16[768,3072]{1,0:T(8,128)(2,1)} %collective-permute-done.19, bf16[768,3072]{1,0:T(8,128)(2,1)} %get-tuple-element.56), kind=kLoop, calls=%fused_computation.2 | loop fusion | flops 9437184 | bytes 14155776 | tf_op jit(solution)/shard_map/convert_element_type | solution.py:545
  191.1 0.8 copy-done.25
  192.2 41.4 %attention_back.1 = (bf16[192,2048]{1,0:T(8,128)(2,1)}, bf16[2048,192]{1,0:T(8,128)(2,1)}, bf16[2048,192]{1,0:T(8,128)(2,1)}, f32[192,128]{1,0:T(8,128)}, f32[8,192]{1,0:T(8,128)}) custom-call(s32[8]{0:T(128)} %get-tuple-element.162.lo_ref, s32[8]{0:T(128)} %get-tuple-element.161.hi_ref, s32[1]{0:T(128)} %bitcast.1.flip_ref, ...), custom_call_target="tpu_custom_call" | custom-call | flops 48318382080 | bytes 7864320 | tf_op jit(solution)/shard_map/attention_back/pallas_call | solution.py:144
  233.6 1.0 reduce_sum.77
  234.8 0.7 reduce_sum.78
  235.8 0.7 copy.62
  236.4 6.2 %all-to-all-start.2 = ((f32[32,8,128]{2,1,0:T(8,128)}), f32[32,8,128]{2,1,0:T(8,128)S(1)}, u32[]{:S(2)}, u32[]{:S(2)}) async-start(f32[32,8,128]{2,1,0:T(8,128)} %bitcast.20), calls=%async_computation.2 | async-start | bytes 262144 | tf_op jit(solution)/shard_map/all_to_all | solution.py:569
  242.6 12.8 %projection_grads.1.refs_1_ = bf16[768,768]{1,0:T(8,128)(2,1)} custom-call(bf16[512,768]{1,0:T(8,128)(2,1)} %x0.3, bf16[512,768]{1,0:T(8,128)(2,1)} %collective-permute-done.3.x1, bf16[512,768]{1,0:T(8,128)(2,1)} %copy-done.23, bf16[512,768]{1,0:T(8,128)(2,1)} %collective-permute-done.5.x3, bf16[512,768]{1,0:T(8,128)(2,1)} %get-tuple-element.47.g0, ...), custom_call_target="tpu_custom_call" | custom-call | flops 9059696640 | bytes 9437184 | tf_op jit(solution)/shard_map/projection_grads/pallas_call | solution.py:415
  255.4 1.3 copy-done.2
  256.7 2.3 fusion.6
  259.0 1.0 fusion.4
  260.2 1.9 add_convert_fusion.1
  262.2 1.3 pad_maximum_fusion.1
  263.8 5.6 %all-to-all-start.1 = ((bf16[8,96,768]{2,1,0:T(8,128)(2,1)}), bf16[8,96,768]{2,1,0:T(8,128)(2,1)}, u32[]{:S(2)}, u32[]{:S(2)}) async-start(bf16[8,96,768]{2,1,0:T(8,128)(2,1)} %bitcast.31), calls=%async_computation.1 | async-start | bytes 2359296 | tf_op jit(solution)/shard_map/all_to_all | solution.py:551
  269.4 2.2 add_convert_fusion.3
  271.6 1.5 collective-permute-start.18
  273.2 0.6 slice.171
  273.7 0.6 fusion.12
  274.3 36.4 %all-to-all-done.1 = bf16[8,96,768]{2,1,0:T(8,128)(2,1)} async-done(((bf16[8,96,768]{2,1,0:T(8,128)(2,1)}), bf16[8,96,768]{2,1,0:T(8,128)(2,1)}, u32[]{:S(2)}, u32[]{:S(2)}) %all-to-all-start.1) | async-done | bytes 1179680 | tf_op jit(solution)/shard_map/all_to_all | solution.py:551
  310.7 1.5 convert_reduce_fusion
  312.2 0.8 slice_bitcast_fusion.1
  312.9 0.7 copy.60
  313.7 1.0 slice.206
  314.7 1.5 collective-permute-start.20
  316.2 3.1 add_convert_fusion.2
  319.3 4.4 %collective-permute-done.20 = bf16[96,1536]{1,0:T(8,128)(2,1)S(1)} collective-permute-done((bf16[96,1536]{1,0:T(8,128)(2,1)S(1)}, bf16[96,1536]{1,0:T(8,128)(2,1)S(1)}, u32[]{:S(2)}, u32[]{:S(2)}) %collective-permute-start.20) | collective-permute-done | bytes 294944 | tf_op jit(solution)/shard_map/ppermute | solution.py:455
  323.8 0.9 slice_bitcast_fusion
  (134 shorter events, 6.8 us)
Async XLA Ops:
  7.2 13.2 %copy-start.22 = (bf16[512,768]{1,0:T(8,128)(2,1)S(1)}, bf16[512,768]{1,0:T(8,128)(2,1)}, u32[]{:S(2)}) copy-start(bf16[512,768]{1,0:T(8,128)(2,1)} %x0.3) | copy-start | bytes 2359300
  7.2 15.0 %copy-start.10 = (bf16[192,96]{1,0:T(8,128)(2,1)S(1)}, bf16[192,96]{1,0:T(8,128)(2,1)}, u32[]{:S(2)}) copy-start(bf16[192,96]{1,0:T(8,128)(2,1)} %param.27) | copy-start | bytes 110596
  7.2 15.1 %copy-start.8 = (bf16[96,192]{1,0:T(8,128)(2,1)S(1)}, bf16[96,192]{1,0:T(8,128)(2,1)}, u32[]{:S(2)}) copy-start(bf16[96,192]{1,0:T(8,128)(2,1)} %param.22) | copy-start | bytes 110596
  7.2 15.1 %copy-start.7 = (bf16[96,192]{1,0:T(8,128)(2,1)S(1)}, bf16[96,192]{1,0:T(8,128)(2,1)}, u32[]{:S(2)}) copy-start(bf16[96,192]{1,0:T(8,128)(2,1)} %param.24) | copy-start | bytes 110596
  7.2 15.1 %copy-start.6 = (bf16[96,192]{1,0:T(8,128)(2,1)S(1)}, bf16[96,192]{1,0:T(8,128)(2,1)}, u32[]{:S(2)}) copy-start(bf16[96,192]{1,0:T(8,128)(2,1)} %param.25) | copy-start | bytes 110596
  7.2 19.7 %copy-start.12 = (s32[1,512]{1,0:T(1,128)S(1)}, s32[1,512]{1,0:T(1,128)}, u32[]{:S(2)}) copy-start(s32[1,512]{1,0:T(1,128)} %param.21) | copy-start | bytes 6148
  7.3 20.0 %copy-start.13 = (f32[24]{0:T(128)S(1)}, f32[24]{0:T(128)}, u32[]{:S(2)}) copy-start(f32[24]{0:T(128)} %param.23) | copy-start | bytes 292
  7.3 20.0 %copy-start.14 = (f32[24]{0:T(128)S(1)}, f32[24]{0:T(128)}, u32[]{:S(2)}) copy-start(f32[24]{0:T(128)} %param.26) | copy-start | bytes 292
  7.3 20.0 %copy-start.15 = (f32[24]{0:T(128)S(1)}, f32[24]{0:T(128)}, u32[]{:S(2)}) copy-start(f32[24]{0:T(128)} %param.28) | copy-start | bytes 292
  7.3 20.0 %copy-start.16 = (f32[24]{0:T(128)S(1)}, f32[24]{0:T(128)}, u32[]{:S(2)}) copy-start(f32[24]{0:T(128)} %param.29) | copy-start | bytes 292
  7.3 20.0 %copy-start.17 = (f32[24]{0:T(128)S(1)}, f32[24]{0:T(128)}, u32[]{:S(2)}) copy-start(f32[24]{0:T(128)} %param.30) | copy-start | bytes 292
  7.3 20.0 %copy-start.21 = (f32[96]{0:T(128)S(1)}, f32[96]{0:T(128)}, u32[]{:S(2)}) copy-start(f32[96]{0:T(128)} %param.32) | copy-start | bytes 1156
  7.3 20.0 %copy-start.18 = (f32[24]{0:T(128)S(1)}, f32[24]{0:T(128)}, u32[]{:S(2)}) copy-start(f32[24]{0:T(128)} %param.34) | copy-start | bytes 292
  7.3 20.0 %copy-start.19 = (f32[24]{0:T(128)S(1)}, f32[24]{0:T(128)}, u32[]{:S(2)}) copy-start(f32[24]{0:T(128)} %param.35) | copy-start | bytes 292
  7.3 20.0 %copy-start.20 = (f32[24]{0:T(128)S(1)}, f32[24]{0:T(128)}, u32[]{:S(2)}) copy-start(f32[24]{0:T(128)} %param.36) | copy-start | bytes 292
  7.3 102.1 %all-gather.2.cloned.1.call-start = ((), (), s32[]{:S(2)}) async-start(), calls=%async_computation.4 | async-start | bytes 5308416 | tf_op jit(solution)/shard_map/all_gather | solution.py:510
  8.5 10.0 %collective-permute-start.12 = (bf16[96,1536]{1,0:T(8,128)(2,1)S(1)}, bf16[96,1536]{1,0:T(8,128)(2,1)S(1)}, u32[]{:S(2)}, u32[]{:S(2)}) collective-permute-start(bf16[96,1536]{1,0:T(8,128)(2,1)S(1)} %pad_maximum_fusion.4), channel_id=1, source_target_pairs={{0,2},{1,3},{2,0},{3,1},{4,6},{5,7},{6,4},{7,5},{8,10},{9,11},{10,... | collective-permute-start | bytes 884744 | tf_op jit(solution)/shard_map/ppermute | solution.py:455
  20.4 23.1 %collective-permute-start.4 = (bf16[512,768]{1,0:T(8,128)(2,1)S(1)}, bf16[512,768]{1,0:T(8,128)(2,1)S(1)}, u32[]{:S(2)}, u32[]{:S(2)}) collective-permute-start(bf16[512,768]{1,0:T(8,128)(2,1)S(1)} %copy-done.22), channel_id=1, source_target_pairs={{0,2},{1,3},{2,0},{3,1},{4,6},{5,7},{6,4},{7,5},{8,10},{9,11},{10,... | collective-permute-start | bytes 2359304 | tf_op jit(solution)/shard_map/ppermute | solution.py:455
  22.5 17.2 %collective-permute-start.6 = (bf16[96,768]{1,0:T(8,128)(2,1)S(1)}, bf16[96,768]{1,0:T(8,128)(2,1)S(1)}, u32[]{:S(2)}, u32[]{:S(2)}) collective-permute-start(bf16[96,768]{1,0:T(8,128)(2,1)S(1)} %pad_maximum_fusion.5), channel_id=1, source_target_pairs={{0,8},{4,12},{8,0},{12,4},{16,24},{20,28},{24,16},{28,20},{1,9},{5... | collective-permute-start | bytes 442376 | tf_op jit(solution)/shard_map/ppermute | solution.py:429
  24.1 19.4 %collective-permute-start.7 = (bf16[96,768]{1,0:T(8,128)(2,1)S(1)}, bf16[96,768]{1,0:T(8,128)(2,1)S(1)}, u32[]{:S(2)}, u32[]{:S(2)}) collective-permute-start(bf16[96,768]{1,0:T(8,128)(2,1)S(1)} %pad_maximum_fusion.5), channel_id=1, source_target_pairs={{0,16},{4,20},{8,24},{12,28},{16,0},{20,4},{24,8},{28,12},{1,17},{... | collective-permute-start | bytes 442376 | tf_op jit(solution)/shard_map/ppermute | solution.py:429
  26.7 17.3 %collective-permute-start.8 = (bf16[96,768]{1,0:T(8,128)(2,1)S(1)}, bf16[96,768]{1,0:T(8,128)(2,1)S(1)}, u32[]{:S(2)}, u32[]{:S(2)}) collective-permute-start(bf16[96,768]{1,0:T(8,128)(2,1)S(1)} %pad_maximum_fusion.5), channel_id=1, source_target_pairs={{0,24},{4,28},{8,16},{12,20},{16,8},{20,12},{24,0},{28,4},{1,25},{... | collective-permute-start | bytes 442376 | tf_op jit(solution)/shard_map/ppermute | solution.py:429
  26.9 12.8 %collective-permute-start.1 = (s32[512]{0:T(512)S(1)}, s32[512]{0:T(512)S(1)}, u32[]{:S(2)}, u32[]{:S(2)}) collective-permute-start(s32[512]{0:T(512)S(1)} %bitcast.49), channel_id=1, source_target_pairs={{0,2},{1,3},{2,0},{3,1},{4,6},{5,7},{6,4},{7,5},{8,10},{9,11},{10,... | collective-permute-start | bytes 6152 | tf_op jit(solution)/shard_map/ppermute | solution.py:455
  28.1 27.6 %all-to-all-start = ((f32[32,8,128]{2,1,0:T(8,128)}), f32[32,8,128]{2,1,0:T(8,128)S(1)}, u32[]{:S(2)}, u32[]{:S(2)}) async-start(f32[32,8,128]{2,1,0:T(8,128)} %broadcast_in_dim.45), calls=%async_computation | async-start | bytes 262144 | tf_op jit(solution)/shard_map/all_to_all | solution.py:516
  34.1 279.5 %reduce-scatter.2.cloned.1.call-start = ((), (), s32[]{:S(2)}) async-start(), calls=%async_computation.5 | async-start | bytes 5308416 | tf_op jit(solution)/shard_map/reduce_scatter | solution.py:546
  39.7 20.1 %collective-permute-start.3 = (bf16[512,768]{1,0:T(8,128)(2,1)S(1)}, bf16[512,768]{1,0:T(8,128)(2,1)}, u32[]{:S(2)}, u32[]{:S(2)}) collective-permute-start(bf16[512,768]{1,0:T(8,128)(2,1)S(1)} %copy-done.22), channel_id=1, source_target_pairs={{0,1},{1,0},{2,3},{3,2},{4,5},{5,4},{6,7},{7,6},{8,9},{9,8},{10,11... | collective-permute-start | bytes 2359304 | tf_op jit(solution)/shard_map/ppermute | solution.py:455
  39.7 6.0 %collective-permute-start = (s32[512]{0:T(512)S(1)}, s32[512]{0:T(512)S(1)}, u32[]{:S(2)}, u32[]{:S(2)}) collective-permute-start(s32[512]{0:T(512)S(1)} %bitcast.50), channel_id=1, source_target_pairs={{0,1},{1,0},{2,3},{3,2},{4,5},{5,4},{6,7},{7,6},{8,9},{9,8},{10,11... | collective-permute-start | bytes 6152 | tf_op jit(solution)/shard_map/ppermute | solution.py:455
  43.5 2.2 collective-permute-start.2
  43.5 16.3 %copy-start.23 = (bf16[512,768]{1,0:T(8,128)(2,1)}, bf16[512,768]{1,0:T(8,128)(2,1)S(1)}, u32[]{:S(2)}) copy-start(bf16[512,768]{1,0:T(8,128)(2,1)S(1)} %collective-permute-done.4.x2) | copy-start | bytes 2359300
  43.5 16.3 %collective-permute-start.5 = (bf16[512,768]{1,0:T(8,128)(2,1)S(1)}, bf16[512,768]{1,0:T(8,128)(2,1)}, u32[]{:S(2)}, u32[]{:S(2)}) collective-permute-start(bf16[512,768]{1,0:T(8,128)(2,1)S(1)} %collective-permute-done.4.x2), channel_id=1, source_target_pairs={{0,1},{1,0},{2,3},{3,2},{4,5},{5,4},{6,7},{7,6},{8,9},{9,8},{10,11... | collective-permute-start | bytes 2359304 | tf_op jit(solution)/shard_map/ppermute | solution.py:455
  44.1 15.7 %copy-start.4 = (bf16[384,768]{1,0:T(8,128)(2,1)}, bf16[384,768]{1,0:T(8,128)(2,1)S(1)}, u32[]{:S(2)}) copy-start(bf16[384,768]{1,0:T(8,128)(2,1)S(1)} %pad_maximum_fusion.2.wa_ref) | copy-start | bytes 1769476
  44.1 15.7 %collective-permute-start.9 = (bf16[384,768]{1,0:T(8,128)(2,1)S(1)}, bf16[384,768]{1,0:T(8,128)(2,1)}, u32[]{:S(2)}, u32[]{:S(2)}) collective-permute-start(bf16[384,768]{1,0:T(8,128)(2,1)S(1)} %pad_maximum_fusion.2.wa_ref), channel_id=1, source_target_pairs={{0,4},{4,0},{8,12},{12,8},{16,20},{20,16},{24,28},{28,24},{1,5},{5... | collective-permute-start | bytes 1769480 | tf_op jit(solution)/shard_map/ppermute | solution.py:429
  45.7 26.4 %copy-start.9 = (s32[2048]{0:T(1024)}, s32[2048]{0:T(1024)S(1)}, u32[]{:S(2)}) copy-start(s32[2048]{0:T(1024)S(1)} %pad_add_fusion) | copy-start | bytes 24580
  56.0 3.8 %copy-start.11 = (f32[192]{0:T(256)}, f32[192]{0:T(256)S(1)}, u32[]{:S(2)}) copy-start(f32[192]{0:T(256)S(1)} %dynamic_slice.7) | copy-start | bytes 2308
  98.6 3.5 %collective-permute-start.10 = (bf16[1024,768]{1,0:T(8,128)(2,1)S(1)}, bf16[1024,768]{1,0:T(8,128)(2,1)S(1)}, u32[]{:S(2)}, u32[]{:S(2)}) collective-permute-start(bf16[1024,768]{1,0:T(8,128)(2,1)S(1)} %pad_maximum_fusion), channel_id=1, source_target_pairs={{0,1},{1,0},{2,3},{3,2},{4,5},{5,4},{6,7},{7,6},{8,9},{9,8},{10,11... | collective-permute-start | bytes 4718600 | tf_op jit(solution)/shard_map/ppermute | solution.py:455
  103.2 6.3 %copy-start = (bf16[512,768]{1,0:T(8,128)(2,1)S(1)}, bf16[512,768]{1,0:T(8,128)(2,1)}, u32[]{:S(2)}) copy-start(bf16[512,768]{1,0:T(8,128)(2,1)} %add_convert_fusion.4.refs_1_) | copy-start | bytes 2359300
  109.5 20.0 %collective-permute-start.13 = (bf16[768,3072]{1,0:T(8,128)(2,1)}, bf16[768,3072]{1,0:T(8,128)(2,1)}, u32[]{:S(2)}, u32[]{:S(2)}) collective-permute-start(bf16[768,3072]{1,0:T(8,128)(2,1)} %later.2.wa_ref), channel_id=1, source_target_pairs={{0,1},{1,0},{2,3},{3,2},{4,5},{5,4},{6,7},{7,6},{8,9},{9,8},{10,11... | collective-permute-start | bytes 14155784 | tf_op jit(solution)/shard_map/ppermute | solution.py:455
  109.5 20.0 %collective-permute-start.11 = (bf16[512,768]{1,0:T(8,128)(2,1)S(1)}, bf16[512,768]{1,0:T(8,128)(2,1)S(1)}, u32[]{:S(2)}, u32[]{:S(2)}) collective-permute-start(bf16[512,768]{1,0:T(8,128)(2,1)S(1)} %copy-done), channel_id=1, source_target_pairs={{0,2},{1,3},{2,0},{3,1},{4,6},{5,7},{6,4},{7,5},{8,10},{9,11},{10,... | collective-permute-start | bytes 2359304 | tf_op jit(solution)/shard_map/ppermute | solution.py:455
  129.4 0.9 copy-start.27
  162.6 20.3 %collective-permute-start.19 = (bf16[768,3072]{1,0:T(8,128)(2,1)}, bf16[768,3072]{1,0:T(8,128)(2,1)}, u32[]{:S(2)}, u32[]{:S(2)}) collective-permute-start(bf16[768,3072]{1,0:T(8,128)(2,1)} %get-tuple-element.57), channel_id=1, source_target_pairs={{0,1},{1,0},{2,3},{3,2},{4,5},{5,4},{6,7},{7,6},{8,9},{9,8},{10,11... | collective-permute-start | bytes 14155784 | tf_op jit(solution)/shard_map/ppermute | solution.py:455
  162.7 20.2 %collective-permute-start.15 = (bf16[512,768]{1,0:T(8,128)(2,1)}, bf16[512,768]{1,0:T(8,128)(2,1)S(1)}, u32[]{:S(2)}, u32[]{:S(2)}) collective-permute-start(bf16[512,768]{1,0:T(8,128)(2,1)} %get-tuple-element.47.g0), channel_id=1, source_target_pairs={{0,2},{1,3},{2,0},{3,1},{4,6},{5,7},{6,4},{7,5},{8,10},{9,11},{10,... | collective-permute-start | bytes 2359304 | tf_op jit(solution)/shard_map/ppermute | solution.py:455
  164.2 26.9 %collective-permute-start.14 = (bf16[512,768]{1,0:T(8,128)(2,1)}, bf16[512,768]{1,0:T(8,128)(2,1)S(1)}, u32[]{:S(2)}, u32[]{:S(2)}) collective-permute-start(bf16[512,768]{1,0:T(8,128)(2,1)} %get-tuple-element.47.g0), channel_id=1, source_target_pairs={{0,1},{1,0},{2,3},{3,2},{4,5},{5,4},{6,7},{7,6},{8,9},{9,8},{10,11... | collective-permute-start | bytes 2359304 | tf_op jit(solution)/shard_map/ppermute | solution.py:455
  182.9 8.2 %copy-start.24 = (bf16[512,768]{1,0:T(8,128)(2,1)}, bf16[512,768]{1,0:T(8,128)(2,1)S(1)}, u32[]{:S(2)}) copy-start(bf16[512,768]{1,0:T(8,128)(2,1)S(1)} %collective-permute-done.15.g2) | copy-start | bytes 2359300
  182.9 8.2 %collective-permute-start.16 = (bf16[512,768]{1,0:T(8,128)(2,1)S(1)}, bf16[512,768]{1,0:T(8,128)(2,1)S(1)}, u32[]{:S(2)}, u32[]{:S(2)}) collective-permute-start(bf16[512,768]{1,0:T(8,128)(2,1)S(1)} %collective-permute-done.15.g2), channel_id=1, source_target_pairs={{0,1},{1,0},{2,3},{3,2},{4,5},{5,4},{6,7},{7,6},{8,9},{9,8},{10,11... | collective-permute-start | bytes 2359304 | tf_op jit(solution)/shard_map/ppermute | solution.py:455
  191.1 0.9 copy-start.25
  191.1 1.1 copy-start.26
  236.4 27.3 %all-to-all-start.2 = ((f32[32,8,128]{2,1,0:T(8,128)}), f32[32,8,128]{2,1,0:T(8,128)S(1)}, u32[]{:S(2)}, u32[]{:S(2)}) async-start(f32[32,8,128]{2,1,0:T(8,128)} %bitcast.20), calls=%async_computation.2 | async-start | bytes 262144 | tf_op jit(solution)/shard_map/all_to_all | solution.py:569
  255.4 1.3 copy-start.2
  256.7 2.3 copy-start.1
  259.0 1.2 copy-start.3
  263.5 5.9 %collective-permute-start.17 = (bf16[1024,768]{1,0:T(8,128)(2,1)}, bf16[1024,768]{1,0:T(8,128)(2,1)}, u32[]{:S(2)}, u32[]{:S(2)}) collective-permute-start(bf16[1024,768]{1,0:T(8,128)(2,1)} %pad_maximum_fusion.1), channel_id=1, source_target_pairs={{0,1},{1,0},{2,3},{3,2},{4,5},{5,4},{6,7},{7,6},{8,9},{9,8},{10,11... | collective-permute-start | bytes 4718600 | tf_op jit(solution)/shard_map/ppermute | solution.py:455
  263.8 46.9 %all-to-all-start.1 = ((bf16[8,96,768]{2,1,0:T(8,128)(2,1)}), bf16[8,96,768]{2,1,0:T(8,128)(2,1)}, u32[]{:S(2)}, u32[]{:S(2)}) async-start(bf16[8,96,768]{2,1,0:T(8,128)(2,1)} %bitcast.31), calls=%async_computation.1 | async-start | bytes 2359296 | tf_op jit(solution)/shard_map/all_to_all | solution.py:551
  271.6 44.6 %collective-permute-start.18 = (bf16[512,768]{1,0:T(8,128)(2,1)}, bf16[512,768]{1,0:T(8,128)(2,1)}, u32[]{:S(2)}, u32[]{:S(2)}) collective-permute-start(bf16[512,768]{1,0:T(8,128)(2,1)} %add_convert_fusion.3), channel_id=1, source_target_pairs={{0,2},{1,3},{2,0},{3,1},{4,6},{5,7},{6,4},{7,5},{8,10},{9,11},{10,... | collective-permute-start | bytes 2359304 | tf_op jit(solution)/shard_map/ppermute | solution.py:455
  314.7 9.0 %collective-permute-start.20 = (bf16[96,1536]{1,0:T(8,128)(2,1)S(1)}, bf16[96,1536]{1,0:T(8,128)(2,1)S(1)}, u32[]{:S(2)}, u32[]{:S(2)}) collective-permute-start(bf16[96,1536]{1,0:T(8,128)(2,1)S(1)} %slice.206), channel_id=1, source_target_pairs={{0,2},{1,3},{2,0},{3,1},{4,6},{5,7},{6,4},{7,5},{8,10},{9,11},{10,... | collective-permute-start | bytes 884744 | tf_op jit(solution)/shard_map/ppermute | solution.py:455
  316.2 7.5 %copy-start.5 = (bf16[96,3072]{1,0:T(8,128)(2,1)S(1)}, bf16[96,3072]{1,0:T(8,128)(2,1)}, u32[]{:S(2)}) copy-start(bf16[96,3072]{1,0:T(8,128)(2,1)} %reduce-scatter.2.cloned.1.call-done) | copy-start | bytes 1769476
Sparse Core Ops, SparseCore 0:
  20.5 88.9 all-gather.1
  191.2 104.0 reduce-scatter.1

commit v3 on v2

--- a/solution.py
+++ b/solution.py
@@ -5,8 +5,8 @@
 from jax.experimental.pallas import tpu as pltpu
 
 HD=64
-BQ=256
-BK=256
+BQ=512
+BK=512
 LOG2E=1.4426950408889634
 NN=(((1,),(0,)),((),()))
 NT=(((1,),(1,)),((),()))
@@ -25,7 +25,7 @@
     zero = jnp.zeros_like(piece)
     return jnp.concatenate([piece, zero] if h%2==0 else [zero, piece], axis=0)
 
-def fwd_kernel(lo_ref, hi_ref, flip_ref, q_ref, k_ref, v_ref, segc_ref, segr_ref, o_ref, lse_ref, s_ref):
+def fwd_kernel(lo_ref, hi_ref, flip_ref, q_ref, k_ref, v_ref, w_ref, segc_ref, segr_ref, o_ref, lse_ref, near_ref, side_ref, far_ref, s_ref):
     heads = q_ref.shape[0]//HD
     i = pl.program_id(0)
     lo = lo_ref[i]; hi = hi_ref[i]; flip = flip_ref[0]
@@ -59,26 +59,38 @@
         total = jnp.sum(sums[h],axis=0,keepdims=True)
         o_ref[h*HD:(h+1)*HD,:] = (outs[h]/total).astype(bf16)
         lse_ref[h:h+1,:] = peaks[h]+jnp.log2(total)
-
-def attn_fwd(qT,k,vT,segc,segr,lo,hi,flip):
+    context = jnp.transpose(o_ref[...].astype(f32)).astype(bf16)
+    merged = jnp.dot(context, w_ref[...], preferred_element_type=f32).astype(bf16)
+    size = near_ref.shape[0]
+    per = size//BQ
+    for n, ref in enumerate((near_ref, side_ref, far_ref, side_ref)):
+        @pl.when(i//per==n)
+        def _():
+            at = pl.multiple_of((i%per)*BQ, BQ) + (size if n==3 else 0)
+            ref[pl.ds(pl.multiple_of(at, BQ), BQ),:] = merged
+
+def attn_fwd(qT,k,vT,wT,segc,segr,lo,hi,flip):
     width,length=qT.shape
+    size,model=length//4,wT.shape[1]
+    whole=lambda rows: pl.BlockSpec((rows,model),lambda i,*_:(0,0))
     heads=width//HD
     blocks=length//BQ
     return pl.pallas_call(
         fwd_kernel,
-        out_shape=(jax.ShapeDtypeStruct((width,length),bf16), jax.ShapeDtypeStruct((heads,length),f32)),
+        out_shape=(jax.ShapeDtypeStruct((width,length),bf16), jax.ShapeDtypeStruct((heads,length),f32))+tuple(jax.ShapeDtypeStruct((n*size,model),bf16) for n in (1,2,1)),
         grid_spec=pltpu.PrefetchScalarGridSpec(num_scalar_prefetch=3, grid=(blocks,),
             in_specs=[pl.BlockSpec((width,BQ),lambda i,*_:(0,i)),
                       pl.BlockSpec((length,width),lambda i,*_:(0,0)),
                       pl.BlockSpec((width,length),lambda i,*_:(0,0)),
+                      pl.BlockSpec((width,model),lambda i,*_:(model//width-1,0)),
                       pl.BlockSpec((length,1),lambda i,*_:(0,0)),
                       pl.BlockSpec((1,BQ),lambda i,*_:(0,i))],
-            out_specs=[pl.BlockSpec((width,BQ),lambda i,*_:(0,i)),pl.BlockSpec((heads,BQ),lambda i,*_:(0,i))],
+            out_specs=[pl.BlockSpec((width,BQ),lambda i,*_:(0,i)),pl.BlockSpec((heads,BQ),lambda i,*_:(0,i)),whole(size),whole(2*size),whole(size)],
             scratch_shapes=[pltpu.VMEM((heads,length//BK,BK,BQ),f32)]),
         compiler_params=pltpu.CompilerParams(dimension_semantics=("arbitrary",),vmem_limit_bytes=60<<20),
         cost_estimate=pl.CostEstimate(flops=30*length*length*width,bytes_accessed=8*length*width,transcendentals=heads*length*length//2),
         name="attention",
-    )(lo,hi,flip,qT,k,vT,segc,segr)
+    )(lo,hi,flip,qT,k,vT,wT,segc,segr)
 
 def bwd_kernel(lo_ref, hi_ref, flip_ref, q_ref, k_ref, kT_ref, v_ref, wT_ref, g0, g1, g2, g3, o_ref, lse_ref, segc_ref, segr_ref,
                dq_ref, dk_ref, dv_ref, qb_ref, vb_ref, dk_acc, dv_acc, do_ref):
@@ -96,7 +108,7 @@
         @pl.when(i//per==n)
         def _():
             at = pl.multiple_of((i%per)*BQ, BQ)
-            do_ref[...] = lax.dot_general(wT_ref[3*width:,:], g_ref[pl.ds(at,BQ),:], NT, preferred_element_type=f32).astype(bf16)
+            do_ref[...] = lax.dot_general(wT_ref[...], g_ref[pl.ds(at,BQ),:], NT, preferred_element_type=f32).astype(bf16)
     c = LOG2E*scale
     qz = [padded(q_ref, h, heads, slice(None)) for h in range(heads)]
     dz = [padded(do_ref, h, heads, slice(None)) for h in range(heads)]
@@ -145,14 +157,14 @@
         bwd_kernel,
         out_shape=(jax.ShapeDtypeStruct((width,length),bf16), jax.ShapeDtypeStruct((length,width),bf16), jax.ShapeDtypeStruct((length,width),bf16), jax.ShapeDtypeStruct((width,128),f32), jax.ShapeDtypeStruct((8,width),f32)),
         grid_spec=pltpu.PrefetchScalarGridSpec(num_scalar_prefetch=3, grid=(blocks,),
-            in_specs=[col,row,pl.BlockSpec((width,length),lambda i,*_:(0,0)),row,pl.BlockSpec(wT.shape,lambda i,*_:(0,0))]+[pl.BlockSpec(g.shape,lambda i,*_:(0,0)) for g in grads]+[col,
+            in_specs=[col,row,pl.BlockSpec((width,length),lambda i,*_:(0,0)),row,pl.BlockSpec((width,wT.shape[1]),lambda i,*_:(wT.shape[1]//width-1,0))]+[pl.BlockSpec(g.shape,lambda i,*_:(0,0)) for g in grads]+[col,
                       pl.BlockSpec((heads,BQ),lambda i,*_:(0,i)),
                       pl.BlockSpec((length,1),lambda i,*_:(0,0)),
                       pl.BlockSpec((1,BQ),lambda i,*_:(0,i))],
             out_specs=[col,row,row,pl.BlockSpec((width,128),lambda i,*_:(0,0)),pl.BlockSpec((8,width),lambda i,*_:(0,0))],
             scratch_shapes=[pltpu.VMEM((length,width),f32),pltpu.VMEM((length,width),f32),pltpu.VMEM((width,BQ),bf16)]),
         compiler_params=pltpu.CompilerParams(dimension_semantics=("arbitrary",),vmem_limit_bytes=60<<20),
-        cost_estimate=pl.CostEstimate(flops=60*length*length*width,bytes_accessed=20*length*width,transcendentals=heads*length*length//2),
+        cost_estimate=pl.CostEstimate(flops=38*length*length*width,bytes_accessed=20*length*width,transcendentals=heads*length*length//2),
         name="attention_back",
     )(lo,hi,flip,qT,k,kT,v,wT,*grads,oT,lse,segc,segr)
 
@@ -320,11 +332,12 @@
 
 
 def proj_kernel(home_ref, x0, x1, x2, x3, wa_ref, wb_ref, bq_ref, bvc_ref, bvr_ref,
-                q_ref, kT_ref, vT_ref, k_ref, v_ref, wT, w_ref, sem):
+                q_ref, kT_ref, vT_ref, k_ref, v_ref, wT, w_ref, wk, wv, x_buf, sem, x_sem):
     model = w_ref.shape[0]
     count, rows = sem.shape[0], model // sem.shape[0]
     width = q_ref.shape[0]
     home = home_ref[0]
+    step = pl.program_id(0)
     def copy(r):
         src = (wa_ref, wb_ref)[r % 2].at[(r // 2) * rows : (r // 2 + 1) * rows]
         at = pl.multiple_of(jnp.bitwise_xor(home, r) * rows, rows)
@@ -332,52 +345,61 @@
     if wa_ref.shape[0] == model:
         count = 1
         copy = lambda r: pltpu.make_async_copy(wa_ref, w_ref, sem.at[r])
-    for r in range(count):
-        copy(r).start()
-    for r in range(count):
-        copy(r).wait()
-    def turn(i, _):
-        at = pl.multiple_of(i * 256, 256)
-        wT[:, pl.ds(at, 256)] = jnp.transpose(w_ref[pl.ds(at, 256), :].astype(f32)).astype(bf16)
-        return 0
-    lax.fori_loop(0, model // 256, turn, 0)
-    for n, x_ref in enumerate((x0, x1, x2, x3)):
-        size = x_ref.shape[0]
-        def part(i, _):
+    fetch = [pltpu.make_async_copy(x, x_buf.at[n], x_sem.at[n]) for n, x in enumerate((x0, x1, x2, x3))]
+    @pl.when(step == 0)
+    def _():
+        for r in range(count):
+            copy(r).start()
+        for x in fetch:
+            x.start()
+        for r in range(count):
+            copy(r).wait()
+        def turn(i, _):
             at = pl.multiple_of(i * 256, 256)
-            to = pl.multiple_of(n * size + at, 256)
-            x = x_ref[pl.ds(at, 256), :]
-            kv = jnp.dot(x, w_ref[:, width : 3 * width], preferred_element_type=f32)
-            k_ref[pl.ds(to, 256), :] = kv[:, 0:width].astype(bf16)
-            v_ref[pl.ds(to, 256), :] = (kv[:, width:] + bvr_ref[...]).astype(bf16)
-            t = lax.dot_general(wT[0 : 3 * width], x, NT, preferred_element_type=f32)
-            q_ref[:, pl.ds(to, 256)] = (t[0:width] + bq_ref[...]).astype(bf16)
-            kT_ref[:, pl.ds(to, 256)] = t[width : 2 * width].astype(bf16)
-            vT_ref[:, pl.ds(to, 256)] = (t[2 * width :] + bvc_ref[...]).astype(bf16)
-            return 0
-        lax.fori_loop(0, size // 256, part, 0)
+            wT[:, pl.ds(at, 256)] = jnp.transpose(w_ref[pl.ds(at, 256), :].astype(f32)).astype(bf16)
+            return 0
+        lax.fori_loop(0, model // 256, turn, 0)
+        wk[...] = w_ref[:, width : 2 * width]
+        wv[...] = w_ref[:, 2 * width : 3 * width]
+    for n, x in enumerate(fetch):
+        @pl.when(step == n)
+        def _():
+            x.wait()
+    x = x_buf[step]
+    k_ref[...] = jnp.dot(x, wk[...], preferred_element_type=f32).astype(bf16)
+    v_ref[...] = (jnp.dot(x, wv[...], preferred_element_type=f32) + bvr_ref[...]).astype(bf16)
+    q_ref[...] = (lax.dot_general(wT[0:width], x, NT, preferred_element_type=f32) + bq_ref[...]).astype(bf16)
+    kT_ref[...] = lax.dot_general(wT[width : 2 * width], x, NT, preferred_element_type=f32).astype(bf16)
+    vT_ref[...] = (lax.dot_general(wT[2 * width : 3 * width], x, NT, preferred_element_type=f32) + bvc_ref[...]).astype(bf16)
 
 
 def project(home, tokens, wa, wb, count, bq, bv):
-    length = 4 * tokens[0].shape[0]
-    model = tokens[0].shape[1]
+    size, model = tokens[0].shape
+    length = 4 * size
     width = bq.shape[0]
-    v = pl.BlockSpec(memory_space=pltpu.VMEM)
+    hbm = pl.BlockSpec(memory_space=pltpu.HBM)
+    column = pl.BlockSpec((width, 1), lambda i: (0, 0))
     tall = jax.ShapeDtypeStruct((length, width), bf16)
     flat = jax.ShapeDtypeStruct((width, length), bf16)
+    across = pl.BlockSpec((width, size), lambda i: (0, i))
+    down = pl.BlockSpec((size, width), lambda i: (i, 0))
     return pl.pallas_call(
         proj_kernel,
+        grid=(4,),
         out_shape=(flat, flat, flat, tall, tall, jax.ShapeDtypeStruct((model, model), bf16)),
-        in_specs=[pl.BlockSpec(memory_space=pltpu.SMEM)] + [v] * 9,
-        out_specs=[v] * 6,
-        scratch_shapes=[pltpu.VMEM((model, model), bf16), pltpu.SemaphoreType.DMA((count,))],
-        compiler_params=pltpu.CompilerParams(vmem_limit_bytes=60 << 20),
+        in_specs=[pl.BlockSpec(memory_space=pltpu.SMEM)] + [hbm] * 6 + [column, column, pl.BlockSpec((1, width), lambda i: (0, 0))],
+        out_specs=[across, across, across, down, down, pl.BlockSpec((model, model), lambda i: (0, 0))],
+        scratch_shapes=[pltpu.VMEM((model, model), bf16), pltpu.VMEM((model, width), bf16), pltpu.VMEM((model, width), bf16),
+            pltpu.VMEM((4, size, model), bf16), pltpu.SemaphoreType.DMA((count,)), pltpu.SemaphoreType.DMA((4,))],
+        compiler_params=pltpu.CompilerParams(dimension_semantics=("arbitrary",), vmem_limit_bytes=60 << 20),
         cost_estimate=pl.CostEstimate(flops=30 * length * model * width, bytes_accessed=4 * length * model, transcendentals=0),
         name="projection",
     )(home, *tokens, wa, wb, bq[:, None], bv[:, None], bv[None, :])
 
 
-def grads_kernel(x0, x1, x2, x3, g0, g1, g2, g3, c_ref, q_ref, k_ref, v_ref, o_ref, acc, xT, gT):
+def grads_kernel(home_ref, x0, x1, x2, x3, g0, g1, g2, g3, c_ref, q_ref, k_ref, v_ref, *rest):
+    *outs, acc, xT, gT = rest
+    home = home_ref[0]
     width = q_ref.shape[0]
     model = x0.shape[1]
     for n, (x_ref, g_ref) in enumerate(zip((x0, x1, x2, x3), (g0, g1, g2, g3))):
@@ -399,29 +421,36 @@
                 lax.dot_general(gT[at, :], c_ref[:, rows], NT, preferred_element_type=f32),
             )
             for m, piece in enumerate(pieces):
-                total = piece if n == 0 else acc[m, at, :] + piece
-                if n == 3:
-                    o_ref[at, m * width : (m + 1) * width] = total.astype(bf16)
-                else:
-                    acc[m, at, :] = total
+                acc[m, at, :] = piece if n == 0 else acc[m, at, :] + piece
             return 0
         lax.fori_loop(0, model // 256, part, 0)
-
-
-def attn_grads(tokens, grads, contextT, dqT, dk, dv):
+    if len(outs) == 1:
+        for m in range(4):
+            outs[0][:, m * width : (m + 1) * width] = acc[m].astype(bf16)
+        return
+    rows = model // 8
+    for r in range(8):
+        at = pl.ds(pl.multiple_of(jnp.bitwise_xor(home, r) * rows, rows), rows)
+        to = slice(r // 2 * rows, (r // 2 + 1) * rows)
+        for m in range(4):
+            outs[r % 2][to, m * width : (m + 1) * width] = acc[m, at, :].astype(bf16)
+
+
+def attn_grads(home, count, tokens, grads, contextT, dqT, dk, dv):
     size, model = tokens[0].shape
     width = dqT.shape[0]
     v = pl.BlockSpec(memory_space=pltpu.VMEM)
+    parts = 2 if count == 8 else 1
     return pl.pallas_call(
         grads_kernel,
-        out_shape=jax.ShapeDtypeStruct((model, 4 * width), bf16),
-        in_specs=[v] * 12,
-        out_specs=v,
+        out_shape=[jax.ShapeDtypeStruct((model // parts, 4 * width), bf16)] * parts,
+        in_specs=[pl.BlockSpec(memory_space=pltpu.SMEM)] + [v] * 12,
+        out_specs=[v] * parts,
         scratch_shapes=[pltpu.VMEM((4, model, width), f32), pltpu.VMEM((model, size), bf16), pltpu.VMEM((model, size), bf16)],
         compiler_params=pltpu.CompilerParams(vmem_limit_bytes=60 << 20),
         cost_estimate=pl.CostEstimate(flops=120 * size * model * width, bytes_accessed=24 * size * model, transcendentals=0),
         name="projection_grads",
-    )(*tokens, *grads, contextT, dqT, dk, dv)
+    )(home, *tokens, *grads, contextT, dqT, dk, dv)
 
 
 def hop(value, bit):
@@ -438,7 +467,17 @@
     return even, hop(even, 1)
 
 
-def later(value, *markers):
+def scatter_shards(parts):
+    if len(parts) == 1:
+        count = lax.axis_size("dp")
+        swapped = lax.all_to_all(parts[0], "dp", 0, 0, tiled=True)
+        return jnp.sum(swapped.reshape(count, -1, swapped.shape[1]).astype(f32), axis=0)
+    even = (parts[0].astype(f32) + hop(parts[1], 1).astype(f32)).astype(bf16)
+    even = even.reshape(4, -1, even.shape[1])
+    return even[0].astype(f32) + sum(hop(even[n], 2 * n).astype(f32) for n in (1, 2, 3))
+
+
+def later(value, *markers, flops=0):
     anywhere = pl.BlockSpec(memory_space=pl.ANY)
     return pl.pallas_call(
         lambda *refs: None,
@@ -446,7 +485,7 @@
         in_specs=[anywhere] * (1 + len(markers)),
         out_specs=anywhere,
         input_output_aliases={0: 0},
-        cost_estimate=pl.CostEstimate(flops=0, bytes_accessed=0, transcendentals=0),
+        cost_estimate=pl.CostEstimate(flops=flops, bytes_accessed=0, transcendentals=0),
         name="later",
     )(value, *markers)
 
@@ -462,15 +501,20 @@
 
 def gather_rows(own):
     return jnp.concatenate(row_blocks(own), axis=0)
+
+
+def scatter_pieces(near, side, far):
+    rows = near.shape[0]
+    beside = exchange(side, 1)
+    ahead = (far.astype(f32) + beside[rows:].astype(f32)).astype(bf16)
+    return (near, beside[:rows], exchange(ahead, 2)), ahead
 
 
 def scatter_rows(partial):
     rows = partial.shape[0] // 4
     low = partial.astype(bf16)
     piece = lambda r: low[r * rows : (r + 1) * rows]
-    beside = exchange(jnp.concatenate([piece(1), piece(3)], axis=0), 1)
-    ahead = (piece(2).astype(f32) + beside[rows:].astype(f32)).astype(bf16)
-    return (piece(0), beside[:rows], exchange(ahead, 2)), ahead
+    return scatter_pieces(piece(0), jnp.concatenate([piece(1), piece(3)], axis=0), piece(2))
 
 
 def on_device(
@@ -511,6 +555,9 @@
     own = jnp.concatenate(
         [query_bias, value_bias, merge_bias, first_gain, first_shift, shrink_bias, second_gain, second_shift, expand_bias]
     )
+    rows = tokens.shape[0]
+    count = own.shape[0]
+    own = jnp.concatenate([own, segments.reshape(-1).astype(f32)])
     slots = -(-own.shape[0] // 1024) * 8
     own = jnp.pad(own, (0, slots * 128 - own.shape[0])).reshape(1, slots, 128)
     vectors = lax.all_to_all(jnp.broadcast_to(own, (world, slots, 128)), everyone, 0, 0, tiled=True)
@@ -518,44 +565,47 @@
     whole = [vectors[:, n * share : (n + 1) * share].reshape(model) for n in range(8)]
     unit_bias = vectors[:, 8 * share : 8 * share + unit_share].reshape(4, units)
     flips = jnp.bitwise_xor(jnp.arange(4), part)
+    seg = lax.dynamic_slice(vectors, (lax.axis_index("dp") * 4, count), (4, rows))
+    seg = jnp.take(seg, flips, axis=0).reshape(-1).astype(jnp.int32)
     unit_bias = jnp.take(unit_bias, flips, axis=0)
     query_b = lax.dynamic_slice_in_dim(whole[0], part * width, width)
     value_b = lax.dynamic_slice_in_dim(whole[1], part * width, width)
     rows_b = jnp.stack(whole[2:8])
 
     blocks = row_blocks(tokens)
-    seg = jnp.concatenate(row_blocks(segments.reshape(-1)), axis=0)
     segc, segr = seg[:, None], seg[None, :]
     lo, hi = spans(seg)
     flip = (part * (tokens.shape[0] // BK)).astype(jnp.int32).reshape(1)
     home = lax.axis_index("dp").astype(jnp.int32).reshape(1)
     query_t, key_t, value_t, keys, values, attn_wt = project(home, blocks, *shards, dp, query_b, value_b)
-    wq, wk, wv, wm = (attn_wt[n * width : (n + 1) * width] for n in range(4))
+    wq, wk, wv, _ = (attn_wt[n * width : (n + 1) * width] for n in range(4))
     dot = lambda a, b, dims: lax.dot_general(a, b, dims, preferred_element_type=f32)
-    context_t, logsum = attn_fwd(query_t, keys, value_t, segc, segr, lo, hi, flip)
-    (a0, a1, a2), ahead = scatter_rows(dot(context_t, wm, TN))
-
-    w_own = later(w_own, ahead)
+    context_t, logsum, *pieces = attn_fwd(query_t, keys, value_t, attn_wt, segc, segr, lo, hi, flip)
+    (a0, a1, a2), ahead = scatter_pieces(*pieces)
+
     w_other = exchange(w_own, 1)
+    rows_b = later(rows_b, ahead, flops=7 * 10**10)
     out = ffn(tokens, a0, a1, a2, cotangent, rows_b, unit_bias, w_own, w_other)
     output, grad_mixed, mixed_low, row_sums, unit_sums = out[:5]
     g_own, g_other = out[5:]
 
-    mixed_blocks = row_blocks(mixed_low)
+    across = exchange(mixed_low, 2)
+    beside = exchange(mixed_low, 1)
     wide_local = (g_own.astype(f32) + exchange(g_other, 1).astype(f32)).astype(bf16)
+    mixed_blocks = [mixed_low, beside, across, exchange(across, 1)]
     wide_local = lax.psum_scatter(wide_local, "dp", scatter_dimension=0, tiled=True)
     dq_t, dk, dv, q_sums, v_sums = attn_bwd(
         query_t, keys, key_t, values, attn_wt, mixed_blocks, context_t, logsum, segc, segr, lo, hi, flip
     )
-    attn_local = attn_grads(blocks, mixed_blocks, context_t, dq_t, dk, dv)
-    swapped = lax.all_to_all(attn_local, "dp", 0, 0, tiled=True)
-    dq_late = later(dq_t, attn_local)
+    attn_local = attn_grads(home, dp, blocks, mixed_blocks, context_t, dq_t, dk, dv)
+    attn_grad = scatter_shards(attn_local)
+    dq_late = later(dq_t, attn_local[0])
     total = dot(dq_late, wq, TN) + dot(dk, wk, NN) + dot(dv, wv, NN)
     (b0, b1, b2), _ = scatter_rows(total)
     tokens_grad = (grad_mixed + (b0.astype(f32) + b1.astype(f32) + b2.astype(f32))).astype(bf16)
-    attn_grad = jnp.sum(swapped.reshape(dp, -1, model).astype(f32), axis=0)
+    wide_far = exchange(wide_local[:, 2 * units :], 2)
     querygrad, keygrad, valuegrad, mergegrad = (attn_grad[:, n * width : (n + 1) * width] for n in range(4))
-    wide_grad = wide_local[:, : 2 * units].astype(f32) + exchange(wide_local[:, 2 * units :], 2).astype(f32)
+    wide_grad = wide_local[:, : 2 * units].astype(f32) + wide_far.astype(f32)
     expandgrad = wide_grad[:, :units]
     shrinkgrad = wide_grad[:, units:].T
 

time: 332 us -> 301 us (0.907)
  waiting for transfers between devices: 106 us -> 77.9 us
  Pallas kernels: 122 us -> 99.8 us
  blocking collectives: 0 us -> 21.1 us
  other arithmetic: 25.8 us -> 21 us
  starting transfers between devices: 36.6 us -> 40.2 us
    all_to_all x2 -> x0, waiting for transfers between devices: 36.4 us -> none  [the longest x1 36.4 us: on_device(): swapped = lax.all_to_all(attn_local, 'dp', 0, 0, tiled=True)]
    all_to_all x0 -> x1, blocking collectives: none -> 21.1 us  [on_device(): lax.all_to_all(send, everyone, 0, 0, tiled=True).reshape(world, slots * 128)]
    ppermute x4 -> x8, starting transfers between devices: 6.02 us -> 25.7 us  [hop(): return lax.ppermute(value, 'dp', [(i, i ^ bit) for i in range(count)])]
    ppermute x17 -> x14, waiting for transfers between devices: 50.6 us -> 32 us  [exchange(): return lax.ppermute(value, 'tensor', [(i, i ^ bit) for i in range(4)])]
    ppermute x4 -> x8, waiting for transfers between devices: 5.38 us -> 21.2 us  [hop(): return lax.ppermute(value, 'dp', [(i, i ^ bit) for i in range(count)])]
    pallas_call x1, Pallas kernels: 41.4 us -> 27.2 us  [attn_bwd(): pl.pallas_call(bwd_kernel, out_shape=(jax.ShapeDtypeStruct((width, length...]
    all_to_all x2 -> x0, starting transfers between devices: 11.8 us -> none  [the longest x1 6.16 us: on_device(): lax.all_to_all(send, everyone, 0, 0, tiled=True).reshape(world, slots * 128)]
    all_gather x1, waiting for transfers between devices: 6.32 us -> 14.1 us  [on_device(): w_own = lax.all_gather(wide, 'dp', axis=0, tiled=True)]
  transfers between devices with their start and end apart: 26 -> 25, of which waited for: 11 -> 13; matrix products, arithmetic and copies ran while one was open for 13% -> 12% of each run, Pallas kernels for 27% -> 23%
where the time goes in v3:
time: 301 us; the launch traced here: 299 us
  Pallas kernels  99.8 us (33%)
  waiting for transfers between devices  77.9 us (26%)
  starting transfers between devices  40.2 us (13%)
  blocking collectives  21.1 us (7%)
  other arithmetic  21 us (7%)
  local copies, waits for them, and re-layouts  19 us (6%)
  between operations  14.8 us (5%)
  matrix products  5.19 us (2%)
    pallas_call x1, Pallas kernels, ffn(): pl.pallas_call(ffn_kernel, out_shape=(jax.ShapeDtypeStruct((rows, width),...  32.3 us
    ppermute x14, waiting for transfers between devices, exchange(): return lax.ppermute(value, 'tensor', [(i, i ^ bit) for i in range(4)])  32 us
    pallas_call x1, Pallas kernels, attn_bwd(): pl.pallas_call(bwd_kernel, out_shape=(jax.ShapeDtypeStruct((width, length...  27.2 us
    ppermute x8, starting transfers between devices, hop(): return lax.ppermute(value, 'dp', [(i, i ^ bit) for i in range(count)])  25.7 us
    ppermute x8, waiting for transfers between devices, hop(): return lax.ppermute(value, 'dp', [(i, i ^ bit) for i in range(count)])  21.2 us
    all_to_all x1, blocking collectives, on_device(): lax.all_to_all(send, everyone, 0, 0, tiled=True).reshape(world, slots * 128)  21.1 us
    pallas_call x1, Pallas kernels, attn_fwd(): pl.pallas_call(fwd_kernel, out_shape=(jax.ShapeDtypeStruct((width, length...  17.7 us
    all_gather x1, waiting for transfers between devices, on_device(): w_own = lax.all_gather(wide, 'dp', axis=0, tiled=True)  14.1 us
  transfers between devices with their start and end apart: 25, of which 13 were waited for; matrix products, arithmetic and copies ran while one was open for 12% of the time, Pallas kernels for 23%

profile of v3, /device:TPU:0, one launch (start us, length us, event | category | flops | bytes accessed | tf_op | source)
XLA Modules:
  0.0 299.1 jit_solution(10604380502671864553)
XLA Ops:
  7.4 1.1 pad_maximum_fusion.3
  8.5 3.0 %collective-permute-start.9 = (bf16[96,1536]{1,0:T(8,128)(2,1)S(1)}, bf16[96,1536]{1,0:T(8,128)(2,1)S(1)}, u32[]{:S(2)}, u32[]{:S(2)}) collective-permute-start(bf16[96,1536]{1,0:T(8,128)(2,1)S(1)} %pad_maximum_fusion.3), channel_id=1, source_target_pairs={{0,2},{1,3},{2,0},{3,1},{4,6},{5,7},{6,4},{7,5},{8,10},{9,11},{10,... | collective-permute-start | bytes 884744 | tf_op jit(solution)/shard_map/ppermute | solution.py:494
  11.5 7.0 %collective-permute-done.9 = bf16[96,1536]{1,0:T(8,128)(2,1)S(1)} collective-permute-done((bf16[96,1536]{1,0:T(8,128)(2,1)S(1)}, bf16[96,1536]{1,0:T(8,128)(2,1)S(1)}, u32[]{:S(2)}, u32[]{:S(2)}) %collective-permute-start.9) | collective-permute-done | bytes 294944 | tf_op jit(solution)/shard_map/ppermute | solution.py:494
  18.5 1.8 pad_maximum_fusion.2
  20.4 1.8 collective-permute-start.1
  22.4 1.7 collective-permute-start.3
  24.1 2.6 collective-permute-start.4
  27.1 0.7 broadcast_in_dim.52
  27.8 5.0 %all-to-all-start = ((f32[32,8,128]{2,1,0:T(8,128)}), f32[32,8,128]{2,1,0:T(8,128)S(1)}, u32[]{:S(2)}, u32[]{:S(2)}) async-start(f32[32,8,128]{2,1,0:T(8,128)} %broadcast_in_dim.52), calls=%async_computation | async-start | bytes 262144 | tf_op jit(solution)/shard_map/all_to_all | solution.py:563
  32.9 10.5 %collective-permute-done.4 = bf16[96,768]{1,0:T(8,128)(2,1)S(1)} collective-permute-done((bf16[96,768]{1,0:T(8,128)(2,1)S(1)}, bf16[96,768]{1,0:T(8,128)(2,1)S(1)}, u32[]{:S(2)}, u32[]{:S(2)}) %collective-permute-start.4) | collective-permute-done | bytes 147488 | tf_op jit(solution)/shard_map/ppermute | solution.py:458
  43.6 1.6 collective-permute-start.6
  45.2 10.5 %all-to-all-done = f32[32,8,128]{2,1,0:T(8,128)S(1)} async-done(((f32[32,8,128]{2,1,0:T(8,128)}), f32[32,8,128]{2,1,0:T(8,128)S(1)}, u32[]{:S(2)}, u32[]{:S(2)}) %all-to-all-start) | async-done | bytes 131104 | tf_op jit(solution)/shard_map/all_to_all | solution.py:563
  55.8 0.6 gather_fusion
  57.0 0.8 copy.47.bvc_ref
  57.9 0.8 copy.46.bq_ref
  58.7 1.4 copy.54
  60.3 0.5 and_select_fusion
  60.9 0.8 copy-done.36
  61.9 9.9 %projection.1 = (bf16[192,2048]{1,0:T(8,128)(2,1)}, bf16[192,2048]{1,0:T(8,128)(2,1)}, bf16[192,2048]{1,0:T(8,128)(2,1)}, bf16[2048,192]{1,0:T(8,128)(2,1)}, bf1...) custom-call(s32[1]{0:T(128)} %bitcast.4.home_ref, bf16[512,768]{1,0:T(8,128)(2,1)} %x0.3, ...), custom_call_target="tpu_custom_call" | custom-call | flops 9059696640 | bytes 6291456 | tf_op jit(solution)/shard_map/projection/pallas_call | solution.py:386
  71.9 17.7 %attention.1 = (bf16[192,2048]{1,0:T(8,128)(2,1)}, f32[3,2048]{1,0:T(4,128)}, bf16[512,768]{1,0:T(8,128)(2,1)}, bf16[1024,768]{1,0:T(8,128)(2,1)}, bf16[512,768]{1,0:T(8,128)(2,1)}) custom-call(s32[4]{0:T(128)} %get-tuple-element.157.lo_ref, s32[4]{0:T(128)} %get-tuple-element.156.hi_ref, s32[1]{0:T(128)} %bitcast.3.flip_ref, ...), custom_call_target="tpu_custom_call" | custom-call | flops 24159191040 | bytes 3145728 | tf_op jit(solution)/shard_map/attention/pallas_call | solution.py:78
  89.6 0.5 collective-permute-start.7
  90.9 0.6 gather_fusion.1
  91.5 0.6 stack.3.refs_0_
  92.1 0.7 broadcast_select_fusion.1.be_ref
  92.8 0.6 collective-permute-done.7
  93.4 1.4 add_convert_fusion.4.refs_1_
  94.8 0.5 collective-permute-start.8
  95.3 14.1 %all-gather.2.cloned.1.call-done.wa_ref = bf16[768,3072]{1,0:T(8,128)(2,1)} async-done(((bf16[96,3072]{1,0:T(8,128)(2,1)}), bf16[768,3072]{1,0:T(8,128)(2,1)}) %all-gather.2.cloned.1.call-update) | async-done | bytes 4718608 | tf_op jit(solution)/shard_map/all_gather | solution.py:554
  109.4 0.9 slice.184.a1_ref
  110.4 4.3 %collective-permute-done.8.a2_ref = bf16[512,768]{1,0:T(8,128)(2,1)S(1)} collective-permute-done((bf16[512,768]{1,0:T(8,128)(2,1)S(1)}, bf16[512,768]{1,0:T(8,128)(2,1)S(1)}, u32[]{:S(2)}, u32[]{:S(2)}) %collective-permute-start.8) | collective-permute-done | bytes 786464 | tf_op jit(solution)/shard_map/ppermute | solution.py:494
  114.7 3.0 %collective-permute-done.10.wb_ref = bf16[768,3072]{1,0:T(8,128)(2,1)} collective-permute-done((bf16[768,3072]{1,0:T(8,128)(2,1)}, bf16[768,3072]{1,0:T(8,128)(2,1)}, u32[]{:S(2)}, u32[]{:S(2)}) %collective-permute-start.10) | collective-permute-done | bytes 4718624 | tf_op jit(solution)/shard_map/ppermute | solution.py:494
  117.7 32.3 %feed_forward.1 = (bf16[512,768]{1,0:T(8,128)(2,1)}, f32[512,768]{1,0:T(8,128)}, bf16[512,768]{1,0:T(8,128)(2,1)}, f32[6,8,768]{2,1,0:T(8,128)}, f32[4,8,768]{2,...) custom-call(bf16[512,768]{1,0:T(8,128)(2,1)} %x0.3, bf16[512,768]{1,0:T(8,128)(2,1)} %get-tuple-element.47.a0_ref, ...), custom_call_target="tpu_custom_call" | custom-call | flops 36238786560 | bytes 18874368 | tf_op jit(solution)/shard_map/feed_forward/pallas_call | solution.py:317
  150.2 1.5 collective-permute-start.12
  151.8 6.4 %collective-permute-done.20 = bf16[768,3072]{1,0:T(8,128)(2,1)S(1)} collective-permute-done((bf16[768,3072]{1,0:T(8,128)(2,1)}, bf16[768,3072]{1,0:T(8,128)(2,1)S(1)}, u32[]{:S(2)}, u32[]{:S(2)}) %collective-permute-start.20) | collective-permute-done | bytes 4718624 | tf_op jit(solution)/shard_map/ppermute | solution.py:494
  158.2 6.5 %add_convert_fusion = bf16[768,3072]{1,0:T(8,128)(2,1)} fusion(bf16[768,3072]{1,0:T(8,128)(2,1)S(1)} %collective-permute-done.20, bf16[768,3072]{1,0:T(8,128)(2,1)} %get-tuple-element.66), kind=kLoop, calls=%fused_computation.3 | loop fusion | flops 9437184 | bytes 14155776 | tf_op jit(solution)/shard_map/convert_element_type | solution.py:594
  164.7 1.1 copy-done.31
  166.0 4.3 %collective-permute-done.12.g2 = bf16[512,768]{1,0:T(8,128)(2,1)S(1)} collective-permute-done((bf16[512,768]{1,0:T(8,128)(2,1)}, bf16[512,768]{1,0:T(8,128)(2,1)S(1)}, u32[]{:S(2)}, u32[]{:S(2)}) %collective-permute-start.12) | collective-permute-done | bytes 786464 | tf_op jit(solution)/shard_map/ppermute | solution.py:494
  170.3 2.3 collective-permute-done.13.g3
  172.6 0.9 copy-done.34
  173.4 27.2 %attention_back.1 = (bf16[192,2048]{1,0:T(8,128)(2,1)}, bf16[2048,192]{1,0:T(8,128)(2,1)}, bf16[2048,192]{1,0:T(8,128)(2,1)}, f32[192,128]{1,0:T(8,128)}, f32[8,192]{1,0:T(8,128)}) custom-call(s32[4]{0:T(128)} %get-tuple-element.157.lo_ref, s32[4]{0:T(128)} %get-tuple-element.156.hi_ref, s32[1]{0:T(128)} %bitcast.3.flip_ref, ...), custom_call_target="tpu_custom_call" | custom-call | flops 30601641984 | bytes 7864320 | tf_op jit(solution)/shard_map/attention_back/pallas_call | solution.py:156
  200.6 12.6 %projection_grads.1 = (bf16[384,768]{1,0:T(8,128)(2,1)}, bf16[384,768]{1,0:T(8,128)(2,1)}) custom-call(s32[1]{0:T(128)} %bitcast.4.home_ref, bf16[512,768]{1,0:T(8,128)(2,1)} %x0.3, bf16[512,768]{1,0:T(8,128)(2,1)} %collective-permute-done.x1, bf16[512,768]{1,0:T(8,128)(2,1)} %collective-permute-done.1.x2, bf16[512,768]{1,0:T(8,128)(2,1)} %copy-done.30, ...), custom_call_target="tpu_custom_call" | custom-call | flops 9059696640 | bytes 9437184 | tf_op jit(solution)/shard_map/projection_grads/pallas_call | solution.py:444
  213.2 1.3 copy-done.3
  214.5 2.3 fusion.6
  216.8 1.0 fusion.4
  218.1 1.9 add_convert_fusion.1
  220.2 1.3 pad_maximum_fusion
  222.3 0.7 gather_fusion.2
  223.0 13.3 %collective-permute-start.16 = (bf16[384,768]{1,0:T(8,128)(2,1)}, bf16[384,768]{1,0:T(8,128)(2,1)}, u32[]{:S(2)}, u32[]{:S(2)}) collective-permute-start(bf16[384,768]{1,0:T(8,128)(2,1)} %get-tuple-element.61), channel_id=1, source_target_pairs={{0,4},{4,0},{8,12},{12,8},{16,20},{20,16},{24,28},{28,24},{1,5},{5... | collective-permute-start | bytes 1769480 | tf_op jit(solution)/shard_map/ppermute | solution.py:458
  237.0 21.1 %all_to_all.10 = f32[32,8,128]{2,1,0:T(8,128)S(1)} all-to-all(f32[32,8,128]{2,1,0:T(8,128)S(1)} %bitcast.48), channel_id=1, replica_groups=mesh['dp'=8,'tensor'=4] {'dp','tensor'}, dimensions={0} | all-to-all | bytes 262144 | tf_op jit(solution)/shard_map/all_to_all | solution.py:619
  258.2 0.6 slice.171
  258.7 1.4 add_convert_fusion.5
  260.2 2.2 add_convert_fusion.3
  262.4 2.2 collective-permute-start.17
  264.7 3.8 %collective-permute-start.18 = (bf16[96,768]{1,0:T(8,128)(2,1)S(1)}, bf16[96,768]{1,0:T(8,128)(2,1)S(1)}, u32[]{:S(2)}, u32[]{:S(2)}) collective-permute-start(bf16[96,768]{1,0:T(8,128)(2,1)S(1)} %get-tuple-element.133), channel_id=1, source_target_pairs={{0,16},{4,20},{8,24},{12,28},{16,0},{20,4},{24,8},{28,12},{1,17},{... | collective-permute-start | bytes 442376 | tf_op jit(solution)/shard_map/ppermute | solution.py:458
  268.8 0.6 fusion.12
  269.4 5.5 %collective-permute-done.17 = bf16[96,768]{1,0:T(8,128)(2,1)S(1)} collective-permute-done((bf16[96,768]{1,0:T(8,128)(2,1)S(1)}, bf16[96,768]{1,0:T(8,128)(2,1)S(1)}, u32[]{:S(2)}, u32[]{:S(2)}) %collective-permute-start.17) | collective-permute-done | bytes 147488 | tf_op jit(solution)/shard_map/ppermute | solution.py:458
  274.9 5.1 %collective-permute-done.19 = bf16[96,768]{1,0:T(8,128)(2,1)S(1)} collective-permute-done((bf16[96,768]{1,0:T(8,128)(2,1)S(1)}, bf16[96,768]{1,0:T(8,128)(2,1)S(1)}, u32[]{:S(2)}, u32[]{:S(2)}) %collective-permute-start.19) | collective-permute-done | bytes 147488 | tf_op jit(solution)/shard_map/ppermute | solution.py:458
  280.1 0.8 slice_bitcast_fusion.1
  280.9 0.7 copy.50
  281.6 1.0 slice.208
  282.6 1.5 collective-permute-start.21
  284.2 3.1 %add_convert_fusion.2 = bf16[512,768]{1,0:T(8,128)(2,1)} fusion(f32[512,768]{1,0:T(8,128)} %get-tuple-element.51, bf16[512,768]{1,0:T(8,128)(2,1)} %collective-permute-done.15, bf16[1024,768]{1,0:T(8,128)(2,1)} %collective-permute-done.14, bf16[2048,768]{1,0:T(8,128)(2,1)S(1)} %add_convert_fusion.1), kind=kLoop, calls=%fused_computation.6 | loop fusion | flops 2752512 | bytes 4718592 | tf_op jit(solution)/shard_map/convert_element_type | solution.py:605
  287.3 4.0 %collective-permute-done.21 = bf16[96,1536]{1,0:T(8,128)(2,1)S(1)} collective-permute-done((bf16[96,1536]{1,0:T(8,128)(2,1)S(1)}, bf16[96,1536]{1,0:T(8,128)(2,1)S(1)}, u32[]{:S(2)}, u32[]{:S(2)}) %collective-permute-start.21) | collective-permute-done | bytes 294944 | tf_op jit(solution)/shard_map/ppermute | solution.py:494
  291.4 0.9 slice_bitcast_fusion
  (157 shorter events, 5.7 us)
Async XLA Ops:
  7.2 13.2 %copy-start.29 = (bf16[512,768]{1,0:T(8,128)(2,1)S(1)}, bf16[512,768]{1,0:T(8,128)(2,1)}, u32[]{:S(2)}) copy-start(bf16[512,768]{1,0:T(8,128)(2,1)} %x0.3) | copy-start | bytes 2359300
  7.2 15.0 %copy-start.12 = (bf16[192,96]{1,0:T(8,128)(2,1)S(1)}, bf16[192,96]{1,0:T(8,128)(2,1)}, u32[]{:S(2)}) copy-start(bf16[192,96]{1,0:T(8,128)(2,1)} %param.27) | copy-start | bytes 110596
  7.2 15.1 %copy-start.8 = (bf16[96,192]{1,0:T(8,128)(2,1)S(1)}, bf16[96,192]{1,0:T(8,128)(2,1)}, u32[]{:S(2)}) copy-start(bf16[96,192]{1,0:T(8,128)(2,1)} %param.22) | copy-start | bytes 110596
  7.2 15.1 %copy-start.7 = (bf16[96,192]{1,0:T(8,128)(2,1)S(1)}, bf16[96,192]{1,0:T(8,128)(2,1)}, u32[]{:S(2)}) copy-start(bf16[96,192]{1,0:T(8,128)(2,1)} %param.24) | copy-start | bytes 110596
  7.2 15.1 %copy-start.6 = (bf16[96,192]{1,0:T(8,128)(2,1)S(1)}, bf16[96,192]{1,0:T(8,128)(2,1)}, u32[]{:S(2)}) copy-start(bf16[96,192]{1,0:T(8,128)(2,1)} %param.25) | copy-start | bytes 110596
  7.2 19.7 %copy-start.19 = (s32[1,512]{1,0:T(1,128)S(1)}, s32[1,512]{1,0:T(1,128)}, u32[]{:S(2)}) copy-start(s32[1,512]{1,0:T(1,128)} %param.21) | copy-start | bytes 6148
  7.3 19.7 %copy-start.20 = (f32[24]{0:T(128)S(1)}, f32[24]{0:T(128)}, u32[]{:S(2)}) copy-start(f32[24]{0:T(128)} %param.23) | copy-start | bytes 292
  7.3 19.7 %copy-start.21 = (f32[24]{0:T(128)S(1)}, f32[24]{0:T(128)}, u32[]{:S(2)}) copy-start(f32[24]{0:T(128)} %param.26) | copy-start | bytes 292
  7.3 19.7 %copy-start.22 = (f32[24]{0:T(128)S(1)}, f32[24]{0:T(128)}, u32[]{:S(2)}) copy-start(f32[24]{0:T(128)} %param.28) | copy-start | bytes 292
  7.3 19.7 %copy-start.23 = (f32[24]{0:T(128)S(1)}, f32[24]{0:T(128)}, u32[]{:S(2)}) copy-start(f32[24]{0:T(128)} %param.29) | copy-start | bytes 292
  7.3 19.7 %copy-start.24 = (f32[24]{0:T(128)S(1)}, f32[24]{0:T(128)}, u32[]{:S(2)}) copy-start(f32[24]{0:T(128)} %param.30) | copy-start | bytes 292
  7.3 19.7 %copy-start.28 = (f32[96]{0:T(128)S(1)}, f32[96]{0:T(128)}, u32[]{:S(2)}) copy-start(f32[96]{0:T(128)} %param.32) | copy-start | bytes 1156
  7.3 19.7 %copy-start.25 = (f32[24]{0:T(128)S(1)}, f32[24]{0:T(128)}, u32[]{:S(2)}) copy-start(f32[24]{0:T(128)} %param.34) | copy-start | bytes 292
  7.3 19.7 %copy-start.26 = (f32[24]{0:T(128)S(1)}, f32[24]{0:T(128)}, u32[]{:S(2)}) copy-start(f32[24]{0:T(128)} %param.35) | copy-start | bytes 292
  7.3 19.7 %copy-start.27 = (f32[24]{0:T(128)S(1)}, f32[24]{0:T(128)}, u32[]{:S(2)}) copy-start(f32[24]{0:T(128)} %param.36) | copy-start | bytes 292
  7.3 102.1 %all-gather.2.cloned.1.call-start = ((), (), s32[]{:S(2)}) async-start(), calls=%async_computation.3 | async-start | bytes 5308416 | tf_op jit(solution)/shard_map/all_gather | solution.py:554
  8.5 10.0 %collective-permute-start.9 = (bf16[96,1536]{1,0:T(8,128)(2,1)S(1)}, bf16[96,1536]{1,0:T(8,128)(2,1)S(1)}, u32[]{:S(2)}, u32[]{:S(2)}) collective-permute-start(bf16[96,1536]{1,0:T(8,128)(2,1)S(1)} %pad_maximum_fusion.3), channel_id=1, source_target_pairs={{0,2},{1,3},{2,0},{3,1},{4,6},{5,7},{6,4},{7,5},{8,10},{9,11},{10,... | collective-permute-start | bytes 884744 | tf_op jit(solution)/shard_map/ppermute | solution.py:494
  20.4 35.9 %collective-permute-start.1 = (bf16[512,768]{1,0:T(8,128)(2,1)S(1)}, bf16[512,768]{1,0:T(8,128)(2,1)}, u32[]{:S(2)}, u32[]{:S(2)}) collective-permute-start(bf16[512,768]{1,0:T(8,128)(2,1)S(1)} %copy-done.29), channel_id=1, source_target_pairs={{0,2},{1,3},{2,0},{3,1},{4,6},{5,7},{6,4},{7,5},{8,10},{9,11},{10,... | collective-permute-start | bytes 2359304 | tf_op jit(solution)/shard_map/ppermute | solution.py:494
  22.4 10.5 %collective-permute-start.3 = (bf16[96,768]{1,0:T(8,128)(2,1)S(1)}, bf16[96,768]{1,0:T(8,128)(2,1)S(1)}, u32[]{:S(2)}, u32[]{:S(2)}) collective-permute-start(bf16[96,768]{1,0:T(8,128)(2,1)S(1)} %pad_maximum_fusion.4), channel_id=1, source_target_pairs={{0,8},{4,12},{8,0},{12,4},{16,24},{20,28},{24,16},{28,20},{1,9},{5... | collective-permute-start | bytes 442376 | tf_op jit(solution)/shard_map/ppermute | solution.py:458
  24.1 19.4 %collective-permute-start.4 = (bf16[96,768]{1,0:T(8,128)(2,1)S(1)}, bf16[96,768]{1,0:T(8,128)(2,1)S(1)}, u32[]{:S(2)}, u32[]{:S(2)}) collective-permute-start(bf16[96,768]{1,0:T(8,128)(2,1)S(1)} %pad_maximum_fusion.4), channel_id=1, source_target_pairs={{0,16},{4,20},{8,24},{12,28},{16,0},{20,4},{24,8},{28,12},{1,17},{... | collective-permute-start | bytes 442376 | tf_op jit(solution)/shard_map/ppermute | solution.py:458
  26.7 16.8 %collective-permute-start.5 = (bf16[96,768]{1,0:T(8,128)(2,1)S(1)}, bf16[96,768]{1,0:T(8,128)(2,1)S(1)}, u32[]{:S(2)}, u32[]{:S(2)}) collective-permute-start(bf16[96,768]{1,0:T(8,128)(2,1)S(1)} %pad_maximum_fusion.4), channel_id=1, source_target_pairs={{0,24},{4,28},{8,16},{12,20},{16,8},{20,12},{24,0},{28,4},{1,25},{... | collective-permute-start | bytes 442376 | tf_op jit(solution)/shard_map/ppermute | solution.py:458
  26.9 33.9 %collective-permute-start = (bf16[512,768]{1,0:T(8,128)(2,1)S(1)}, bf16[512,768]{1,0:T(8,128)(2,1)}, u32[]{:S(2)}, u32[]{:S(2)}) collective-permute-start(bf16[512,768]{1,0:T(8,128)(2,1)S(1)} %copy-done.29), channel_id=1, source_target_pairs={{0,1},{1,0},{2,3},{3,2},{4,5},{5,4},{6,7},{7,6},{8,9},{9,8},{10,11... | collective-permute-start | bytes 2359304 | tf_op jit(solution)/shard_map/ppermute | solution.py:494
  27.8 27.9 %all-to-all-start = ((f32[32,8,128]{2,1,0:T(8,128)}), f32[32,8,128]{2,1,0:T(8,128)S(1)}, u32[]{:S(2)}, u32[]{:S(2)}) async-start(f32[32,8,128]{2,1,0:T(8,128)} %broadcast_in_dim.52), calls=%async_computation | async-start | bytes 262144 | tf_op jit(solution)/shard_map/all_to_all | solution.py:563
  32.8 248.8 %reduce-scatter.2.cloned.1.call-start = ((), (), s32[]{:S(2)}) async-start(), calls=%async_computation.4 | async-start | bytes 5308416 | tf_op jit(solution)/shard_map/reduce_scatter | solution.py:596
  32.9 59.2 %copy-start.16 = (pred[4]{0:T(512)(128)(4,1)}, pred[4]{0:T(512)(128)(4,1)S(1)}, u32[]{:S(2)}) copy-start(pred[4]{0:T(512)(128)(4,1)S(1)} %compare_and_fusion) | copy-start | bytes 16
  43.6 17.3 %copy-start.4 = (bf16[384,768]{1,0:T(8,128)(2,1)}, bf16[384,768]{1,0:T(8,128)(2,1)S(1)}, u32[]{:S(2)}) copy-start(bf16[384,768]{1,0:T(8,128)(2,1)S(1)} %pad_maximum_fusion.1.wa_ref) | copy-start | bytes 1769476
  43.6 17.2 %collective-permute-start.6 = (bf16[384,768]{1,0:T(8,128)(2,1)S(1)}, bf16[384,768]{1,0:T(8,128)(2,1)S(1)}, u32[]{:S(2)}, u32[]{:S(2)}) collective-permute-start(bf16[384,768]{1,0:T(8,128)(2,1)S(1)} %pad_maximum_fusion.1.wa_ref), channel_id=1, source_target_pairs={{0,4},{4,0},{8,12},{12,8},{16,20},{20,16},{24,28},{28,24},{1,5},{5... | collective-permute-start | bytes 1769480 | tf_op jit(solution)/shard_map/ppermute | solution.py:458
  56.3 4.5 %collective-permute-start.2 = (bf16[512,768]{1,0:T(8,128)(2,1)}, bf16[512,768]{1,0:T(8,128)(2,1)S(1)}, u32[]{:S(2)}, u32[]{:S(2)}) collective-permute-start(bf16[512,768]{1,0:T(8,128)(2,1)} %collective-permute-done.1.x2), channel_id=1, source_target_pairs={{0,1},{1,0},{2,3},{3,2},{4,5},{5,4},{6,7},{7,6},{8,9},{9,8},{10,11... | collective-permute-start | bytes 2359304 | tf_op jit(solution)/shard_map/ppermute | solution.py:494
  57.0 3.9 %copy-start.18 = (f32[192]{0:T(256)}, f32[192]{0:T(256)S(1)}, u32[]{:S(2)}) copy-start(f32[192]{0:T(256)S(1)} %dynamic_slice.11) | copy-start | bytes 2308
  58.7 13.2 %copy-start.13 = (s32[1,1,4,512]{3,1,2,0:T(1,128)}, s32[1,1,4,512]{3,1,2,0:T(1,128)S(1)}, u32[]{:S(2)}) copy-start(s32[1,1,4,512]{3,1,2,0:T(1,128)S(1)} %copy.53) | copy-start | bytes 24580
  60.8 0.8 copy-start.36
  60.9 1.1 copy-start.30
  89.6 3.8 %collective-permute-start.7 = (bf16[1024,768]{1,0:T(8,128)(2,1)}, bf16[1024,768]{1,0:T(8,128)(2,1)S(1)}, u32[]{:S(2)}, u32[]{:S(2)}) collective-permute-start(bf16[1024,768]{1,0:T(8,128)(2,1)} %get-tuple-element.48), channel_id=1, source_target_pairs={{0,1},{1,0},{2,3},{3,2},{4,5},{5,4},{6,7},{7,6},{8,9},{9,8},{10,11... | collective-permute-start | bytes 4718600 | tf_op jit(solution)/shard_map/ppermute | solution.py:494
  90.2 3.2 %copy-start.15 = (s32[1024]{0:T(1024)}, s32[1024]{0:T(1024)S(1)}, u32[]{:S(2)}) copy-start(s32[1024]{0:T(1024)S(1)} %pad_clamp_fusion) | copy-start | bytes 12292
  94.8 14.6 %copy-start.2 = (bf16[512,768]{1,0:T(8,128)(2,1)}, bf16[512,768]{1,0:T(8,128)(2,1)S(1)}, u32[]{:S(2)}) copy-start(bf16[512,768]{1,0:T(8,128)(2,1)S(1)} %add_convert_fusion.4.refs_1_) | copy-start | bytes 2359300
  94.8 19.8 %collective-permute-start.8 = (bf16[512,768]{1,0:T(8,128)(2,1)S(1)}, bf16[512,768]{1,0:T(8,128)(2,1)S(1)}, u32[]{:S(2)}, u32[]{:S(2)}) collective-permute-start(bf16[512,768]{1,0:T(8,128)(2,1)S(1)} %add_convert_fusion.4.refs_1_), channel_id=1, source_target_pairs={{0,2},{1,3},{2,0},{3,1},{4,6},{5,7},{6,4},{7,5},{8,10},{9,11},{10,... | collective-permute-start | bytes 2359304 | tf_op jit(solution)/shard_map/ppermute | solution.py:494
  109.4 8.3 %collective-permute-start.10 = (bf16[768,3072]{1,0:T(8,128)(2,1)}, bf16[768,3072]{1,0:T(8,128)(2,1)}, u32[]{:S(2)}, u32[]{:S(2)}) collective-permute-start(bf16[768,3072]{1,0:T(8,128)(2,1)} %all-gather.2.cloned.1.call-done.wa_ref), channel_id=1, source_target_pairs={{0,1},{1,0},{2,3},{3,2},{4,5},{5,4},{6,7},{7,6},{8,9},{9,8},{10,11... | collective-permute-start | bytes 14155784 | tf_op jit(solution)/shard_map/ppermute | solution.py:494
  114.7 3.0 %copy-start.35 = (bf16[512,768]{1,0:T(8,128)(2,1)}, bf16[512,768]{1,0:T(8,128)(2,1)S(1)}, u32[]{:S(2)}) copy-start(bf16[512,768]{1,0:T(8,128)(2,1)S(1)} %collective-permute-done.8.a2_ref) | copy-start | bytes 2359300
  150.0 8.2 %collective-permute-start.20 = (bf16[768,3072]{1,0:T(8,128)(2,1)}, bf16[768,3072]{1,0:T(8,128)(2,1)S(1)}, u32[]{:S(2)}, u32[]{:S(2)}) collective-permute-start(bf16[768,3072]{1,0:T(8,128)(2,1)} %get-tuple-element.67), channel_id=1, source_target_pairs={{0,1},{1,0},{2,3},{3,2},{4,5},{5,4},{6,7},{7,6},{8,9},{9,8},{10,11... | collective-permute-start | bytes 14155784 | tf_op jit(solution)/shard_map/ppermute | solution.py:494
  150.2 20.0 %collective-permute-start.12 = (bf16[512,768]{1,0:T(8,128)(2,1)}, bf16[512,768]{1,0:T(8,128)(2,1)S(1)}, u32[]{:S(2)}, u32[]{:S(2)}) collective-permute-start(bf16[512,768]{1,0:T(8,128)(2,1)} %get-tuple-element.54.g0), channel_id=1, source_target_pairs={{0,2},{1,3},{2,0},{3,1},{4,6},{5,7},{6,4},{7,5},{8,10},{9,11},{10,... | collective-permute-start | bytes 2359304 | tf_op jit(solution)/shard_map/ppermute | solution.py:494
  164.7 1.1 copy-start.31
  165.8 4.4 %collective-permute-start.11 = (bf16[512,768]{1,0:T(8,128)(2,1)S(1)}, bf16[512,768]{1,0:T(8,128)(2,1)S(1)}, u32[]{:S(2)}, u32[]{:S(2)}) collective-permute-start(bf16[512,768]{1,0:T(8,128)(2,1)S(1)} %copy-done.31), channel_id=1, source_target_pairs={{0,1},{1,0},{2,3},{3,2},{4,5},{5,4},{6,7},{7,6},{8,9},{9,8},{10,11... | collective-permute-start | bytes 2359304 | tf_op jit(solution)/shard_map/ppermute | solution.py:494
  170.3 2.3 copy-start.32
  170.3 2.3 collective-permute-start.13
  170.3 2.3 copy-start.33
  172.6 0.9 copy-start.34
  213.2 1.3 copy-start.3
  214.5 2.3 copy-start
  216.8 1.3 copy-start.1
  220.2 1.4 copy-start.9
  220.2 2.0 copy-start.10
  220.2 16.1 %copy-start.17 = (pred[4]{0:T(512)(128)(4,1)S(1)}, pred[4]{0:T(512)(128)(4,1)}, u32[]{:S(2)}) copy-start(pred[4]{0:T(512)(128)(4,1)} %copy-done.16) | copy-start | bytes 16
  220.2 16.2 %copy-start.11 = (f32[192,128]{1,0:T(8,128)S(1)}, f32[192,128]{1,0:T(8,128)}, u32[]{:S(2)}) copy-start(f32[192,128]{1,0:T(8,128)} %get-tuple-element.62) | copy-start | bytes 294916
  220.2 16.5 %copy-start.14 = (f32[8,192]{1,0:T(8,128)S(1)}, f32[8,192]{1,0:T(8,128)}, u32[]{:S(2)}) copy-start(f32[8,192]{1,0:T(8,128)} %get-tuple-element.63) | copy-start | bytes 18436
  221.5 38.7 %collective-permute-start.14 = (bf16[1024,768]{1,0:T(8,128)(2,1)}, bf16[1024,768]{1,0:T(8,128)(2,1)}, u32[]{:S(2)}, u32[]{:S(2)}) collective-permute-start(bf16[1024,768]{1,0:T(8,128)(2,1)} %pad_maximum_fusion), channel_id=1, source_target_pairs={{0,1},{1,0},{2,3},{3,2},{4,5},{5,4},{6,7},{7,6},{8,9},{9,8},{10,11... | collective-permute-start | bytes 4718600 | tf_op jit(solution)/shard_map/ppermute | solution.py:494
  223.0 35.8 %collective-permute-start.16 = (bf16[384,768]{1,0:T(8,128)(2,1)}, bf16[384,768]{1,0:T(8,128)(2,1)}, u32[]{:S(2)}, u32[]{:S(2)}) collective-permute-start(bf16[384,768]{1,0:T(8,128)(2,1)} %get-tuple-element.61), channel_id=1, source_target_pairs={{0,4},{4,0},{8,12},{12,8},{16,20},{20,16},{24,28},{28,24},{1,5},{5... | collective-permute-start | bytes 1769480 | tf_op jit(solution)/shard_map/ppermute | solution.py:458
  262.4 21.8 %collective-permute-start.15 = (bf16[512,768]{1,0:T(8,128)(2,1)}, bf16[512,768]{1,0:T(8,128)(2,1)}, u32[]{:S(2)}, u32[]{:S(2)}) collective-permute-start(bf16[512,768]{1,0:T(8,128)(2,1)} %add_convert_fusion.3), channel_id=1, source_target_pairs={{0,2},{1,3},{2,0},{3,1},{4,6},{5,7},{6,4},{7,5},{8,10},{9,11},{10,... | collective-permute-start | bytes 2359304 | tf_op jit(solution)/shard_map/ppermute | solution.py:494
  262.4 12.5 %collective-permute-start.17 = (bf16[96,768]{1,0:T(8,128)(2,1)S(1)}, bf16[96,768]{1,0:T(8,128)(2,1)S(1)}, u32[]{:S(2)}, u32[]{:S(2)}) collective-permute-start(bf16[96,768]{1,0:T(8,128)(2,1)S(1)} %get-tuple-element.131), channel_id=1, source_target_pairs={{0,8},{4,12},{8,0},{12,4},{16,24},{20,28},{24,16},{28,20},{1,9},{5... | collective-permute-start | bytes 442376 | tf_op jit(solution)/shard_map/ppermute | solution.py:458
  264.7 10.3 %collective-permute-start.18 = (bf16[96,768]{1,0:T(8,128)(2,1)S(1)}, bf16[96,768]{1,0:T(8,128)(2,1)S(1)}, u32[]{:S(2)}, u32[]{:S(2)}) collective-permute-start(bf16[96,768]{1,0:T(8,128)(2,1)S(1)} %get-tuple-element.133), channel_id=1, source_target_pairs={{0,16},{4,20},{8,24},{12,28},{16,0},{20,4},{24,8},{28,12},{1,17},{... | collective-permute-start | bytes 442376 | tf_op jit(solution)/shard_map/ppermute | solution.py:458
  268.4 11.6 %collective-permute-start.19 = (bf16[96,768]{1,0:T(8,128)(2,1)S(1)}, bf16[96,768]{1,0:T(8,128)(2,1)S(1)}, u32[]{:S(2)}, u32[]{:S(2)}) collective-permute-start(bf16[96,768]{1,0:T(8,128)(2,1)S(1)} %get-tuple-element.132), channel_id=1, source_target_pairs={{0,24},{4,28},{8,16},{12,20},{16,8},{20,12},{24,0},{28,4},{1,25},{... | collective-permute-start | bytes 442376 | tf_op jit(solution)/shard_map/ppermute | solution.py:458
  282.6 8.7 %collective-permute-start.21 = (bf16[96,1536]{1,0:T(8,128)(2,1)S(1)}, bf16[96,1536]{1,0:T(8,128)(2,1)S(1)}, u32[]{:S(2)}, u32[]{:S(2)}) collective-permute-start(bf16[96,1536]{1,0:T(8,128)(2,1)S(1)} %slice.208), channel_id=1, source_target_pairs={{0,2},{1,3},{2,0},{3,1},{4,6},{5,7},{6,4},{7,5},{8,10},{9,11},{10,... | collective-permute-start | bytes 884744 | tf_op jit(solution)/shard_map/ppermute | solution.py:494
  284.2 7.2 %copy-start.5 = (bf16[96,3072]{1,0:T(8,128)(2,1)S(1)}, bf16[96,3072]{1,0:T(8,128)(2,1)}, u32[]{:S(2)}) copy-start(bf16[96,3072]{1,0:T(8,128)(2,1)} %reduce-scatter.2.cloned.1.call-done) | copy-start | bytes 1769476
Sparse Core Ops, SparseCore 0:
  20.5 88.8 all-gather.1
  164.8 109.3 reduce-scatter.1

commit v4 on v3

--- a/solution.py
+++ b/solution.py
@@ -1,4 +1,7 @@
-import jax, jax.numpy as jnp
+import functools
+
+import jax
+import jax.numpy as jnp
 from jax import lax
 from jax.sharding import PartitionSpec as P
 from jax.experimental import pallas as pl
@@ -25,10 +28,10 @@
     zero = jnp.zeros_like(piece)
     return jnp.concatenate([piece, zero] if h%2==0 else [zero, piece], axis=0)
 
-def fwd_kernel(lo_ref, hi_ref, flip_ref, q_ref, k_ref, v_ref, w_ref, segc_ref, segr_ref, o_ref, lse_ref, near_ref, side_ref, far_ref, s_ref):
+def fwd_kernel(start_at, lo_ref, hi_ref, flip_ref, q_ref, k_ref, v_ref, w_ref, segc_ref, segr_ref, o_ref, lse_ref, first_ref, second_ref, s_ref):
     heads = q_ref.shape[0]//HD
     i = pl.program_id(0)
-    lo = lo_ref[i]; hi = hi_ref[i]; flip = flip_ref[0]
+    lo = lo_ref[start_at+i]; hi = hi_ref[start_at+i]; flip = flip_ref[0]
     c = LOG2E * HD**-0.5
     qz = [padded(q_ref, h, heads, slice(None)) for h in range(heads)]
     segq = segr_ref[...]
@@ -61,39 +64,43 @@
         lse_ref[h:h+1,:] = peaks[h]+jnp.log2(total)
     context = jnp.transpose(o_ref[...].astype(f32)).astype(bf16)
     merged = jnp.dot(context, w_ref[...], preferred_element_type=f32).astype(bf16)
-    size = near_ref.shape[0]
-    per = size//BQ
-    for n, ref in enumerate((near_ref, side_ref, far_ref, side_ref)):
+    per = first_ref.shape[0]//BQ
+    for n, ref in enumerate((first_ref, second_ref)):
         @pl.when(i//per==n)
         def _():
-            at = pl.multiple_of((i%per)*BQ, BQ) + (size if n==3 else 0)
-            ref[pl.ds(pl.multiple_of(at, BQ), BQ),:] = merged
-
-def attn_fwd(qT,k,vT,wT,segc,segr,lo,hi,flip):
+            ref[pl.ds(pl.multiple_of((i%per)*BQ, BQ), BQ),:] = merged
+
+def attn_fwd(second,qT,k,vT,wT,segc,segr,lo,hi,flip):
     width,length=qT.shape
     size,model=length//4,wT.shape[1]
-    whole=lambda rows: pl.BlockSpec((rows,model),lambda i,*_:(0,0))
     heads=width//HD
-    blocks=length//BQ
+    blocks=length//BQ//2
+    first=blocks*second
+    col=pl.BlockSpec((width,BQ),lambda i,*_:(0,first+i))
+    whole=pl.BlockSpec((size,model),lambda i,*_:(0,0))
+    part=jax.ShapeDtypeStruct((size,model),bf16)
     return pl.pallas_call(
-        fwd_kernel,
-        out_shape=(jax.ShapeDtypeStruct((width,length),bf16), jax.ShapeDtypeStruct((heads,length),f32))+tuple(jax.ShapeDtypeStruct((n*size,model),bf16) for n in (1,2,1)),
+        functools.partial(fwd_kernel,first),
+        out_shape=(jax.ShapeDtypeStruct((width,length//2),bf16), jax.ShapeDtypeStruct((8,length//2),f32), part, part),
         grid_spec=pltpu.PrefetchScalarGridSpec(num_scalar_prefetch=3, grid=(blocks,),
-            in_specs=[pl.BlockSpec((width,BQ),lambda i,*_:(0,i)),
+            in_specs=[col,
                       pl.BlockSpec((length,width),lambda i,*_:(0,0)),
                       pl.BlockSpec((width,length),lambda i,*_:(0,0)),
                       pl.BlockSpec((width,model),lambda i,*_:(model//width-1,0)),
                       pl.BlockSpec((length,1),lambda i,*_:(0,0)),
-                      pl.BlockSpec((1,BQ),lambda i,*_:(0,i))],
-            out_specs=[pl.BlockSpec((width,BQ),lambda i,*_:(0,i)),pl.BlockSpec((heads,BQ),lambda i,*_:(0,i)),whole(size),whole(2*size),whole(size)],
+                      pl.BlockSpec((1,BQ),lambda i,*_:(0,first+i))],
+            out_specs=[pl.BlockSpec((width,BQ),lambda i,*_:(0,i)),pl.BlockSpec((8,BQ),lambda i,*_:(0,i)),whole,whole],
             scratch_shapes=[pltpu.VMEM((heads,length//BK,BK,BQ),f32)]),
         compiler_params=pltpu.CompilerParams(dimension_semantics=("arbitrary",),vmem_limit_bytes=60<<20),
-        cost_estimate=pl.CostEstimate(flops=30*length*length*width,bytes_accessed=8*length*width,transcendentals=heads*length*length//2),
+        cost_estimate=pl.CostEstimate(flops=25*length*length*width,bytes_accessed=4*length*width,transcendentals=heads*length*length//4),
         name="attention",
     )(lo,hi,flip,qT,k,vT,wT,segc,segr)
 
-def bwd_kernel(lo_ref, hi_ref, flip_ref, q_ref, k_ref, kT_ref, v_ref, wT_ref, g0, g1, g2, g3, o_ref, lse_ref, segc_ref, segr_ref,
-               dq_ref, dk_ref, dv_ref, qb_ref, vb_ref, dk_acc, dv_acc, do_ref):
+def bwd_kernel(start_at, lo_ref, hi_ref, flip_ref, q_ref, k_ref, kT_ref, v_ref, wT_ref, g0, g1, o_ref, lse_ref, segc_ref, segr_ref, *rest):
+    if start_at:
+        dk_old, dv_old, dq_ref, dk_ref, dv_ref, qb_ref, vb_ref, dk_acc, dv_acc, do_ref = rest
+    else:
+        dq_ref, dk_ref, dv_ref, qb_ref, dk_acc, dv_acc, do_ref = rest
     heads = q_ref.shape[0]//HD
     width = q_ref.shape[0]
     i = pl.program_id(0)
@@ -101,10 +108,10 @@
     def _():
         dk_acc[...]=jnp.zeros_like(dk_acc); dv_acc[...]=jnp.zeros_like(dv_acc)
         qb_ref[...]=jnp.zeros_like(qb_ref)
-    lo = lo_ref[i]; hi = hi_ref[i]; flip = flip_ref[0]
+    lo = lo_ref[start_at+i]; hi = hi_ref[start_at+i]; flip = flip_ref[0]
     scale = HD**-0.5
     per = g0.shape[0]//BQ
-    for n, g_ref in enumerate((g0, g1, g2, g3)):
+    for n, g_ref in enumerate((g0, g1)):
         @pl.when(i//per==n)
         def _():
             at = pl.multiple_of((i%per)*BQ, BQ)
@@ -143,30 +150,38 @@
         qb_ref[h*HD:(h+1)*HD,:]+=part
     @pl.when(i==pl.num_programs(0)-1)
     def _():
-        dk_ref[...]=dk_acc[...].astype(bf16)
-        dv_ref[...]=dv_acc[...].astype(bf16)
-        vb_ref[...]=jnp.sum(dv_acc[...].reshape(dv_acc.shape[0]//8,8,width),axis=0)
-
-def attn_bwd(qT,k,kT,v,wT,grads,oT,lse,segc,segr,lo,hi,flip):
+        if start_at:
+            dk_ref[...]=(dk_acc[...]+dk_old[...]).astype(bf16)
+            dv=dv_acc[...]+dv_old[...]
+            dv_ref[...]=dv.astype(bf16)
+            vb_ref[...]=jnp.sum(dv.reshape(dv.shape[0]//8,8,width),axis=0)
+        else:
+            dk_ref[...]=dk_acc[...]
+            dv_ref[...]=dv_acc[...]
+
+def attn_bwd(qT,k,kT,v,wT,grads,oT,lse,segc,segr,lo,hi,flip,sums=()):
     width,length=qT.shape
     heads=width//HD
-    blocks=length//BQ
-    col=pl.BlockSpec((width,BQ),lambda i,*_:(0,i))
+    blocks=length//BQ//2
+    first=blocks if sums else 0
+    col=pl.BlockSpec((width,BQ),lambda i,*_:(0,first+i))
     row=pl.BlockSpec((length,width),lambda i,*_:(0,0))
+    tall=jax.ShapeDtypeStruct((length,width),bf16 if sums else f32)
+    eight=((jax.ShapeDtypeStruct((8,width),f32),),[pl.BlockSpec((8,width),lambda i,*_:(0,0))]) if sums else ((),[])
     return pl.pallas_call(
-        bwd_kernel,
-        out_shape=(jax.ShapeDtypeStruct((width,length),bf16), jax.ShapeDtypeStruct((length,width),bf16), jax.ShapeDtypeStruct((length,width),bf16), jax.ShapeDtypeStruct((width,128),f32), jax.ShapeDtypeStruct((8,width),f32)),
+        functools.partial(bwd_kernel,first),
+        out_shape=(jax.ShapeDtypeStruct((width,length//2),bf16), tall, tall, jax.ShapeDtypeStruct((width,128),f32))+eight[0],
         grid_spec=pltpu.PrefetchScalarGridSpec(num_scalar_prefetch=3, grid=(blocks,),
-            in_specs=[col,row,pl.BlockSpec((width,length),lambda i,*_:(0,0)),row,pl.BlockSpec((width,wT.shape[1]),lambda i,*_:(wT.shape[1]//width-1,0))]+[pl.BlockSpec(g.shape,lambda i,*_:(0,0)) for g in grads]+[col,
-                      pl.BlockSpec((heads,BQ),lambda i,*_:(0,i)),
+            in_specs=[col,row,pl.BlockSpec((width,length),lambda i,*_:(0,0)),row,pl.BlockSpec((width,wT.shape[1]),lambda i,*_:(wT.shape[1]//width-1,0))]+[pl.BlockSpec(g.shape,lambda i,*_:(0,0)) for g in grads]+[pl.BlockSpec((width,BQ),lambda i,*_:(0,i)),
+                      pl.BlockSpec((8,BQ),lambda i,*_:(0,i)),
                       pl.BlockSpec((length,1),lambda i,*_:(0,0)),
-                      pl.BlockSpec((1,BQ),lambda i,*_:(0,i))],
-            out_specs=[col,row,row,pl.BlockSpec((width,128),lambda i,*_:(0,0)),pl.BlockSpec((8,width),lambda i,*_:(0,0))],
+                      pl.BlockSpec((1,BQ),lambda i,*_:(0,first+i))]+[row]*len(sums),
+            out_specs=[pl.BlockSpec((width,BQ),lambda i,*_:(0,i)),row,row,pl.BlockSpec((width,128),lambda i,*_:(0,0))]+eight[1],
             scratch_shapes=[pltpu.VMEM((length,width),f32),pltpu.VMEM((length,width),f32),pltpu.VMEM((width,BQ),bf16)]),
         compiler_params=pltpu.CompilerParams(dimension_semantics=("arbitrary",),vmem_limit_bytes=60<<20),
-        cost_estimate=pl.CostEstimate(flops=38*length*length*width,bytes_accessed=20*length*width,transcendentals=heads*length*length//2),
+        cost_estimate=pl.CostEstimate(flops=30*length*length*width,bytes_accessed=10*length*width,transcendentals=heads*length*length//4),
         name="attention_back",
-    )(lo,hi,flip,qT,k,kT,v,wT,*grads,oT,lse,segc,segr)
+    )(lo,hi,flip,qT,k,kT,v,wT,*grads,oT,lse,segc,segr,*sums)
 
 def spans(seg_row):
     length=seg_row.shape[0]
@@ -189,17 +204,60 @@
 def fold(values):
     return jnp.sum(values.reshape(values.shape[0]//8,8,values.shape[1]),axis=0)
 
-def ffn_kernel(tok_ref, a0_ref, a1_ref, a2_ref, cot_ref, vec_ref, be_ref,
-               wa_ref,wb_ref,
-               out_ref, gm_ref, gml_ref, vg_ref, eb_ref, ga_ref,gb_ref,
-               we, ws, hl, hlT, hid, xhat, rs1, act, gp, acc, sl, slT, gsum, il, de, dt, wsem, osem):
+def placements(count, model, blocks):
+    if count != 8:
+        return [[(r % 2, 0, r % 2, 0, None, model)] for r in range(blocks)]
+    rows = model // 8
+    every = []
+    for r in range(blocks):
+        core, beyond = r % 2, r // 2
+        block = []
+        for shard in range(8):
+            odd, place = shard % 2, shard // 2
+            if not beyond:
+                source, first = odd, place
+            elif not odd:
+                source, first = 2, place
+            else:
+                source, first = (3, 0) if place == 0 else (4, place - 1)
+            group = beyond and odd
+            target = 0 if group else beyond * 2 + odd
+            block.append((core * 5 + source, first * rows, core * 2 + group, (target * 4 + place) * rows, shard, rows))
+        every.append(block)
+    return every
+
+
+def ffn_kernel(count, home_ref, tok_ref, a0_ref, a1_ref, a2_ref, cot_ref, vec_ref, be_ref, *refs):
     rows, width = tok_ref.shape
-    blocks,_,units=we.shape
-    es=[(wa_ref,wb_ref)[r%2].at[:,(r//2)*2*units:(r//2+1)*2*units] for r in range(blocks)]
-    ds=[(ga_ref,gb_ref)[r%2].at[:,(r//2)*2*units:(r//2+1)*2*units] for r in range(blocks)]
+    blocks, units = be_ref.shape
+    table = placements(count, width, blocks)
+    n_in = 1 + max(item[0] for block in table for item in block)
+    n_out = 1 + max(item[2] for block in table for item in block)
+    pieces, refs = refs[:n_in], refs[n_in:]
+    (out_ref, gm_ref, gml_ref, vg_ref, eb_ref), refs = refs[:5], refs[5:]
+    grads, refs = refs[:n_out], refs[n_out:]
+    we, ws, hl, hlT, hid, xhat, rs1, act, gp, acc, sl, slT, gsum, il, de, dt, wsem, osem = refs
+    home = home_ref[0]
+    def columns(ref, r, half):
+        start = half * units + (r // 2 * 2 * units if len(table[0]) == 1 else 0)
+        return ref.at[:, start : start + units]
+    def spot(shard, size):
+        return pl.ds(0 if shard is None else pl.multiple_of(jnp.bitwise_xor(home, shard) * size, size), size)
+    def fetched(r, half):
+        return [
+            pltpu.make_async_copy(columns(pieces[p], r, half).at[first : first + size], (we, ws)[half].at[r, spot(shard, size)], wsem.at[half, r, k])
+            for k, (p, first, _, _, shard, size) in enumerate(table[r])
+        ]
+    def sent(slot, r):
+        return [
+            pltpu.make_async_copy((de, dt)[half].at[slot, spot(shard, size)], columns(grads[g], r, half).at[first : first + size], osem.at[half, slot, k])
+            for half in range(2)
+            for k, (_, _, g, first, shard, size) in enumerate(table[r])
+        ]
     for r in range(blocks):
-        pltpu.make_async_copy(es[r].at[:,0:units],we.at[r],wsem.at[0,r]).start()
-        pltpu.make_async_copy(es[r].at[:,units:],ws.at[r],wsem.at[1,r]).start()
+        for half in range(2):
+            for c in fetched(r, half):
+                c.start()
     mb=vec_ref[0:1,:]; g1=vec_ref[1:2,:]; b1=vec_ref[2:3,:]; sb=vec_ref[3:4,:]; g2=vec_ref[4:5,:]; b2=vec_ref[5:6,:]
     def first(i,_):
         at=pl.ds(pl.multiple_of(i*RC,RC),RC)
@@ -225,7 +283,7 @@
         for k in range(blocks):
             @pl.when(r==k)
             def _():
-                pltpu.make_async_copy(es[k].at[:,0:units],we.at[k],wsem.at[0,k]).wait()
+                for c in fetched(k, 0): c.wait()
         def tile(j,_):
             n=pl.multiple_of((j//mt)*T,T); m=pl.multiple_of((j%mt)*TM,TM)
             u=lax.dot_general(hl[pl.ds(m,TM),:],we[r,:,pl.ds(n,T)],NN,preferred_element_type=f32)+be_ref[pl.ds(r,1),pl.ds(n,T)]
@@ -237,7 +295,7 @@
         for k in range(blocks):
             @pl.when(r==k)
             def _():
-                pltpu.make_async_copy(es[k].at[:,units:],ws.at[k],wsem.at[1,k]).wait()
+                for c in fetched(k, 1): c.wait()
         def shrink(j,_):
             n=pl.multiple_of((j//mt)*T,T); m=pl.multiple_of((j%mt)*TM,TM)
             acc[pl.ds(m,TM),pl.ds(n,T)]+=lax.dot_general(act[r,pl.ds(m,TM),:],ws[r,pl.ds(n,T),:],NT,preferred_element_type=f32)
@@ -260,8 +318,6 @@
     zero=jnp.zeros((8,width),f32)
     sg,sh,sbg=lax.fori_loop(0,rows//RC,second,(zero,zero,zero),unroll=4)
     turn(sl,slT)
-    def sent(r,slot,k):
-        return (pltpu.make_async_copy(de.at[slot],ds[k].at[:,0:units],osem.at[0,slot]),pltpu.make_async_copy(dt.at[slot],ds[k].at[:,units:],osem.at[1,slot]))
     def backward(r,_):
         slot=r%2
         def tile(j,_):
@@ -281,7 +337,7 @@
         for k in range(2,blocks):
             @pl.when(r==k)
             def _():
-                for c in sent(r,k%2,k-2): c.wait()
+                for c in sent(k%2,k-2): c.wait()
         def grads(j,_):
             n=pl.multiple_of((j//(width//TG))*T,T); m=pl.multiple_of((j%(width//TG))*TG,TG)
             dt[slot,pl.ds(m,TG),pl.ds(n,T)]=lax.dot_general(slT[pl.ds(m,TG),:],act[r,:,pl.ds(n,T)],NN,preferred_element_type=f32).astype(bf16)
@@ -291,7 +347,7 @@
         for k in range(blocks):
             @pl.when(r==k)
             def _():
-                for c in sent(r,k%2,k): c.start()
+                for c in sent(k%2,k): c.start()
         return 0
     lax.fori_loop(0,blocks,backward,0)
     def last(i,sums):
@@ -307,28 +363,34 @@
     for n,v in enumerate((mbg,fg,fs,sbg,sg,sh)):
         vg_ref[n]=v
     for k in range(max(0,blocks-2),blocks):
-        for c in sent(k,k%2,k): c.wait()
-
-def ffn(tok,a0,a1,a2,cot,vec,be,w_own,w_other):
-    rows,width=tok.shape; blocks,units=be.shape
-    v=pl.BlockSpec(memory_space=pltpu.VMEM); h=pl.BlockSpec(memory_space=pltpu.HBM)
-    g=jax.ShapeDtypeStruct((width,blocks*units),bf16)
-    V=pltpu.VMEM
+        for c in sent(k%2,k): c.wait()
+
+def ffn(home, count, tok, a0, a1, a2, cot, vec, be, pieces):
+    rows, width = tok.shape
+    blocks, units = be.shape
+    table = placements(count, width, blocks)
+    n_out = 1 + max(item[2] for block in table for item in block)
+    each = len(table[0])
+    sizes = [(width * 3 // 2, 2 * units), (width // 2, 2 * units)] * 2 if each > 1 else [(width, blocks * units)] * 2
+    grads = tuple(jax.ShapeDtypeStruct(size, bf16) for size in sizes)
+    v = pl.BlockSpec(memory_space=pltpu.VMEM)
+    h = pl.BlockSpec(memory_space=pltpu.HBM)
+    V = pltpu.VMEM
     return pl.pallas_call(
-        ffn_kernel,
-        out_shape=(jax.ShapeDtypeStruct((rows,width),bf16),jax.ShapeDtypeStruct((rows,width),f32),jax.ShapeDtypeStruct((rows,width),bf16),
-                   jax.ShapeDtypeStruct((6,8,width),f32),jax.ShapeDtypeStruct((blocks,8,units),f32))+(g,g),
-        in_specs=[v]*7+[h]*2,
-        out_specs=[v]*5+[h]*2,
-        scratch_shapes=[V((blocks,width,units),bf16),V((blocks,width,units),bf16),
-            V((rows,width),bf16),V((width,rows),bf16),V((rows,width),f32),V((rows,width),f32),V((rows,128),f32),
-            V((blocks,rows,units),bf16),V((blocks,rows,units),f32),V((rows,width),f32),V((rows,width),bf16),V((width,rows),bf16),V((rows,width),f32),
-            V((rows,units),bf16),V((2,width,units),bf16),V((2,width,units),bf16),
-            pltpu.SemaphoreType.DMA((2,blocks)),pltpu.SemaphoreType.DMA((2,2))],
-        compiler_params=pltpu.CompilerParams(vmem_limit_bytes=60<<20),
-        cost_estimate=pl.CostEstimate(flops=30*rows*width*units*blocks,bytes_accessed=8*blocks*width*units,transcendentals=2*rows*units*blocks),
+        functools.partial(ffn_kernel, count),
+        out_shape=(jax.ShapeDtypeStruct((rows, width), bf16), jax.ShapeDtypeStruct((rows, width), f32), jax.ShapeDtypeStruct((rows, width), bf16),
+            jax.ShapeDtypeStruct((6, 8, width), f32), jax.ShapeDtypeStruct((blocks, 8, units), f32)) + grads,
+        in_specs=[pl.BlockSpec(memory_space=pltpu.SMEM)] + [v] * 7 + [h] * len(pieces),
+        out_specs=[v] * 5 + [h] * n_out,
+        scratch_shapes=[V((blocks, width, units), bf16), V((blocks, width, units), bf16),
+            V((rows, width), bf16), V((width, rows), bf16), V((rows, width), f32), V((rows, width), f32), V((rows, 128), f32),
+            V((blocks, rows, units), bf16), V((blocks, rows, units), f32), V((rows, width), f32), V((rows, width), bf16), V((width, rows), bf16), V((rows, width), f32),
+            V((rows, units), bf16), V((2, width, units), bf16), V((2, width, units), bf16),
+            pltpu.SemaphoreType.DMA((2, blocks, each)), pltpu.SemaphoreType.DMA((2, 2, each))],
+        compiler_params=pltpu.CompilerParams(vmem_limit_bytes=60 << 20),
+        cost_estimate=pl.CostEstimate(flops=30 * rows * width * units * blocks, bytes_accessed=8 * blocks * width * units, transcendentals=2 * rows * units * blocks),
         name="feed_forward",
-    )(tok,a0,a1,a2,cot,vec,be,w_own,w_other)
+    )(home, tok, a0, a1, a2, cot, vec, be, *pieces)
 
 
 def proj_kernel(home_ref, x0, x1, x2, x3, wa_ref, wb_ref, bq_ref, bvc_ref, bvr_ref,
@@ -397,60 +459,113 @@
     )(home, *tokens, wa, wb, bq[:, None], bv[:, None], bv[None, :])
 
 
-def grads_kernel(home_ref, x0, x1, x2, x3, g0, g1, g2, g3, c_ref, q_ref, k_ref, v_ref, *rest):
-    *outs, acc, xT, gT = rest
+def grads_kernel(home_ref, x0, x1, x2, x3, g0, g1, g2, g3, ca_ref, cb_ref, qa_ref, qb_ref, k_ref, v_ref, *rest):
+    *outs, acc, x_buf, g_buf, xT, gT, sem = rest
     home = home_ref[0]
-    width = q_ref.shape[0]
-    model = x0.shape[1]
-    for n, (x_ref, g_ref) in enumerate(zip((x0, x1, x2, x3), (g0, g1, g2, g3))):
-        size = x_ref.shape[0]
-        rows = slice(n * size, (n + 1) * size)
-        def turn(i, _):
-            at = pl.multiple_of(i * 256, 256)
-            xT[:, pl.ds(at, 256)] = jnp.transpose(x_ref[pl.ds(at, 256), :].astype(f32)).astype(bf16)
-            gT[:, pl.ds(at, 256)] = jnp.transpose(g_ref[pl.ds(at, 256), :].astype(f32)).astype(bf16)
-            return 0
-        lax.fori_loop(0, size // 256, turn, 0)
-        def part(i, _):
-            at = pl.ds(pl.multiple_of(i * 256, 256), 256)
-            x = xT[at, :]
-            pieces = (
-                lax.dot_general(x, q_ref[:, rows], NT, preferred_element_type=f32),
-                jnp.dot(x, k_ref[rows, :], preferred_element_type=f32),
-                jnp.dot(x, v_ref[rows, :], preferred_element_type=f32),
-                lax.dot_general(gT[at, :], c_ref[:, rows], NT, preferred_element_type=f32),
-            )
-            for m, piece in enumerate(pieces):
-                acc[m, at, :] = piece if n == 0 else acc[m, at, :] + piece
-            return 0
-        lax.fori_loop(0, model // 256, part, 0)
-    if len(outs) == 1:
-        for m in range(4):
-            outs[0][:, m * width : (m + 1) * width] = acc[m].astype(bf16)
-        return
-    rows = model // 8
-    for r in range(8):
-        at = pl.ds(pl.multiple_of(jnp.bitwise_xor(home, r) * rows, rows), rows)
-        to = slice(r // 2 * rows, (r // 2 + 1) * rows)
-        for m in range(4):
-            outs[r % 2][to, m * width : (m + 1) * width] = acc[m, at, :].astype(bf16)
+    step = pl.program_id(0)
+    size, model = xT.shape[1], xT.shape[0]
+    width = k_ref.shape[1]
+    fetch = [
+        (pltpu.make_async_copy(x, x_buf.at[n], sem.at[0, n]), pltpu.make_async_copy(g, g_buf.at[n], sem.at[1, n]))
+        for n, (x, g) in enumerate(zip((x0, x1, x2, x3), (g0, g1, g2, g3)))
+    ]
+    @pl.when(step == 0)
+    def _():
+        for x, g in fetch:
+            x.start()
+            g.start()
+    for n, (x, g) in enumerate(fetch):
+        @pl.when(step == n)
+        def _():
+            x.wait()
+            g.wait()
+    for i in range(0, size, 256):
+        xT[:, i : i + 256] = jnp.transpose(x_buf[step, i : i + 256, :].astype(f32)).astype(bf16)
+        gT[:, i : i + 256] = jnp.transpose(g_buf[step, i : i + 256, :].astype(f32)).astype(bf16)
+    q = jnp.where(step < 2, qa_ref[...], qb_ref[...])
+    c = jnp.where(step < 2, ca_ref[...], cb_ref[...])
+    pieces = (
+        lax.dot_general(xT[...], q, NT, preferred_element_type=f32),
+        jnp.dot(xT[...], k_ref[...], preferred_element_type=f32),
+        jnp.dot(xT[...], v_ref[...], preferred_element_type=f32),
+        lax.dot_general(gT[...], c, NT, preferred_element_type=f32),
+    )
+    @pl.when(step == 0)
+    def _():
+        for m, piece in enumerate(pieces):
+            acc[m] = piece
+    @pl.when(step > 0)
+    def _():
+        for m, piece in enumerate(pieces):
+            acc[m] += piece
+    @pl.when(step == 3)
+    def _():
+        if len(outs) == 1:
+            for m in range(4):
+                outs[0][:, m * width : (m + 1) * width] = acc[m].astype(bf16)
+            return
+        rows = model // 8
+        for r in range(8):
+            at = pl.ds(pl.multiple_of(jnp.bitwise_xor(home, r) * rows, rows), rows)
+            to = slice(r // 2 * rows, (r // 2 + 1) * rows)
+            for m in range(4):
+                outs[r % 2][to, m * width : (m + 1) * width] = acc[m, at, :].astype(bf16)
+
+
+def halves(width, size):
+    return [pl.BlockSpec((width, size), lambda i: (0, jnp.minimum(i, 1))), pl.BlockSpec((width, size), lambda i: (0, jnp.maximum(i, 2) - 2))]
 
 
 def attn_grads(home, count, tokens, grads, contextT, dqT, dk, dv):
     size, model = tokens[0].shape
-    width = dqT.shape[0]
-    v = pl.BlockSpec(memory_space=pltpu.VMEM)
+    width = dk.shape[1]
+    hbm = pl.BlockSpec(memory_space=pltpu.HBM)
+    down = pl.BlockSpec((size, width), lambda i: (i, 0))
     parts = 2 if count == 8 else 1
+    V = pltpu.VMEM
     return pl.pallas_call(
         grads_kernel,
+        grid=(4,),
         out_shape=[jax.ShapeDtypeStruct((model // parts, 4 * width), bf16)] * parts,
-        in_specs=[pl.BlockSpec(memory_space=pltpu.SMEM)] + [v] * 12,
-        out_specs=[v] * parts,
-        scratch_shapes=[pltpu.VMEM((4, model, width), f32), pltpu.VMEM((model, size), bf16), pltpu.VMEM((model, size), bf16)],
-        compiler_params=pltpu.CompilerParams(vmem_limit_bytes=60 << 20),
-        cost_estimate=pl.CostEstimate(flops=120 * size * model * width, bytes_accessed=24 * size * model, transcendentals=0),
+        in_specs=[pl.BlockSpec(memory_space=pltpu.SMEM)] + [hbm] * 8 + halves(width, size) * 2 + [down, down],
+        out_specs=[pl.BlockSpec((model // parts, 4 * width), lambda i: (0, 0))] * parts,
+        scratch_shapes=[V((4, model, width), f32), V((4, size, model), bf16), V((4, size, model), bf16), V((model, size), bf16), V((model, size), bf16),
+            pltpu.SemaphoreType.DMA((2, 4))],
+        compiler_params=pltpu.CompilerParams(dimension_semantics=("arbitrary",), vmem_limit_bytes=60 << 20),
+        cost_estimate=pl.CostEstimate(flops=8 * size * model * width, bytes_accessed=24 * size * model, transcendentals=0),
         name="projection_grads",
-    )(home, *tokens, *grads, contextT, dqT, dk, dv)
+    )(home, *tokens, *grads, *contextT, *dqT, dk, dv)
+
+
+def back_kernel(qa_ref, qb_ref, k_ref, v_ref, wq_ref, wk_ref, wv_ref, near_ref, side_ref, far_ref):
+    i = pl.program_id(0)
+    size = near_ref.shape[0]
+    def block(q_ref):
+        q = jnp.transpose(q_ref[...].astype(f32)).astype(bf16)
+        total = jnp.dot(q, wq_ref[...], preferred_element_type=f32)
+        total = total + jnp.dot(k_ref[...], wk_ref[...], preferred_element_type=f32)
+        return (total + jnp.dot(v_ref[...], wv_ref[...], preferred_element_type=f32)).astype(bf16)
+    for n, ref in enumerate((near_ref, side_ref, far_ref, side_ref)):
+        @pl.when(i == n)
+        def _():
+            ref[size if n == 3 else 0 : 2 * size if n == 3 else size, :] = block((qa_ref, qb_ref)[n // 2])
+
+
+def project_back(dqT, dk, dv, wT):
+    length, width = dk.shape
+    size, model = length // 4, wT.shape[1]
+    down = pl.BlockSpec((size, width), lambda i: (i, 0))
+    weight = [pl.BlockSpec((width, model), functools.partial(lambda n, i: (n, 0), n)) for n in range(3)]
+    return pl.pallas_call(
+        back_kernel,
+        grid=(4,),
+        out_shape=[jax.ShapeDtypeStruct((n * size, model), bf16) for n in (1, 2, 1)],
+        in_specs=halves(width, size) + [down, down] + weight,
+        out_specs=[pl.BlockSpec((n * size, model), lambda i: (0, 0)) for n in (1, 2, 1)],
+        compiler_params=pltpu.CompilerParams(dimension_semantics=("arbitrary",), vmem_limit_bytes=60 << 20),
+        cost_estimate=pl.CostEstimate(flops=70 * length * model * width, bytes_accessed=8 * length * model, transcendentals=0),
+        name="projection_back",
+    )(*dqT, dk, dv, wT, wT, wT)
 
 
 def hop(value, bit):
@@ -465,16 +580,6 @@
         return every, every
     even = jnp.concatenate([own] + [hop(own, bit) for bit in (2, 4, 6)], axis=0)
     return even, hop(even, 1)
-
-
-def scatter_shards(parts):
-    if len(parts) == 1:
-        count = lax.axis_size("dp")
-        swapped = lax.all_to_all(parts[0], "dp", 0, 0, tiled=True)
-        return jnp.sum(swapped.reshape(count, -1, swapped.shape[1]).astype(f32), axis=0)
-    even = (parts[0].astype(f32) + hop(parts[1], 1).astype(f32)).astype(bf16)
-    even = even.reshape(4, -1, even.shape[1])
-    return even[0].astype(f32) + sum(hop(even[n], 2 * n).astype(f32) for n in (1, 2, 3))
 
 
 def later(value, *markers, flops=0):
@@ -510,11 +615,46 @@
     return (near, beside[:rows], exchange(ahead, 2)), ahead
 
 
-def scatter_rows(partial):
-    rows = partial.shape[0] // 4
-    low = partial.astype(bf16)
-    piece = lambda r: low[r * rows : (r + 1) * rows]
-    return scatter_pieces(piece(0), jnp.concatenate([piece(1), piece(3)], axis=0), piece(2))
+def gather_blocks(own):
+    if lax.axis_size("dp") != 8:
+        return [lax.all_gather(jnp.concatenate([own, exchange(own, 2)], axis=1), "dp", axis=0, tiled=True)]
+    even = jnp.concatenate([own] + [hop(own, bit) for bit in (2, 4, 6)], axis=0)
+    return [even, hop(even, 1), exchange(even, 2)]
+
+
+def last_blocks(pieces, *markers):
+    if len(pieces) == 1:
+        return []
+    _, odd, beyond = pieces
+    cut = odd.shape[0] // 4
+    return [later(exchange(odd[:cut], 2), *markers), later(hop(beyond[cut:], 1), *markers)]
+
+
+def total(*terms):
+    result = terms[0].astype(f32)
+    for term in terms[1:]:
+        result = result + term.astype(f32)
+    return result
+
+
+def fold_both(own, got):
+    cut = own.shape[0] // 4
+    return total(own[:cut], got[:cut]).astype(bf16), total(own[cut:], got[cut:]).astype(bf16)
+
+
+def fold_rest(own, got, across, along):
+    rows = own.shape[0] // 3
+    cut = rows // 4
+    part = lambda n: total(own[n * rows : (n + 1) * rows], got[n * rows : (n + 1) * rows])
+    odd, beyond = part(1), part(2)
+    odd = jnp.concatenate([odd[:cut] + across.astype(f32), odd[cut:]], axis=0).astype(bf16)
+    beyond = jnp.concatenate([beyond[:cut], beyond[cut:] + along.astype(f32)], axis=0).astype(bf16)
+    return odd, beyond
+
+
+def fold_even(own, got, odd, beyond):
+    rows = own.shape[0] // 3
+    return total(own[:rows], got[:rows], odd, beyond).astype(bf16).reshape(4, rows // 4, -1)
 
 
 def on_device(
@@ -550,8 +690,7 @@
     shard = jnp.concatenate([query_proj, key_proj, value_proj, merge_proj.T], axis=1)
     shards = gather_shards(shard)
     wide = jnp.concatenate([expand_proj, shrink_proj.T], axis=1)
-    wide = jnp.concatenate([wide, exchange(wide, 2)], axis=1)
-    w_own = lax.all_gather(wide, "dp", axis=0, tiled=True)
+    pieces = gather_blocks(wide)
     own = jnp.concatenate(
         [query_bias, value_bias, merge_bias, first_gain, first_shift, shrink_bias, second_gain, second_shift, expand_bias]
     )
@@ -562,7 +701,7 @@
     own = jnp.pad(own, (0, slots * 128 - own.shape[0])).reshape(1, slots, 128)
     vectors = lax.all_to_all(jnp.broadcast_to(own, (world, slots, 128)), everyone, 0, 0, tiled=True)
     vectors = vectors.reshape(world, slots * 128)
-    whole = [vectors[:, n * share : (n + 1) * share].reshape(model) for n in range(8)]
+    whole = vectors[:, : 8 * share].reshape(world, 8, share).transpose(1, 0, 2).reshape(8, model)
     unit_bias = vectors[:, 8 * share : 8 * share + unit_share].reshape(4, units)
     flips = jnp.bitwise_xor(jnp.arange(4), part)
     seg = lax.dynamic_slice(vectors, (lax.axis_index("dp") * 4, count), (4, rows))
@@ -570,7 +709,7 @@
     unit_bias = jnp.take(unit_bias, flips, axis=0)
     query_b = lax.dynamic_slice_in_dim(whole[0], part * width, width)
     value_b = lax.dynamic_slice_in_dim(whole[1], part * width, width)
-    rows_b = jnp.stack(whole[2:8])
+    rows_b = whole[2:8]
 
     blocks = row_blocks(tokens)
     segc, segr = seg[:, None], seg[None, :]
@@ -578,46 +717,73 @@
     flip = (part * (tokens.shape[0] // BK)).astype(jnp.int32).reshape(1)
     home = lax.axis_index("dp").astype(jnp.int32).reshape(1)
     query_t, key_t, value_t, keys, values, attn_wt = project(home, blocks, *shards, dp, query_b, value_b)
-    wq, wk, wv, _ = (attn_wt[n * width : (n + 1) * width] for n in range(4))
-    dot = lambda a, b, dims: lax.dot_general(a, b, dims, preferred_element_type=f32)
-    context_t, logsum, *pieces = attn_fwd(query_t, keys, value_t, attn_wt, segc, segr, lo, hi, flip)
-    (a0, a1, a2), ahead = scatter_pieces(*pieces)
-
-    w_other = exchange(w_own, 1)
-    rows_b = later(rows_b, ahead, flops=7 * 10**10)
-    out = ffn(tokens, a0, a1, a2, cotangent, rows_b, unit_bias, w_own, w_other)
+    ahead = functools.partial(attn_fwd, 1, query_t, keys, value_t, attn_wt, segc, segr)
+    behind = functools.partial(attn_fwd, 0, query_t, keys, value_t, attn_wt, segc, segr)
+    context_b, logsum_b, far, side = ahead(later(lo, pieces[0]), hi, flip)
+    beside = exchange(side, 1)
+    far = (far.astype(f32) + beside.astype(f32)).astype(bf16)
+    swapped = [exchange(pieces[0], 1)]
+    context_a, logsum_a, a0, side = behind(later(lo, far, swapped[0], *pieces[1:]), hi, flip)
+    a1 = exchange(side, 1)
+    a2 = later(exchange(far, 2), context_a)
+
+    swapped = swapped + [later(exchange(piece, 1), context_a) for piece in pieces[1:]]
+    last = last_blocks(pieces, context_a, a2)
+    pieces = pieces + last + swapped + [exchange(piece, 1) for piece in last]
+    out = ffn(home, dp, tokens, a0, a1, a2, cotangent, rows_b, unit_bias, pieces)
     output, grad_mixed, mixed_low, row_sums, unit_sums = out[:5]
-    g_own, g_other = out[5:]
-
+    beside = exchange(mixed_low, 1)
     across = exchange(mixed_low, 2)
-    beside = exchange(mixed_low, 1)
-    wide_local = (g_own.astype(f32) + exchange(g_other, 1).astype(f32)).astype(bf16)
+    grads = out[5:]
+    local = len(grads) // 2
+    swapped = [exchange(grad, 1) for grad in grads[local:]]
+    back = functools.partial(attn_bwd, query_t, keys, key_t, values, attn_wt)
+    waits = []
+    if local == 2:
+        waits = fold_both(grads[1], swapped[1])
+    dq_a, dk_a, dv_a, q_sums_a = back((mixed_low, beside), context_a, logsum_a, segc, segr, later(lo, *waits), hi, flip)
+    across = later(across, q_sums_a)
     mixed_blocks = [mixed_low, beside, across, exchange(across, 1)]
-    wide_local = lax.psum_scatter(wide_local, "dp", scatter_dimension=0, tiled=True)
-    dq_t, dk, dv, q_sums, v_sums = attn_bwd(
-        query_t, keys, key_t, values, attn_wt, mixed_blocks, context_t, logsum, segc, segr, lo, hi, flip
+    if local == 2:
+        waits = fold_rest(grads[0], swapped[0], later(exchange(waits[0], 2), q_sums_a), later(hop(waits[1], 1), q_sums_a))
+    dq_b, dk, dv, q_sums_b, v_sums = back(
+        mixed_blocks[2:], context_b, logsum_b, segc, segr, later(lo, *waits), hi, flip, sums=(dk_a, dv_a)
     )
-    attn_local = attn_grads(home, dp, blocks, mixed_blocks, context_t, dq_t, dk, dv)
-    attn_grad = scatter_shards(attn_local)
-    dq_late = later(dq_t, attn_local[0])
-    total = dot(dq_late, wq, TN) + dot(dk, wk, NN) + dot(dv, wv, NN)
-    (b0, b1, b2), _ = scatter_rows(total)
-    tokens_grad = (grad_mixed + (b0.astype(f32) + b1.astype(f32) + b2.astype(f32))).astype(bf16)
-    wide_far = exchange(wide_local[:, 2 * units :], 2)
-    querygrad, keygrad, valuegrad, mergegrad = (attn_grad[:, n * width : (n + 1) * width] for n in range(4))
-    wide_grad = wide_local[:, : 2 * units].astype(f32) + wide_far.astype(f32)
-    expandgrad = wide_grad[:, :units]
-    shrinkgrad = wide_grad[:, units:].T
-
-    zero = jnp.zeros((4, width), f32)
-    q_all = lax.dynamic_update_slice(zero, jnp.sum(q_sums, axis=1)[None], (part, 0)).reshape(world, share)
-    v_all = lax.dynamic_update_slice(zero, jnp.sum(v_sums, axis=0)[None], (part, 0)).reshape(world, share)
+    attn_local = attn_grads(home, dp, blocks, mixed_blocks, (context_a, context_b), (dq_a, dq_b), dk, dv)
+    if local == 2:
+        waits = [fold_even(grads[0], swapped[0], later(hop(waits[0], 1), attn_local[0]), later(exchange(waits[1], 2), attn_local[0]))]
+    even = waits[0] if local == 2 else attn_local[0]
+    b0, side, far = project_back((later(dq_a, even), dq_b), dk, dv, attn_wt)
+
+    if local == 2:
+        wide_grad = even[0].astype(f32) + sum(later(hop(even[n], 2 * n), b0).astype(f32) for n in (1, 2, 3))
+        rows = attn_local[0].shape[0] // 4
+        even = total(attn_local[0], later(hop(attn_local[1], 1), wide_grad)).astype(bf16).reshape(4, rows, -1)
+        attn_grad = even[0].astype(f32) + sum(hop(even[n], 2 * n).astype(f32) for n in (1, 2, 3))
+    else:
+        mine = lax.psum_scatter(total(grads[0], swapped[0]).astype(bf16), "dp", scatter_dimension=0, tiled=True)
+        wide_grad = total(mine[:, : 2 * units], exchange(mine[:, 2 * units :], 2))
+        attn_grad = lax.all_to_all(attn_local[0], "dp", 0, 0, tiled=True)
+        attn_grad = jnp.sum(attn_grad.reshape(dp, -1, model).astype(f32), axis=0)
+    q_sums = later(q_sums_a + q_sums_b, wide_grad)
+    v_sums = later(v_sums, wide_grad)
+    mine = (jnp.arange(4) == part).astype(f32)[:, None]
+    q_all = (mine * jnp.sum(q_sums, axis=1)[None]).reshape(1, model)
+    v_all = (mine * jnp.sum(v_sums, axis=0)[None]).reshape(1, model)
+    early = jnp.sum(row_sums, axis=1).reshape(6, world, share).transpose(1, 0, 2).reshape(world, 6 * share)
+    late = jnp.concatenate([q_all, v_all], axis=0).reshape(2, world, share).transpose(1, 0, 2).reshape(world, 2 * share)
     u_all = jnp.take(jnp.sum(unit_sums, axis=1), flips, axis=0).reshape(world, unit_share)
-    row_all = [v.reshape(world, share) for v in jnp.sum(row_sums, axis=1)]
-    send = jnp.concatenate([q_all, v_all] + row_all + [u_all], axis=1)
+    send = jnp.concatenate([late, early, u_all], axis=1)
     send = jnp.pad(send, ((0, 0), (0, slots * 128 - send.shape[1]))).reshape(world, slots, 128)
     got = jnp.sum(lax.all_to_all(send, everyone, 0, 0, tiled=True).reshape(world, slots * 128), axis=0)
     small = [got[n * share : (n + 1) * share] for n in range(8)]
+
+    (b0, b1, b2), _ = scatter_pieces(b0, side, far)
+    tokens_grad = (grad_mixed + (b0.astype(f32) + b1.astype(f32) + b2.astype(f32))).astype(bf16)
+    querygrad, keygrad, valuegrad, mergegrad = (attn_grad[:, n * width : (n + 1) * width] for n in range(4))
+    expandgrad = wide_grad[:, :units]
+    shrinkgrad = wide_grad[:, units:].T
+
     qbiasgrad, vbiasgrad, mbiasgrad, fgaingrad, fshiftgrad, sbiasgrad, sgaingrad, sshiftgrad = small
     ebiasgrad = got[8 * share : 8 * share + unit_share]
     return (

time: 301 us -> 301 us (level)
  Pallas kernels: 99.8 us -> 129 us
  waiting for transfers between devices: 77.9 us -> 50.1 us
  blocking collectives: 21.1 us -> 0 us
  starting transfers between devices: 40.2 us -> 55.2 us
  local copies, waits for them, and re-layouts: 19 us -> 32.6 us
  between operations: 14.8 us -> 1.3 us
  other arithmetic: 21 us -> 31.5 us
  matrix products: 5.19 us -> 0 us
    pallas_call x4 -> x7, Pallas kernels: 89.9 us -> 119 us  [the longest x2 42.8 us: attn_bwd(): pl.pallas_call(functools.partial(bwd_kernel, first), out_shape=(jax.Shape...]
    all_to_all x1 -> x0, blocking collectives: 21.1 us -> none  [on_device(): lax.all_to_all(send, everyone, 0, 0, tiled=True).reshape(world, slots * 128)]
    ppermute x14 -> x22, waiting for transfers between devices: 32 us -> 12.4 us  [exchange(): return lax.ppermute(value, 'tensor', [(i, i ^ bit) for i in range(4)])]
    all_gather x1 -> x0, waiting for transfers between devices: 14.1 us -> none  [on_device(): w_own = lax.all_gather(wide, 'dp', axis=0, tiled=True)]
    unnamed x82 -> x86, local copies, waits for them, and re-layouts: 7.02 us -> 18.4 us
    all_to_all x0 -> x1, waiting for transfers between devices: none -> 8.36 us  [on_device(): lax.all_to_all(send, everyone, 0, 0, tiled=True).reshape(world, slots * 128)]
    ppermute x8 -> x18, starting transfers between devices: 25.7 us -> 33.4 us  [hop(): return lax.ppermute(value, 'dp', [(i, i ^ bit) for i in range(count)])]
    add x2 -> x4, other arithmetic: 0.14 us -> 7.68 us  [the longest x1 3.13 us: total(): result = result + term.astype(f32)]
  transfers between devices with their start and end apart: 25 -> 42, of which waited for: 13 -> 10; matrix products, arithmetic and copies ran while one was open for 12% -> 15% of each run, Pallas kernels for 23% -> 32%
where the time goes in v4:
time: 301 us; the launch traced here: 300 us
  Pallas kernels  129 us (43%)
  starting transfers between devices  55.2 us (18%)
  waiting for transfers between devices  50.1 us (17%)
  local copies, waits for them, and re-layouts  32.6 us (11%)
  other arithmetic  31.5 us (10%)
    pallas_call x2, Pallas kernels, attn_bwd(): pl.pallas_call(functools.partial(bwd_kernel, first), out_shape=(jax.Shape...  42.8 us
    pallas_call x1, Pallas kernels, ffn(): pl.pallas_call(functools.partial(ffn_kernel, count), out_shape=(jax.Shape...  33.8 us
    ppermute x18, starting transfers between devices, hop(): return lax.ppermute(value, 'dp', [(i, i ^ bit) for i in range(count)])  33.4 us
    pallas_call x2, Pallas kernels, attn_fwd(): pl.pallas_call(functools.partial(fwd_kernel, first), out_shape=(jax.Shape...  26.3 us
    ppermute x18, waiting for transfers between devices, hop(): return lax.ppermute(value, 'dp', [(i, i ^ bit) for i in range(count)])  24.4 us
    unnamed x86, local copies, waits for them, and re-layouts  18.4 us
    ppermute x22, starting transfers between devices, exchange(): return lax.ppermute(value, 'tensor', [(i, i ^ bit) for i in range(4)])  13.1 us
    ppermute x22, waiting for transfers between devices, exchange(): return lax.ppermute(value, 'tensor', [(i, i ^ bit) for i in range(4)])  12.4 us
  transfers between devices with their start and end apart: 42, of which 10 were waited for; matrix products, arithmetic and copies ran while one was open for 15% of the time, Pallas kernels for 32%

profile of v4, /device:TPU:0, one launch (start us, length us, event | category | flops | bytes accessed | tf_op | source)
XLA Modules:
  0.0 300.1 jit_solution(4486341190146026359)
XLA Ops:
  1.5 1.0 pad_maximum_fusion.5
  2.5 3.1 %collective-permute-start.6 = (bf16[96,768]{1,0:T(8,128)(2,1)S(1)}, bf16[96,768]{1,0:T(8,128)(2,1)S(1)}, u32[]{:S(2)}, u32[]{:S(2)}) collective-permute-start(bf16[96,768]{1,0:T(8,128)(2,1)S(1)} %pad_maximum_fusion.5), channel_id=1, source_target_pairs={{0,8},{4,12},{8,0},{12,4},{16,24},{20,28},{24,16},{28,20},{1,9},{5... | collective-permute-start | bytes 442376 | tf_op jit(solution)/shard_map/ppermute | solution.py:573
  5.6 2.6 collective-permute-start.7
  8.2 1.7 collective-permute-start.4
  12.1 5.0 %all-to-all-start = ((f32[32,8,128]{2,1,0:T(8,128)}), f32[32,8,128]{2,1,0:T(8,128)S(1)}, u32[]{:S(2)}, u32[]{:S(2)}) async-start(f32[32,8,128]{2,1,0:T(8,128)} %broadcast_in_dim.46), calls=%async_computation | async-start | bytes 262144 | tf_op jit(solution)/shard_map/all_to_all | solution.py:702
  17.2 1.0 pad_maximum_fusion.4
  18.3 1.8 collective-permute-start
  20.1 2.4 collective-permute-start.1
  22.7 1.8 pad_maximum_fusion.3.wa_ref
  24.5 5.0 %all-to-all-done = f32[32,8,128]{2,1,0:T(8,128)S(1)} async-done(((f32[32,8,128]{2,1,0:T(8,128)}), f32[32,8,128]{2,1,0:T(8,128)S(1)}, u32[]{:S(2)}, u32[]{:S(2)}) %all-to-all-start) | async-done | bytes 131104 | tf_op jit(solution)/shard_map/all_to_all | solution.py:702
  32.5 2.4 collective-permute-done
  35.0 1.6 collective-permute-start.9
  38.6 1.4 copy.111
  40.5 3.1 %collective-permute-done.1 = bf16[96,1536]{1,0:T(8,128)(2,1)S(1)} collective-permute-done((bf16[96,1536]{1,0:T(8,128)(2,1)S(1)}, bf16[96,1536]{1,0:T(8,128)(2,1)S(1)}, u32[]{:S(2)}, u32[]{:S(2)}) %collective-permute-start.1) | collective-permute-done | bytes 294944 | tf_op jit(solution)/shard_map/ppermute | solution.py:573
  43.5 1.0 pad_maximum_fusion.refs_1_.refs_0_
  44.6 1.5 collective-permute-start.12
  46.2 1.5 collective-permute-start.13
  47.6 3.9 %collective-permute-done.9.wb_ref = bf16[384,768]{1,0:T(8,128)(2,1)} collective-permute-done((bf16[384,768]{1,0:T(8,128)(2,1)}, bf16[384,768]{1,0:T(8,128)(2,1)}, u32[]{:S(2)}, u32[]{:S(2)}) %collective-permute-start.9) | collective-permute-done | bytes 589856 | tf_op jit(solution)/shard_map/ppermute | solution.py:573
  51.5 10.0 %projection.1 = (bf16[192,2048]{1,0:T(8,128)(2,1)}, bf16[192,2048]{1,0:T(8,128)(2,1)}, bf16[192,2048]{1,0:T(8,128)(2,1)}, bf16[2048,192]{1,0:T(8,128)(2,1)}, bf1...) custom-call(s32[1]{0:T(128)} %bitcast.home_ref, bf16[512,768]{1,0:T(8,128)(2,1)} %x0.3, ...), custom_call_target="tpu_custom_call" | custom-call | flops 9059696640 | bytes 6291456 | tf_op jit(solution)/shard_map/projection/pallas_call | solution.py:448
  61.6 13.1 %attention.2 = (bf16[192,1024]{1,0:T(8,128)(2,1)}, f32[8,1024]{1,0:T(8,128)}, bf16[512,768]{1,0:T(8,128)(2,1)}, bf16[512,768]{1,0:T(8,128)(2,1)}) custom-call(s32[4]{0:T(128)} %later.21.lo_ref, s32[4]{0:T(128)} %and_select_fusion.hi_ref, s32[1]{0:T(128)} %bitcast.5.flip_ref, bf16[192,2048]{1,0:T(8,128)(2,1)} %get-tuple-element.55.q_ref, ...), custom_call_target="tpu_custom_call" | custom-call | flops 20132659200 | bytes 1572864 | tf_op jit(solution)/shard_map/attention/pallas_call | solution.py:82
  75.3 1.1 slice.220
  76.4 1.6 collective-permute-start.17
  78.7 1.6 collective-permute-start.15
  80.2 13.1 %attention.3 = (bf16[192,1024]{1,0:T(8,128)(2,1)}, f32[8,1024]{1,0:T(8,128)}, bf16[512,768]{1,0:T(8,128)(2,1)}, bf16[512,768]{1,0:T(8,128)(2,1)}) custom-call(s32[4]{0:T(128)} %later.22.lo_ref, s32[4]{0:T(128)} %and_select_fusion.hi_ref, s32[1]{0:T(128)} %bitcast.5.flip_ref, bf16[192,2048]{1,0:T(8,128)(2,1)} %get-tuple-element.55.q_ref, ...), custom_call_target="tpu_custom_call" | custom-call | flops 20132659200 | bytes 1572864 | tf_op jit(solution)/shard_map/attention/pallas_call | solution.py:82
  93.4 4.8 %collective-permute-done.15.refs_0_ = bf16[512,768]{1,0:T(8,128)(2,1)S(1)} collective-permute-done((bf16[512,768]{1,0:T(8,128)(2,1)S(1)}, bf16[512,768]{1,0:T(8,128)(2,1)S(1)}, u32[]{:S(2)}, u32[]{:S(2)}) %collective-permute-start.15) | collective-permute-done | bytes 786464 | tf_op jit(solution)/shard_map/ppermute | solution.py:599
  99.6 1.0 slice.219
  100.6 1.6 collective-permute-start.16
  102.2 7.5 %collective-permute-done.16.refs_0_ = bf16[96,1536]{1,0:T(8,128)(2,1)S(1)} collective-permute-done((bf16[96,1536]{1,0:T(8,128)(2,1)S(1)}, bf16[96,1536]{1,0:T(8,128)(2,1)S(1)}, u32[]{:S(2)}, u32[]{:S(2)}) %collective-permute-start.16) | collective-permute-done | bytes 294944 | tf_op jit(solution)/shard_map/ppermute | solution.py:599
  113.6 33.8 %feed_forward.1 = (bf16[512,768]{1,0:T(8,128)(2,1)}, f32[512,768]{1,0:T(8,128)}, bf16[512,768]{1,0:T(8,128)(2,1)}, f32[6,8,768]{2,1,0:T(8,128)}, f32[4,8,768]{2,...) custom-call(s32[1]{0:T(128)} %bitcast.home_ref, ...), custom_call_target="tpu_custom_call" | custom-call | flops 36238786560 | bytes 18874368 | tf_op jit(solution)/shard_map/feed_forward/pallas_call | solution.py:379
  149.1 1.5 collective-permute-start.27
  150.6 0.9 reduce_sum.69
  154.1 1.0 copy-done.22
  155.1 1.7 add_convert_fusion.1.refs_2_
  156.8 1.0 collective-permute-start.29
  157.7 1.8 add_convert_fusion.6.refs_1_
  160.1 20.8 %attention_back.2 = (bf16[192,1024]{1,0:T(8,128)(2,1)}, f32[2048,192]{1,0:T(8,128)}, f32[2048,192]{1,0:T(8,128)}, f32[192,128]{1,0:T(8,128)}) custom-call(s32[4]{0:T(128)} %later.28.lo_ref, s32[4]{0:T(128)} %and_select_fusion.hi_ref, s32[1]{0:T(128)} %bitcast.5.flip_ref, bf16[192,2048]{1,0:T(8,128)(2,1)} %get-tuple-element.55.q_ref, ...), custom_call_target="tpu_custom_call" | custom-call | flops 24159191040 | bytes 3932160 | tf_op jit(solution)/shard_map/attention_back/pallas_call | solution.py:171
  183.5 3.1 %convert_add_fusion.1 = (f32[384,1536]{1,0:T(8,128)S(1)}, f32[384,1536]{1,0:T(8,128)S(1)}) fusion(bf16[1152,1536]{1,0:T(8,128)(2,1)} %collective-permute-done.24, bf16[1152,1536]{1,0:T(8,128)(2,1)} %get-tuple-element.73), kind=kLoop, calls=%fused_computation.5 | loop fusion | flops 3538944 | bytes 9437184 | tf_op jit(solution)/shard_map/add | solution.py:636
  188.0 1.2 pad_maximum_fusion.1
  189.2 1.1 collective-permute-start.26
  190.8 1.5 collective-permute-start.30
  192.3 22.0 %attention_back.3 = (bf16[192,1024]{1,0:T(8,128)(2,1)}, bf16[2048,192]{1,0:T(8,128)(2,1)}, bf16[2048,192]{1,0:T(8,128)(2,1)}, f32[192,128]{1,0:T(8,128)}, f32[8,192]{1,0:T(8,128)}) custom-call(s32[4]{0:T(128)} %later.32.lo_ref, s32[4]{0:T(128)} %and_select_fusion.hi_ref, s32[1]{0:T(128)} %bitcast.5.flip_ref, bf16[192,2048]{1,0:T(8,128)(2,1)} %get-tuple-element.55.q_ref, ...), custom_call_target="tpu_custom_call" | custom-call | flops 24159191040 | bytes 3932160 | tf_op jit(solution)/shard_map/attention_back/pallas_call | solution.py:171
  214.3 1.5 add.126.refs_0_
  215.9 9.8 %projection_grads.1 = (bf16[384,768]{1,0:T(8,128)(2,1)}, bf16[384,768]{1,0:T(8,128)(2,1)}) custom-call(s32[1]{0:T(128)} %bitcast.home_ref, bf16[512,768]{1,0:T(8,128)(2,1)} %x0.3, bf16[512,768]{1,0:T(8,128)(2,1)} %collective-permute-done.3.x1, bf16[512,768]{1,0:T(8,128)(2,1)} %copy-done.25, bf16[512,768]{1,0:T(8,128)(2,1)} %collective-permute-done.5.x3, ...), custom_call_target="tpu_custom_call" | custom-call | flops 603979776 | bytes 9437184 | tf_op jit(solution)/shard_map/projection_grads/pallas_call | solution.py:526
  225.6 1.2 collective-permute-start.33
  226.9 1.0 copy-done.8
  227.9 1.3 copy-done.9
  229.2 2.6 add_convert_fusion
  232.8 4.4 %collective-permute-start.35 = (bf16[96,1536]{1,0:T(8,128)(2,1)S(1)}, bf16[96,1536]{1,0:T(8,128)(2,1)S(1)}, u32[]{:S(2)}, u32[]{:S(2)}) collective-permute-start(bf16[96,1536]{1,0:T(8,128)(2,1)S(1)} %get-tuple-element.185), channel_id=1, source_target_pairs={{0,16},{4,20},{8,24},{12,28},{16,0},{20,4},{24,8},{28,12},{1,17},{... | collective-permute-start | bytes 884744 | tf_op jit(solution)/shard_map/ppermute | solution.py:573
  237.1 1.5 collective-permute-start.36
  238.6 6.7 %projection_back.1 = (bf16[512,768]{1,0:T(8,128)(2,1)}, bf16[1024,768]{1,0:T(8,128)(2,1)}, bf16[512,768]{1,0:T(8,128)(2,1)}) custom-call(bf16[192,1024]{1,0:T(8,128)(2,1)} %later.35.qa_ref, bf16[192,1024]{1,0:T(8,128)(2,1)} %get-tuple-element.80.qb_ref, bf16[2048,192]{1,0:T(8,128)(2,1)} %get-tuple-element.81.k_ref, ...), custom_call_target="tpu_custom_call" | custom-call | flops 21139292160 | bytes 12582912 | tf_op jit(solution)/shard_map/projection_back/pallas_call | solution.py:559
  245.3 2.6 collective-permute-done.34.refs_0_
  249.4 8.8 %collective-permute-done.36.refs_0_ = bf16[96,1536]{1,0:T(8,128)(2,1)S(1)} collective-permute-done((bf16[96,1536]{1,0:T(8,128)(2,1)S(1)}, bf16[96,1536]{1,0:T(8,128)(2,1)S(1)}, u32[]{:S(2)}, u32[]{:S(2)}) %collective-permute-start.36) | collective-permute-done | bytes 294944 | tf_op jit(solution)/shard_map/ppermute | solution.py:573
  258.9 2.0 add_add_fusion.refs_1_
  261.8 1.0 reduce_sum.67
  263.1 1.3 add_convert_fusion.5
  265.2 6.1 %collective-permute-start.37 = (bf16[96,768]{1,0:T(8,128)(2,1)}, bf16[96,768]{1,0:T(8,128)(2,1)S(1)}, u32[]{:S(2)}, u32[]{:S(2)}) collective-permute-start(bf16[96,768]{1,0:T(8,128)(2,1)} %get-tuple-element.188), channel_id=1, source_target_pairs={{0,8},{4,12},{8,0},{12,4},{16,24},{20,28},{24,16},{28,20},{1,9},{5... | collective-permute-start | bytes 442376 | tf_op jit(solution)/shard_map/ppermute | solution.py:573
  271.3 1.9 collective-permute-start.38
  273.2 1.5 collective-permute-start.39
  275.6 1.1 add_convert_fusion.3
  277.9 3.6 %all-to-all-start.1 = ((f32[32,8,128]{2,1,0:T(8,128)}), f32[32,8,128]{2,1,0:T(8,128)S(1)}, u32[]{:S(2)}, u32[]{:S(2)}) async-start(f32[32,8,128]{2,1,0:T(8,128)} %bitcast.33), calls=%async_computation.1 | async-start | bytes 262144 | tf_op jit(solution)/shard_map/all_to_all | solution.py:778
  281.6 3.6 %collective-permute-done.38 = bf16[96,768]{1,0:T(8,128)(2,1)S(1)} collective-permute-done((bf16[96,768]{1,0:T(8,128)(2,1)}, bf16[96,768]{1,0:T(8,128)(2,1)S(1)}, u32[]{:S(2)}, u32[]{:S(2)}) %collective-permute-start.38) | collective-permute-done | bytes 147488 | tf_op jit(solution)/shard_map/ppermute | solution.py:573
  285.2 1.0 add_add_fusion.1
  287.7 8.4 %all-to-all-done.1 = f32[32,8,128]{2,1,0:T(8,128)S(1)} async-done(((f32[32,8,128]{2,1,0:T(8,128)}), f32[32,8,128]{2,1,0:T(8,128)S(1)}, u32[]{:S(2)}, u32[]{:S(2)}) %all-to-all-start.1) | async-done | bytes 131104 | tf_op jit(solution)/shard_map/all_to_all | solution.py:778
  297.3 2.8 add_convert_fusion.2
  (217 shorter events, 34.7 us)
Async XLA Ops:
  2.5 15.7 %collective-permute-start.6 = (bf16[96,768]{1,0:T(8,128)(2,1)S(1)}, bf16[96,768]{1,0:T(8,128)(2,1)S(1)}, u32[]{:S(2)}, u32[]{:S(2)}) collective-permute-start(bf16[96,768]{1,0:T(8,128)(2,1)S(1)} %pad_maximum_fusion.5), channel_id=1, source_target_pairs={{0,8},{4,12},{8,0},{12,4},{16,24},{20,28},{24,16},{28,20},{1,9},{5... | collective-permute-start | bytes 442376 | tf_op jit(solution)/shard_map/ppermute | solution.py:573
  5.6 14.5 %collective-permute-start.7 = (bf16[96,768]{1,0:T(8,128)(2,1)S(1)}, bf16[96,768]{1,0:T(8,128)(2,1)S(1)}, u32[]{:S(2)}, u32[]{:S(2)}) collective-permute-start(bf16[96,768]{1,0:T(8,128)(2,1)S(1)} %pad_maximum_fusion.5), channel_id=1, source_target_pairs={{0,16},{4,20},{8,24},{12,28},{16,0},{20,4},{24,8},{28,12},{1,17},{... | collective-permute-start | bytes 442376 | tf_op jit(solution)/shard_map/ppermute | solution.py:573
  8.2 14.3 %collective-permute-start.8 = (bf16[96,768]{1,0:T(8,128)(2,1)S(1)}, bf16[96,768]{1,0:T(8,128)(2,1)S(1)}, u32[]{:S(2)}, u32[]{:S(2)}) collective-permute-start(bf16[96,768]{1,0:T(8,128)(2,1)S(1)} %pad_maximum_fusion.5), channel_id=1, source_target_pairs={{0,24},{4,28},{8,16},{12,20},{16,8},{20,12},{24,0},{28,4},{1,25},{... | collective-permute-start | bytes 442376 | tf_op jit(solution)/shard_map/ppermute | solution.py:573
  8.2 22.5 %collective-permute-start.4 = (bf16[512,768]{1,0:T(8,128)(2,1)}, bf16[512,768]{1,0:T(8,128)(2,1)S(1)}, u32[]{:S(2)}, u32[]{:S(2)}) collective-permute-start(bf16[512,768]{1,0:T(8,128)(2,1)} %x0.3), channel_id=1, source_target_pairs={{0,2},{1,3},{2,0},{3,1},{4,6},{5,7},{6,4},{7,5},{8,10},{9,11},{10,... | collective-permute-start | bytes 2359304 | tf_op jit(solution)/shard_map/ppermute | solution.py:599
  9.9 41.6 %collective-permute-start.3 = (bf16[512,768]{1,0:T(8,128)(2,1)}, bf16[512,768]{1,0:T(8,128)(2,1)}, u32[]{:S(2)}, u32[]{:S(2)}) collective-permute-start(bf16[512,768]{1,0:T(8,128)(2,1)} %x0.3), channel_id=1, source_target_pairs={{0,1},{1,0},{2,3},{3,2},{4,5},{5,4},{6,7},{7,6},{8,9},{9,8},{10,11... | collective-permute-start | bytes 2359304 | tf_op jit(solution)/shard_map/ppermute | solution.py:599
  12.1 17.4 %all-to-all-start = ((f32[32,8,128]{2,1,0:T(8,128)}), f32[32,8,128]{2,1,0:T(8,128)S(1)}, u32[]{:S(2)}, u32[]{:S(2)}) async-start(f32[32,8,128]{2,1,0:T(8,128)} %broadcast_in_dim.46), calls=%async_computation | async-start | bytes 262144 | tf_op jit(solution)/shard_map/all_to_all | solution.py:702
  18.2 25.3 %copy-start.28 = (bf16[768,96]{0,1:T(8,128)(2,1)S(1)}, bf16[768,96]{0,1:T(8,128)(2,1)}, u32[]{:S(2)}) copy-start(bf16[768,96]{0,1:T(8,128)(2,1)} %param.33) | copy-start | bytes 442372
  18.2 25.3 %copy-start.29 = (bf16[96,768]{1,0:T(8,128)(2,1)S(1)}, bf16[96,768]{1,0:T(8,128)(2,1)}, u32[]{:S(2)}) copy-start(bf16[96,768]{1,0:T(8,128)(2,1)} %param.31) | copy-start | bytes 442372
  18.3 16.7 %collective-permute-start = (bf16[96,1536]{1,0:T(8,128)(2,1)S(1)}, bf16[96,1536]{1,0:T(8,128)(2,1)S(1)}, u32[]{:S(2)}, u32[]{:S(2)}) collective-permute-start(bf16[96,1536]{1,0:T(8,128)(2,1)S(1)} %pad_maximum_fusion.4), channel_id=1, source_target_pairs={{0,8},{4,12},{8,0},{12,4},{16,24},{20,28},{24,16},{28,20},{1,9},{5... | collective-permute-start | bytes 884744 | tf_op jit(solution)/shard_map/ppermute | solution.py:573
  20.1 23.4 %collective-permute-start.1 = (bf16[96,1536]{1,0:T(8,128)(2,1)S(1)}, bf16[96,1536]{1,0:T(8,128)(2,1)S(1)}, u32[]{:S(2)}, u32[]{:S(2)}) collective-permute-start(bf16[96,1536]{1,0:T(8,128)(2,1)S(1)} %pad_maximum_fusion.4), channel_id=1, source_target_pairs={{0,16},{4,20},{8,24},{12,28},{16,0},{20,4},{24,8},{28,12},{1,17},{... | collective-permute-start | bytes 884744 | tf_op jit(solution)/shard_map/ppermute | solution.py:573
  22.5 21.0 %collective-permute-start.2 = (bf16[96,1536]{1,0:T(8,128)(2,1)S(1)}, bf16[96,1536]{1,0:T(8,128)(2,1)}, u32[]{:S(2)}, u32[]{:S(2)}) collective-permute-start(bf16[96,1536]{1,0:T(8,128)(2,1)S(1)} %pad_maximum_fusion.4), channel_id=1, source_target_pairs={{0,24},{4,28},{8,16},{12,20},{16,8},{20,12},{24,0},{28,4},{1,25},{... | collective-permute-start | bytes 884744 | tf_op jit(solution)/shard_map/ppermute | solution.py:573
  30.7 13.9 %copy-start.25 = (bf16[512,768]{1,0:T(8,128)(2,1)}, bf16[512,768]{1,0:T(8,128)(2,1)S(1)}, u32[]{:S(2)}) copy-start(bf16[512,768]{1,0:T(8,128)(2,1)S(1)} %collective-permute-done.4.x2) | copy-start | bytes 2359300
  30.7 20.8 %collective-permute-start.5 = (bf16[512,768]{1,0:T(8,128)(2,1)S(1)}, bf16[512,768]{1,0:T(8,128)(2,1)}, u32[]{:S(2)}, u32[]{:S(2)}) collective-permute-start(bf16[512,768]{1,0:T(8,128)(2,1)S(1)} %collective-permute-done.4.x2), channel_id=1, source_target_pairs={{0,1},{1,0},{2,3},{3,2},{4,5},{5,4},{6,7},{7,6},{8,9},{9,8},{10,11... | collective-permute-start | bytes 2359304 | tf_op jit(solution)/shard_map/ppermute | solution.py:599
  30.8 13.8 %copy-start.35 = (s32[4]{0:T(128)}, s32[4]{0:T(128)S(1)}, u32[]{:S(2)}) copy-start(s32[4]{0:T(128)S(1)} %and_select_fusion.1.refs_0_) | copy-start | bytes 52
  35.0 16.6 %collective-permute-start.9 = (bf16[384,768]{1,0:T(8,128)(2,1)}, bf16[384,768]{1,0:T(8,128)(2,1)}, u32[]{:S(2)}, u32[]{:S(2)}) collective-permute-start(bf16[384,768]{1,0:T(8,128)(2,1)} %pad_maximum_fusion.3.wa_ref), channel_id=1, source_target_pairs={{0,4},{4,0},{8,12},{12,8},{16,20},{20,16},{24,28},{28,24},{1,5},{5... | collective-permute-start | bytes 1769480 | tf_op jit(solution)/shard_map/ppermute | solution.py:573
  36.8 7.8 %copy-start.33 = (f32[192]{0:T(256)}, f32[192]{0:T(256)S(1)}, u32[]{:S(2)}) copy-start(f32[192]{0:T(256)S(1)} %dynamic_slice.11) | copy-start | bytes 2308
  38.5 6.1 %copy-start.32 = (s32[1,1,4,512]{3,1,2,0:T(1,128)}, s32[1,1,4,512]{3,1,2,0:T(1,128)S(1)}, u32[]{:S(2)}) copy-start(s32[1,1,4,512]{3,1,2,0:T(1,128)S(1)} %copy.110) | copy-start | bytes 24580
  44.6 3.0 copy-start.5
  44.6 33.3 %collective-permute-start.12 = (bf16[384,1536]{1,0:T(8,128)(2,1)S(1)}, bf16[384,1536]{1,0:T(8,128)(2,1)}, u32[]{:S(2)}, u32[]{:S(2)}) collective-permute-start(bf16[384,1536]{1,0:T(8,128)(2,1)S(1)} %pad_maximum_fusion.refs_1_.refs_0_), channel_id=1, source_target_pairs={{0,4},{4,0},{8,12},{12,8},{16,20},{20,16},{24,28},{28,24},{1,5},{5... | collective-permute-start | bytes 3538952 | tf_op jit(solution)/shard_map/ppermute | solution.py:573
  46.2 29.1 %collective-permute-start.13 = (bf16[384,1536]{1,0:T(8,128)(2,1)S(1)}, bf16[384,1536]{1,0:T(8,128)(2,1)S(1)}, u32[]{:S(2)}, u32[]{:S(2)}) collective-permute-start(bf16[384,1536]{1,0:T(8,128)(2,1)S(1)} %pad_maximum_fusion.refs_1_.refs_0_), channel_id=1, source_target_pairs={{0,2},{1,3},{2,0},{3,1},{4,6},{5,7},{6,4},{7,5},{8,10},{9,11},{10,... | collective-permute-start | bytes 3538952 | tf_op jit(solution)/shard_map/ppermute | solution.py:599
  51.5 28.7 %collective-permute-start.11 = (bf16[384,1536]{1,0:T(8,128)(2,1)}, bf16[384,1536]{1,0:T(8,128)(2,1)}, u32[]{:S(2)}, u32[]{:S(2)}) collective-permute-start(bf16[384,1536]{1,0:T(8,128)(2,1)} %copy-done.5), channel_id=1, source_target_pairs={{0,1},{1,0},{2,3},{3,2},{4,5},{5,4},{6,7},{7,6},{8,9},{9,8},{10,11... | collective-permute-start | bytes 3538952 | tf_op jit(solution)/shard_map/ppermute | solution.py:599
  74.7 3.7 %copy-start.27 = (bf16[512,768]{1,0:T(8,128)(2,1)S(1)}, bf16[512,768]{1,0:T(8,128)(2,1)}, u32[]{:S(2)}) copy-start(bf16[512,768]{1,0:T(8,128)(2,1)} %get-tuple-element.59) | copy-start | bytes 2359300
  74.7 3.7 %collective-permute-start.10 = (bf16[512,768]{1,0:T(8,128)(2,1)}, bf16[512,768]{1,0:T(8,128)(2,1)S(1)}, u32[]{:S(2)}, u32[]{:S(2)}) collective-permute-start(bf16[512,768]{1,0:T(8,128)(2,1)} %get-tuple-element.60), channel_id=1, source_target_pairs={{0,1},{1,0},{2,3},{3,2},{4,5},{5,4},{6,7},{7,6},{8,9},{9,8},{10,11... | collective-permute-start | bytes 2359304 | tf_op jit(solution)/shard_map/ppermute | solution.py:599
  75.3 3.4 %copy-start.10 = (bf16[384,1536]{1,0:T(8,128)(2,1)}, bf16[384,1536]{1,0:T(8,128)(2,1)S(1)}, u32[]{:S(2)}) copy-start(bf16[384,1536]{1,0:T(8,128)(2,1)S(1)} %collective-permute-done.13.refs_4_.refs_2_) | copy-start | bytes 3538948
  76.4 22.7 %collective-permute-start.17 = (bf16[288,1536]{1,0:T(8,128)(2,1)}, bf16[288,1536]{1,0:T(8,128)(2,1)}, u32[]{:S(2)}, u32[]{:S(2)}) collective-permute-start(bf16[288,1536]{1,0:T(8,128)(2,1)} %slice.220), channel_id=1, source_target_pairs={{0,4},{4,0},{8,12},{12,8},{16,20},{20,16},{24,28},{28,24},{1,5},{5... | collective-permute-start | bytes 2654216 | tf_op jit(solution)/shard_map/ppermute | solution.py:573
  77.9 34.6 %collective-permute-start.19 = (bf16[384,1536]{1,0:T(8,128)(2,1)S(1)}, bf16[384,1536]{1,0:T(8,128)(2,1)}, u32[]{:S(2)}, u32[]{:S(2)}) collective-permute-start(bf16[384,1536]{1,0:T(8,128)(2,1)S(1)} %collective-permute-done.13.refs_4_.refs_2_), channel_id=1, source_target_pairs={{0,1},{1,0},{2,3},{3,2},{4,5},{5,4},{6,7},{7,6},{8,9},{9,8},{10,11... | collective-permute-start | bytes 3538952 | tf_op jit(solution)/shard_map/ppermute | solution.py:599
  78.0 34.6 %collective-permute-start.18 = (bf16[384,1536]{1,0:T(8,128)(2,1)}, bf16[384,1536]{1,0:T(8,128)(2,1)}, u32[]{:S(2)}, u32[]{:S(2)}) collective-permute-start(bf16[384,1536]{1,0:T(8,128)(2,1)} %collective-permute-done.12.refs_3_.refs_1_), channel_id=1, source_target_pairs={{0,1},{1,0},{2,3},{3,2},{4,5},{5,4},{6,7},{7,6},{8,9},{9,8},{10,11... | collective-permute-start | bytes 3538952 | tf_op jit(solution)/shard_map/ppermute | solution.py:599
  78.7 1.6 copy-start.15
  78.7 19.5 %collective-permute-start.15 = (bf16[512,768]{1,0:T(8,128)(2,1)S(1)}, bf16[512,768]{1,0:T(8,128)(2,1)S(1)}, u32[]{:S(2)}, u32[]{:S(2)}) collective-permute-start(bf16[512,768]{1,0:T(8,128)(2,1)S(1)} %add_convert_fusion.4.refs_1_), channel_id=1, source_target_pairs={{0,2},{1,3},{2,0},{3,1},{4,6},{5,7},{6,4},{7,5},{8,10},{9,11},{10,... | collective-permute-start | bytes 2359304 | tf_op jit(solution)/shard_map/ppermute | solution.py:599
  99.1 13.5 %collective-permute-start.21 = (bf16[288,1536]{1,0:T(8,128)(2,1)}, bf16[288,1536]{1,0:T(8,128)(2,1)S(1)}, u32[]{:S(2)}, u32[]{:S(2)}) collective-permute-start(bf16[288,1536]{1,0:T(8,128)(2,1)} %later.25.refs_4_), channel_id=1, source_target_pairs={{0,1},{1,0},{2,3},{3,2},{4,5},{5,4},{6,7},{7,6},{8,9},{9,8},{10,11... | collective-permute-start | bytes 2654216 | tf_op jit(solution)/shard_map/ppermute | solution.py:599
  99.1 13.4 %collective-permute-start.14 = (bf16[512,768]{1,0:T(8,128)(2,1)}, bf16[512,768]{1,0:T(8,128)(2,1)}, u32[]{:S(2)}, u32[]{:S(2)}) collective-permute-start(bf16[512,768]{1,0:T(8,128)(2,1)} %get-tuple-element.62), channel_id=1, source_target_pairs={{0,1},{1,0},{2,3},{3,2},{4,5},{5,4},{6,7},{7,6},{8,9},{9,8},{10,11... | collective-permute-start | bytes 2359304 | tf_op jit(solution)/shard_map/ppermute | solution.py:599
  100.6 9.0 %collective-permute-start.16 = (bf16[96,1536]{1,0:T(8,128)(2,1)S(1)}, bf16[96,1536]{1,0:T(8,128)(2,1)S(1)}, u32[]{:S(2)}, u32[]{:S(2)}) collective-permute-start(bf16[96,1536]{1,0:T(8,128)(2,1)S(1)} %slice.219), channel_id=1, source_target_pairs={{0,2},{1,3},{2,0},{3,1},{4,6},{5,7},{6,4},{7,5},{8,10},{9,11},{10,... | collective-permute-start | bytes 884744 | tf_op jit(solution)/shard_map/ppermute | solution.py:599
  110.4 2.2 collective-permute-start.20
  147.4 6.8 %collective-permute-start.22 = (bf16[384,1536]{1,0:T(8,128)(2,1)}, bf16[384,1536]{1,0:T(8,128)(2,1)S(1)}, u32[]{:S(2)}, u32[]{:S(2)}) collective-permute-start(bf16[384,1536]{1,0:T(8,128)(2,1)} %get-tuple-element.67), channel_id=1, source_target_pairs={{0,1},{1,0},{2,3},{3,2},{4,5},{5,4},{6,7},{7,6},{8,9},{9,8},{10,11... | collective-permute-start | bytes 3538952 | tf_op jit(solution)/shard_map/ppermute | solution.py:599
  147.9 35.6 %collective-permute-start.24 = (bf16[1152,1536]{1,0:T(8,128)(2,1)}, bf16[1152,1536]{1,0:T(8,128)(2,1)}, u32[]{:S(2)}, u32[]{:S(2)}) collective-permute-start(bf16[1152,1536]{1,0:T(8,128)(2,1)} %get-tuple-element.74), channel_id=1, source_target_pairs={{0,1},{1,0},{2,3},{3,2},{4,5},{5,4},{6,7},{7,6},{8,9},{9,8},{10,11... | collective-permute-start | bytes 10616840 | tf_op jit(solution)/shard_map/ppermute | solution.py:599
  148.7 11.4 %collective-permute-start.23 = (bf16[512,768]{1,0:T(8,128)(2,1)}, bf16[512,768]{1,0:T(8,128)(2,1)}, u32[]{:S(2)}, u32[]{:S(2)}) collective-permute-start(bf16[512,768]{1,0:T(8,128)(2,1)} %get-tuple-element.70.g0), channel_id=1, source_target_pairs={{0,1},{1,0},{2,3},{3,2},{4,5},{5,4},{6,7},{7,6},{8,9},{9,8},{10,11... | collective-permute-start | bytes 2359304 | tf_op jit(solution)/shard_map/ppermute | solution.py:599
  149.1 31.8 %collective-permute-start.27 = (bf16[512,768]{1,0:T(8,128)(2,1)}, bf16[512,768]{1,0:T(8,128)(2,1)S(1)}, u32[]{:S(2)}, u32[]{:S(2)}) collective-permute-start(bf16[512,768]{1,0:T(8,128)(2,1)} %get-tuple-element.70.g0), channel_id=1, source_target_pairs={{0,2},{1,3},{2,0},{3,1},{4,6},{5,7},{6,4},{7,5},{8,10},{9,11},{10,... | collective-permute-start | bytes 2359304 | tf_op jit(solution)/shard_map/ppermute | solution.py:599
  156.8 2.8 copy-start.13
  156.8 25.8 %collective-permute-start.29 = (bf16[288,1536]{1,0:T(8,128)(2,1)S(1)}, bf16[288,1536]{1,0:T(8,128)(2,1)S(1)}, u32[]{:S(2)}, u32[]{:S(2)}) collective-permute-start(bf16[288,1536]{1,0:T(8,128)(2,1)S(1)} %add_convert_fusion.1.refs_2_), channel_id=1, source_target_pairs={{0,4},{4,0},{8,12},{12,8},{16,20},{20,16},{24,28},{28,24},{1,5},{5... | collective-permute-start | bytes 2654216 | tf_op jit(solution)/shard_map/ppermute | solution.py:573
  159.6 22.3 %collective-permute-start.25 = (bf16[96,1536]{1,0:T(8,128)(2,1)}, bf16[96,1536]{1,0:T(8,128)(2,1)S(1)}, u32[]{:S(2)}, u32[]{:S(2)}) collective-permute-start(bf16[96,1536]{1,0:T(8,128)(2,1)} %add_convert_fusion.6.refs_1_), channel_id=1, source_target_pairs={{0,2},{1,3},{2,0},{3,1},{4,6},{5,7},{6,4},{7,5},{8,10},{9,11},{10,... | collective-permute-start | bytes 884744 | tf_op jit(solution)/shard_map/ppermute | solution.py:599
  181.8 10.5 %collective-permute-start.28 = (bf16[512,768]{1,0:T(8,128)(2,1)}, bf16[512,768]{1,0:T(8,128)(2,1)}, u32[]{:S(2)}, u32[]{:S(2)}) collective-permute-start(bf16[512,768]{1,0:T(8,128)(2,1)} %later.30.g0.g2), channel_id=1, source_target_pairs={{0,1},{1,0},{2,3},{3,2},{4,5},{5,4},{6,7},{7,6},{8,9},{9,8},{10,11... | collective-permute-start | bytes 2359304 | tf_op jit(solution)/shard_map/ppermute | solution.py:599
  183.5 3.2 %copy-start.12 = (bf16[288,1536]{1,0:T(8,128)(2,1)S(1)}, bf16[288,1536]{1,0:T(8,128)(2,1)}, u32[]{:S(2)}) copy-start(bf16[288,1536]{1,0:T(8,128)(2,1)} %later.31) | copy-start | bytes 2654212
  189.1 1.7 copy-start.6
  189.2 37.7 %collective-permute-start.26 = (bf16[384,1536]{1,0:T(8,128)(2,1)S(1)}, bf16[384,1536]{1,0:T(8,128)(2,1)S(1)}, u32[]{:S(2)}, u32[]{:S(2)}) collective-permute-start(bf16[384,1536]{1,0:T(8,128)(2,1)S(1)} %get-tuple-element.207.refs_1_), channel_id=1, source_target_pairs={{0,4},{4,0},{8,12},{12,8},{16,20},{20,16},{24,28},{28,24},{1,5},{5... | collective-permute-start | bytes 3538952 | tf_op jit(solution)/shard_map/ppermute | solution.py:573
  190.8 37.0 %collective-permute-start.30 = (bf16[384,1536]{1,0:T(8,128)(2,1)S(1)}, bf16[384,1536]{1,0:T(8,128)(2,1)}, u32[]{:S(2)}, u32[]{:S(2)}) collective-permute-start(bf16[384,1536]{1,0:T(8,128)(2,1)S(1)} %copy-done.6), channel_id=1, source_target_pairs={{0,2},{1,3},{2,0},{3,1},{4,6},{5,7},{6,4},{7,5},{8,10},{9,11},{10,... | collective-permute-start | bytes 3538952 | tf_op jit(solution)/shard_map/ppermute | solution.py:599
  192.3 22.0 %copy-start.16 = (f32[192,128]{1,0:T(8,128)S(1)}, f32[192,128]{1,0:T(8,128)}, u32[]{:S(2)}) copy-start(f32[192,128]{1,0:T(8,128)} %get-tuple-element.75.refs_1_) | copy-start | bytes 294916
  225.6 37.5 %collective-permute-start.33 = (bf16[384,768]{1,0:T(8,128)(2,1)}, bf16[384,768]{1,0:T(8,128)(2,1)}, u32[]{:S(2)}, u32[]{:S(2)}) collective-permute-start(bf16[384,768]{1,0:T(8,128)(2,1)} %get-tuple-element.87), channel_id=1, source_target_pairs={{0,4},{4,0},{8,12},{12,8},{16,20},{20,16},{24,28},{28,24},{1,5},{5... | collective-permute-start | bytes 1769480 | tf_op jit(solution)/shard_map/ppermute | solution.py:573
  232.8 15.2 %collective-permute-start.34 = (bf16[96,1536]{1,0:T(8,128)(2,1)S(1)}, bf16[96,1536]{1,0:T(8,128)(2,1)S(1)}, u32[]{:S(2)}, u32[]{:S(2)}) collective-permute-start(bf16[96,1536]{1,0:T(8,128)(2,1)S(1)} %get-tuple-element.183), channel_id=1, source_target_pairs={{0,8},{4,12},{8,0},{12,4},{16,24},{20,28},{24,16},{28,20},{1,9},{5... | collective-permute-start | bytes 884744 | tf_op jit(solution)/shard_map/ppermute | solution.py:573
  232.8 15.9 %collective-permute-start.35 = (bf16[96,1536]{1,0:T(8,128)(2,1)S(1)}, bf16[96,1536]{1,0:T(8,128)(2,1)S(1)}, u32[]{:S(2)}, u32[]{:S(2)}) collective-permute-start(bf16[96,1536]{1,0:T(8,128)(2,1)S(1)} %get-tuple-element.185), channel_id=1, source_target_pairs={{0,16},{4,20},{8,24},{12,28},{16,0},{20,4},{24,8},{28,12},{1,17},{... | collective-permute-start | bytes 884744 | tf_op jit(solution)/shard_map/ppermute | solution.py:573
  237.1 21.1 %collective-permute-start.36 = (bf16[96,1536]{1,0:T(8,128)(2,1)S(1)}, bf16[96,1536]{1,0:T(8,128)(2,1)S(1)}, u32[]{:S(2)}, u32[]{:S(2)}) collective-permute-start(bf16[96,1536]{1,0:T(8,128)(2,1)S(1)} %get-tuple-element.184), channel_id=1, source_target_pairs={{0,24},{4,28},{8,16},{12,20},{16,8},{20,12},{24,0},{28,4},{1,25},{... | collective-permute-start | bytes 884744 | tf_op jit(solution)/shard_map/ppermute | solution.py:573
  245.3 30.2 %collective-permute-start.31 = (bf16[1024,768]{1,0:T(8,128)(2,1)}, bf16[1024,768]{1,0:T(8,128)(2,1)S(1)}, u32[]{:S(2)}, u32[]{:S(2)}) collective-permute-start(bf16[1024,768]{1,0:T(8,128)(2,1)} %get-tuple-element.85), channel_id=1, source_target_pairs={{0,1},{1,0},{2,3},{3,2},{4,5},{5,4},{6,7},{7,6},{8,9},{9,8},{10,11... | collective-permute-start | bytes 4718600 | tf_op jit(solution)/shard_map/ppermute | solution.py:599
  248.7 10.2 %copy-start.21 = (bf16[96,1536]{1,0:T(8,128)(2,1)S(1)}, bf16[96,1536]{1,0:T(8,128)(2,1)}, u32[]{:S(2)}) copy-start(bf16[96,1536]{1,0:T(8,128)(2,1)} %later.36) | copy-start | bytes 884740
  249.4 9.5 %copy-start.19 = (bf16[96,1536]{1,0:T(8,128)(2,1)S(1)}, bf16[96,1536]{1,0:T(8,128)(2,1)}, u32[]{:S(2)}) copy-start(bf16[96,1536]{1,0:T(8,128)(2,1)} %later.37) | copy-start | bytes 884740
  258.9 4.0 %copy-start.34 = (f32[32]{0:T(128)S(1)}, f32[32]{0:T(128)}, u32[]{:S(2)}) copy-start(f32[32]{0:T(128)} %mul.62) | copy-start | bytes 388
  260.9 2.2 copy-start.4
  263.1 11.6 %copy-start = (f32[96,1536]{1,0:T(8,128)S(1)}, f32[96,1536]{1,0:T(8,128)}, u32[]{:S(2)}) copy-start(f32[96,1536]{1,0:T(8,128)} %add_add_fusion.refs_1_) | copy-start | bytes 1769476
  263.1 12.4 %copy-start.26 = (bf16[512,768]{1,0:T(8,128)(2,1)S(1)}, bf16[512,768]{1,0:T(8,128)(2,1)}, u32[]{:S(2)}) copy-start(bf16[512,768]{1,0:T(8,128)(2,1)} %get-tuple-element.86) | copy-start | bytes 2359300
  265.2 16.4 %collective-permute-start.37 = (bf16[96,768]{1,0:T(8,128)(2,1)}, bf16[96,768]{1,0:T(8,128)(2,1)S(1)}, u32[]{:S(2)}, u32[]{:S(2)}) collective-permute-start(bf16[96,768]{1,0:T(8,128)(2,1)} %get-tuple-element.188), channel_id=1, source_target_pairs={{0,8},{4,12},{8,0},{12,4},{16,24},{20,28},{24,16},{28,20},{1,9},{5... | collective-permute-start | bytes 442376 | tf_op jit(solution)/shard_map/ppermute | solution.py:573
  271.3 13.8 %collective-permute-start.38 = (bf16[96,768]{1,0:T(8,128)(2,1)}, bf16[96,768]{1,0:T(8,128)(2,1)S(1)}, u32[]{:S(2)}, u32[]{:S(2)}) collective-permute-start(bf16[96,768]{1,0:T(8,128)(2,1)} %get-tuple-element.190), channel_id=1, source_target_pairs={{0,16},{4,20},{8,24},{12,28},{16,0},{20,4},{24,8},{28,12},{1,17},{... | collective-permute-start | bytes 442376 | tf_op jit(solution)/shard_map/ppermute | solution.py:573
  273.2 4.0 %copy-start.31 = (f32[32,144]{1,0:T(8,128)S(1)}, f32[32,144]{1,0:T(8,128)}, u32[]{:S(2)}) copy-start(f32[32,144]{1,0:T(8,128)} %copy.106) | copy-start | bytes 55300
  273.2 11.9 %collective-permute-start.39 = (bf16[96,768]{1,0:T(8,128)(2,1)S(1)}, bf16[96,768]{1,0:T(8,128)(2,1)}, u32[]{:S(2)}, u32[]{:S(2)}) collective-permute-start(bf16[96,768]{1,0:T(8,128)(2,1)S(1)} %get-tuple-element.189), channel_id=1, source_target_pairs={{0,24},{4,28},{8,16},{12,20},{16,8},{20,12},{24,0},{28,4},{1,25},{... | collective-permute-start | bytes 442376 | tf_op jit(solution)/shard_map/ppermute | solution.py:573
  276.6 20.6 %copy-start.1 = (bf16[512,768]{1,0:T(8,128)(2,1)S(1)}, bf16[512,768]{1,0:T(8,128)(2,1)}, u32[]{:S(2)}) copy-start(bf16[512,768]{1,0:T(8,128)(2,1)} %get-tuple-element.84.refs_1_) | copy-start | bytes 2359300
  276.6 20.6 %collective-permute-start.32 = (bf16[512,768]{1,0:T(8,128)(2,1)}, bf16[512,768]{1,0:T(8,128)(2,1)}, u32[]{:S(2)}, u32[]{:S(2)}) collective-permute-start(bf16[512,768]{1,0:T(8,128)(2,1)} %add_convert_fusion.3), channel_id=1, source_target_pairs={{0,2},{1,3},{2,0},{3,1},{4,6},{5,7},{6,4},{7,5},{8,10},{9,11},{10,... | collective-permute-start | bytes 2359304 | tf_op jit(solution)/shard_map/ppermute | solution.py:599
  277.9 18.1 %all-to-all-start.1 = ((f32[32,8,128]{2,1,0:T(8,128)}), f32[32,8,128]{2,1,0:T(8,128)S(1)}, u32[]{:S(2)}, u32[]{:S(2)}) async-start(f32[32,8,128]{2,1,0:T(8,128)} %bitcast.33), calls=%async_computation.1 | async-start | bytes 262144 | tf_op jit(solution)/shard_map/all_to_all | solution.py:778
  (16 other events, 14.4 us)

commit v5 on v4

--- a/solution.py
+++ b/solution.py
@@ -192,7 +192,7 @@
 
 EPSILON=1e-12
 T=256
-RC=32
+RC=128
 
 def row_stats(values):
     centre=jnp.mean(values,axis=1,keepdims=True)
@@ -270,7 +270,7 @@
         hl[at,:]=h.astype(bf16)
         acc[at,:]=jnp.zeros((RC,width),f32)
         return 0
-    lax.fori_loop(0,rows//RC,first,0,unroll=4)
+    lax.fori_loop(0,rows//RC,first,0,unroll=2)
     def turn(src,dst):
         def go(i,_):
             at=pl.multiple_of(i*T,T)
@@ -316,7 +316,7 @@
         acc[at,:]=g
         return (sums[0]+fold(cot*z),sums[1]+fold(cot),sums[2]+fold(g))
     zero=jnp.zeros((8,width),f32)
-    sg,sh,sbg=lax.fori_loop(0,rows//RC,second,(zero,zero,zero),unroll=4)
+    sg,sh,sbg=lax.fori_loop(0,rows//RC,second,(zero,zero,zero),unroll=2)
     turn(sl,slT)
     def backward(r,_):
         slot=r%2
@@ -359,7 +359,7 @@
         gm_ref[at,:]=gm
         gml_ref[at,:]=gm.astype(bf16)
         return (sums[0]+fold(g*z),sums[1]+fold(g),sums[2]+fold(gm))
-    fg,fs,mbg=lax.fori_loop(0,rows//RC,last,(zero,zero,zero),unroll=4)
+    fg,fs,mbg=lax.fori_loop(0,rows//RC,last,(zero,zero,zero),unroll=2)
     for n,v in enumerate((mbg,fg,fs,sbg,sg,sh)):
         vg_ref[n]=v
     for k in range(max(0,blocks-2),blocks):
@@ -765,7 +765,7 @@
         wide_grad = total(mine[:, : 2 * units], exchange(mine[:, 2 * units :], 2))
         attn_grad = lax.all_to_all(attn_local[0], "dp", 0, 0, tiled=True)
         attn_grad = jnp.sum(attn_grad.reshape(dp, -1, model).astype(f32), axis=0)
-    q_sums = later(q_sums_a + q_sums_b, wide_grad)
+    q_sums = later(q_sums_a, wide_grad) + later(q_sums_b, wide_grad)
     v_sums = later(v_sums, wide_grad)
     mine = (jnp.arange(4) == part).astype(f32)[:, None]
     q_all = (mine * jnp.sum(q_sums, axis=1)[None]).reshape(1, model)

time: 301 us -> 295 us (0.980)
  Pallas kernels: 129 us -> 112 us
  starting transfers between devices: 55.2 us -> 66.9 us
    ppermute x18, starting transfers between devices: 33.4 us -> 45.1 us  [hop(): return lax.ppermute(value, 'dp', [(i, i ^ bit) for i in range(count)])]
    pallas_call x2, Pallas kernels: 42.8 us -> 33.8 us  [attn_bwd(): pl.pallas_call(functools.partial(bwd_kernel, first), out_shape=(jax.Shape...]
    pallas_call x2, Pallas kernels: 26.3 us -> 21 us  [attn_fwd(): pl.pallas_call(functools.partial(fwd_kernel, first), out_shape=(jax.Shape...]
    pallas_call x1, Pallas kernels: 33.8 us -> 30.7 us  [ffn(): pl.pallas_call(functools.partial(ffn_kernel, count), out_shape=(jax.Shape...]
    unnamed x86 -> x84, local copies, waits for them, and re-layouts: 18.4 us -> 17.9 us
  transfers between devices with their start and end apart: 42 -> 42, of which waited for: 10 -> 11; matrix products, arithmetic and copies ran while one was open for 15% -> 15% of each run, Pallas kernels for 32% -> 28%
where the time goes in v5:
time: 295 us
  Pallas kernels  112 us (38%)
  starting transfers between devices  66.9 us (23%)
  waiting for transfers between devices  53.1 us (18%)
  local copies, waits for them, and re-layouts  32 us (11%)
  other arithmetic  30 us (10%)
    ppermute x18, starting transfers between devices, hop(): return lax.ppermute(value, 'dp', [(i, i ^ bit) for i in range(count)])  45.1 us
    pallas_call x2, Pallas kernels, attn_bwd(): pl.pallas_call(functools.partial(bwd_kernel, first), out_shape=(jax.Shape...  33.8 us
    pallas_call x1, Pallas kernels, ffn(): pl.pallas_call(functools.partial(ffn_kernel, count), out_shape=(jax.Shape...  30.7 us
    ppermute x18, waiting for transfers between devices, hop(): return lax.ppermute(value, 'dp', [(i, i ^ bit) for i in range(count)])  24.4 us
    pallas_call x2, Pallas kernels, attn_fwd(): pl.pallas_call(functools.partial(fwd_kernel, first), out_shape=(jax.Shape...  21 us
    unnamed x84, local copies, waits for them, and re-layouts  17.9 us
    ppermute x22, waiting for transfers between devices, exchange(): return lax.ppermute(value, 'tensor', [(i, i ^ bit) for i in range(4)])  15.3 us
    ppermute x22, starting transfers between devices, exchange(): return lax.ppermute(value, 'tensor', [(i, i ^ bit) for i in range(4)])  13.1 us
  transfers between devices with their start and end apart: 42, of which 11 were waited for; matrix products, arithmetic and copies ran while one was open for 15% of the time, Pallas kernels for 28%

profile of v5, /device:TPU:0, one launch (start us, length us, event | category | flops | bytes accessed | tf_op | source)
XLA Modules:
  0.0 295.4 jit_solution(12418262215619998572)
XLA Ops:
  1.5 1.0 pad_maximum_fusion.5
  2.5 3.1 %collective-permute-start.6 = (bf16[96,768]{1,0:T(8,128)(2,1)S(1)}, bf16[96,768]{1,0:T(8,128)(2,1)S(1)}, u32[]{:S(2)}, u32[]{:S(2)}) collective-permute-start(bf16[96,768]{1,0:T(8,128)(2,1)S(1)} %pad_maximum_fusion.5), channel_id=1, source_target_pairs={{0,8},{4,12},{8,0},{12,4},{16,24},{20,28},{24,16},{28,20},{1,9},{5... | collective-permute-start | bytes 442376 | tf_op jit(solution)/shard_map/ppermute | solution.py:573
  5.6 2.6 collective-permute-start.7
  8.2 1.7 collective-permute-start.4
  12.1 5.0 %all-to-all-start = ((f32[32,8,128]{2,1,0:T(8,128)}), f32[32,8,128]{2,1,0:T(8,128)S(1)}, u32[]{:S(2)}, u32[]{:S(2)}) async-start(f32[32,8,128]{2,1,0:T(8,128)} %broadcast_in_dim.46), calls=%async_computation | async-start | bytes 262144 | tf_op jit(solution)/shard_map/all_to_all | solution.py:702
  17.2 1.0 pad_maximum_fusion.4
  18.3 1.8 collective-permute-start
  20.1 2.4 collective-permute-start.1
  22.7 1.8 pad_maximum_fusion.3.wa_ref
  24.5 5.0 %all-to-all-done = f32[32,8,128]{2,1,0:T(8,128)S(1)} async-done(((f32[32,8,128]{2,1,0:T(8,128)}), f32[32,8,128]{2,1,0:T(8,128)S(1)}, u32[]{:S(2)}, u32[]{:S(2)}) %all-to-all-start) | async-done | bytes 131104 | tf_op jit(solution)/shard_map/all_to_all | solution.py:702
  32.5 2.4 collective-permute-done
  35.0 1.6 collective-permute-start.9
  38.6 1.4 copy.112
  40.5 3.1 %collective-permute-done.1 = bf16[96,1536]{1,0:T(8,128)(2,1)S(1)} collective-permute-done((bf16[96,1536]{1,0:T(8,128)(2,1)S(1)}, bf16[96,1536]{1,0:T(8,128)(2,1)S(1)}, u32[]{:S(2)}, u32[]{:S(2)}) %collective-permute-start.1) | collective-permute-done | bytes 294944 | tf_op jit(solution)/shard_map/ppermute | solution.py:573
  43.5 1.0 pad_maximum_fusion.refs_1_.refs_0_
  44.6 1.5 collective-permute-start.12
  46.2 1.5 collective-permute-start.13
  47.6 3.9 %collective-permute-done.9.wb_ref = bf16[384,768]{1,0:T(8,128)(2,1)} collective-permute-done((bf16[384,768]{1,0:T(8,128)(2,1)}, bf16[384,768]{1,0:T(8,128)(2,1)}, u32[]{:S(2)}, u32[]{:S(2)}) %collective-permute-start.9) | collective-permute-done | bytes 589856 | tf_op jit(solution)/shard_map/ppermute | solution.py:573
  51.5 10.0 %projection.1 = (bf16[192,2048]{1,0:T(8,128)(2,1)}, bf16[192,2048]{1,0:T(8,128)(2,1)}, bf16[192,2048]{1,0:T(8,128)(2,1)}, bf16[2048,192]{1,0:T(8,128)(2,1)}, bf1...) custom-call(s32[1]{0:T(128)} %bitcast.home_ref, bf16[512,768]{1,0:T(8,128)(2,1)} %x0.3, ...), custom_call_target="tpu_custom_call" | custom-call | flops 9059696640 | bytes 6291456 | tf_op jit(solution)/shard_map/projection/pallas_call | solution.py:448
  61.6 10.5 %attention.2 = (bf16[192,1024]{1,0:T(8,128)(2,1)}, f32[8,1024]{1,0:T(8,128)}, bf16[512,768]{1,0:T(8,128)(2,1)}, bf16[512,768]{1,0:T(8,128)(2,1)}) custom-call(s32[4]{0:T(128)} %later.22.lo_ref, s32[4]{0:T(128)} %and_select_fusion.hi_ref, s32[1]{0:T(128)} %bitcast.5.flip_ref, bf16[192,2048]{1,0:T(8,128)(2,1)} %get-tuple-element.55.q_ref, ...), custom_call_target="tpu_custom_call" | custom-call | flops 20132659200 | bytes 1572864 | tf_op jit(solution)/shard_map/attention/pallas_call | solution.py:82
  73.0 1.1 slice.220
  74.0 3.9 %collective-permute-start.17 = (bf16[288,1536]{1,0:T(8,128)(2,1)}, bf16[288,1536]{1,0:T(8,128)(2,1)}, u32[]{:S(2)}, u32[]{:S(2)}) collective-permute-start(bf16[288,1536]{1,0:T(8,128)(2,1)} %slice.220), channel_id=1, source_target_pairs={{0,4},{4,0},{8,12},{12,8},{16,20},{20,16},{24,28},{28,24},{1,5},{5... | collective-permute-start | bytes 2654216 | tf_op jit(solution)/shard_map/ppermute | solution.py:573
  78.7 1.6 collective-permute-start.15
  80.2 10.5 %attention.3 = (bf16[192,1024]{1,0:T(8,128)(2,1)}, f32[8,1024]{1,0:T(8,128)}, bf16[512,768]{1,0:T(8,128)(2,1)}, bf16[512,768]{1,0:T(8,128)(2,1)}) custom-call(s32[4]{0:T(128)} %later.23.lo_ref, s32[4]{0:T(128)} %and_select_fusion.hi_ref, s32[1]{0:T(128)} %bitcast.5.flip_ref, bf16[192,2048]{1,0:T(8,128)(2,1)} %get-tuple-element.55.q_ref, ...), custom_call_target="tpu_custom_call" | custom-call | flops 20132659200 | bytes 1572864 | tf_op jit(solution)/shard_map/attention/pallas_call | solution.py:82
  90.7 7.5 %collective-permute-done.15.refs_0_ = bf16[512,768]{1,0:T(8,128)(2,1)S(1)} collective-permute-done((bf16[512,768]{1,0:T(8,128)(2,1)S(1)}, bf16[512,768]{1,0:T(8,128)(2,1)S(1)}, u32[]{:S(2)}, u32[]{:S(2)}) %collective-permute-start.15) | collective-permute-done | bytes 786464 | tf_op jit(solution)/shard_map/ppermute | solution.py:599
  99.6 1.0 slice.219
  100.6 1.6 collective-permute-start.16
  102.2 7.5 %collective-permute-done.16.refs_0_ = bf16[96,1536]{1,0:T(8,128)(2,1)S(1)} collective-permute-done((bf16[96,1536]{1,0:T(8,128)(2,1)S(1)}, bf16[96,1536]{1,0:T(8,128)(2,1)S(1)}, u32[]{:S(2)}, u32[]{:S(2)}) %collective-permute-start.16) | collective-permute-done | bytes 294944 | tf_op jit(solution)/shard_map/ppermute | solution.py:599
  113.6 30.7 %feed_forward.1 = (bf16[512,768]{1,0:T(8,128)(2,1)}, f32[512,768]{1,0:T(8,128)}, bf16[512,768]{1,0:T(8,128)(2,1)}, f32[6,8,768]{2,1,0:T(8,128)}, f32[4,8,768]{2,...) custom-call(s32[1]{0:T(128)} %bitcast.home_ref, ...), custom_call_target="tpu_custom_call" | custom-call | flops 36238786560 | bytes 18874368 | tf_op jit(solution)/shard_map/feed_forward/pallas_call | solution.py:379
  146.0 1.5 collective-permute-start.27
  147.5 0.9 reduce_sum.69
  151.0 1.0 copy-done.21
  152.0 1.7 add_convert_fusion.1.refs_2_
  153.7 1.0 collective-permute-start.29
  154.7 1.8 add_convert_fusion.6.refs_1_
  157.0 16.4 %attention_back.2 = (bf16[192,1024]{1,0:T(8,128)(2,1)}, f32[2048,192]{1,0:T(8,128)}, f32[2048,192]{1,0:T(8,128)}, f32[192,128]{1,0:T(8,128)}) custom-call(s32[4]{0:T(128)} %later.29.lo_ref, s32[4]{0:T(128)} %and_select_fusion.hi_ref, s32[1]{0:T(128)} %bitcast.5.flip_ref, bf16[192,2048]{1,0:T(8,128)(2,1)} %get-tuple-element.55.q_ref, ...), custom_call_target="tpu_custom_call" | custom-call | flops 24159191040 | bytes 3932160 | tf_op jit(solution)/shard_map/attention_back/pallas_call | solution.py:171
  176.1 3.1 %convert_add_fusion.1 = (f32[384,1536]{1,0:T(8,128)S(1)}, f32[384,1536]{1,0:T(8,128)S(1)}) fusion(bf16[1152,1536]{1,0:T(8,128)(2,1)} %collective-permute-done.24, bf16[1152,1536]{1,0:T(8,128)(2,1)} %get-tuple-element.73), kind=kLoop, calls=%fused_computation.5 | loop fusion | flops 3538944 | bytes 9437184 | tf_op jit(solution)/shard_map/add | solution.py:636
  180.5 1.2 pad_maximum_fusion.1
  181.7 5.5 %collective-permute-start.26 = (bf16[384,1536]{1,0:T(8,128)(2,1)S(1)}, bf16[384,1536]{1,0:T(8,128)(2,1)S(1)}, u32[]{:S(2)}, u32[]{:S(2)}) collective-permute-start(bf16[384,1536]{1,0:T(8,128)(2,1)S(1)} %get-tuple-element.207.refs_1_), channel_id=1, source_target_pairs={{0,4},{4,0},{8,12},{12,8},{16,20},{20,16},{24,28},{28,24},{1,5},{5... | collective-permute-start | bytes 3538952 | tf_op jit(solution)/shard_map/ppermute | solution.py:573
  187.2 1.5 collective-permute-start.30
  188.7 17.4 %attention_back.3 = (bf16[192,1024]{1,0:T(8,128)(2,1)}, bf16[2048,192]{1,0:T(8,128)(2,1)}, bf16[2048,192]{1,0:T(8,128)(2,1)}, f32[192,128]{1,0:T(8,128)}, f32[8,192]{1,0:T(8,128)}) custom-call(s32[4]{0:T(128)} %later.33.lo_ref, s32[4]{0:T(128)} %and_select_fusion.hi_ref, s32[1]{0:T(128)} %bitcast.5.flip_ref, bf16[192,2048]{1,0:T(8,128)(2,1)} %get-tuple-element.55.q_ref, ...), custom_call_target="tpu_custom_call" | custom-call | flops 24159191040 | bytes 3932160 | tf_op jit(solution)/shard_map/attention_back/pallas_call | solution.py:171
  206.2 9.8 %projection_grads.1 = (bf16[384,768]{1,0:T(8,128)(2,1)}, bf16[384,768]{1,0:T(8,128)(2,1)}) custom-call(s32[1]{0:T(128)} %bitcast.home_ref, bf16[512,768]{1,0:T(8,128)(2,1)} %x0.3, bf16[512,768]{1,0:T(8,128)(2,1)} %collective-permute-done.3.x1, bf16[512,768]{1,0:T(8,128)(2,1)} %copy-done.24, bf16[512,768]{1,0:T(8,128)(2,1)} %collective-permute-done.5.x3, ...), custom_call_target="tpu_custom_call" | custom-call | flops 603979776 | bytes 9437184 | tf_op jit(solution)/shard_map/projection_grads/pallas_call | solution.py:526
  216.0 6.2 %collective-permute-start.33 = (bf16[384,768]{1,0:T(8,128)(2,1)}, bf16[384,768]{1,0:T(8,128)(2,1)}, u32[]{:S(2)}, u32[]{:S(2)}) collective-permute-start(bf16[384,768]{1,0:T(8,128)(2,1)} %get-tuple-element.87), channel_id=1, source_target_pairs={{0,4},{4,0},{8,12},{12,8},{16,20},{20,16},{24,28},{28,24},{1,5},{5... | collective-permute-start | bytes 1769480 | tf_op jit(solution)/shard_map/ppermute | solution.py:573
  222.2 1.0 copy-done.8
  223.2 1.3 copy-done.9
  224.4 2.6 add_convert_fusion
  227.1 1.0 copy-done.2
  228.0 4.4 %collective-permute-start.35 = (bf16[96,1536]{1,0:T(8,128)(2,1)S(1)}, bf16[96,1536]{1,0:T(8,128)(2,1)S(1)}, u32[]{:S(2)}, u32[]{:S(2)}) collective-permute-start(bf16[96,1536]{1,0:T(8,128)(2,1)S(1)} %get-tuple-element.185), channel_id=1, source_target_pairs={{0,16},{4,20},{8,24},{12,28},{16,0},{20,4},{24,8},{28,12},{1,17},{... | collective-permute-start | bytes 884744 | tf_op jit(solution)/shard_map/ppermute | solution.py:573
  232.4 1.5 collective-permute-start.36
  233.9 6.7 %projection_back.1 = (bf16[512,768]{1,0:T(8,128)(2,1)}, bf16[1024,768]{1,0:T(8,128)(2,1)}, bf16[512,768]{1,0:T(8,128)(2,1)}) custom-call(bf16[192,1024]{1,0:T(8,128)(2,1)} %later.36.qa_ref, bf16[192,1024]{1,0:T(8,128)(2,1)} %get-tuple-element.80.qb_ref, bf16[2048,192]{1,0:T(8,128)(2,1)} %get-tuple-element.81.k_ref, ...), custom_call_target="tpu_custom_call" | custom-call | flops 21139292160 | bytes 12582912 | tf_op jit(solution)/shard_map/projection_back/pallas_call | solution.py:559
  240.6 2.6 collective-permute-done.34.refs_0_
  244.7 8.8 %collective-permute-done.36.refs_0_ = bf16[96,1536]{1,0:T(8,128)(2,1)S(1)} collective-permute-done((bf16[96,1536]{1,0:T(8,128)(2,1)S(1)}, bf16[96,1536]{1,0:T(8,128)(2,1)S(1)}, u32[]{:S(2)}, u32[]{:S(2)}) %collective-permute-start.36) | collective-permute-done | bytes 294944 | tf_op jit(solution)/shard_map/ppermute | solution.py:573
  254.2 2.0 add_add_fusion.refs_1_
  257.0 1.1 add_reduce_fusion
  258.5 1.3 add_convert_fusion.5
  260.5 6.1 %collective-permute-start.37 = (bf16[96,768]{1,0:T(8,128)(2,1)}, bf16[96,768]{1,0:T(8,128)(2,1)S(1)}, u32[]{:S(2)}, u32[]{:S(2)}) collective-permute-start(bf16[96,768]{1,0:T(8,128)(2,1)} %get-tuple-element.188), channel_id=1, source_target_pairs={{0,8},{4,12},{8,0},{12,4},{16,24},{20,28},{24,16},{28,20},{1,9},{5... | collective-permute-start | bytes 442376 | tf_op jit(solution)/shard_map/ppermute | solution.py:573
  266.6 1.9 collective-permute-start.38
  268.5 1.5 collective-permute-start.39
  270.9 1.1 add_convert_fusion.3
  273.3 3.6 %all-to-all-start.1 = ((f32[32,8,128]{2,1,0:T(8,128)}), f32[32,8,128]{2,1,0:T(8,128)S(1)}, u32[]{:S(2)}, u32[]{:S(2)}) async-start(f32[32,8,128]{2,1,0:T(8,128)} %bitcast.33), calls=%async_computation.1 | async-start | bytes 262144 | tf_op jit(solution)/shard_map/all_to_all | solution.py:778
  276.9 3.5 %collective-permute-done.38 = bf16[96,768]{1,0:T(8,128)(2,1)S(1)} collective-permute-done((bf16[96,768]{1,0:T(8,128)(2,1)}, bf16[96,768]{1,0:T(8,128)(2,1)S(1)}, u32[]{:S(2)}, u32[]{:S(2)}) %collective-permute-start.38) | collective-permute-done | bytes 147488 | tf_op jit(solution)/shard_map/ppermute | solution.py:573
  280.4 1.0 add_add_fusion.1
  282.9 8.3 %all-to-all-done.1 = f32[32,8,128]{2,1,0:T(8,128)S(1)} async-done(((f32[32,8,128]{2,1,0:T(8,128)}), f32[32,8,128]{2,1,0:T(8,128)S(1)}, u32[]{:S(2)}, u32[]{:S(2)}) %all-to-all-start.1) | async-done | bytes 131104 | tf_op jit(solution)/shard_map/all_to_all | solution.py:778
  292.5 2.8 add_convert_fusion.2
  (215 shorter events, 33.6 us)
Async XLA Ops:
  2.5 15.7 %collective-permute-start.6 = (bf16[96,768]{1,0:T(8,128)(2,1)S(1)}, bf16[96,768]{1,0:T(8,128)(2,1)S(1)}, u32[]{:S(2)}, u32[]{:S(2)}) collective-permute-start(bf16[96,768]{1,0:T(8,128)(2,1)S(1)} %pad_maximum_fusion.5), channel_id=1, source_target_pairs={{0,8},{4,12},{8,0},{12,4},{16,24},{20,28},{24,16},{28,20},{1,9},{5... | collective-permute-start | bytes 442376 | tf_op jit(solution)/shard_map/ppermute | solution.py:573
  5.6 14.5 %collective-permute-start.7 = (bf16[96,768]{1,0:T(8,128)(2,1)S(1)}, bf16[96,768]{1,0:T(8,128)(2,1)S(1)}, u32[]{:S(2)}, u32[]{:S(2)}) collective-permute-start(bf16[96,768]{1,0:T(8,128)(2,1)S(1)} %pad_maximum_fusion.5), channel_id=1, source_target_pairs={{0,16},{4,20},{8,24},{12,28},{16,0},{20,4},{24,8},{28,12},{1,17},{... | collective-permute-start | bytes 442376 | tf_op jit(solution)/shard_map/ppermute | solution.py:573
  8.2 14.3 %collective-permute-start.8 = (bf16[96,768]{1,0:T(8,128)(2,1)S(1)}, bf16[96,768]{1,0:T(8,128)(2,1)S(1)}, u32[]{:S(2)}, u32[]{:S(2)}) collective-permute-start(bf16[96,768]{1,0:T(8,128)(2,1)S(1)} %pad_maximum_fusion.5), channel_id=1, source_target_pairs={{0,24},{4,28},{8,16},{12,20},{16,8},{20,12},{24,0},{28,4},{1,25},{... | collective-permute-start | bytes 442376 | tf_op jit(solution)/shard_map/ppermute | solution.py:573
  8.2 22.5 %collective-permute-start.4 = (bf16[512,768]{1,0:T(8,128)(2,1)}, bf16[512,768]{1,0:T(8,128)(2,1)S(1)}, u32[]{:S(2)}, u32[]{:S(2)}) collective-permute-start(bf16[512,768]{1,0:T(8,128)(2,1)} %x0.3), channel_id=1, source_target_pairs={{0,2},{1,3},{2,0},{3,1},{4,6},{5,7},{6,4},{7,5},{8,10},{9,11},{10,... | collective-permute-start | bytes 2359304 | tf_op jit(solution)/shard_map/ppermute | solution.py:599
  9.9 41.6 %collective-permute-start.3 = (bf16[512,768]{1,0:T(8,128)(2,1)}, bf16[512,768]{1,0:T(8,128)(2,1)}, u32[]{:S(2)}, u32[]{:S(2)}) collective-permute-start(bf16[512,768]{1,0:T(8,128)(2,1)} %x0.3), channel_id=1, source_target_pairs={{0,1},{1,0},{2,3},{3,2},{4,5},{5,4},{6,7},{7,6},{8,9},{9,8},{10,11... | collective-permute-start | bytes 2359304 | tf_op jit(solution)/shard_map/ppermute | solution.py:599
  12.1 17.4 %all-to-all-start = ((f32[32,8,128]{2,1,0:T(8,128)}), f32[32,8,128]{2,1,0:T(8,128)S(1)}, u32[]{:S(2)}, u32[]{:S(2)}) async-start(f32[32,8,128]{2,1,0:T(8,128)} %broadcast_in_dim.46), calls=%async_computation | async-start | bytes 262144 | tf_op jit(solution)/shard_map/all_to_all | solution.py:702
  18.2 25.3 %copy-start.27 = (bf16[768,96]{0,1:T(8,128)(2,1)S(1)}, bf16[768,96]{0,1:T(8,128)(2,1)}, u32[]{:S(2)}) copy-start(bf16[768,96]{0,1:T(8,128)(2,1)} %param.33) | copy-start | bytes 442372
  18.2 25.3 %copy-start.28 = (bf16[96,768]{1,0:T(8,128)(2,1)S(1)}, bf16[96,768]{1,0:T(8,128)(2,1)}, u32[]{:S(2)}) copy-start(bf16[96,768]{1,0:T(8,128)(2,1)} %param.31) | copy-start | bytes 442372
  18.3 16.7 %collective-permute-start = (bf16[96,1536]{1,0:T(8,128)(2,1)S(1)}, bf16[96,1536]{1,0:T(8,128)(2,1)S(1)}, u32[]{:S(2)}, u32[]{:S(2)}) collective-permute-start(bf16[96,1536]{1,0:T(8,128)(2,1)S(1)} %pad_maximum_fusion.4), channel_id=1, source_target_pairs={{0,8},{4,12},{8,0},{12,4},{16,24},{20,28},{24,16},{28,20},{1,9},{5... | collective-permute-start | bytes 884744 | tf_op jit(solution)/shard_map/ppermute | solution.py:573
  20.1 23.4 %collective-permute-start.1 = (bf16[96,1536]{1,0:T(8,128)(2,1)S(1)}, bf16[96,1536]{1,0:T(8,128)(2,1)S(1)}, u32[]{:S(2)}, u32[]{:S(2)}) collective-permute-start(bf16[96,1536]{1,0:T(8,128)(2,1)S(1)} %pad_maximum_fusion.4), channel_id=1, source_target_pairs={{0,16},{4,20},{8,24},{12,28},{16,0},{20,4},{24,8},{28,12},{1,17},{... | collective-permute-start | bytes 884744 | tf_op jit(solution)/shard_map/ppermute | solution.py:573
  22.5 21.0 %collective-permute-start.2 = (bf16[96,1536]{1,0:T(8,128)(2,1)S(1)}, bf16[96,1536]{1,0:T(8,128)(2,1)}, u32[]{:S(2)}, u32[]{:S(2)}) collective-permute-start(bf16[96,1536]{1,0:T(8,128)(2,1)S(1)} %pad_maximum_fusion.4), channel_id=1, source_target_pairs={{0,24},{4,28},{8,16},{12,20},{16,8},{20,12},{24,0},{28,4},{1,25},{... | collective-permute-start | bytes 884744 | tf_op jit(solution)/shard_map/ppermute | solution.py:573
  30.7 13.9 %copy-start.24 = (bf16[512,768]{1,0:T(8,128)(2,1)}, bf16[512,768]{1,0:T(8,128)(2,1)S(1)}, u32[]{:S(2)}) copy-start(bf16[512,768]{1,0:T(8,128)(2,1)S(1)} %collective-permute-done.4.x2) | copy-start | bytes 2359300
  30.7 20.8 %collective-permute-start.5 = (bf16[512,768]{1,0:T(8,128)(2,1)S(1)}, bf16[512,768]{1,0:T(8,128)(2,1)}, u32[]{:S(2)}, u32[]{:S(2)}) collective-permute-start(bf16[512,768]{1,0:T(8,128)(2,1)S(1)} %collective-permute-done.4.x2), channel_id=1, source_target_pairs={{0,1},{1,0},{2,3},{3,2},{4,5},{5,4},{6,7},{7,6},{8,9},{9,8},{10,11... | collective-permute-start | bytes 2359304 | tf_op jit(solution)/shard_map/ppermute | solution.py:599
  30.8 13.8 %copy-start.34 = (s32[4]{0:T(128)}, s32[4]{0:T(128)S(1)}, u32[]{:S(2)}) copy-start(s32[4]{0:T(128)S(1)} %and_select_fusion.1.refs_0_) | copy-start | bytes 52
  35.0 16.6 %collective-permute-start.9 = (bf16[384,768]{1,0:T(8,128)(2,1)}, bf16[384,768]{1,0:T(8,128)(2,1)}, u32[]{:S(2)}, u32[]{:S(2)}) collective-permute-start(bf16[384,768]{1,0:T(8,128)(2,1)} %pad_maximum_fusion.3.wa_ref), channel_id=1, source_target_pairs={{0,4},{4,0},{8,12},{12,8},{16,20},{20,16},{24,28},{28,24},{1,5},{5... | collective-permute-start | bytes 1769480 | tf_op jit(solution)/shard_map/ppermute | solution.py:573
  36.8 7.8 %copy-start.32 = (f32[192]{0:T(256)}, f32[192]{0:T(256)S(1)}, u32[]{:S(2)}) copy-start(f32[192]{0:T(256)S(1)} %dynamic_slice.11) | copy-start | bytes 2308
  38.5 6.1 %copy-start.31 = (s32[1,1,4,512]{3,1,2,0:T(1,128)}, s32[1,1,4,512]{3,1,2,0:T(1,128)S(1)}, u32[]{:S(2)}) copy-start(s32[1,1,4,512]{3,1,2,0:T(1,128)S(1)} %copy.111) | copy-start | bytes 24580
  44.6 3.0 %copy-start.5 = (bf16[384,1536]{1,0:T(8,128)(2,1)}, bf16[384,1536]{1,0:T(8,128)(2,1)S(1)}, u32[]{:S(2)}) copy-start(bf16[384,1536]{1,0:T(8,128)(2,1)S(1)} %pad_maximum_fusion.refs_1_.refs_0_) | copy-start | bytes 3538948
  44.6 33.3 %collective-permute-start.12 = (bf16[384,1536]{1,0:T(8,128)(2,1)S(1)}, bf16[384,1536]{1,0:T(8,128)(2,1)}, u32[]{:S(2)}, u32[]{:S(2)}) collective-permute-start(bf16[384,1536]{1,0:T(8,128)(2,1)S(1)} %pad_maximum_fusion.refs_1_.refs_0_), channel_id=1, source_target_pairs={{0,4},{4,0},{8,12},{12,8},{16,20},{20,16},{24,28},{28,24},{1,5},{5... | collective-permute-start | bytes 3538952 | tf_op jit(solution)/shard_map/ppermute | solution.py:573
  46.2 26.8 %collective-permute-start.13 = (bf16[384,1536]{1,0:T(8,128)(2,1)S(1)}, bf16[384,1536]{1,0:T(8,128)(2,1)S(1)}, u32[]{:S(2)}, u32[]{:S(2)}) collective-permute-start(bf16[384,1536]{1,0:T(8,128)(2,1)S(1)} %pad_maximum_fusion.refs_1_.refs_0_), channel_id=1, source_target_pairs={{0,2},{1,3},{2,0},{3,1},{4,6},{5,7},{6,4},{7,5},{8,10},{9,11},{10,... | collective-permute-start | bytes 3538952 | tf_op jit(solution)/shard_map/ppermute | solution.py:599
  51.5 28.7 %collective-permute-start.11 = (bf16[384,1536]{1,0:T(8,128)(2,1)}, bf16[384,1536]{1,0:T(8,128)(2,1)}, u32[]{:S(2)}, u32[]{:S(2)}) collective-permute-start(bf16[384,1536]{1,0:T(8,128)(2,1)} %copy-done.5), channel_id=1, source_target_pairs={{0,1},{1,0},{2,3},{3,2},{4,5},{5,4},{6,7},{7,6},{8,9},{9,8},{10,11... | collective-permute-start | bytes 3538952 | tf_op jit(solution)/shard_map/ppermute | solution.py:599
  72.1 6.4 %copy-start.26 = (bf16[512,768]{1,0:T(8,128)(2,1)S(1)}, bf16[512,768]{1,0:T(8,128)(2,1)}, u32[]{:S(2)}) copy-start(bf16[512,768]{1,0:T(8,128)(2,1)} %get-tuple-element.59) | copy-start | bytes 2359300
  72.1 6.4 %collective-permute-start.10 = (bf16[512,768]{1,0:T(8,128)(2,1)}, bf16[512,768]{1,0:T(8,128)(2,1)S(1)}, u32[]{:S(2)}, u32[]{:S(2)}) collective-permute-start(bf16[512,768]{1,0:T(8,128)(2,1)} %get-tuple-element.60), channel_id=1, source_target_pairs={{0,1},{1,0},{2,3},{3,2},{4,5},{5,4},{6,7},{7,6},{8,9},{9,8},{10,11... | collective-permute-start | bytes 2359304 | tf_op jit(solution)/shard_map/ppermute | solution.py:599
  73.0 5.7 %copy-start.10 = (bf16[384,1536]{1,0:T(8,128)(2,1)}, bf16[384,1536]{1,0:T(8,128)(2,1)S(1)}, u32[]{:S(2)}) copy-start(bf16[384,1536]{1,0:T(8,128)(2,1)S(1)} %collective-permute-done.13.refs_4_.refs_2_) | copy-start | bytes 3538948
  74.0 25.1 %collective-permute-start.17 = (bf16[288,1536]{1,0:T(8,128)(2,1)}, bf16[288,1536]{1,0:T(8,128)(2,1)}, u32[]{:S(2)}, u32[]{:S(2)}) collective-permute-start(bf16[288,1536]{1,0:T(8,128)(2,1)} %slice.220), channel_id=1, source_target_pairs={{0,4},{4,0},{8,12},{12,8},{16,20},{20,16},{24,28},{28,24},{1,5},{5... | collective-permute-start | bytes 2654216 | tf_op jit(solution)/shard_map/ppermute | solution.py:573
  78.0 34.6 %collective-permute-start.19 = (bf16[384,1536]{1,0:T(8,128)(2,1)S(1)}, bf16[384,1536]{1,0:T(8,128)(2,1)}, u32[]{:S(2)}, u32[]{:S(2)}) collective-permute-start(bf16[384,1536]{1,0:T(8,128)(2,1)S(1)} %collective-permute-done.13.refs_4_.refs_2_), channel_id=1, source_target_pairs={{0,1},{1,0},{2,3},{3,2},{4,5},{5,4},{6,7},{7,6},{8,9},{9,8},{10,11... | collective-permute-start | bytes 3538952 | tf_op jit(solution)/shard_map/ppermute | solution.py:599
  78.0 34.6 %collective-permute-start.18 = (bf16[384,1536]{1,0:T(8,128)(2,1)}, bf16[384,1536]{1,0:T(8,128)(2,1)}, u32[]{:S(2)}, u32[]{:S(2)}) collective-permute-start(bf16[384,1536]{1,0:T(8,128)(2,1)} %collective-permute-done.12.refs_3_.refs_1_), channel_id=1, source_target_pairs={{0,1},{1,0},{2,3},{3,2},{4,5},{5,4},{6,7},{7,6},{8,9},{9,8},{10,11... | collective-permute-start | bytes 3538952 | tf_op jit(solution)/shard_map/ppermute | solution.py:599
  78.7 1.6 copy-start.15
  78.7 19.5 %collective-permute-start.15 = (bf16[512,768]{1,0:T(8,128)(2,1)S(1)}, bf16[512,768]{1,0:T(8,128)(2,1)S(1)}, u32[]{:S(2)}, u32[]{:S(2)}) collective-permute-start(bf16[512,768]{1,0:T(8,128)(2,1)S(1)} %add_convert_fusion.4.refs_1_), channel_id=1, source_target_pairs={{0,2},{1,3},{2,0},{3,1},{4,6},{5,7},{6,4},{7,5},{8,10},{9,11},{10,... | collective-permute-start | bytes 2359304 | tf_op jit(solution)/shard_map/ppermute | solution.py:599
  99.1 13.5 %collective-permute-start.21 = (bf16[288,1536]{1,0:T(8,128)(2,1)}, bf16[288,1536]{1,0:T(8,128)(2,1)S(1)}, u32[]{:S(2)}, u32[]{:S(2)}) collective-permute-start(bf16[288,1536]{1,0:T(8,128)(2,1)} %later.26.refs_4_), channel_id=1, source_target_pairs={{0,1},{1,0},{2,3},{3,2},{4,5},{5,4},{6,7},{7,6},{8,9},{9,8},{10,11... | collective-permute-start | bytes 2654216 | tf_op jit(solution)/shard_map/ppermute | solution.py:599
  99.1 13.4 %collective-permute-start.14 = (bf16[512,768]{1,0:T(8,128)(2,1)}, bf16[512,768]{1,0:T(8,128)(2,1)}, u32[]{:S(2)}, u32[]{:S(2)}) collective-permute-start(bf16[512,768]{1,0:T(8,128)(2,1)} %get-tuple-element.62), channel_id=1, source_target_pairs={{0,1},{1,0},{2,3},{3,2},{4,5},{5,4},{6,7},{7,6},{8,9},{9,8},{10,11... | collective-permute-start | bytes 2359304 | tf_op jit(solution)/shard_map/ppermute | solution.py:599
  100.6 9.0 %collective-permute-start.16 = (bf16[96,1536]{1,0:T(8,128)(2,1)S(1)}, bf16[96,1536]{1,0:T(8,128)(2,1)S(1)}, u32[]{:S(2)}, u32[]{:S(2)}) collective-permute-start(bf16[96,1536]{1,0:T(8,128)(2,1)S(1)} %slice.219), channel_id=1, source_target_pairs={{0,2},{1,3},{2,0},{3,1},{4,6},{5,7},{6,4},{7,5},{8,10},{9,11},{10,... | collective-permute-start | bytes 884744 | tf_op jit(solution)/shard_map/ppermute | solution.py:599
  110.4 2.2 collective-permute-start.20
  144.3 6.8 %collective-permute-start.22 = (bf16[384,1536]{1,0:T(8,128)(2,1)}, bf16[384,1536]{1,0:T(8,128)(2,1)S(1)}, u32[]{:S(2)}, u32[]{:S(2)}) collective-permute-start(bf16[384,1536]{1,0:T(8,128)(2,1)} %get-tuple-element.67), channel_id=1, source_target_pairs={{0,1},{1,0},{2,3},{3,2},{4,5},{5,4},{6,7},{7,6},{8,9},{9,8},{10,11... | collective-permute-start | bytes 3538952 | tf_op jit(solution)/shard_map/ppermute | solution.py:599
  144.8 31.2 %collective-permute-start.24 = (bf16[1152,1536]{1,0:T(8,128)(2,1)}, bf16[1152,1536]{1,0:T(8,128)(2,1)}, u32[]{:S(2)}, u32[]{:S(2)}) collective-permute-start(bf16[1152,1536]{1,0:T(8,128)(2,1)} %get-tuple-element.74), channel_id=1, source_target_pairs={{0,1},{1,0},{2,3},{3,2},{4,5},{5,4},{6,7},{7,6},{8,9},{9,8},{10,11... | collective-permute-start | bytes 10616840 | tf_op jit(solution)/shard_map/ppermute | solution.py:599
  145.6 11.4 %collective-permute-start.23 = (bf16[512,768]{1,0:T(8,128)(2,1)}, bf16[512,768]{1,0:T(8,128)(2,1)}, u32[]{:S(2)}, u32[]{:S(2)}) collective-permute-start(bf16[512,768]{1,0:T(8,128)(2,1)} %get-tuple-element.70.g0), channel_id=1, source_target_pairs={{0,1},{1,0},{2,3},{3,2},{4,5},{5,4},{6,7},{7,6},{8,9},{9,8},{10,11... | collective-permute-start | bytes 2359304 | tf_op jit(solution)/shard_map/ppermute | solution.py:599
  146.0 27.4 %collective-permute-start.27 = (bf16[512,768]{1,0:T(8,128)(2,1)}, bf16[512,768]{1,0:T(8,128)(2,1)S(1)}, u32[]{:S(2)}, u32[]{:S(2)}) collective-permute-start(bf16[512,768]{1,0:T(8,128)(2,1)} %get-tuple-element.70.g0), channel_id=1, source_target_pairs={{0,2},{1,3},{2,0},{3,1},{4,6},{5,7},{6,4},{7,5},{8,10},{9,11},{10,... | collective-permute-start | bytes 2359304 | tf_op jit(solution)/shard_map/ppermute | solution.py:599
  153.7 2.8 copy-start.13
  153.7 21.4 %collective-permute-start.29 = (bf16[288,1536]{1,0:T(8,128)(2,1)S(1)}, bf16[288,1536]{1,0:T(8,128)(2,1)S(1)}, u32[]{:S(2)}, u32[]{:S(2)}) collective-permute-start(bf16[288,1536]{1,0:T(8,128)(2,1)S(1)} %add_convert_fusion.1.refs_2_), channel_id=1, source_target_pairs={{0,4},{4,0},{8,12},{12,8},{16,20},{20,16},{24,28},{28,24},{1,5},{5... | collective-permute-start | bytes 2654216 | tf_op jit(solution)/shard_map/ppermute | solution.py:573
  156.5 17.9 %collective-permute-start.25 = (bf16[96,1536]{1,0:T(8,128)(2,1)}, bf16[96,1536]{1,0:T(8,128)(2,1)S(1)}, u32[]{:S(2)}, u32[]{:S(2)}) collective-permute-start(bf16[96,1536]{1,0:T(8,128)(2,1)} %add_convert_fusion.6.refs_1_), channel_id=1, source_target_pairs={{0,2},{1,3},{2,0},{3,1},{4,6},{5,7},{6,4},{7,5},{8,10},{9,11},{10,... | collective-permute-start | bytes 884744 | tf_op jit(solution)/shard_map/ppermute | solution.py:599
  174.3 14.4 %collective-permute-start.28 = (bf16[512,768]{1,0:T(8,128)(2,1)}, bf16[512,768]{1,0:T(8,128)(2,1)}, u32[]{:S(2)}, u32[]{:S(2)}) collective-permute-start(bf16[512,768]{1,0:T(8,128)(2,1)} %later.31.g0.g2), channel_id=1, source_target_pairs={{0,1},{1,0},{2,3},{3,2},{4,5},{5,4},{6,7},{7,6},{8,9},{9,8},{10,11... | collective-permute-start | bytes 2359304 | tf_op jit(solution)/shard_map/ppermute | solution.py:599
  176.1 3.2 %copy-start.12 = (bf16[288,1536]{1,0:T(8,128)(2,1)S(1)}, bf16[288,1536]{1,0:T(8,128)(2,1)}, u32[]{:S(2)}) copy-start(bf16[288,1536]{1,0:T(8,128)(2,1)} %later.32) | copy-start | bytes 2654212
  181.7 5.5 %copy-start.7 = (bf16[384,1536]{1,0:T(8,128)(2,1)}, bf16[384,1536]{1,0:T(8,128)(2,1)S(1)}, u32[]{:S(2)}) copy-start(bf16[384,1536]{1,0:T(8,128)(2,1)S(1)} %get-tuple-element.207.refs_1_) | copy-start | bytes 3538948
  181.7 5.5 %copy-start.6 = (bf16[384,1536]{1,0:T(8,128)(2,1)S(1)}, bf16[384,1536]{1,0:T(8,128)(2,1)}, u32[]{:S(2)}) copy-start(bf16[384,1536]{1,0:T(8,128)(2,1)} %get-tuple-element.208.refs_2_) | copy-start | bytes 3538948
  181.7 40.4 %collective-permute-start.26 = (bf16[384,1536]{1,0:T(8,128)(2,1)S(1)}, bf16[384,1536]{1,0:T(8,128)(2,1)S(1)}, u32[]{:S(2)}, u32[]{:S(2)}) collective-permute-start(bf16[384,1536]{1,0:T(8,128)(2,1)S(1)} %get-tuple-element.207.refs_1_), channel_id=1, source_target_pairs={{0,4},{4,0},{8,12},{12,8},{16,20},{20,16},{24,28},{28,24},{1,5},{5... | collective-permute-start | bytes 3538952 | tf_op jit(solution)/shard_map/ppermute | solution.py:573
  187.2 35.9 %collective-permute-start.30 = (bf16[384,1536]{1,0:T(8,128)(2,1)S(1)}, bf16[384,1536]{1,0:T(8,128)(2,1)}, u32[]{:S(2)}, u32[]{:S(2)}) collective-permute-start(bf16[384,1536]{1,0:T(8,128)(2,1)S(1)} %copy-done.6), channel_id=1, source_target_pairs={{0,2},{1,3},{2,0},{3,1},{4,6},{5,7},{6,4},{7,5},{8,10},{9,11},{10,... | collective-permute-start | bytes 3538952 | tf_op jit(solution)/shard_map/ppermute | solution.py:599
  216.0 42.4 %collective-permute-start.33 = (bf16[384,768]{1,0:T(8,128)(2,1)}, bf16[384,768]{1,0:T(8,128)(2,1)}, u32[]{:S(2)}, u32[]{:S(2)}) collective-permute-start(bf16[384,768]{1,0:T(8,128)(2,1)} %get-tuple-element.87), channel_id=1, source_target_pairs={{0,4},{4,0},{8,12},{12,8},{16,20},{20,16},{24,28},{28,24},{1,5},{5... | collective-permute-start | bytes 1769480 | tf_op jit(solution)/shard_map/ppermute | solution.py:573
  228.0 15.2 %collective-permute-start.34 = (bf16[96,1536]{1,0:T(8,128)(2,1)S(1)}, bf16[96,1536]{1,0:T(8,128)(2,1)S(1)}, u32[]{:S(2)}, u32[]{:S(2)}) collective-permute-start(bf16[96,1536]{1,0:T(8,128)(2,1)S(1)} %get-tuple-element.183), channel_id=1, source_target_pairs={{0,8},{4,12},{8,0},{12,4},{16,24},{20,28},{24,16},{28,20},{1,9},{5... | collective-permute-start | bytes 884744 | tf_op jit(solution)/shard_map/ppermute | solution.py:573
  228.0 15.9 %collective-permute-start.35 = (bf16[96,1536]{1,0:T(8,128)(2,1)S(1)}, bf16[96,1536]{1,0:T(8,128)(2,1)S(1)}, u32[]{:S(2)}, u32[]{:S(2)}) collective-permute-start(bf16[96,1536]{1,0:T(8,128)(2,1)S(1)} %get-tuple-element.185), channel_id=1, source_target_pairs={{0,16},{4,20},{8,24},{12,28},{16,0},{20,4},{24,8},{28,12},{1,17},{... | collective-permute-start | bytes 884744 | tf_op jit(solution)/shard_map/ppermute | solution.py:573
  232.4 21.0 %collective-permute-start.36 = (bf16[96,1536]{1,0:T(8,128)(2,1)S(1)}, bf16[96,1536]{1,0:T(8,128)(2,1)S(1)}, u32[]{:S(2)}, u32[]{:S(2)}) collective-permute-start(bf16[96,1536]{1,0:T(8,128)(2,1)S(1)} %get-tuple-element.184), channel_id=1, source_target_pairs={{0,24},{4,28},{8,16},{12,20},{16,8},{20,12},{24,0},{28,4},{1,25},{... | collective-permute-start | bytes 884744 | tf_op jit(solution)/shard_map/ppermute | solution.py:573
  240.6 30.3 %collective-permute-start.31 = (bf16[1024,768]{1,0:T(8,128)(2,1)}, bf16[1024,768]{1,0:T(8,128)(2,1)S(1)}, u32[]{:S(2)}, u32[]{:S(2)}) collective-permute-start(bf16[1024,768]{1,0:T(8,128)(2,1)} %get-tuple-element.85), channel_id=1, source_target_pairs={{0,1},{1,0},{2,3},{3,2},{4,5},{5,4},{6,7},{7,6},{8,9},{9,8},{10,11... | collective-permute-start | bytes 4718600 | tf_op jit(solution)/shard_map/ppermute | solution.py:599
  243.9 10.2 %copy-start.20 = (bf16[96,1536]{1,0:T(8,128)(2,1)S(1)}, bf16[96,1536]{1,0:T(8,128)(2,1)}, u32[]{:S(2)}) copy-start(bf16[96,1536]{1,0:T(8,128)(2,1)} %later.37) | copy-start | bytes 884740
  244.7 9.5 %copy-start.18 = (bf16[96,1536]{1,0:T(8,128)(2,1)S(1)}, bf16[96,1536]{1,0:T(8,128)(2,1)}, u32[]{:S(2)}) copy-start(bf16[96,1536]{1,0:T(8,128)(2,1)} %later.38) | copy-start | bytes 884740
  256.2 2.0 copy-start.33
  256.2 2.2 copy-start.4
  258.4 11.6 %copy-start = (f32[96,1536]{1,0:T(8,128)S(1)}, f32[96,1536]{1,0:T(8,128)}, u32[]{:S(2)}) copy-start(f32[96,1536]{1,0:T(8,128)} %add_add_fusion.refs_1_) | copy-start | bytes 1769476
  258.4 12.4 %copy-start.25 = (bf16[512,768]{1,0:T(8,128)(2,1)S(1)}, bf16[512,768]{1,0:T(8,128)(2,1)}, u32[]{:S(2)}) copy-start(bf16[512,768]{1,0:T(8,128)(2,1)} %get-tuple-element.86) | copy-start | bytes 2359300
  260.5 16.4 %collective-permute-start.37 = (bf16[96,768]{1,0:T(8,128)(2,1)}, bf16[96,768]{1,0:T(8,128)(2,1)S(1)}, u32[]{:S(2)}, u32[]{:S(2)}) collective-permute-start(bf16[96,768]{1,0:T(8,128)(2,1)} %get-tuple-element.188), channel_id=1, source_target_pairs={{0,8},{4,12},{8,0},{12,4},{16,24},{20,28},{24,16},{28,20},{1,9},{5... | collective-permute-start | bytes 442376 | tf_op jit(solution)/shard_map/ppermute | solution.py:573
  266.6 13.8 %collective-permute-start.38 = (bf16[96,768]{1,0:T(8,128)(2,1)}, bf16[96,768]{1,0:T(8,128)(2,1)S(1)}, u32[]{:S(2)}, u32[]{:S(2)}) collective-permute-start(bf16[96,768]{1,0:T(8,128)(2,1)} %get-tuple-element.190), channel_id=1, source_target_pairs={{0,16},{4,20},{8,24},{12,28},{16,0},{20,4},{24,8},{28,12},{1,17},{... | collective-permute-start | bytes 442376 | tf_op jit(solution)/shard_map/ppermute | solution.py:573
  268.5 4.0 %copy-start.30 = (f32[32,144]{1,0:T(8,128)S(1)}, f32[32,144]{1,0:T(8,128)}, u32[]{:S(2)}) copy-start(f32[32,144]{1,0:T(8,128)} %copy.107) | copy-start | bytes 55300
  268.5 11.9 %collective-permute-start.39 = (bf16[96,768]{1,0:T(8,128)(2,1)S(1)}, bf16[96,768]{1,0:T(8,128)(2,1)}, u32[]{:S(2)}, u32[]{:S(2)}) collective-permute-start(bf16[96,768]{1,0:T(8,128)(2,1)S(1)} %get-tuple-element.189), channel_id=1, source_target_pairs={{0,24},{4,28},{8,16},{12,20},{16,8},{20,12},{24,0},{28,4},{1,25},{... | collective-permute-start | bytes 442376 | tf_op jit(solution)/shard_map/ppermute | solution.py:573
  271.9 20.6 %copy-start.1 = (bf16[512,768]{1,0:T(8,128)(2,1)S(1)}, bf16[512,768]{1,0:T(8,128)(2,1)}, u32[]{:S(2)}) copy-start(bf16[512,768]{1,0:T(8,128)(2,1)} %get-tuple-element.84.refs_1_) | copy-start | bytes 2359300
  271.9 20.6 %collective-permute-start.32 = (bf16[512,768]{1,0:T(8,128)(2,1)}, bf16[512,768]{1,0:T(8,128)(2,1)}, u32[]{:S(2)}, u32[]{:S(2)}) collective-permute-start(bf16[512,768]{1,0:T(8,128)(2,1)} %add_convert_fusion.3), channel_id=1, source_target_pairs={{0,2},{1,3},{2,0},{3,1},{4,6},{5,7},{6,4},{7,5},{8,10},{9,11},{10,... | collective-permute-start | bytes 2359304 | tf_op jit(solution)/shard_map/ppermute | solution.py:599
  273.3 18.0 %all-to-all-start.1 = ((f32[32,8,128]{2,1,0:T(8,128)}), f32[32,8,128]{2,1,0:T(8,128)S(1)}, u32[]{:S(2)}, u32[]{:S(2)}) async-start(f32[32,8,128]{2,1,0:T(8,128)} %bitcast.33), calls=%async_computation.1 | async-start | bytes 262144 | tf_op jit(solution)/shard_map/all_to_all | solution.py:778
  (15 other events, 13.3 us)

commit v6 on v5

--- a/solution.py
+++ b/solution.py
@@ -755,18 +755,8 @@
     even = waits[0] if local == 2 else attn_local[0]
     b0, side, far = project_back((later(dq_a, even), dq_b), dk, dv, attn_wt)
 
-    if local == 2:
-        wide_grad = even[0].astype(f32) + sum(later(hop(even[n], 2 * n), b0).astype(f32) for n in (1, 2, 3))
-        rows = attn_local[0].shape[0] // 4
-        even = total(attn_local[0], later(hop(attn_local[1], 1), wide_grad)).astype(bf16).reshape(4, rows, -1)
-        attn_grad = even[0].astype(f32) + sum(hop(even[n], 2 * n).astype(f32) for n in (1, 2, 3))
-    else:
-        mine = lax.psum_scatter(total(grads[0], swapped[0]).astype(bf16), "dp", scatter_dimension=0, tiled=True)
-        wide_grad = total(mine[:, : 2 * units], exchange(mine[:, 2 * units :], 2))
-        attn_grad = lax.all_to_all(attn_local[0], "dp", 0, 0, tiled=True)
-        attn_grad = jnp.sum(attn_grad.reshape(dp, -1, model).astype(f32), axis=0)
-    q_sums = later(q_sums_a, wide_grad) + later(q_sums_b, wide_grad)
-    v_sums = later(v_sums, wide_grad)
+    q_sums = later(q_sums_a, even) + later(q_sums_b, even)
+    v_sums = later(v_sums, even)
     mine = (jnp.arange(4) == part).astype(f32)[:, None]
     q_all = (mine * jnp.sum(q_sums, axis=1)[None]).reshape(1, model)
     v_all = (mine * jnp.sum(v_sums, axis=0)[None]).reshape(1, model)
@@ -778,7 +768,18 @@
     got = jnp.sum(lax.all_to_all(send, everyone, 0, 0, tiled=True).reshape(world, slots * 128), axis=0)
     small = [got[n * share : (n + 1) * share] for n in range(8)]
 
-    (b0, b1, b2), _ = scatter_pieces(b0, side, far)
+    if local == 2:
+        y_came = hop(attn_local[1], 1)
+        wide_grad = even[0].astype(f32) + sum(later(hop(even[n], 2 * n), b0, got, y_came).astype(f32) for n in (1, 2, 3))
+        rows = attn_local[0].shape[0] // 4
+        even = total(attn_local[0], y_came).astype(bf16).reshape(4, rows, -1)
+        attn_grad = even[0].astype(f32) + sum(hop(even[n], 2 * n).astype(f32) for n in (1, 2, 3))
+    else:
+        mine = lax.psum_scatter(total(grads[0], swapped[0]).astype(bf16), "dp", scatter_dimension=0, tiled=True)
+        wide_grad = total(mine[:, : 2 * units], exchange(mine[:, 2 * units :], 2))
+        attn_grad = lax.all_to_all(attn_local[0], "dp", 0, 0, tiled=True)
+        attn_grad = jnp.sum(attn_grad.reshape(dp, -1, model).astype(f32), axis=0)
+    (b0, b1, b2), _ = scatter_pieces(b0, later(side, got), far)
     tokens_grad = (grad_mixed + (b0.astype(f32) + b1.astype(f32) + b2.astype(f32))).astype(bf16)
     querygrad, keygrad, valuegrad, mergegrad = (attn_grad[:, n * width : (n + 1) * width] for n in range(4))
     expandgrad = wide_grad[:, :units]

time: 295 us -> 295 us (level)
  waiting for transfers between devices: 53.1 us -> 58.3 us
  starting transfers between devices: 66.9 us -> 62.9 us
  local copies, waits for them, and re-layouts: 32 us -> 29 us
    ppermute x18, starting transfers between devices: 45.1 us -> 26.8 us  [hop(): return lax.ppermute(value, 'dp', [(i, i ^ bit) for i in range(count)])]
    all_to_all x1, starting transfers between devices: 3.61 us -> 17 us  [on_device(): lax.all_to_all(send, everyone, 0, 0, tiled=True).reshape(world, slots * 128)]
    ppermute x18, waiting for transfers between devices: 24.4 us -> 36.4 us  [hop(): return lax.ppermute(value, 'dp', [(i, i ^ bit) for i in range(count)])]
    all_to_all x1, waiting for transfers between devices: 8.35 us -> 1.45 us  [on_device(): lax.all_to_all(send, everyone, 0, 0, tiled=True).reshape(world, slots * 128)]
    unnamed x84 -> x76, local copies, waits for them, and re-layouts: 17.9 us -> 15.9 us
  transfers between devices with their start and end apart: 42 -> 42, of which waited for: 11 -> 13; matrix products, arithmetic and copies ran while one was open for 15% -> 15% of each run, Pallas kernels for 28% -> 28%
where the time goes in v6:
time: 295 us; the launch traced here: 293 us
  Pallas kernels  112 us (38%)
  starting transfers between devices  62.9 us (21%)
  waiting for transfers between devices  58.3 us (20%)
  other arithmetic  29.9 us (10%)
  local copies, waits for them, and re-layouts  29 us (10%)
    ppermute x18, waiting for transfers between devices, hop(): return lax.ppermute(value, 'dp', [(i, i ^ bit) for i in range(count)])  36.4 us
    pallas_call x2, Pallas kernels, attn_bwd(): pl.pallas_call(functools.partial(bwd_kernel, first), out_shape=(jax.Shape...  33.8 us
    pallas_call x1, Pallas kernels, ffn(): pl.pallas_call(functools.partial(ffn_kernel, count), out_shape=(jax.Shape...  30.6 us
    ppermute x18, starting transfers between devices, hop(): return lax.ppermute(value, 'dp', [(i, i ^ bit) for i in range(count)])  26.8 us
    pallas_call x2, Pallas kernels, attn_fwd(): pl.pallas_call(functools.partial(fwd_kernel, first), out_shape=(jax.Shape...  21 us
    all_to_all x1, starting transfers between devices, on_device(): lax.all_to_all(send, everyone, 0, 0, tiled=True).reshape(world, slots * 128)  17 us
    unnamed x76, local copies, waits for them, and re-layouts  15.9 us
    ppermute x22, waiting for transfers between devices, exchange(): return lax.ppermute(value, 'tensor', [(i, i ^ bit) for i in range(4)])  15.5 us
  transfers between devices with their start and end apart: 42, of which 13 were waited for; matrix products, arithmetic and copies ran while one was open for 15% of the time, Pallas kernels for 28%

profile of v6, /device:TPU:0, one launch (start us, length us, event | category | flops | bytes accessed | tf_op | source)
XLA Modules:
  0.0 293.4 jit_solution(17607806115130743475)
XLA Ops:
  0.7 0.9 copy.96
  1.5 1.0 pad_maximum_fusion.5
  2.5 3.1 %collective-permute-start.6 = (bf16[96,768]{1,0:T(8,128)(2,1)S(1)}, bf16[96,768]{1,0:T(8,128)(2,1)S(1)}, u32[]{:S(2)}, u32[]{:S(2)}) collective-permute-start(bf16[96,768]{1,0:T(8,128)(2,1)S(1)} %pad_maximum_fusion.5), channel_id=1, source_target_pairs={{0,8},{4,12},{8,0},{12,4},{16,24},{20,28},{24,16},{28,20},{1,9},{5... | collective-permute-start | bytes 442376 | tf_op jit(solution)/shard_map/ppermute | solution.py:573
  5.6 2.6 collective-permute-start.7
  8.2 1.7 collective-permute-start.4
  12.1 5.0 %all-to-all-start = ((f32[32,8,128]{2,1,0:T(8,128)}), f32[32,8,128]{2,1,0:T(8,128)S(1)}, u32[]{:S(2)}, u32[]{:S(2)}) async-start(f32[32,8,128]{2,1,0:T(8,128)} %broadcast_in_dim.46), calls=%async_computation | async-start | bytes 262144 | tf_op jit(solution)/shard_map/all_to_all | solution.py:702
  17.2 1.0 pad_maximum_fusion.4
  18.3 1.8 collective-permute-start
  20.1 2.4 collective-permute-start.1
  22.7 1.8 pad_maximum_fusion.3.wa_ref
  24.5 5.0 %all-to-all-done = f32[32,8,128]{2,1,0:T(8,128)S(1)} async-done(((f32[32,8,128]{2,1,0:T(8,128)}), f32[32,8,128]{2,1,0:T(8,128)S(1)}, u32[]{:S(2)}, u32[]{:S(2)}) %all-to-all-start) | async-done | bytes 131104 | tf_op jit(solution)/shard_map/all_to_all | solution.py:702
  32.5 2.4 collective-permute-done
  35.0 1.6 collective-permute-start.9
  38.6 1.4 copy.112
  40.5 3.1 %collective-permute-done.1 = bf16[96,1536]{1,0:T(8,128)(2,1)S(1)} collective-permute-done((bf16[96,1536]{1,0:T(8,128)(2,1)S(1)}, bf16[96,1536]{1,0:T(8,128)(2,1)S(1)}, u32[]{:S(2)}, u32[]{:S(2)}) %collective-permute-start.1) | collective-permute-done | bytes 294944 | tf_op jit(solution)/shard_map/ppermute | solution.py:573
  43.5 1.0 pad_maximum_fusion.refs_1_.refs_0_
  44.6 1.5 collective-permute-start.12
  46.2 1.5 collective-permute-start.13
  47.6 3.9 %collective-permute-done.9.wb_ref = bf16[384,768]{1,0:T(8,128)(2,1)} collective-permute-done((bf16[384,768]{1,0:T(8,128)(2,1)}, bf16[384,768]{1,0:T(8,128)(2,1)}, u32[]{:S(2)}, u32[]{:S(2)}) %collective-permute-start.9) | collective-permute-done | bytes 589856 | tf_op jit(solution)/shard_map/ppermute | solution.py:573
  51.5 10.0 %projection.1 = (bf16[192,2048]{1,0:T(8,128)(2,1)}, bf16[192,2048]{1,0:T(8,128)(2,1)}, bf16[192,2048]{1,0:T(8,128)(2,1)}, bf16[2048,192]{1,0:T(8,128)(2,1)}, bf1...) custom-call(s32[1]{0:T(128)} %bitcast.home_ref, bf16[512,768]{1,0:T(8,128)(2,1)} %x0.3, ...), custom_call_target="tpu_custom_call" | custom-call | flops 9059696640 | bytes 6291456 | tf_op jit(solution)/shard_map/projection/pallas_call | solution.py:448
  61.6 10.5 %attention.2 = (bf16[192,1024]{1,0:T(8,128)(2,1)}, f32[8,1024]{1,0:T(8,128)}, bf16[512,768]{1,0:T(8,128)(2,1)}, bf16[512,768]{1,0:T(8,128)(2,1)}) custom-call(s32[4]{0:T(128)} %later.22.lo_ref, s32[4]{0:T(128)} %and_select_fusion.hi_ref, s32[1]{0:T(128)} %bitcast.5.flip_ref, bf16[192,2048]{1,0:T(8,128)(2,1)} %get-tuple-element.55.q_ref, ...), custom_call_target="tpu_custom_call" | custom-call | flops 20132659200 | bytes 1572864 | tf_op jit(solution)/shard_map/attention/pallas_call | solution.py:82
  73.0 1.0 slice.220
  74.0 1.2 collective-permute-start.17
  76.0 1.6 collective-permute-start.15
  77.5 10.5 %attention.3 = (bf16[192,1024]{1,0:T(8,128)(2,1)}, f32[8,1024]{1,0:T(8,128)}, bf16[512,768]{1,0:T(8,128)(2,1)}, bf16[512,768]{1,0:T(8,128)(2,1)}) custom-call(s32[4]{0:T(128)} %later.23.lo_ref, s32[4]{0:T(128)} %and_select_fusion.hi_ref, s32[1]{0:T(128)} %bitcast.5.flip_ref, bf16[192,2048]{1,0:T(8,128)(2,1)} %get-tuple-element.55.q_ref, ...), custom_call_target="tpu_custom_call" | custom-call | flops 20132659200 | bytes 1572864 | tf_op jit(solution)/shard_map/attention/pallas_call | solution.py:82
  88.0 7.7 %collective-permute-done.15.refs_0_ = bf16[512,768]{1,0:T(8,128)(2,1)S(1)} collective-permute-done((bf16[512,768]{1,0:T(8,128)(2,1)S(1)}, bf16[512,768]{1,0:T(8,128)(2,1)S(1)}, u32[]{:S(2)}, u32[]{:S(2)}) %collective-permute-start.15) | collective-permute-done | bytes 786464 | tf_op jit(solution)/shard_map/ppermute | solution.py:599
  95.7 0.9 copy-done.3
  97.1 1.0 slice.219
  98.1 1.6 collective-permute-start.16
  99.7 7.4 %collective-permute-done.16.refs_0_ = bf16[96,1536]{1,0:T(8,128)(2,1)S(1)} collective-permute-done((bf16[96,1536]{1,0:T(8,128)(2,1)S(1)}, bf16[96,1536]{1,0:T(8,128)(2,1)S(1)}, u32[]{:S(2)}, u32[]{:S(2)}) %collective-permute-start.16) | collective-permute-done | bytes 294944 | tf_op jit(solution)/shard_map/ppermute | solution.py:599
  111.1 30.6 %feed_forward.1 = (bf16[512,768]{1,0:T(8,128)(2,1)}, f32[512,768]{1,0:T(8,128)}, bf16[512,768]{1,0:T(8,128)(2,1)}, f32[6,8,768]{2,1,0:T(8,128)}, f32[4,8,768]{2,...) custom-call(s32[1]{0:T(128)} %bitcast.home_ref, ...), custom_call_target="tpu_custom_call" | custom-call | flops 36238786560 | bytes 18874368 | tf_op jit(solution)/shard_map/feed_forward/pallas_call | solution.py:379
  142.9 1.6 collective-permute-start.27
  144.5 0.9 reduce_sum.69
  145.7 0.9 reduce_sum.70
  147.4 1.0 copy-done.19
  148.4 1.7 add_convert_fusion.1.refs_2_
  150.1 1.6 collective-permute-start.29
  151.6 1.8 add_convert_fusion.6.refs_1_
  154.0 16.4 %attention_back.2 = (bf16[192,1024]{1,0:T(8,128)(2,1)}, f32[2048,192]{1,0:T(8,128)}, f32[2048,192]{1,0:T(8,128)}, f32[192,128]{1,0:T(8,128)}) custom-call(s32[4]{0:T(128)} %later.29.lo_ref, s32[4]{0:T(128)} %and_select_fusion.hi_ref, s32[1]{0:T(128)} %bitcast.5.flip_ref, bf16[192,2048]{1,0:T(8,128)(2,1)} %get-tuple-element.55.q_ref, ...), custom_call_target="tpu_custom_call" | custom-call | flops 24159191040 | bytes 3932160 | tf_op jit(solution)/shard_map/attention_back/pallas_call | solution.py:171
  170.4 0.9 copy-done.12
  172.0 0.9 copy-done.9
  173.0 3.1 %convert_add_fusion.1 = (f32[384,1536]{1,0:T(8,128)S(1)}, f32[384,1536]{1,0:T(8,128)S(1)}) fusion(bf16[1152,1536]{1,0:T(8,128)(2,1)} %collective-permute-done.24, bf16[1152,1536]{1,0:T(8,128)(2,1)} %get-tuple-element.73), kind=kLoop, calls=%fused_computation.5 | loop fusion | flops 3538944 | bytes 9437184 | tf_op jit(solution)/shard_map/add | solution.py:636
  177.4 1.2 pad_maximum_fusion.1
  178.6 0.9 collective-permute-start.26
  180.3 1.5 collective-permute-start.30
  181.8 17.4 %attention_back.3 = (bf16[192,1024]{1,0:T(8,128)(2,1)}, bf16[2048,192]{1,0:T(8,128)(2,1)}, bf16[2048,192]{1,0:T(8,128)(2,1)}, f32[192,128]{1,0:T(8,128)}, f32[8,192]{1,0:T(8,128)}) custom-call(s32[4]{0:T(128)} %later.33.lo_ref, s32[4]{0:T(128)} %and_select_fusion.hi_ref, s32[1]{0:T(128)} %bitcast.5.flip_ref, bf16[192,2048]{1,0:T(8,128)(2,1)} %get-tuple-element.55.q_ref, ...), custom_call_target="tpu_custom_call" | custom-call | flops 24159191040 | bytes 3932160 | tf_op jit(solution)/shard_map/attention_back/pallas_call | solution.py:171
  199.2 9.8 %projection_grads.1 = (bf16[384,768]{1,0:T(8,128)(2,1)}, bf16[384,768]{1,0:T(8,128)(2,1)}) custom-call(s32[1]{0:T(128)} %bitcast.home_ref, bf16[512,768]{1,0:T(8,128)(2,1)} %x0.3, bf16[512,768]{1,0:T(8,128)(2,1)} %collective-permute-done.3.x1, bf16[512,768]{1,0:T(8,128)(2,1)} %copy-done.22, bf16[512,768]{1,0:T(8,128)(2,1)} %collective-permute-done.5.x3, ...), custom_call_target="tpu_custom_call" | custom-call | flops 603979776 | bytes 9437184 | tf_op jit(solution)/shard_map/projection_grads/pallas_call | solution.py:526
  209.6 3.9 %add_convert_fusion = bf16[384,1536]{1,0:T(8,128)(2,1)} fusion(bf16[384,1536]{1,0:T(8,128)(2,1)} %later.35, bf16[384,1536]{1,0:T(8,128)(2,1)} %later.34, bf16[1152,1536]{1,0:T(8,128)(2,1)} %collective-permute-done.24, bf16[1152,1536]{1,0:T(8,128)(2,1)} %get-tuple-element.73), kind=kLoop, calls=%fused_computation.3 | loop fusion | flops 4718592 | bytes 5898240 | tf_op jit(solution)/shard_map/convert_element_type | solution.py:657
  214.4 1.0 add_reduce_fusion
  216.6 17.0 %all-to-all-start.1 = ((f32[32,8,128]{2,1,0:T(8,128)}), f32[32,8,128]{2,1,0:T(8,128)S(1)}, u32[]{:S(2)}, u32[]{:S(2)}) async-start(f32[32,8,128]{2,1,0:T(8,128)} %bitcast.33), calls=%async_computation.1 | async-start | bytes 262144 | tf_op jit(solution)/shard_map/all_to_all | solution.py:768
  233.5 6.8 %projection_back.1 = (bf16[512,768]{1,0:T(8,128)(2,1)}, bf16[1024,768]{1,0:T(8,128)(2,1)}, bf16[512,768]{1,0:T(8,128)(2,1)}) custom-call(bf16[192,1024]{1,0:T(8,128)(2,1)} %later.36.qa_ref, bf16[192,1024]{1,0:T(8,128)(2,1)} %get-tuple-element.80.qb_ref, bf16[2048,192]{1,0:T(8,128)(2,1)} %get-tuple-element.81.k_ref, ...), custom_call_target="tpu_custom_call" | custom-call | flops 21139292160 | bytes 12582912 | tf_op jit(solution)/shard_map/projection_back/pallas_call | solution.py:559
  240.3 1.5 all-to-all-done.1
  244.4 2.1 collective-permute-start.35
  246.4 1.7 collective-permute-start.36
  248.1 3.9 %collective-permute-done.34 = bf16[96,768]{1,0:T(8,128)(2,1)S(1)} collective-permute-done((bf16[96,768]{1,0:T(8,128)(2,1)S(1)}, bf16[96,768]{1,0:T(8,128)(2,1)S(1)}, u32[]{:S(2)}, u32[]{:S(2)}) %collective-permute-start.34) | collective-permute-done | bytes 147488 | tf_op jit(solution)/shard_map/ppermute | solution.py:573
  252.0 6.3 %collective-permute-done.35 = bf16[96,768]{1,0:T(8,128)(2,1)S(1)} collective-permute-done((bf16[96,768]{1,0:T(8,128)(2,1)S(1)}, bf16[96,768]{1,0:T(8,128)(2,1)S(1)}, u32[]{:S(2)}, u32[]{:S(2)}) %collective-permute-start.35) | collective-permute-done | bytes 147488 | tf_op jit(solution)/shard_map/ppermute | solution.py:573
  260.8 2.4 collective-permute-start.37
  264.0 1.6 collective-permute-start.39
  265.6 2.2 add_convert_fusion.3
  267.8 1.4 collective-permute-start.32
  270.4 3.8 %collective-permute-done.37.refs_0_ = bf16[96,1536]{1,0:T(8,128)(2,1)} collective-permute-done((bf16[96,1536]{1,0:T(8,128)(2,1)S(1)}, bf16[96,1536]{1,0:T(8,128)(2,1)}, u32[]{:S(2)}, u32[]{:S(2)}) %collective-permute-start.37) | collective-permute-done | bytes 294944 | tf_op jit(solution)/shard_map/ppermute | solution.py:573
  274.2 12.7 %collective-permute-done.38.refs_0_ = bf16[96,1536]{1,0:T(8,128)(2,1)S(1)} collective-permute-done((bf16[96,1536]{1,0:T(8,128)(2,1)}, bf16[96,1536]{1,0:T(8,128)(2,1)S(1)}, u32[]{:S(2)}, u32[]{:S(2)}) %collective-permute-start.38) | collective-permute-done | bytes 294944 | tf_op jit(solution)/shard_map/ppermute | solution.py:573
  288.7 1.3 add_add_fusion
  290.9 2.4 add_convert_fusion.2
  (207 shorter events, 31.8 us)
Async XLA Ops:
  2.5 15.7 %collective-permute-start.6 = (bf16[96,768]{1,0:T(8,128)(2,1)S(1)}, bf16[96,768]{1,0:T(8,128)(2,1)S(1)}, u32[]{:S(2)}, u32[]{:S(2)}) collective-permute-start(bf16[96,768]{1,0:T(8,128)(2,1)S(1)} %pad_maximum_fusion.5), channel_id=1, source_target_pairs={{0,8},{4,12},{8,0},{12,4},{16,24},{20,28},{24,16},{28,20},{1,9},{5... | collective-permute-start | bytes 442376 | tf_op jit(solution)/shard_map/ppermute | solution.py:573
  5.6 14.5 %collective-permute-start.7 = (bf16[96,768]{1,0:T(8,128)(2,1)S(1)}, bf16[96,768]{1,0:T(8,128)(2,1)S(1)}, u32[]{:S(2)}, u32[]{:S(2)}) collective-permute-start(bf16[96,768]{1,0:T(8,128)(2,1)S(1)} %pad_maximum_fusion.5), channel_id=1, source_target_pairs={{0,16},{4,20},{8,24},{12,28},{16,0},{20,4},{24,8},{28,12},{1,17},{... | collective-permute-start | bytes 442376 | tf_op jit(solution)/shard_map/ppermute | solution.py:573
  8.2 14.3 %collective-permute-start.8 = (bf16[96,768]{1,0:T(8,128)(2,1)S(1)}, bf16[96,768]{1,0:T(8,128)(2,1)S(1)}, u32[]{:S(2)}, u32[]{:S(2)}) collective-permute-start(bf16[96,768]{1,0:T(8,128)(2,1)S(1)} %pad_maximum_fusion.5), channel_id=1, source_target_pairs={{0,24},{4,28},{8,16},{12,20},{16,8},{20,12},{24,0},{28,4},{1,25},{... | collective-permute-start | bytes 442376 | tf_op jit(solution)/shard_map/ppermute | solution.py:573
  8.2 22.5 %collective-permute-start.4 = (bf16[512,768]{1,0:T(8,128)(2,1)}, bf16[512,768]{1,0:T(8,128)(2,1)S(1)}, u32[]{:S(2)}, u32[]{:S(2)}) collective-permute-start(bf16[512,768]{1,0:T(8,128)(2,1)} %x0.3), channel_id=1, source_target_pairs={{0,2},{1,3},{2,0},{3,1},{4,6},{5,7},{6,4},{7,5},{8,10},{9,11},{10,... | collective-permute-start | bytes 2359304 | tf_op jit(solution)/shard_map/ppermute | solution.py:599
  9.9 41.6 %collective-permute-start.3 = (bf16[512,768]{1,0:T(8,128)(2,1)}, bf16[512,768]{1,0:T(8,128)(2,1)}, u32[]{:S(2)}, u32[]{:S(2)}) collective-permute-start(bf16[512,768]{1,0:T(8,128)(2,1)} %x0.3), channel_id=1, source_target_pairs={{0,1},{1,0},{2,3},{3,2},{4,5},{5,4},{6,7},{7,6},{8,9},{9,8},{10,11... | collective-permute-start | bytes 2359304 | tf_op jit(solution)/shard_map/ppermute | solution.py:599
  12.1 17.4 %all-to-all-start = ((f32[32,8,128]{2,1,0:T(8,128)}), f32[32,8,128]{2,1,0:T(8,128)S(1)}, u32[]{:S(2)}, u32[]{:S(2)}) async-start(f32[32,8,128]{2,1,0:T(8,128)} %broadcast_in_dim.46), calls=%async_computation | async-start | bytes 262144 | tf_op jit(solution)/shard_map/all_to_all | solution.py:702
  18.2 25.3 %copy-start.24 = (bf16[768,96]{0,1:T(8,128)(2,1)S(1)}, bf16[768,96]{0,1:T(8,128)(2,1)}, u32[]{:S(2)}) copy-start(bf16[768,96]{0,1:T(8,128)(2,1)} %param.33) | copy-start | bytes 442372
  18.2 25.3 %copy-start.25 = (bf16[96,768]{1,0:T(8,128)(2,1)S(1)}, bf16[96,768]{1,0:T(8,128)(2,1)}, u32[]{:S(2)}) copy-start(bf16[96,768]{1,0:T(8,128)(2,1)} %param.31) | copy-start | bytes 442372
  18.3 16.7 %collective-permute-start = (bf16[96,1536]{1,0:T(8,128)(2,1)S(1)}, bf16[96,1536]{1,0:T(8,128)(2,1)S(1)}, u32[]{:S(2)}, u32[]{:S(2)}) collective-permute-start(bf16[96,1536]{1,0:T(8,128)(2,1)S(1)} %pad_maximum_fusion.4), channel_id=1, source_target_pairs={{0,8},{4,12},{8,0},{12,4},{16,24},{20,28},{24,16},{28,20},{1,9},{5... | collective-permute-start | bytes 884744 | tf_op jit(solution)/shard_map/ppermute | solution.py:573
  20.1 23.4 %collective-permute-start.1 = (bf16[96,1536]{1,0:T(8,128)(2,1)S(1)}, bf16[96,1536]{1,0:T(8,128)(2,1)S(1)}, u32[]{:S(2)}, u32[]{:S(2)}) collective-permute-start(bf16[96,1536]{1,0:T(8,128)(2,1)S(1)} %pad_maximum_fusion.4), channel_id=1, source_target_pairs={{0,16},{4,20},{8,24},{12,28},{16,0},{20,4},{24,8},{28,12},{1,17},{... | collective-permute-start | bytes 884744 | tf_op jit(solution)/shard_map/ppermute | solution.py:573
  22.5 21.0 %collective-permute-start.2 = (bf16[96,1536]{1,0:T(8,128)(2,1)S(1)}, bf16[96,1536]{1,0:T(8,128)(2,1)}, u32[]{:S(2)}, u32[]{:S(2)}) collective-permute-start(bf16[96,1536]{1,0:T(8,128)(2,1)S(1)} %pad_maximum_fusion.4), channel_id=1, source_target_pairs={{0,24},{4,28},{8,16},{12,20},{16,8},{20,12},{24,0},{28,4},{1,25},{... | collective-permute-start | bytes 884744 | tf_op jit(solution)/shard_map/ppermute | solution.py:573
  30.7 13.9 %copy-start.22 = (bf16[512,768]{1,0:T(8,128)(2,1)}, bf16[512,768]{1,0:T(8,128)(2,1)S(1)}, u32[]{:S(2)}) copy-start(bf16[512,768]{1,0:T(8,128)(2,1)S(1)} %collective-permute-done.4.x2) | copy-start | bytes 2359300
  30.7 20.8 %collective-permute-start.5 = (bf16[512,768]{1,0:T(8,128)(2,1)S(1)}, bf16[512,768]{1,0:T(8,128)(2,1)}, u32[]{:S(2)}, u32[]{:S(2)}) collective-permute-start(bf16[512,768]{1,0:T(8,128)(2,1)S(1)} %collective-permute-done.4.x2), channel_id=1, source_target_pairs={{0,1},{1,0},{2,3},{3,2},{4,5},{5,4},{6,7},{7,6},{8,9},{9,8},{10,11... | collective-permute-start | bytes 2359304 | tf_op jit(solution)/shard_map/ppermute | solution.py:599
  30.8 13.8 %copy-start.30 = (s32[4]{0:T(128)}, s32[4]{0:T(128)S(1)}, u32[]{:S(2)}) copy-start(s32[4]{0:T(128)S(1)} %and_select_fusion.1.refs_0_) | copy-start | bytes 52
  35.0 16.6 %collective-permute-start.9 = (bf16[384,768]{1,0:T(8,128)(2,1)}, bf16[384,768]{1,0:T(8,128)(2,1)}, u32[]{:S(2)}, u32[]{:S(2)}) collective-permute-start(bf16[384,768]{1,0:T(8,128)(2,1)} %pad_maximum_fusion.3.wa_ref), channel_id=1, source_target_pairs={{0,4},{4,0},{8,12},{12,8},{16,20},{20,16},{24,28},{28,24},{1,5},{5... | collective-permute-start | bytes 1769480 | tf_op jit(solution)/shard_map/ppermute | solution.py:573
  36.8 7.8 %copy-start.29 = (f32[192]{0:T(256)}, f32[192]{0:T(256)S(1)}, u32[]{:S(2)}) copy-start(f32[192]{0:T(256)S(1)} %dynamic_slice.11) | copy-start | bytes 2308
  38.5 6.1 %copy-start.28 = (s32[1,1,4,512]{3,1,2,0:T(1,128)}, s32[1,1,4,512]{3,1,2,0:T(1,128)S(1)}, u32[]{:S(2)}) copy-start(s32[1,1,4,512]{3,1,2,0:T(1,128)S(1)} %copy.111) | copy-start | bytes 24580
  44.6 3.0 %copy-start.5 = (bf16[384,1536]{1,0:T(8,128)(2,1)}, bf16[384,1536]{1,0:T(8,128)(2,1)S(1)}, u32[]{:S(2)}) copy-start(bf16[384,1536]{1,0:T(8,128)(2,1)S(1)} %pad_maximum_fusion.refs_1_.refs_0_) | copy-start | bytes 3538948
  44.6 30.8 %collective-permute-start.12 = (bf16[384,1536]{1,0:T(8,128)(2,1)S(1)}, bf16[384,1536]{1,0:T(8,128)(2,1)}, u32[]{:S(2)}, u32[]{:S(2)}) collective-permute-start(bf16[384,1536]{1,0:T(8,128)(2,1)S(1)} %pad_maximum_fusion.refs_1_.refs_0_), channel_id=1, source_target_pairs={{0,4},{4,0},{8,12},{12,8},{16,20},{20,16},{24,28},{28,24},{1,5},{5... | collective-permute-start | bytes 3538952 | tf_op jit(solution)/shard_map/ppermute | solution.py:573
  46.2 26.8 %collective-permute-start.13 = (bf16[384,1536]{1,0:T(8,128)(2,1)S(1)}, bf16[384,1536]{1,0:T(8,128)(2,1)S(1)}, u32[]{:S(2)}, u32[]{:S(2)}) collective-permute-start(bf16[384,1536]{1,0:T(8,128)(2,1)S(1)} %pad_maximum_fusion.refs_1_.refs_0_), channel_id=1, source_target_pairs={{0,2},{1,3},{2,0},{3,1},{4,6},{5,7},{6,4},{7,5},{8,10},{9,11},{10,... | collective-permute-start | bytes 3538952 | tf_op jit(solution)/shard_map/ppermute | solution.py:599
  51.5 26.0 %collective-permute-start.11 = (bf16[384,1536]{1,0:T(8,128)(2,1)}, bf16[384,1536]{1,0:T(8,128)(2,1)}, u32[]{:S(2)}, u32[]{:S(2)}) collective-permute-start(bf16[384,1536]{1,0:T(8,128)(2,1)} %copy-done.5), channel_id=1, source_target_pairs={{0,1},{1,0},{2,3},{3,2},{4,5},{5,4},{6,7},{7,6},{8,9},{9,8},{10,11... | collective-permute-start | bytes 3538952 | tf_op jit(solution)/shard_map/ppermute | solution.py:599
  72.1 3.7 %copy-start.23 = (bf16[512,768]{1,0:T(8,128)(2,1)S(1)}, bf16[512,768]{1,0:T(8,128)(2,1)}, u32[]{:S(2)}) copy-start(bf16[512,768]{1,0:T(8,128)(2,1)} %get-tuple-element.59) | copy-start | bytes 2359300
  72.1 3.7 %collective-permute-start.10 = (bf16[512,768]{1,0:T(8,128)(2,1)}, bf16[512,768]{1,0:T(8,128)(2,1)S(1)}, u32[]{:S(2)}, u32[]{:S(2)}) collective-permute-start(bf16[512,768]{1,0:T(8,128)(2,1)} %get-tuple-element.60), channel_id=1, source_target_pairs={{0,1},{1,0},{2,3},{3,2},{4,5},{5,4},{6,7},{7,6},{8,9},{9,8},{10,11... | collective-permute-start | bytes 2359304 | tf_op jit(solution)/shard_map/ppermute | solution.py:599
  73.0 3.0 %copy-start.8 = (bf16[384,1536]{1,0:T(8,128)(2,1)}, bf16[384,1536]{1,0:T(8,128)(2,1)S(1)}, u32[]{:S(2)}) copy-start(bf16[384,1536]{1,0:T(8,128)(2,1)S(1)} %collective-permute-done.13.refs_4_.refs_2_) | copy-start | bytes 3538948
  74.0 22.5 %collective-permute-start.17 = (bf16[288,1536]{1,0:T(8,128)(2,1)}, bf16[288,1536]{1,0:T(8,128)(2,1)}, u32[]{:S(2)}, u32[]{:S(2)}) collective-permute-start(bf16[288,1536]{1,0:T(8,128)(2,1)} %slice.220), channel_id=1, source_target_pairs={{0,4},{4,0},{8,12},{12,8},{16,20},{20,16},{24,28},{28,24},{1,5},{5... | collective-permute-start | bytes 2654216 | tf_op jit(solution)/shard_map/ppermute | solution.py:573
  75.3 34.7 %collective-permute-start.19 = (bf16[384,1536]{1,0:T(8,128)(2,1)S(1)}, bf16[384,1536]{1,0:T(8,128)(2,1)}, u32[]{:S(2)}, u32[]{:S(2)}) collective-permute-start(bf16[384,1536]{1,0:T(8,128)(2,1)S(1)} %collective-permute-done.13.refs_4_.refs_2_), channel_id=1, source_target_pairs={{0,1},{1,0},{2,3},{3,2},{4,5},{5,4},{6,7},{7,6},{8,9},{9,8},{10,11... | collective-permute-start | bytes 3538952 | tf_op jit(solution)/shard_map/ppermute | solution.py:599
  75.4 34.5 %collective-permute-start.18 = (bf16[384,1536]{1,0:T(8,128)(2,1)}, bf16[384,1536]{1,0:T(8,128)(2,1)}, u32[]{:S(2)}, u32[]{:S(2)}) collective-permute-start(bf16[384,1536]{1,0:T(8,128)(2,1)} %collective-permute-done.12.refs_3_.refs_1_), channel_id=1, source_target_pairs={{0,1},{1,0},{2,3},{3,2},{4,5},{5,4},{6,7},{7,6},{8,9},{9,8},{10,11... | collective-permute-start | bytes 3538952 | tf_op jit(solution)/shard_map/ppermute | solution.py:599
  76.0 1.6 copy-start.13
  76.0 19.7 %collective-permute-start.15 = (bf16[512,768]{1,0:T(8,128)(2,1)S(1)}, bf16[512,768]{1,0:T(8,128)(2,1)S(1)}, u32[]{:S(2)}, u32[]{:S(2)}) collective-permute-start(bf16[512,768]{1,0:T(8,128)(2,1)S(1)} %add_convert_fusion.4.refs_1_), channel_id=1, source_target_pairs={{0,2},{1,3},{2,0},{3,1},{4,6},{5,7},{6,4},{7,5},{8,10},{9,11},{10,... | collective-permute-start | bytes 2359304 | tf_op jit(solution)/shard_map/ppermute | solution.py:599
  96.6 13.5 %collective-permute-start.21 = (bf16[288,1536]{1,0:T(8,128)(2,1)}, bf16[288,1536]{1,0:T(8,128)(2,1)S(1)}, u32[]{:S(2)}, u32[]{:S(2)}) collective-permute-start(bf16[288,1536]{1,0:T(8,128)(2,1)} %later.26.refs_4_), channel_id=1, source_target_pairs={{0,1},{1,0},{2,3},{3,2},{4,5},{5,4},{6,7},{7,6},{8,9},{9,8},{10,11... | collective-permute-start | bytes 2654216 | tf_op jit(solution)/shard_map/ppermute | solution.py:599
  96.6 13.4 %collective-permute-start.14 = (bf16[512,768]{1,0:T(8,128)(2,1)}, bf16[512,768]{1,0:T(8,128)(2,1)}, u32[]{:S(2)}, u32[]{:S(2)}) collective-permute-start(bf16[512,768]{1,0:T(8,128)(2,1)} %get-tuple-element.62), channel_id=1, source_target_pairs={{0,1},{1,0},{2,3},{3,2},{4,5},{5,4},{6,7},{7,6},{8,9},{9,8},{10,11... | collective-permute-start | bytes 2359304 | tf_op jit(solution)/shard_map/ppermute | solution.py:599
  98.1 9.0 %collective-permute-start.16 = (bf16[96,1536]{1,0:T(8,128)(2,1)S(1)}, bf16[96,1536]{1,0:T(8,128)(2,1)S(1)}, u32[]{:S(2)}, u32[]{:S(2)}) collective-permute-start(bf16[96,1536]{1,0:T(8,128)(2,1)S(1)} %slice.219), channel_id=1, source_target_pairs={{0,2},{1,3},{2,0},{3,1},{4,6},{5,7},{6,4},{7,5},{8,10},{9,11},{10,... | collective-permute-start | bytes 884744 | tf_op jit(solution)/shard_map/ppermute | solution.py:599
  107.8 2.2 collective-permute-start.20
  141.7 5.7 %collective-permute-start.22 = (bf16[384,1536]{1,0:T(8,128)(2,1)}, bf16[384,1536]{1,0:T(8,128)(2,1)S(1)}, u32[]{:S(2)}, u32[]{:S(2)}) collective-permute-start(bf16[384,1536]{1,0:T(8,128)(2,1)} %get-tuple-element.67), channel_id=1, source_target_pairs={{0,1},{1,0},{2,3},{3,2},{4,5},{5,4},{6,7},{7,6},{8,9},{9,8},{10,11... | collective-permute-start | bytes 3538952 | tf_op jit(solution)/shard_map/ppermute | solution.py:599
  142.2 30.7 %collective-permute-start.24 = (bf16[1152,1536]{1,0:T(8,128)(2,1)}, bf16[1152,1536]{1,0:T(8,128)(2,1)}, u32[]{:S(2)}, u32[]{:S(2)}) collective-permute-start(bf16[1152,1536]{1,0:T(8,128)(2,1)} %get-tuple-element.74), channel_id=1, source_target_pairs={{0,1},{1,0},{2,3},{3,2},{4,5},{5,4},{6,7},{7,6},{8,9},{9,8},{10,11... | collective-permute-start | bytes 10616840 | tf_op jit(solution)/shard_map/ppermute | solution.py:599
  142.5 11.5 %collective-permute-start.23 = (bf16[512,768]{1,0:T(8,128)(2,1)}, bf16[512,768]{1,0:T(8,128)(2,1)}, u32[]{:S(2)}, u32[]{:S(2)}) collective-permute-start(bf16[512,768]{1,0:T(8,128)(2,1)} %get-tuple-element.70.g0), channel_id=1, source_target_pairs={{0,1},{1,0},{2,3},{3,2},{4,5},{5,4},{6,7},{7,6},{8,9},{9,8},{10,11... | collective-permute-start | bytes 2359304 | tf_op jit(solution)/shard_map/ppermute | solution.py:599
  142.9 27.5 %collective-permute-start.27 = (bf16[512,768]{1,0:T(8,128)(2,1)}, bf16[512,768]{1,0:T(8,128)(2,1)S(1)}, u32[]{:S(2)}, u32[]{:S(2)}) collective-permute-start(bf16[512,768]{1,0:T(8,128)(2,1)} %get-tuple-element.70.g0), channel_id=1, source_target_pairs={{0,2},{1,3},{2,0},{3,1},{4,6},{5,7},{6,4},{7,5},{8,10},{9,11},{10,... | collective-permute-start | bytes 2359304 | tf_op jit(solution)/shard_map/ppermute | solution.py:599
  147.4 1.0 copy-start.19
  150.0 3.4 %copy-start.11 = (bf16[288,1536]{1,0:T(8,128)(2,1)}, bf16[288,1536]{1,0:T(8,128)(2,1)S(1)}, u32[]{:S(2)}) copy-start(bf16[288,1536]{1,0:T(8,128)(2,1)S(1)} %add_convert_fusion.1.refs_2_) | copy-start | bytes 2654212
  150.1 22.0 %collective-permute-start.29 = (bf16[288,1536]{1,0:T(8,128)(2,1)S(1)}, bf16[288,1536]{1,0:T(8,128)(2,1)S(1)}, u32[]{:S(2)}, u32[]{:S(2)}) collective-permute-start(bf16[288,1536]{1,0:T(8,128)(2,1)S(1)} %add_convert_fusion.1.refs_2_), channel_id=1, source_target_pairs={{0,4},{4,0},{8,12},{12,8},{16,20},{20,16},{24,28},{28,24},{1,5},{5... | collective-permute-start | bytes 2654216 | tf_op jit(solution)/shard_map/ppermute | solution.py:573
  153.5 17.8 %collective-permute-start.25 = (bf16[96,1536]{1,0:T(8,128)(2,1)}, bf16[96,1536]{1,0:T(8,128)(2,1)S(1)}, u32[]{:S(2)}, u32[]{:S(2)}) collective-permute-start(bf16[96,1536]{1,0:T(8,128)(2,1)} %add_convert_fusion.6.refs_1_), channel_id=1, source_target_pairs={{0,2},{1,3},{2,0},{3,1},{4,6},{5,7},{6,4},{7,5},{8,10},{9,11},{10,... | collective-permute-start | bytes 884744 | tf_op jit(solution)/shard_map/ppermute | solution.py:599
  171.3 10.5 %collective-permute-start.28 = (bf16[512,768]{1,0:T(8,128)(2,1)}, bf16[512,768]{1,0:T(8,128)(2,1)}, u32[]{:S(2)}, u32[]{:S(2)}) collective-permute-start(bf16[512,768]{1,0:T(8,128)(2,1)} %later.31.g0.g2), channel_id=1, source_target_pairs={{0,1},{1,0},{2,3},{3,2},{4,5},{5,4},{6,7},{7,6},{8,9},{9,8},{10,11... | collective-permute-start | bytes 2359304 | tf_op jit(solution)/shard_map/ppermute | solution.py:599
  173.0 3.2 %copy-start.10 = (bf16[288,1536]{1,0:T(8,128)(2,1)S(1)}, bf16[288,1536]{1,0:T(8,128)(2,1)}, u32[]{:S(2)}) copy-start(bf16[288,1536]{1,0:T(8,128)(2,1)} %later.32) | copy-start | bytes 2654212
  178.6 1.0 copy-start.7
  178.6 1.7 copy-start.6
  178.6 31.0 %collective-permute-start.26 = (bf16[384,1536]{1,0:T(8,128)(2,1)S(1)}, bf16[384,1536]{1,0:T(8,128)(2,1)}, u32[]{:S(2)}, u32[]{:S(2)}) collective-permute-start(bf16[384,1536]{1,0:T(8,128)(2,1)S(1)} %get-tuple-element.207.refs_1_), channel_id=1, source_target_pairs={{0,4},{4,0},{8,12},{12,8},{16,20},{20,16},{24,28},{28,24},{1,5},{5... | collective-permute-start | bytes 3538952 | tf_op jit(solution)/shard_map/ppermute | solution.py:573
  180.3 29.3 %collective-permute-start.30 = (bf16[384,1536]{1,0:T(8,128)(2,1)S(1)}, bf16[384,1536]{1,0:T(8,128)(2,1)}, u32[]{:S(2)}, u32[]{:S(2)}) collective-permute-start(bf16[384,1536]{1,0:T(8,128)(2,1)S(1)} %copy-done.6), channel_id=1, source_target_pairs={{0,2},{1,3},{2,0},{3,1},{4,6},{5,7},{6,4},{7,5},{8,10},{9,11},{10,... | collective-permute-start | bytes 3538952 | tf_op jit(solution)/shard_map/ppermute | solution.py:599
  209.0 33.6 %collective-permute-start.33 = (bf16[384,768]{1,0:T(8,128)(2,1)}, bf16[384,768]{1,0:T(8,128)(2,1)S(1)}, u32[]{:S(2)}, u32[]{:S(2)}) collective-permute-start(bf16[384,768]{1,0:T(8,128)(2,1)} %get-tuple-element.91), channel_id=1, source_target_pairs={{0,4},{4,0},{8,12},{12,8},{16,20},{20,16},{24,28},{28,24},{1,5},{5... | collective-permute-start | bytes 1769480 | tf_op jit(solution)/shard_map/ppermute | solution.py:573
  216.6 25.2 %all-to-all-start.1 = ((f32[32,8,128]{2,1,0:T(8,128)}), f32[32,8,128]{2,1,0:T(8,128)S(1)}, u32[]{:S(2)}, u32[]{:S(2)}) async-start(f32[32,8,128]{2,1,0:T(8,128)} %bitcast.33), calls=%async_computation.1 | async-start | bytes 262144 | tf_op jit(solution)/shard_map/all_to_all | solution.py:768
  242.4 1.1 copy-start.4
  242.4 23.2 %collective-permute-start.31 = (bf16[1024,768]{1,0:T(8,128)(2,1)}, bf16[1024,768]{1,0:T(8,128)(2,1)S(1)}, u32[]{:S(2)}, u32[]{:S(2)}) collective-permute-start(bf16[1024,768]{1,0:T(8,128)(2,1)} %later.40), channel_id=1, source_target_pairs={{0,1},{1,0},{2,3},{3,2},{4,5},{5,4},{6,7},{7,6},{8,9},{9,8},{10,11... | collective-permute-start | bytes 4718600 | tf_op jit(solution)/shard_map/ppermute | solution.py:599
  243.5 15.0 %copy-start.2 = (bf16[384,768]{1,0:T(8,128)(2,1)}, bf16[384,768]{1,0:T(8,128)(2,1)S(1)}, u32[]{:S(2)}) copy-start(bf16[384,768]{1,0:T(8,128)(2,1)S(1)} %collective-permute-done.33.refs_3_) | copy-start | bytes 1769476
  243.6 16.4 %copy-start = (bf16[384,1536]{1,0:T(8,128)(2,1)S(1)}, bf16[384,1536]{1,0:T(8,128)(2,1)}, u32[]{:S(2)}) copy-start(bf16[384,1536]{1,0:T(8,128)(2,1)} %add_convert_fusion) | copy-start | bytes 3538948
  243.6 8.4 %collective-permute-start.34 = (bf16[96,768]{1,0:T(8,128)(2,1)S(1)}, bf16[96,768]{1,0:T(8,128)(2,1)S(1)}, u32[]{:S(2)}, u32[]{:S(2)}) collective-permute-start(bf16[96,768]{1,0:T(8,128)(2,1)S(1)} %get-tuple-element.188), channel_id=1, source_target_pairs={{0,8},{4,12},{8,0},{12,4},{16,24},{20,28},{24,16},{28,20},{1,9},{5... | collective-permute-start | bytes 442376 | tf_op jit(solution)/shard_map/ppermute | solution.py:573
  244.4 14.0 %collective-permute-start.35 = (bf16[96,768]{1,0:T(8,128)(2,1)S(1)}, bf16[96,768]{1,0:T(8,128)(2,1)S(1)}, u32[]{:S(2)}, u32[]{:S(2)}) collective-permute-start(bf16[96,768]{1,0:T(8,128)(2,1)S(1)} %get-tuple-element.190), channel_id=1, source_target_pairs={{0,16},{4,20},{8,24},{12,28},{16,0},{20,4},{24,8},{28,12},{1,17},{... | collective-permute-start | bytes 442376 | tf_op jit(solution)/shard_map/ppermute | solution.py:573
  246.4 11.9 %collective-permute-start.36 = (bf16[96,768]{1,0:T(8,128)(2,1)S(1)}, bf16[96,768]{1,0:T(8,128)(2,1)S(1)}, u32[]{:S(2)}, u32[]{:S(2)}) collective-permute-start(bf16[96,768]{1,0:T(8,128)(2,1)S(1)} %get-tuple-element.189), channel_id=1, source_target_pairs={{0,24},{4,28},{8,16},{12,20},{16,8},{20,12},{24,0},{28,4},{1,25},{... | collective-permute-start | bytes 442376 | tf_op jit(solution)/shard_map/ppermute | solution.py:573
  260.8 8.4 %copy-start.27 = (f32[8,128]{1,0:T(8,128)S(1)}, f32[8,128]{1,0:T(8,128)}, u32[]{:S(2)}) copy-start(f32[8,128]{1,0:T(8,128)} %reduce_sum.71) | copy-start | bytes 12292
  260.8 13.4 %collective-permute-start.37 = (bf16[96,1536]{1,0:T(8,128)(2,1)S(1)}, bf16[96,1536]{1,0:T(8,128)(2,1)}, u32[]{:S(2)}, u32[]{:S(2)}) collective-permute-start(bf16[96,1536]{1,0:T(8,128)(2,1)S(1)} %get-tuple-element.183), channel_id=1, source_target_pairs={{0,8},{4,12},{8,0},{12,4},{16,24},{20,28},{24,16},{28,20},{1,9},{5... | collective-permute-start | bytes 884744 | tf_op jit(solution)/shard_map/ppermute | solution.py:573
  263.2 23.7 %collective-permute-start.38 = (bf16[96,1536]{1,0:T(8,128)(2,1)}, bf16[96,1536]{1,0:T(8,128)(2,1)S(1)}, u32[]{:S(2)}, u32[]{:S(2)}) collective-permute-start(bf16[96,1536]{1,0:T(8,128)(2,1)} %get-tuple-element.185), channel_id=1, source_target_pairs={{0,16},{4,20},{8,24},{12,28},{16,0},{20,4},{24,8},{28,12},{1,17},{... | collective-permute-start | bytes 884744 | tf_op jit(solution)/shard_map/ppermute | solution.py:573
  264.0 23.7 %collective-permute-start.39 = (bf16[96,1536]{1,0:T(8,128)(2,1)}, bf16[96,1536]{1,0:T(8,128)(2,1)S(1)}, u32[]{:S(2)}, u32[]{:S(2)}) collective-permute-start(bf16[96,1536]{1,0:T(8,128)(2,1)} %get-tuple-element.184), channel_id=1, source_target_pairs={{0,24},{4,28},{8,16},{12,20},{16,8},{20,12},{24,0},{28,4},{1,25},{... | collective-permute-start | bytes 884744 | tf_op jit(solution)/shard_map/ppermute | solution.py:573
  267.8 23.1 %collective-permute-start.32 = (bf16[512,768]{1,0:T(8,128)(2,1)}, bf16[512,768]{1,0:T(8,128)(2,1)}, u32[]{:S(2)}, u32[]{:S(2)}) collective-permute-start(bf16[512,768]{1,0:T(8,128)(2,1)} %add_convert_fusion.3), channel_id=1, source_target_pairs={{0,2},{1,3},{2,0},{3,1},{4,6},{5,7},{6,4},{7,5},{8,10},{9,11},{10,... | collective-permute-start | bytes 2359304 | tf_op jit(solution)/shard_map/ppermute | solution.py:599
  287.6 1.1 copy-start.18
  288.7 2.2 copy-start.1
  288.7 2.2 copy-start.15
  (11 other events, 9.2 us)

commit v7 on v6

--- a/solution.py
+++ b/solution.py
@@ -532,7 +532,7 @@
         scratch_shapes=[V((4, model, width), f32), V((4, size, model), bf16), V((4, size, model), bf16), V((model, size), bf16), V((model, size), bf16),
             pltpu.SemaphoreType.DMA((2, 4))],
         compiler_params=pltpu.CompilerParams(dimension_semantics=("arbitrary",), vmem_limit_bytes=60 << 20),
-        cost_estimate=pl.CostEstimate(flops=8 * size * model * width, bytes_accessed=24 * size * model, transcendentals=0),
+        cost_estimate=pl.CostEstimate(flops=40 * size * model * width, bytes_accessed=24 * size * model, transcendentals=0),
         name="projection_grads",
     )(home, *tokens, *grads, *contextT, *dqT, dk, dv)
 

time: 295 us -> 292 us (0.990)
  Pallas kernels: 112 us -> 126 us
  starting transfers between devices: 62.9 us -> 51.3 us
    all_to_all x1, starting transfers between devices: 17 us -> 4.8 us  [on_device(): lax.all_to_all(send, everyone, 0, 0, tiled=True).reshape(world, slots * 128)]
    pallas_call x2, Pallas kernels: 33.8 us -> 42.6 us  [attn_bwd(): pl.pallas_call(functools.partial(bwd_kernel, first), out_shape=(jax.Shape...]
    pallas_call x2, Pallas kernels: 21 us -> 26.3 us  [attn_fwd(): pl.pallas_call(functools.partial(fwd_kernel, first), out_shape=(jax.Shape...]
    ppermute x22, waiting for transfers between devices: 15.5 us -> 12.4 us  [exchange(): return lax.ppermute(value, 'tensor', [(i, i ^ bit) for i in range(4)])]
    unnamed x76 -> x72, local copies, waits for them, and re-layouts: 15.9 us -> 13.4 us
  transfers between devices with their start and end apart: 42 -> 42, of which waited for: 13 -> 11; matrix products, arithmetic and copies ran while one was open for 15% -> 15% of each run, Pallas kernels for 28% -> 33%
where the time goes in v7:
time: 292 us; the launch traced here: 291 us
  Pallas kernels  126 us (43%)
  waiting for transfers between devices  56.7 us (19%)
  starting transfers between devices  51.3 us (18%)
  other arithmetic  27.9 us (10%)
  local copies, waits for them, and re-layouts  27.3 us (9%)
    pallas_call x2, Pallas kernels, attn_bwd(): pl.pallas_call(functools.partial(bwd_kernel, first), out_shape=(jax.Shape...  42.6 us
    ppermute x18, waiting for transfers between devices, hop(): return lax.ppermute(value, 'dp', [(i, i ^ bit) for i in range(count)])  37.1 us
    pallas_call x1, Pallas kernels, ffn(): pl.pallas_call(functools.partial(ffn_kernel, count), out_shape=(jax.Shape...  30.6 us
    ppermute x18, starting transfers between devices, hop(): return lax.ppermute(value, 'dp', [(i, i ^ bit) for i in range(count)])  27.3 us
    pallas_call x2, Pallas kernels, attn_fwd(): pl.pallas_call(functools.partial(fwd_kernel, first), out_shape=(jax.Shape...  26.3 us
    ppermute x22, starting transfers between devices, exchange(): return lax.ppermute(value, 'tensor', [(i, i ^ bit) for i in range(4)])  14.2 us
    unnamed x72, local copies, waits for them, and re-layouts  13.4 us
    ppermute x22, waiting for transfers between devices, exchange(): return lax.ppermute(value, 'tensor', [(i, i ^ bit) for i in range(4)])  12.4 us
  transfers between devices with their start and end apart: 42, of which 11 were waited for; matrix products, arithmetic and copies ran while one was open for 15% of the time, Pallas kernels for 33%

profile of v7, /device:TPU:0, one launch (start us, length us, event | category | flops | bytes accessed | tf_op | source)
XLA Modules:
  0.0 290.7 jit_solution(2990725884310350617)
XLA Ops:
  0.7 0.9 copy.96
  1.5 1.0 pad_maximum_fusion.5
  2.5 3.1 %collective-permute-start.6 = (bf16[96,768]{1,0:T(8,128)(2,1)S(1)}, bf16[96,768]{1,0:T(8,128)(2,1)S(1)}, u32[]{:S(2)}, u32[]{:S(2)}) collective-permute-start(bf16[96,768]{1,0:T(8,128)(2,1)S(1)} %pad_maximum_fusion.5), channel_id=1, source_target_pairs={{0,8},{4,12},{8,0},{12,4},{16,24},{20,28},{24,16},{28,20},{1,9},{5... | collective-permute-start | bytes 442376 | tf_op jit(solution)/shard_map/ppermute | solution.py:573
  5.6 2.6 collective-permute-start.7
  8.2 1.7 collective-permute-start.4
  10.6 0.9 concatenate.30
  12.1 5.0 %all-to-all-start = ((f32[32,8,128]{2,1,0:T(8,128)}), f32[32,8,128]{2,1,0:T(8,128)S(1)}, u32[]{:S(2)}, u32[]{:S(2)}) async-start(f32[32,8,128]{2,1,0:T(8,128)} %broadcast_in_dim.46), calls=%async_computation | async-start | bytes 262144 | tf_op jit(solution)/shard_map/all_to_all | solution.py:702
  17.2 1.0 pad_maximum_fusion.4
  18.3 1.8 collective-permute-start
  20.1 2.4 collective-permute-start.1
  22.7 1.0 pad_maximum_fusion.3.wa_ref
  23.7 5.8 %all-to-all-done = f32[32,8,128]{2,1,0:T(8,128)S(1)} async-done(((f32[32,8,128]{2,1,0:T(8,128)}), f32[32,8,128]{2,1,0:T(8,128)S(1)}, u32[]{:S(2)}, u32[]{:S(2)}) %all-to-all-start) | async-done | bytes 131104 | tf_op jit(solution)/shard_map/all_to_all | solution.py:702
  32.4 2.5 collective-permute-done
  35.0 1.6 collective-permute-start.9
  38.6 1.4 copy.112
  40.4 3.1 %collective-permute-done.1 = bf16[96,1536]{1,0:T(8,128)(2,1)S(1)} collective-permute-done((bf16[96,1536]{1,0:T(8,128)(2,1)S(1)}, bf16[96,1536]{1,0:T(8,128)(2,1)S(1)}, u32[]{:S(2)}, u32[]{:S(2)}) %collective-permute-start.1) | collective-permute-done | bytes 294944 | tf_op jit(solution)/shard_map/ppermute | solution.py:573
  43.7 1.5 collective-permute-start.12
  45.2 1.5 collective-permute-start.13
  46.7 4.6 %collective-permute-done.9.wb_ref = bf16[384,768]{1,0:T(8,128)(2,1)} collective-permute-done((bf16[384,768]{1,0:T(8,128)(2,1)S(1)}, bf16[384,768]{1,0:T(8,128)(2,1)}, u32[]{:S(2)}, u32[]{:S(2)}) %collective-permute-start.9) | collective-permute-done | bytes 589856 | tf_op jit(solution)/shard_map/ppermute | solution.py:573
  51.3 10.0 %projection.1 = (bf16[192,2048]{1,0:T(8,128)(2,1)}, bf16[192,2048]{1,0:T(8,128)(2,1)}, bf16[192,2048]{1,0:T(8,128)(2,1)}, bf16[2048,192]{1,0:T(8,128)(2,1)}, bf1...) custom-call(s32[1]{0:T(128)} %bitcast.home_ref, bf16[512,768]{1,0:T(8,128)(2,1)} %x0.3, ...), custom_call_target="tpu_custom_call" | custom-call | flops 9059696640 | bytes 6291456 | tf_op jit(solution)/shard_map/projection/pallas_call | solution.py:448
  61.3 13.2 %attention.2 = (bf16[192,1024]{1,0:T(8,128)(2,1)}, f32[8,1024]{1,0:T(8,128)}, bf16[512,768]{1,0:T(8,128)(2,1)}, bf16[512,768]{1,0:T(8,128)(2,1)}) custom-call(s32[4]{0:T(128)} %later.22.lo_ref, s32[4]{0:T(128)} %and_select_fusion.hi_ref, s32[1]{0:T(128)} %bitcast.5.flip_ref, bf16[192,2048]{1,0:T(8,128)(2,1)} %get-tuple-element.55.q_ref, ...), custom_call_target="tpu_custom_call" | custom-call | flops 20132659200 | bytes 1572864 | tf_op jit(solution)/shard_map/attention/pallas_call | solution.py:82
  75.1 1.1 slice.220
  76.2 1.6 collective-permute-start.17
  78.5 1.6 collective-permute-start.15
  80.0 13.1 %attention.3 = (bf16[192,1024]{1,0:T(8,128)(2,1)}, f32[8,1024]{1,0:T(8,128)}, bf16[512,768]{1,0:T(8,128)(2,1)}, bf16[512,768]{1,0:T(8,128)(2,1)}) custom-call(s32[4]{0:T(128)} %later.23.lo_ref, s32[4]{0:T(128)} %and_select_fusion.hi_ref, s32[1]{0:T(128)} %bitcast.5.flip_ref, bf16[192,2048]{1,0:T(8,128)(2,1)} %get-tuple-element.55.q_ref, ...), custom_call_target="tpu_custom_call" | custom-call | flops 20132659200 | bytes 1572864 | tf_op jit(solution)/shard_map/attention/pallas_call | solution.py:82
  93.2 4.8 %collective-permute-done.15.refs_0_ = bf16[512,768]{1,0:T(8,128)(2,1)S(1)} collective-permute-done((bf16[512,768]{1,0:T(8,128)(2,1)S(1)}, bf16[512,768]{1,0:T(8,128)(2,1)S(1)}, u32[]{:S(2)}, u32[]{:S(2)}) %collective-permute-start.15) | collective-permute-done | bytes 786464 | tf_op jit(solution)/shard_map/ppermute | solution.py:599
  98.0 0.9 copy-done.3
  99.4 1.0 slice.219
  100.4 1.6 collective-permute-start.16
  102.0 7.5 %collective-permute-done.16.refs_0_ = bf16[96,1536]{1,0:T(8,128)(2,1)S(1)} collective-permute-done((bf16[96,1536]{1,0:T(8,128)(2,1)S(1)}, bf16[96,1536]{1,0:T(8,128)(2,1)S(1)}, u32[]{:S(2)}, u32[]{:S(2)}) %collective-permute-start.16) | collective-permute-done | bytes 294944 | tf_op jit(solution)/shard_map/ppermute | solution.py:599
  113.8 30.6 %feed_forward.1 = (bf16[512,768]{1,0:T(8,128)(2,1)}, f32[512,768]{1,0:T(8,128)}, bf16[512,768]{1,0:T(8,128)(2,1)}, f32[6,8,768]{2,1,0:T(8,128)}, f32[4,8,768]{2,...) custom-call(s32[1]{0:T(128)} %bitcast.home_ref, ...), custom_call_target="tpu_custom_call" | custom-call | flops 36238786560 | bytes 18874368 | tf_op jit(solution)/shard_map/feed_forward/pallas_call | solution.py:379
  145.7 1.5 collective-permute-start.27
  147.2 0.9 reduce_sum.69
  148.4 0.9 reduce_sum.70
  150.1 1.4 add_convert_fusion.1.refs_2_
  151.5 0.9 collective-permute-start.29
  152.4 1.7 add_convert_fusion.6.refs_1_
  154.7 20.8 %attention_back.2 = (bf16[192,1024]{1,0:T(8,128)(2,1)}, f32[2048,192]{1,0:T(8,128)}, f32[2048,192]{1,0:T(8,128)}, f32[192,128]{1,0:T(8,128)}) custom-call(s32[4]{0:T(128)} %later.29.lo_ref, s32[4]{0:T(128)} %and_select_fusion.hi_ref, s32[1]{0:T(128)} %bitcast.5.flip_ref, bf16[192,2048]{1,0:T(8,128)(2,1)} %get-tuple-element.55.q_ref, ...), custom_call_target="tpu_custom_call" | custom-call | flops 24159191040 | bytes 3932160 | tf_op jit(solution)/shard_map/attention_back/pallas_call | solution.py:171
  176.4 0.9 copy-done.9
  177.3 3.1 %convert_add_fusion.1 = (f32[384,1536]{1,0:T(8,128)S(1)}, f32[384,1536]{1,0:T(8,128)S(1)}) fusion(bf16[1152,1536]{1,0:T(8,128)(2,1)} %collective-permute-done.24, bf16[1152,1536]{1,0:T(8,128)(2,1)} %get-tuple-element.73), kind=kLoop, calls=%fused_computation.5 | loop fusion | flops 3538944 | bytes 9437184 | tf_op jit(solution)/shard_map/add | solution.py:636
  181.7 1.3 pad_maximum_fusion.1
  183.0 1.1 collective-permute-start.26
  184.7 1.5 collective-permute-start.30
  186.2 21.8 %attention_back.3 = (bf16[192,1024]{1,0:T(8,128)(2,1)}, bf16[2048,192]{1,0:T(8,128)(2,1)}, bf16[2048,192]{1,0:T(8,128)(2,1)}, f32[192,128]{1,0:T(8,128)}, f32[8,192]{1,0:T(8,128)}) custom-call(s32[4]{0:T(128)} %later.33.lo_ref, s32[4]{0:T(128)} %and_select_fusion.hi_ref, s32[1]{0:T(128)} %bitcast.5.flip_ref, bf16[192,2048]{1,0:T(8,128)(2,1)} %get-tuple-element.55.q_ref, ...), custom_call_target="tpu_custom_call" | custom-call | flops 24159191040 | bytes 3932160 | tf_op jit(solution)/shard_map/attention_back/pallas_call | solution.py:171
  208.0 9.8 %projection_grads.1 = (bf16[384,768]{1,0:T(8,128)(2,1)}, bf16[384,768]{1,0:T(8,128)(2,1)}) custom-call(s32[1]{0:T(128)} %bitcast.home_ref, bf16[512,768]{1,0:T(8,128)(2,1)} %x0.3, bf16[512,768]{1,0:T(8,128)(2,1)} %collective-permute-done.3.x1, bf16[512,768]{1,0:T(8,128)(2,1)} %collective-permute-done.4.x2, bf16[512,768]{1,0:T(8,128)(2,1)} %collective-permute-done.5.x3, ...), custom_call_target="tpu_custom_call" | custom-call | flops 3019898880 | bytes 9437184 | tf_op jit(solution)/shard_map/projection_grads/pallas_call | solution.py:526
  217.8 1.2 collective-permute-start.33
  219.0 4.0 %add_convert_fusion = bf16[384,1536]{1,0:T(8,128)(2,1)} fusion(bf16[384,1536]{1,0:T(8,128)(2,1)} %later.35, bf16[384,1536]{1,0:T(8,128)(2,1)} %later.34, bf16[1152,1536]{1,0:T(8,128)(2,1)} %collective-permute-done.24, bf16[1152,1536]{1,0:T(8,128)(2,1)} %get-tuple-element.73), kind=kLoop, calls=%fused_computation.3 | loop fusion | flops 4718592 | bytes 5898240 | tf_op jit(solution)/shard_map/convert_element_type | solution.py:657
  223.9 1.0 add_reduce_fusion
  226.0 4.8 %all-to-all-start.1 = ((f32[32,8,128]{2,1,0:T(8,128)}), f32[32,8,128]{2,1,0:T(8,128)S(1)}, u32[]{:S(2)}, u32[]{:S(2)}) async-start(f32[32,8,128]{2,1,0:T(8,128)} %bitcast.33), calls=%async_computation.1 | async-start | bytes 262144 | tf_op jit(solution)/shard_map/all_to_all | solution.py:768
  230.8 6.8 %projection_back.1 = (bf16[512,768]{1,0:T(8,128)(2,1)}, bf16[1024,768]{1,0:T(8,128)(2,1)}, bf16[512,768]{1,0:T(8,128)(2,1)}) custom-call(bf16[192,1024]{1,0:T(8,128)(2,1)} %later.36.qa_ref, bf16[192,1024]{1,0:T(8,128)(2,1)} %get-tuple-element.80.qb_ref, bf16[2048,192]{1,0:T(8,128)(2,1)} %get-tuple-element.81.k_ref, ...), custom_call_target="tpu_custom_call" | custom-call | flops 21139292160 | bytes 12582912 | tf_op jit(solution)/shard_map/projection_back/pallas_call | solution.py:559
  237.6 1.4 all-to-all-done.1
  241.7 2.1 collective-permute-start.35
  243.7 1.6 collective-permute-start.36
  245.4 3.9 %collective-permute-done.34 = bf16[96,768]{1,0:T(8,128)(2,1)S(1)} collective-permute-done((bf16[96,768]{1,0:T(8,128)(2,1)S(1)}, bf16[96,768]{1,0:T(8,128)(2,1)S(1)}, u32[]{:S(2)}, u32[]{:S(2)}) %collective-permute-start.34) | collective-permute-done | bytes 147488 | tf_op jit(solution)/shard_map/ppermute | solution.py:573
  249.3 6.3 %collective-permute-done.35 = bf16[96,768]{1,0:T(8,128)(2,1)S(1)} collective-permute-done((bf16[96,768]{1,0:T(8,128)(2,1)S(1)}, bf16[96,768]{1,0:T(8,128)(2,1)S(1)}, u32[]{:S(2)}, u32[]{:S(2)}) %collective-permute-start.35) | collective-permute-done | bytes 147488 | tf_op jit(solution)/shard_map/ppermute | solution.py:573
  257.3 0.9 fusion.4
  258.1 2.4 collective-permute-start.37
  261.3 1.6 collective-permute-start.39
  262.9 2.2 add_convert_fusion.3
  265.1 1.4 collective-permute-start.32
  267.7 3.8 %collective-permute-done.37.refs_0_ = bf16[96,1536]{1,0:T(8,128)(2,1)} collective-permute-done((bf16[96,1536]{1,0:T(8,128)(2,1)S(1)}, bf16[96,1536]{1,0:T(8,128)(2,1)}, u32[]{:S(2)}, u32[]{:S(2)}) %collective-permute-start.37) | collective-permute-done | bytes 294944 | tf_op jit(solution)/shard_map/ppermute | solution.py:573
  271.5 12.7 %collective-permute-done.38.refs_0_ = bf16[96,1536]{1,0:T(8,128)(2,1)S(1)} collective-permute-done((bf16[96,1536]{1,0:T(8,128)(2,1)}, bf16[96,1536]{1,0:T(8,128)(2,1)S(1)}, u32[]{:S(2)}, u32[]{:S(2)}) %collective-permute-start.38) | collective-permute-done | bytes 294944 | tf_op jit(solution)/shard_map/ppermute | solution.py:573
  286.0 1.3 add_add_fusion
  288.2 2.4 add_convert_fusion.2
  (203 shorter events, 29.4 us)
Async XLA Ops:
  2.5 15.7 %collective-permute-start.6 = (bf16[96,768]{1,0:T(8,128)(2,1)S(1)}, bf16[96,768]{1,0:T(8,128)(2,1)S(1)}, u32[]{:S(2)}, u32[]{:S(2)}) collective-permute-start(bf16[96,768]{1,0:T(8,128)(2,1)S(1)} %pad_maximum_fusion.5), channel_id=1, source_target_pairs={{0,8},{4,12},{8,0},{12,4},{16,24},{20,28},{24,16},{28,20},{1,9},{5... | collective-permute-start | bytes 442376 | tf_op jit(solution)/shard_map/ppermute | solution.py:573
  5.6 14.5 %collective-permute-start.7 = (bf16[96,768]{1,0:T(8,128)(2,1)S(1)}, bf16[96,768]{1,0:T(8,128)(2,1)S(1)}, u32[]{:S(2)}, u32[]{:S(2)}) collective-permute-start(bf16[96,768]{1,0:T(8,128)(2,1)S(1)} %pad_maximum_fusion.5), channel_id=1, source_target_pairs={{0,16},{4,20},{8,24},{12,28},{16,0},{20,4},{24,8},{28,12},{1,17},{... | collective-permute-start | bytes 442376 | tf_op jit(solution)/shard_map/ppermute | solution.py:573
  8.2 14.3 %collective-permute-start.8 = (bf16[96,768]{1,0:T(8,128)(2,1)S(1)}, bf16[96,768]{1,0:T(8,128)(2,1)S(1)}, u32[]{:S(2)}, u32[]{:S(2)}) collective-permute-start(bf16[96,768]{1,0:T(8,128)(2,1)S(1)} %pad_maximum_fusion.5), channel_id=1, source_target_pairs={{0,24},{4,28},{8,16},{12,20},{16,8},{20,12},{24,0},{28,4},{1,25},{... | collective-permute-start | bytes 442376 | tf_op jit(solution)/shard_map/ppermute | solution.py:573
  8.2 22.5 %collective-permute-start.4 = (bf16[512,768]{1,0:T(8,128)(2,1)}, bf16[512,768]{1,0:T(8,128)(2,1)}, u32[]{:S(2)}, u32[]{:S(2)}) collective-permute-start(bf16[512,768]{1,0:T(8,128)(2,1)} %x0.3), channel_id=1, source_target_pairs={{0,2},{1,3},{2,0},{3,1},{4,6},{5,7},{6,4},{7,5},{8,10},{9,11},{10,... | collective-permute-start | bytes 2359304 | tf_op jit(solution)/shard_map/ppermute | solution.py:599
  9.9 41.4 %collective-permute-start.3 = (bf16[512,768]{1,0:T(8,128)(2,1)}, bf16[512,768]{1,0:T(8,128)(2,1)}, u32[]{:S(2)}, u32[]{:S(2)}) collective-permute-start(bf16[512,768]{1,0:T(8,128)(2,1)} %x0.3), channel_id=1, source_target_pairs={{0,1},{1,0},{2,3},{3,2},{4,5},{5,4},{6,7},{7,6},{8,9},{9,8},{10,11... | collective-permute-start | bytes 2359304 | tf_op jit(solution)/shard_map/ppermute | solution.py:599
  12.1 17.4 %all-to-all-start = ((f32[32,8,128]{2,1,0:T(8,128)}), f32[32,8,128]{2,1,0:T(8,128)S(1)}, u32[]{:S(2)}, u32[]{:S(2)}) async-start(f32[32,8,128]{2,1,0:T(8,128)} %broadcast_in_dim.46), calls=%async_computation | async-start | bytes 262144 | tf_op jit(solution)/shard_map/all_to_all | solution.py:702
  18.2 25.3 %copy-start.21 = (bf16[768,96]{0,1:T(8,128)(2,1)S(1)}, bf16[768,96]{0,1:T(8,128)(2,1)}, u32[]{:S(2)}) copy-start(bf16[768,96]{0,1:T(8,128)(2,1)} %param.33) | copy-start | bytes 442372
  18.2 25.3 %copy-start.22 = (bf16[96,768]{1,0:T(8,128)(2,1)S(1)}, bf16[96,768]{1,0:T(8,128)(2,1)}, u32[]{:S(2)}) copy-start(bf16[96,768]{1,0:T(8,128)(2,1)} %param.31) | copy-start | bytes 442372
  18.3 16.7 %collective-permute-start = (bf16[96,1536]{1,0:T(8,128)(2,1)S(1)}, bf16[96,1536]{1,0:T(8,128)(2,1)S(1)}, u32[]{:S(2)}, u32[]{:S(2)}) collective-permute-start(bf16[96,1536]{1,0:T(8,128)(2,1)S(1)} %pad_maximum_fusion.4), channel_id=1, source_target_pairs={{0,8},{4,12},{8,0},{12,4},{16,24},{20,28},{24,16},{28,20},{1,9},{5... | collective-permute-start | bytes 884744 | tf_op jit(solution)/shard_map/ppermute | solution.py:573
  20.1 23.4 %collective-permute-start.1 = (bf16[96,1536]{1,0:T(8,128)(2,1)S(1)}, bf16[96,1536]{1,0:T(8,128)(2,1)S(1)}, u32[]{:S(2)}, u32[]{:S(2)}) collective-permute-start(bf16[96,1536]{1,0:T(8,128)(2,1)S(1)} %pad_maximum_fusion.4), channel_id=1, source_target_pairs={{0,16},{4,20},{8,24},{12,28},{16,0},{20,4},{24,8},{28,12},{1,17},{... | collective-permute-start | bytes 884744 | tf_op jit(solution)/shard_map/ppermute | solution.py:573
  22.5 21.0 %collective-permute-start.2 = (bf16[96,1536]{1,0:T(8,128)(2,1)S(1)}, bf16[96,1536]{1,0:T(8,128)(2,1)S(1)}, u32[]{:S(2)}, u32[]{:S(2)}) collective-permute-start(bf16[96,1536]{1,0:T(8,128)(2,1)S(1)} %pad_maximum_fusion.4), channel_id=1, source_target_pairs={{0,24},{4,28},{8,16},{12,20},{16,8},{20,12},{24,0},{28,4},{1,25},{... | collective-permute-start | bytes 884744 | tf_op jit(solution)/shard_map/ppermute | solution.py:573
  23.7 20.0 %copy-start.23 = (bf16[384,768]{1,0:T(8,128)(2,1)}, bf16[384,768]{1,0:T(8,128)(2,1)S(1)}, u32[]{:S(2)}) copy-start(bf16[384,768]{1,0:T(8,128)(2,1)S(1)} %pad_maximum_fusion.3.wa_ref) | copy-start | bytes 1769476
  29.5 14.0 %copy-start.25 = (f32[4,8,8,128]{3,1,2,0:T(8,128)}, f32[4,8,8,128]{3,1,2,0:T(8,128)S(1)}, u32[]{:S(2)}) copy-start(f32[4,8,8,128]{3,1,2,0:T(8,128)S(1)} %copy.116) | copy-start | bytes 393220
  30.7 20.6 %collective-permute-start.5 = (bf16[512,768]{1,0:T(8,128)(2,1)}, bf16[512,768]{1,0:T(8,128)(2,1)}, u32[]{:S(2)}, u32[]{:S(2)}) collective-permute-start(bf16[512,768]{1,0:T(8,128)(2,1)} %collective-permute-done.4.x2), channel_id=1, source_target_pairs={{0,1},{1,0},{2,3},{3,2},{4,5},{5,4},{6,7},{7,6},{8,9},{9,8},{10,11... | collective-permute-start | bytes 2359304 | tf_op jit(solution)/shard_map/ppermute | solution.py:599
  30.8 12.9 %copy-start.29 = (s32[4]{0:T(128)}, s32[4]{0:T(128)S(1)}, u32[]{:S(2)}) copy-start(s32[4]{0:T(128)S(1)} %and_select_fusion.1.refs_0_) | copy-start | bytes 52
  35.0 16.3 %collective-permute-start.9 = (bf16[384,768]{1,0:T(8,128)(2,1)S(1)}, bf16[384,768]{1,0:T(8,128)(2,1)}, u32[]{:S(2)}, u32[]{:S(2)}) collective-permute-start(bf16[384,768]{1,0:T(8,128)(2,1)S(1)} %pad_maximum_fusion.3.wa_ref), channel_id=1, source_target_pairs={{0,4},{4,0},{8,12},{12,8},{16,20},{20,16},{24,28},{28,24},{1,5},{5... | collective-permute-start | bytes 1769480 | tf_op jit(solution)/shard_map/ppermute | solution.py:573
  36.8 6.8 %copy-start.28 = (f32[192]{0:T(256)}, f32[192]{0:T(256)S(1)}, u32[]{:S(2)}) copy-start(f32[192]{0:T(256)S(1)} %dynamic_slice.11) | copy-start | bytes 2308
  38.5 5.1 %copy-start.27 = (s32[1,1,4,512]{3,1,2,0:T(1,128)}, s32[1,1,4,512]{3,1,2,0:T(1,128)S(1)}, u32[]{:S(2)}) copy-start(s32[1,1,4,512]{3,1,2,0:T(1,128)S(1)} %copy.111) | copy-start | bytes 24580
  43.7 3.0 %copy-start.5 = (bf16[384,1536]{1,0:T(8,128)(2,1)}, bf16[384,1536]{1,0:T(8,128)(2,1)S(1)}, u32[]{:S(2)}) copy-start(bf16[384,1536]{1,0:T(8,128)(2,1)S(1)} %pad_maximum_fusion.refs_1_.refs_0_) | copy-start | bytes 3538948
  43.7 34.1 %collective-permute-start.12 = (bf16[384,1536]{1,0:T(8,128)(2,1)S(1)}, bf16[384,1536]{1,0:T(8,128)(2,1)}, u32[]{:S(2)}, u32[]{:S(2)}) collective-permute-start(bf16[384,1536]{1,0:T(8,128)(2,1)S(1)} %pad_maximum_fusion.refs_1_.refs_0_), channel_id=1, source_target_pairs={{0,4},{4,0},{8,12},{12,8},{16,20},{20,16},{24,28},{28,24},{1,5},{5... | collective-permute-start | bytes 3538952 | tf_op jit(solution)/shard_map/ppermute | solution.py:573
  45.2 29.9 %collective-permute-start.13 = (bf16[384,1536]{1,0:T(8,128)(2,1)S(1)}, bf16[384,1536]{1,0:T(8,128)(2,1)S(1)}, u32[]{:S(2)}, u32[]{:S(2)}) collective-permute-start(bf16[384,1536]{1,0:T(8,128)(2,1)S(1)} %pad_maximum_fusion.refs_1_.refs_0_), channel_id=1, source_target_pairs={{0,2},{1,3},{2,0},{3,1},{4,6},{5,7},{6,4},{7,5},{8,10},{9,11},{10,... | collective-permute-start | bytes 3538952 | tf_op jit(solution)/shard_map/ppermute | solution.py:599
  51.3 28.7 %collective-permute-start.11 = (bf16[384,1536]{1,0:T(8,128)(2,1)}, bf16[384,1536]{1,0:T(8,128)(2,1)}, u32[]{:S(2)}, u32[]{:S(2)}) collective-permute-start(bf16[384,1536]{1,0:T(8,128)(2,1)} %copy-done.5), channel_id=1, source_target_pairs={{0,1},{1,0},{2,3},{3,2},{4,5},{5,4},{6,7},{7,6},{8,9},{9,8},{10,11... | collective-permute-start | bytes 3538952 | tf_op jit(solution)/shard_map/ppermute | solution.py:599
  74.5 3.8 %copy-start.20 = (bf16[512,768]{1,0:T(8,128)(2,1)S(1)}, bf16[512,768]{1,0:T(8,128)(2,1)}, u32[]{:S(2)}) copy-start(bf16[512,768]{1,0:T(8,128)(2,1)} %get-tuple-element.59) | copy-start | bytes 2359300
  74.5 3.7 %collective-permute-start.10 = (bf16[512,768]{1,0:T(8,128)(2,1)}, bf16[512,768]{1,0:T(8,128)(2,1)S(1)}, u32[]{:S(2)}, u32[]{:S(2)}) collective-permute-start(bf16[512,768]{1,0:T(8,128)(2,1)} %get-tuple-element.60), channel_id=1, source_target_pairs={{0,1},{1,0},{2,3},{3,2},{4,5},{5,4},{6,7},{7,6},{8,9},{9,8},{10,11... | collective-permute-start | bytes 2359304 | tf_op jit(solution)/shard_map/ppermute | solution.py:599
  75.1 3.4 %copy-start.8 = (bf16[384,1536]{1,0:T(8,128)(2,1)}, bf16[384,1536]{1,0:T(8,128)(2,1)S(1)}, u32[]{:S(2)}) copy-start(bf16[384,1536]{1,0:T(8,128)(2,1)S(1)} %collective-permute-done.13.refs_4_.refs_2_) | copy-start | bytes 3538948
  76.2 22.7 %collective-permute-start.17 = (bf16[288,1536]{1,0:T(8,128)(2,1)}, bf16[288,1536]{1,0:T(8,128)(2,1)}, u32[]{:S(2)}, u32[]{:S(2)}) collective-permute-start(bf16[288,1536]{1,0:T(8,128)(2,1)} %slice.220), channel_id=1, source_target_pairs={{0,4},{4,0},{8,12},{12,8},{16,20},{20,16},{24,28},{28,24},{1,5},{5... | collective-permute-start | bytes 2654216 | tf_op jit(solution)/shard_map/ppermute | solution.py:573
  77.8 35.3 %collective-permute-start.19 = (bf16[384,1536]{1,0:T(8,128)(2,1)S(1)}, bf16[384,1536]{1,0:T(8,128)(2,1)}, u32[]{:S(2)}, u32[]{:S(2)}) collective-permute-start(bf16[384,1536]{1,0:T(8,128)(2,1)S(1)} %collective-permute-done.13.refs_4_.refs_2_), channel_id=1, source_target_pairs={{0,1},{1,0},{2,3},{3,2},{4,5},{5,4},{6,7},{7,6},{8,9},{9,8},{10,11... | collective-permute-start | bytes 3538952 | tf_op jit(solution)/shard_map/ppermute | solution.py:599
  77.8 35.3 %collective-permute-start.18 = (bf16[384,1536]{1,0:T(8,128)(2,1)}, bf16[384,1536]{1,0:T(8,128)(2,1)}, u32[]{:S(2)}, u32[]{:S(2)}) collective-permute-start(bf16[384,1536]{1,0:T(8,128)(2,1)} %collective-permute-done.12.refs_3_.refs_1_), channel_id=1, source_target_pairs={{0,1},{1,0},{2,3},{3,2},{4,5},{5,4},{6,7},{7,6},{8,9},{9,8},{10,11... | collective-permute-start | bytes 3538952 | tf_op jit(solution)/shard_map/ppermute | solution.py:599
  78.5 1.6 copy-start.12
  78.5 19.5 %collective-permute-start.15 = (bf16[512,768]{1,0:T(8,128)(2,1)S(1)}, bf16[512,768]{1,0:T(8,128)(2,1)S(1)}, u32[]{:S(2)}, u32[]{:S(2)}) collective-permute-start(bf16[512,768]{1,0:T(8,128)(2,1)S(1)} %add_convert_fusion.4.refs_1_), channel_id=1, source_target_pairs={{0,2},{1,3},{2,0},{3,1},{4,6},{5,7},{6,4},{7,5},{8,10},{9,11},{10,... | collective-permute-start | bytes 2359304 | tf_op jit(solution)/shard_map/ppermute | solution.py:599
  98.9 14.2 %collective-permute-start.21 = (bf16[288,1536]{1,0:T(8,128)(2,1)}, bf16[288,1536]{1,0:T(8,128)(2,1)}, u32[]{:S(2)}, u32[]{:S(2)}) collective-permute-start(bf16[288,1536]{1,0:T(8,128)(2,1)} %later.26.refs_4_), channel_id=1, source_target_pairs={{0,1},{1,0},{2,3},{3,2},{4,5},{5,4},{6,7},{7,6},{8,9},{9,8},{10,11... | collective-permute-start | bytes 2654216 | tf_op jit(solution)/shard_map/ppermute | solution.py:599
  98.9 14.2 %collective-permute-start.14 = (bf16[512,768]{1,0:T(8,128)(2,1)}, bf16[512,768]{1,0:T(8,128)(2,1)}, u32[]{:S(2)}, u32[]{:S(2)}) collective-permute-start(bf16[512,768]{1,0:T(8,128)(2,1)} %get-tuple-element.62), channel_id=1, source_target_pairs={{0,1},{1,0},{2,3},{3,2},{4,5},{5,4},{6,7},{7,6},{8,9},{9,8},{10,11... | collective-permute-start | bytes 2359304 | tf_op jit(solution)/shard_map/ppermute | solution.py:599
  100.4 9.0 %collective-permute-start.16 = (bf16[96,1536]{1,0:T(8,128)(2,1)S(1)}, bf16[96,1536]{1,0:T(8,128)(2,1)S(1)}, u32[]{:S(2)}, u32[]{:S(2)}) collective-permute-start(bf16[96,1536]{1,0:T(8,128)(2,1)S(1)} %slice.219), channel_id=1, source_target_pairs={{0,2},{1,3},{2,0},{3,1},{4,6},{5,7},{6,4},{7,5},{8,10},{9,11},{10,... | collective-permute-start | bytes 884744 | tf_op jit(solution)/shard_map/ppermute | solution.py:599
  110.2 2.9 %collective-permute-start.20 = (bf16[96,1536]{1,0:T(8,128)(2,1)}, bf16[96,1536]{1,0:T(8,128)(2,1)S(1)}, u32[]{:S(2)}, u32[]{:S(2)}) collective-permute-start(bf16[96,1536]{1,0:T(8,128)(2,1)} %later.25.refs_3_), channel_id=1, source_target_pairs={{0,1},{1,0},{2,3},{3,2},{4,5},{5,4},{6,7},{7,6},{8,9},{9,8},{10,11... | collective-permute-start | bytes 884744 | tf_op jit(solution)/shard_map/ppermute | solution.py:599
  144.4 5.6 %collective-permute-start.22 = (bf16[384,1536]{1,0:T(8,128)(2,1)}, bf16[384,1536]{1,0:T(8,128)(2,1)S(1)}, u32[]{:S(2)}, u32[]{:S(2)}) collective-permute-start(bf16[384,1536]{1,0:T(8,128)(2,1)} %get-tuple-element.67), channel_id=1, source_target_pairs={{0,1},{1,0},{2,3},{3,2},{4,5},{5,4},{6,7},{7,6},{8,9},{9,8},{10,11... | collective-permute-start | bytes 3538952 | tf_op jit(solution)/shard_map/ppermute | solution.py:599
  145.0 32.3 %collective-permute-start.24 = (bf16[1152,1536]{1,0:T(8,128)(2,1)}, bf16[1152,1536]{1,0:T(8,128)(2,1)}, u32[]{:S(2)}, u32[]{:S(2)}) collective-permute-start(bf16[1152,1536]{1,0:T(8,128)(2,1)} %get-tuple-element.74), channel_id=1, source_target_pairs={{0,1},{1,0},{2,3},{3,2},{4,5},{5,4},{6,7},{7,6},{8,9},{9,8},{10,11... | collective-permute-start | bytes 10616840 | tf_op jit(solution)/shard_map/ppermute | solution.py:599
  145.2 9.5 %collective-permute-start.23 = (bf16[512,768]{1,0:T(8,128)(2,1)}, bf16[512,768]{1,0:T(8,128)(2,1)}, u32[]{:S(2)}, u32[]{:S(2)}) collective-permute-start(bf16[512,768]{1,0:T(8,128)(2,1)} %get-tuple-element.70.g0), channel_id=1, source_target_pairs={{0,1},{1,0},{2,3},{3,2},{4,5},{5,4},{6,7},{7,6},{8,9},{9,8},{10,11... | collective-permute-start | bytes 2359304 | tf_op jit(solution)/shard_map/ppermute | solution.py:599
  145.7 29.9 %collective-permute-start.27 = (bf16[512,768]{1,0:T(8,128)(2,1)}, bf16[512,768]{1,0:T(8,128)(2,1)}, u32[]{:S(2)}, u32[]{:S(2)}) collective-permute-start(bf16[512,768]{1,0:T(8,128)(2,1)} %get-tuple-element.70.g0), channel_id=1, source_target_pairs={{0,2},{1,3},{2,0},{3,1},{4,6},{5,7},{6,4},{7,5},{8,10},{9,11},{10,... | collective-permute-start | bytes 2359304 | tf_op jit(solution)/shard_map/ppermute | solution.py:599
  151.5 2.7 copy-start.11
  151.5 24.9 %collective-permute-start.29 = (bf16[288,1536]{1,0:T(8,128)(2,1)S(1)}, bf16[288,1536]{1,0:T(8,128)(2,1)S(1)}, u32[]{:S(2)}, u32[]{:S(2)}) collective-permute-start(bf16[288,1536]{1,0:T(8,128)(2,1)S(1)} %add_convert_fusion.1.refs_2_), channel_id=1, source_target_pairs={{0,4},{4,0},{8,12},{12,8},{16,20},{20,16},{24,28},{28,24},{1,5},{5... | collective-permute-start | bytes 2654216 | tf_op jit(solution)/shard_map/ppermute | solution.py:573
  154.1 21.5 %collective-permute-start.25 = (bf16[96,1536]{1,0:T(8,128)(2,1)}, bf16[96,1536]{1,0:T(8,128)(2,1)S(1)}, u32[]{:S(2)}, u32[]{:S(2)}) collective-permute-start(bf16[96,1536]{1,0:T(8,128)(2,1)} %add_convert_fusion.6.refs_1_), channel_id=1, source_target_pairs={{0,2},{1,3},{2,0},{3,1},{4,6},{5,7},{6,4},{7,5},{8,10},{9,11},{10,... | collective-permute-start | bytes 884744 | tf_op jit(solution)/shard_map/ppermute | solution.py:599
  175.5 10.7 %collective-permute-start.28 = (bf16[512,768]{1,0:T(8,128)(2,1)}, bf16[512,768]{1,0:T(8,128)(2,1)}, u32[]{:S(2)}, u32[]{:S(2)}) collective-permute-start(bf16[512,768]{1,0:T(8,128)(2,1)} %later.31.g0.g2), channel_id=1, source_target_pairs={{0,1},{1,0},{2,3},{3,2},{4,5},{5,4},{6,7},{7,6},{8,9},{9,8},{10,11... | collective-permute-start | bytes 2359304 | tf_op jit(solution)/shard_map/ppermute | solution.py:599
  177.3 3.2 %copy-start.10 = (bf16[288,1536]{1,0:T(8,128)(2,1)S(1)}, bf16[288,1536]{1,0:T(8,128)(2,1)}, u32[]{:S(2)}) copy-start(bf16[288,1536]{1,0:T(8,128)(2,1)} %later.32) | copy-start | bytes 2654212
  183.0 1.1 copy-start.7
  183.0 1.7 copy-start.6
  183.0 36.0 %collective-permute-start.26 = (bf16[384,1536]{1,0:T(8,128)(2,1)S(1)}, bf16[384,1536]{1,0:T(8,128)(2,1)}, u32[]{:S(2)}, u32[]{:S(2)}) collective-permute-start(bf16[384,1536]{1,0:T(8,128)(2,1)S(1)} %get-tuple-element.207.refs_1_), channel_id=1, source_target_pairs={{0,4},{4,0},{8,12},{12,8},{16,20},{20,16},{24,28},{28,24},{1,5},{5... | collective-permute-start | bytes 3538952 | tf_op jit(solution)/shard_map/ppermute | solution.py:573
  184.7 34.3 %collective-permute-start.30 = (bf16[384,1536]{1,0:T(8,128)(2,1)S(1)}, bf16[384,1536]{1,0:T(8,128)(2,1)}, u32[]{:S(2)}, u32[]{:S(2)}) collective-permute-start(bf16[384,1536]{1,0:T(8,128)(2,1)S(1)} %copy-done.6), channel_id=1, source_target_pairs={{0,2},{1,3},{2,0},{3,1},{4,6},{5,7},{6,4},{7,5},{8,10},{9,11},{10,... | collective-permute-start | bytes 3538952 | tf_op jit(solution)/shard_map/ppermute | solution.py:599
  217.8 22.1 %collective-permute-start.33 = (bf16[384,768]{1,0:T(8,128)(2,1)}, bf16[384,768]{1,0:T(8,128)(2,1)S(1)}, u32[]{:S(2)}, u32[]{:S(2)}) collective-permute-start(bf16[384,768]{1,0:T(8,128)(2,1)} %get-tuple-element.91), channel_id=1, source_target_pairs={{0,4},{4,0},{8,12},{12,8},{16,20},{20,16},{24,28},{28,24},{1,5},{5... | collective-permute-start | bytes 1769480 | tf_op jit(solution)/shard_map/ppermute | solution.py:573
  226.0 13.0 %all-to-all-start.1 = ((f32[32,8,128]{2,1,0:T(8,128)}), f32[32,8,128]{2,1,0:T(8,128)S(1)}, u32[]{:S(2)}, u32[]{:S(2)}) async-start(f32[32,8,128]{2,1,0:T(8,128)} %bitcast.33), calls=%async_computation.1 | async-start | bytes 262144 | tf_op jit(solution)/shard_map/all_to_all | solution.py:768
  239.7 1.1 copy-start.4
  239.7 23.2 %collective-permute-start.31 = (bf16[1024,768]{1,0:T(8,128)(2,1)}, bf16[1024,768]{1,0:T(8,128)(2,1)S(1)}, u32[]{:S(2)}, u32[]{:S(2)}) collective-permute-start(bf16[1024,768]{1,0:T(8,128)(2,1)} %later.40), channel_id=1, source_target_pairs={{0,1},{1,0},{2,3},{3,2},{4,5},{5,4},{6,7},{7,6},{8,9},{9,8},{10,11... | collective-permute-start | bytes 4718600 | tf_op jit(solution)/shard_map/ppermute | solution.py:599
  240.7 15.0 %copy-start.2 = (bf16[384,768]{1,0:T(8,128)(2,1)}, bf16[384,768]{1,0:T(8,128)(2,1)S(1)}, u32[]{:S(2)}) copy-start(bf16[384,768]{1,0:T(8,128)(2,1)S(1)} %collective-permute-done.33.refs_3_) | copy-start | bytes 1769476
  240.9 16.4 %copy-start = (bf16[384,1536]{1,0:T(8,128)(2,1)S(1)}, bf16[384,1536]{1,0:T(8,128)(2,1)}, u32[]{:S(2)}) copy-start(bf16[384,1536]{1,0:T(8,128)(2,1)} %add_convert_fusion) | copy-start | bytes 3538948
  240.9 8.4 %collective-permute-start.34 = (bf16[96,768]{1,0:T(8,128)(2,1)S(1)}, bf16[96,768]{1,0:T(8,128)(2,1)S(1)}, u32[]{:S(2)}, u32[]{:S(2)}) collective-permute-start(bf16[96,768]{1,0:T(8,128)(2,1)S(1)} %get-tuple-element.188), channel_id=1, source_target_pairs={{0,8},{4,12},{8,0},{12,4},{16,24},{20,28},{24,16},{28,20},{1,9},{5... | collective-permute-start | bytes 442376 | tf_op jit(solution)/shard_map/ppermute | solution.py:573
  241.7 14.0 %collective-permute-start.35 = (bf16[96,768]{1,0:T(8,128)(2,1)S(1)}, bf16[96,768]{1,0:T(8,128)(2,1)S(1)}, u32[]{:S(2)}, u32[]{:S(2)}) collective-permute-start(bf16[96,768]{1,0:T(8,128)(2,1)S(1)} %get-tuple-element.190), channel_id=1, source_target_pairs={{0,16},{4,20},{8,24},{12,28},{16,0},{20,4},{24,8},{28,12},{1,17},{... | collective-permute-start | bytes 442376 | tf_op jit(solution)/shard_map/ppermute | solution.py:573
  243.7 11.9 %collective-permute-start.36 = (bf16[96,768]{1,0:T(8,128)(2,1)S(1)}, bf16[96,768]{1,0:T(8,128)(2,1)S(1)}, u32[]{:S(2)}, u32[]{:S(2)}) collective-permute-start(bf16[96,768]{1,0:T(8,128)(2,1)S(1)} %get-tuple-element.189), channel_id=1, source_target_pairs={{0,24},{4,28},{8,16},{12,20},{16,8},{20,12},{24,0},{28,4},{1,25},{... | collective-permute-start | bytes 442376 | tf_op jit(solution)/shard_map/ppermute | solution.py:573
  258.1 8.4 %copy-start.26 = (f32[8,128]{1,0:T(8,128)S(1)}, f32[8,128]{1,0:T(8,128)}, u32[]{:S(2)}) copy-start(f32[8,128]{1,0:T(8,128)} %reduce_sum.71) | copy-start | bytes 12292
  258.1 13.4 %collective-permute-start.37 = (bf16[96,1536]{1,0:T(8,128)(2,1)S(1)}, bf16[96,1536]{1,0:T(8,128)(2,1)}, u32[]{:S(2)}, u32[]{:S(2)}) collective-permute-start(bf16[96,1536]{1,0:T(8,128)(2,1)S(1)} %get-tuple-element.183), channel_id=1, source_target_pairs={{0,8},{4,12},{8,0},{12,4},{16,24},{20,28},{24,16},{28,20},{1,9},{5... | collective-permute-start | bytes 884744 | tf_op jit(solution)/shard_map/ppermute | solution.py:573
  260.5 23.7 %collective-permute-start.38 = (bf16[96,1536]{1,0:T(8,128)(2,1)}, bf16[96,1536]{1,0:T(8,128)(2,1)S(1)}, u32[]{:S(2)}, u32[]{:S(2)}) collective-permute-start(bf16[96,1536]{1,0:T(8,128)(2,1)} %get-tuple-element.185), channel_id=1, source_target_pairs={{0,16},{4,20},{8,24},{12,28},{16,0},{20,4},{24,8},{28,12},{1,17},{... | collective-permute-start | bytes 884744 | tf_op jit(solution)/shard_map/ppermute | solution.py:573
  261.3 23.6 %collective-permute-start.39 = (bf16[96,1536]{1,0:T(8,128)(2,1)}, bf16[96,1536]{1,0:T(8,128)(2,1)S(1)}, u32[]{:S(2)}, u32[]{:S(2)}) collective-permute-start(bf16[96,1536]{1,0:T(8,128)(2,1)} %get-tuple-element.184), channel_id=1, source_target_pairs={{0,24},{4,28},{8,16},{12,20},{16,8},{20,12},{24,0},{28,4},{1,25},{... | collective-permute-start | bytes 884744 | tf_op jit(solution)/shard_map/ppermute | solution.py:573
  265.1 23.1 %collective-permute-start.32 = (bf16[512,768]{1,0:T(8,128)(2,1)}, bf16[512,768]{1,0:T(8,128)(2,1)}, u32[]{:S(2)}, u32[]{:S(2)}) collective-permute-start(bf16[512,768]{1,0:T(8,128)(2,1)} %add_convert_fusion.3), channel_id=1, source_target_pairs={{0,2},{1,3},{2,0},{3,1},{4,6},{5,7},{6,4},{7,5},{8,10},{9,11},{10,... | collective-permute-start | bytes 2359304 | tf_op jit(solution)/shard_map/ppermute | solution.py:599
  284.9 1.1 copy-start.17
  286.0 2.2 copy-start.1
  286.0 2.2 copy-start.14
  (9 other events, 7.3 us)

commit v8 on v7

--- a/solution.py
+++ b/solution.py
@@ -532,7 +532,7 @@
         scratch_shapes=[V((4, model, width), f32), V((4, size, model), bf16), V((4, size, model), bf16), V((model, size), bf16), V((model, size), bf16),
             pltpu.SemaphoreType.DMA((2, 4))],
         compiler_params=pltpu.CompilerParams(dimension_semantics=("arbitrary",), vmem_limit_bytes=60 << 20),
-        cost_estimate=pl.CostEstimate(flops=40 * size * model * width, bytes_accessed=24 * size * model, transcendentals=0),
+        cost_estimate=pl.CostEstimate(flops=100 * size * model * width, bytes_accessed=24 * size * model, transcendentals=0),
         name="projection_grads",
     )(home, *tokens, *grads, *contextT, *dqT, dk, dv)
 

time: 292 us -> 292 us (level)
  no operation moved by 1% of the time
where the time goes in v8:
time: 292 us; the launch traced here: 291 us
  Pallas kernels  126 us (43%)
  waiting for transfers between devices  56.7 us (19%)
  starting transfers between devices  51.3 us (18%)
  other arithmetic  27.9 us (10%)
  local copies, waits for them, and re-layouts  27.3 us (9%)
    pallas_call x2, Pallas kernels, attn_bwd(): pl.pallas_call(functools.partial(bwd_kernel, first), out_shape=(jax.Shape...  42.6 us
    ppermute x18, waiting for transfers between devices, hop(): return lax.ppermute(value, 'dp', [(i, i ^ bit) for i in range(count)])  37.1 us
    pallas_call x1, Pallas kernels, ffn(): pl.pallas_call(functools.partial(ffn_kernel, count), out_shape=(jax.Shape...  30.6 us
    ppermute x18, starting transfers between devices, hop(): return lax.ppermute(value, 'dp', [(i, i ^ bit) for i in range(count)])  27.3 us
    pallas_call x2, Pallas kernels, attn_fwd(): pl.pallas_call(functools.partial(fwd_kernel, first), out_shape=(jax.Shape...  26.3 us
    ppermute x22, starting transfers between devices, exchange(): return lax.ppermute(value, 'tensor', [(i, i ^ bit) for i in range(4)])  14.2 us
    unnamed x72, local copies, waits for them, and re-layouts  13.4 us
    ppermute x22, waiting for transfers between devices, exchange(): return lax.ppermute(value, 'tensor', [(i, i ^ bit) for i in range(4)])  12.4 us
  transfers between devices with their start and end apart: 42, of which 11 were waited for; matrix products, arithmetic and copies ran while one was open for 15% of the time, Pallas kernels for 33%

profile of v8, /device:TPU:0, one launch (start us, length us, event | category | flops | bytes accessed | tf_op | source)
XLA Modules:
  0.0 290.7 jit_solution(2990725884310350617)
XLA Ops:
  0.7 0.9 copy.96
  1.5 1.0 pad_maximum_fusion.5
  2.5 3.1 %collective-permute-start.6 = (bf16[96,768]{1,0:T(8,128)(2,1)S(1)}, bf16[96,768]{1,0:T(8,128)(2,1)S(1)}, u32[]{:S(2)}, u32[]{:S(2)}) collective-permute-start(bf16[96,768]{1,0:T(8,128)(2,1)S(1)} %pad_maximum_fusion.5), channel_id=1, source_target_pairs={{0,8},{4,12},{8,0},{12,4},{16,24},{20,28},{24,16},{28,20},{1,9},{5... | collective-permute-start | bytes 442376 | tf_op jit(solution)/shard_map/ppermute | solution.py:573
  5.6 2.6 collective-permute-start.7
  8.2 1.7 collective-permute-start.4
  10.6 0.9 concatenate.30
  12.1 5.0 %all-to-all-start = ((f32[32,8,128]{2,1,0:T(8,128)}), f32[32,8,128]{2,1,0:T(8,128)S(1)}, u32[]{:S(2)}, u32[]{:S(2)}) async-start(f32[32,8,128]{2,1,0:T(8,128)} %broadcast_in_dim.46), calls=%async_computation | async-start | bytes 262144 | tf_op jit(solution)/shard_map/all_to_all | solution.py:702
  17.2 1.0 pad_maximum_fusion.4
  18.3 1.8 collective-permute-start
  20.1 2.4 collective-permute-start.1
  22.7 1.0 pad_maximum_fusion.3.wa_ref
  23.7 5.8 %all-to-all-done = f32[32,8,128]{2,1,0:T(8,128)S(1)} async-done(((f32[32,8,128]{2,1,0:T(8,128)}), f32[32,8,128]{2,1,0:T(8,128)S(1)}, u32[]{:S(2)}, u32[]{:S(2)}) %all-to-all-start) | async-done | bytes 131104 | tf_op jit(solution)/shard_map/all_to_all | solution.py:702
  32.4 2.5 collective-permute-done
  35.0 1.6 collective-permute-start.9
  38.6 1.4 copy.112
  40.4 3.1 %collective-permute-done.1 = bf16[96,1536]{1,0:T(8,128)(2,1)S(1)} collective-permute-done((bf16[96,1536]{1,0:T(8,128)(2,1)S(1)}, bf16[96,1536]{1,0:T(8,128)(2,1)S(1)}, u32[]{:S(2)}, u32[]{:S(2)}) %collective-permute-start.1) | collective-permute-done | bytes 294944 | tf_op jit(solution)/shard_map/ppermute | solution.py:573
  43.7 1.5 collective-permute-start.12
  45.2 1.5 collective-permute-start.13
  46.7 4.6 %collective-permute-done.9.wb_ref = bf16[384,768]{1,0:T(8,128)(2,1)} collective-permute-done((bf16[384,768]{1,0:T(8,128)(2,1)S(1)}, bf16[384,768]{1,0:T(8,128)(2,1)}, u32[]{:S(2)}, u32[]{:S(2)}) %collective-permute-start.9) | collective-permute-done | bytes 589856 | tf_op jit(solution)/shard_map/ppermute | solution.py:573
  51.3 10.0 %projection.1 = (bf16[192,2048]{1,0:T(8,128)(2,1)}, bf16[192,2048]{1,0:T(8,128)(2,1)}, bf16[192,2048]{1,0:T(8,128)(2,1)}, bf16[2048,192]{1,0:T(8,128)(2,1)}, bf1...) custom-call(s32[1]{0:T(128)} %bitcast.home_ref, bf16[512,768]{1,0:T(8,128)(2,1)} %x0.3, ...), custom_call_target="tpu_custom_call" | custom-call | flops 9059696640 | bytes 6291456 | tf_op jit(solution)/shard_map/projection/pallas_call | solution.py:448
  61.3 13.2 %attention.2 = (bf16[192,1024]{1,0:T(8,128)(2,1)}, f32[8,1024]{1,0:T(8,128)}, bf16[512,768]{1,0:T(8,128)(2,1)}, bf16[512,768]{1,0:T(8,128)(2,1)}) custom-call(s32[4]{0:T(128)} %later.22.lo_ref, s32[4]{0:T(128)} %and_select_fusion.hi_ref, s32[1]{0:T(128)} %bitcast.5.flip_ref, bf16[192,2048]{1,0:T(8,128)(2,1)} %get-tuple-element.55.q_ref, ...), custom_call_target="tpu_custom_call" | custom-call | flops 20132659200 | bytes 1572864 | tf_op jit(solution)/shard_map/attention/pallas_call | solution.py:82
  75.1 1.1 slice.220
  76.2 1.6 collective-permute-start.17
  78.5 1.6 collective-permute-start.15
  80.0 13.1 %attention.3 = (bf16[192,1024]{1,0:T(8,128)(2,1)}, f32[8,1024]{1,0:T(8,128)}, bf16[512,768]{1,0:T(8,128)(2,1)}, bf16[512,768]{1,0:T(8,128)(2,1)}) custom-call(s32[4]{0:T(128)} %later.23.lo_ref, s32[4]{0:T(128)} %and_select_fusion.hi_ref, s32[1]{0:T(128)} %bitcast.5.flip_ref, bf16[192,2048]{1,0:T(8,128)(2,1)} %get-tuple-element.55.q_ref, ...), custom_call_target="tpu_custom_call" | custom-call | flops 20132659200 | bytes 1572864 | tf_op jit(solution)/shard_map/attention/pallas_call | solution.py:82
  93.2 4.8 %collective-permute-done.15.refs_0_ = bf16[512,768]{1,0:T(8,128)(2,1)S(1)} collective-permute-done((bf16[512,768]{1,0:T(8,128)(2,1)S(1)}, bf16[512,768]{1,0:T(8,128)(2,1)S(1)}, u32[]{:S(2)}, u32[]{:S(2)}) %collective-permute-start.15) | collective-permute-done | bytes 786464 | tf_op jit(solution)/shard_map/ppermute | solution.py:599
  98.0 0.9 copy-done.3
  99.4 1.0 slice.219
  100.4 1.6 collective-permute-start.16
  102.0 7.5 %collective-permute-done.16.refs_0_ = bf16[96,1536]{1,0:T(8,128)(2,1)S(1)} collective-permute-done((bf16[96,1536]{1,0:T(8,128)(2,1)S(1)}, bf16[96,1536]{1,0:T(8,128)(2,1)S(1)}, u32[]{:S(2)}, u32[]{:S(2)}) %collective-permute-start.16) | collective-permute-done | bytes 294944 | tf_op jit(solution)/shard_map/ppermute | solution.py:599
  113.8 30.6 %feed_forward.1 = (bf16[512,768]{1,0:T(8,128)(2,1)}, f32[512,768]{1,0:T(8,128)}, bf16[512,768]{1,0:T(8,128)(2,1)}, f32[6,8,768]{2,1,0:T(8,128)}, f32[4,8,768]{2,...) custom-call(s32[1]{0:T(128)} %bitcast.home_ref, ...), custom_call_target="tpu_custom_call" | custom-call | flops 36238786560 | bytes 18874368 | tf_op jit(solution)/shard_map/feed_forward/pallas_call | solution.py:379
  145.7 1.5 collective-permute-start.27
  147.2 0.9 reduce_sum.69
  148.4 0.9 reduce_sum.70
  150.1 1.4 add_convert_fusion.1.refs_2_
  151.5 0.9 collective-permute-start.29
  152.4 1.7 add_convert_fusion.6.refs_1_
  154.7 20.8 %attention_back.2 = (bf16[192,1024]{1,0:T(8,128)(2,1)}, f32[2048,192]{1,0:T(8,128)}, f32[2048,192]{1,0:T(8,128)}, f32[192,128]{1,0:T(8,128)}) custom-call(s32[4]{0:T(128)} %later.29.lo_ref, s32[4]{0:T(128)} %and_select_fusion.hi_ref, s32[1]{0:T(128)} %bitcast.5.flip_ref, bf16[192,2048]{1,0:T(8,128)(2,1)} %get-tuple-element.55.q_ref, ...), custom_call_target="tpu_custom_call" | custom-call | flops 24159191040 | bytes 3932160 | tf_op jit(solution)/shard_map/attention_back/pallas_call | solution.py:171
  176.4 0.9 copy-done.9
  177.3 3.1 %convert_add_fusion.1 = (f32[384,1536]{1,0:T(8,128)S(1)}, f32[384,1536]{1,0:T(8,128)S(1)}) fusion(bf16[1152,1536]{1,0:T(8,128)(2,1)} %collective-permute-done.24, bf16[1152,1536]{1,0:T(8,128)(2,1)} %get-tuple-element.73), kind=kLoop, calls=%fused_computation.5 | loop fusion | flops 3538944 | bytes 9437184 | tf_op jit(solution)/shard_map/add | solution.py:636
  181.7 1.3 pad_maximum_fusion.1
  183.0 1.1 collective-permute-start.26
  184.7 1.5 collective-permute-start.30
  186.2 21.8 %attention_back.3 = (bf16[192,1024]{1,0:T(8,128)(2,1)}, bf16[2048,192]{1,0:T(8,128)(2,1)}, bf16[2048,192]{1,0:T(8,128)(2,1)}, f32[192,128]{1,0:T(8,128)}, f32[8,192]{1,0:T(8,128)}) custom-call(s32[4]{0:T(128)} %later.33.lo_ref, s32[4]{0:T(128)} %and_select_fusion.hi_ref, s32[1]{0:T(128)} %bitcast.5.flip_ref, bf16[192,2048]{1,0:T(8,128)(2,1)} %get-tuple-element.55.q_ref, ...), custom_call_target="tpu_custom_call" | custom-call | flops 24159191040 | bytes 3932160 | tf_op jit(solution)/shard_map/attention_back/pallas_call | solution.py:171
  208.0 9.8 %projection_grads.1 = (bf16[384,768]{1,0:T(8,128)(2,1)}, bf16[384,768]{1,0:T(8,128)(2,1)}) custom-call(s32[1]{0:T(128)} %bitcast.home_ref, bf16[512,768]{1,0:T(8,128)(2,1)} %x0.3, bf16[512,768]{1,0:T(8,128)(2,1)} %collective-permute-done.3.x1, bf16[512,768]{1,0:T(8,128)(2,1)} %collective-permute-done.4.x2, bf16[512,768]{1,0:T(8,128)(2,1)} %collective-permute-done.5.x3, ...), custom_call_target="tpu_custom_call" | custom-call | flops 7549747200 | bytes 9437184 | tf_op jit(solution)/shard_map/projection_grads/pallas_call | solution.py:526
  217.8 1.2 collective-permute-start.33
  219.0 4.0 %add_convert_fusion = bf16[384,1536]{1,0:T(8,128)(2,1)} fusion(bf16[384,1536]{1,0:T(8,128)(2,1)} %later.35, bf16[384,1536]{1,0:T(8,128)(2,1)} %later.34, bf16[1152,1536]{1,0:T(8,128)(2,1)} %collective-permute-done.24, bf16[1152,1536]{1,0:T(8,128)(2,1)} %get-tuple-element.73), kind=kLoop, calls=%fused_computation.3 | loop fusion | flops 4718592 | bytes 5898240 | tf_op jit(solution)/shard_map/convert_element_type | solution.py:657
  223.9 1.0 add_reduce_fusion
  226.0 4.8 %all-to-all-start.1 = ((f32[32,8,128]{2,1,0:T(8,128)}), f32[32,8,128]{2,1,0:T(8,128)S(1)}, u32[]{:S(2)}, u32[]{:S(2)}) async-start(f32[32,8,128]{2,1,0:T(8,128)} %bitcast.33), calls=%async_computation.1 | async-start | bytes 262144 | tf_op jit(solution)/shard_map/all_to_all | solution.py:768
  230.8 6.8 %projection_back.1 = (bf16[512,768]{1,0:T(8,128)(2,1)}, bf16[1024,768]{1,0:T(8,128)(2,1)}, bf16[512,768]{1,0:T(8,128)(2,1)}) custom-call(bf16[192,1024]{1,0:T(8,128)(2,1)} %later.36.qa_ref, bf16[192,1024]{1,0:T(8,128)(2,1)} %get-tuple-element.80.qb_ref, bf16[2048,192]{1,0:T(8,128)(2,1)} %get-tuple-element.81.k_ref, ...), custom_call_target="tpu_custom_call" | custom-call | flops 21139292160 | bytes 12582912 | tf_op jit(solution)/shard_map/projection_back/pallas_call | solution.py:559
  237.6 1.4 all-to-all-done.1
  241.7 2.1 collective-permute-start.35
  243.7 1.6 collective-permute-start.36
  245.4 3.9 %collective-permute-done.34 = bf16[96,768]{1,0:T(8,128)(2,1)S(1)} collective-permute-done((bf16[96,768]{1,0:T(8,128)(2,1)S(1)}, bf16[96,768]{1,0:T(8,128)(2,1)S(1)}, u32[]{:S(2)}, u32[]{:S(2)}) %collective-permute-start.34) | collective-permute-done | bytes 147488 | tf_op jit(solution)/shard_map/ppermute | solution.py:573
  249.3 6.3 %collective-permute-done.35 = bf16[96,768]{1,0:T(8,128)(2,1)S(1)} collective-permute-done((bf16[96,768]{1,0:T(8,128)(2,1)S(1)}, bf16[96,768]{1,0:T(8,128)(2,1)S(1)}, u32[]{:S(2)}, u32[]{:S(2)}) %collective-permute-start.35) | collective-permute-done | bytes 147488 | tf_op jit(solution)/shard_map/ppermute | solution.py:573
  257.3 0.9 fusion.4
  258.1 2.4 collective-permute-start.37
  261.3 1.6 collective-permute-start.39
  262.9 2.2 add_convert_fusion.3
  265.1 1.4 collective-permute-start.32
  267.7 3.8 %collective-permute-done.37.refs_0_ = bf16[96,1536]{1,0:T(8,128)(2,1)} collective-permute-done((bf16[96,1536]{1,0:T(8,128)(2,1)S(1)}, bf16[96,1536]{1,0:T(8,128)(2,1)}, u32[]{:S(2)}, u32[]{:S(2)}) %collective-permute-start.37) | collective-permute-done | bytes 294944 | tf_op jit(solution)/shard_map/ppermute | solution.py:573
  271.5 12.7 %collective-permute-done.38.refs_0_ = bf16[96,1536]{1,0:T(8,128)(2,1)S(1)} collective-permute-done((bf16[96,1536]{1,0:T(8,128)(2,1)}, bf16[96,1536]{1,0:T(8,128)(2,1)S(1)}, u32[]{:S(2)}, u32[]{:S(2)}) %collective-permute-start.38) | collective-permute-done | bytes 294944 | tf_op jit(solution)/shard_map/ppermute | solution.py:573
  286.0 1.3 add_add_fusion
  288.2 2.4 add_convert_fusion.2
  (203 shorter events, 29.4 us)
Async XLA Ops:
  2.5 15.7 %collective-permute-start.6 = (bf16[96,768]{1,0:T(8,128)(2,1)S(1)}, bf16[96,768]{1,0:T(8,128)(2,1)S(1)}, u32[]{:S(2)}, u32[]{:S(2)}) collective-permute-start(bf16[96,768]{1,0:T(8,128)(2,1)S(1)} %pad_maximum_fusion.5), channel_id=1, source_target_pairs={{0,8},{4,12},{8,0},{12,4},{16,24},{20,28},{24,16},{28,20},{1,9},{5... | collective-permute-start | bytes 442376 | tf_op jit(solution)/shard_map/ppermute | solution.py:573
  5.6 14.5 %collective-permute-start.7 = (bf16[96,768]{1,0:T(8,128)(2,1)S(1)}, bf16[96,768]{1,0:T(8,128)(2,1)S(1)}, u32[]{:S(2)}, u32[]{:S(2)}) collective-permute-start(bf16[96,768]{1,0:T(8,128)(2,1)S(1)} %pad_maximum_fusion.5), channel_id=1, source_target_pairs={{0,16},{4,20},{8,24},{12,28},{16,0},{20,4},{24,8},{28,12},{1,17},{... | collective-permute-start | bytes 442376 | tf_op jit(solution)/shard_map/ppermute | solution.py:573
  8.2 14.3 %collective-permute-start.8 = (bf16[96,768]{1,0:T(8,128)(2,1)S(1)}, bf16[96,768]{1,0:T(8,128)(2,1)S(1)}, u32[]{:S(2)}, u32[]{:S(2)}) collective-permute-start(bf16[96,768]{1,0:T(8,128)(2,1)S(1)} %pad_maximum_fusion.5), channel_id=1, source_target_pairs={{0,24},{4,28},{8,16},{12,20},{16,8},{20,12},{24,0},{28,4},{1,25},{... | collective-permute-start | bytes 442376 | tf_op jit(solution)/shard_map/ppermute | solution.py:573
  8.2 22.5 %collective-permute-start.4 = (bf16[512,768]{1,0:T(8,128)(2,1)}, bf16[512,768]{1,0:T(8,128)(2,1)}, u32[]{:S(2)}, u32[]{:S(2)}) collective-permute-start(bf16[512,768]{1,0:T(8,128)(2,1)} %x0.3), channel_id=1, source_target_pairs={{0,2},{1,3},{2,0},{3,1},{4,6},{5,7},{6,4},{7,5},{8,10},{9,11},{10,... | collective-permute-start | bytes 2359304 | tf_op jit(solution)/shard_map/ppermute | solution.py:599
  9.9 41.4 %collective-permute-start.3 = (bf16[512,768]{1,0:T(8,128)(2,1)}, bf16[512,768]{1,0:T(8,128)(2,1)}, u32[]{:S(2)}, u32[]{:S(2)}) collective-permute-start(bf16[512,768]{1,0:T(8,128)(2,1)} %x0.3), channel_id=1, source_target_pairs={{0,1},{1,0},{2,3},{3,2},{4,5},{5,4},{6,7},{7,6},{8,9},{9,8},{10,11... | collective-permute-start | bytes 2359304 | tf_op jit(solution)/shard_map/ppermute | solution.py:599
  12.1 17.4 %all-to-all-start = ((f32[32,8,128]{2,1,0:T(8,128)}), f32[32,8,128]{2,1,0:T(8,128)S(1)}, u32[]{:S(2)}, u32[]{:S(2)}) async-start(f32[32,8,128]{2,1,0:T(8,128)} %broadcast_in_dim.46), calls=%async_computation | async-start | bytes 262144 | tf_op jit(solution)/shard_map/all_to_all | solution.py:702
  18.2 25.3 %copy-start.21 = (bf16[768,96]{0,1:T(8,128)(2,1)S(1)}, bf16[768,96]{0,1:T(8,128)(2,1)}, u32[]{:S(2)}) copy-start(bf16[768,96]{0,1:T(8,128)(2,1)} %param.33) | copy-start | bytes 442372
  18.2 25.3 %copy-start.22 = (bf16[96,768]{1,0:T(8,128)(2,1)S(1)}, bf16[96,768]{1,0:T(8,128)(2,1)}, u32[]{:S(2)}) copy-start(bf16[96,768]{1,0:T(8,128)(2,1)} %param.31) | copy-start | bytes 442372
  18.3 16.7 %collective-permute-start = (bf16[96,1536]{1,0:T(8,128)(2,1)S(1)}, bf16[96,1536]{1,0:T(8,128)(2,1)S(1)}, u32[]{:S(2)}, u32[]{:S(2)}) collective-permute-start(bf16[96,1536]{1,0:T(8,128)(2,1)S(1)} %pad_maximum_fusion.4), channel_id=1, source_target_pairs={{0,8},{4,12},{8,0},{12,4},{16,24},{20,28},{24,16},{28,20},{1,9},{5... | collective-permute-start | bytes 884744 | tf_op jit(solution)/shard_map/ppermute | solution.py:573
  20.1 23.4 %collective-permute-start.1 = (bf16[96,1536]{1,0:T(8,128)(2,1)S(1)}, bf16[96,1536]{1,0:T(8,128)(2,1)S(1)}, u32[]{:S(2)}, u32[]{:S(2)}) collective-permute-start(bf16[96,1536]{1,0:T(8,128)(2,1)S(1)} %pad_maximum_fusion.4), channel_id=1, source_target_pairs={{0,16},{4,20},{8,24},{12,28},{16,0},{20,4},{24,8},{28,12},{1,17},{... | collective-permute-start | bytes 884744 | tf_op jit(solution)/shard_map/ppermute | solution.py:573
  22.5 21.0 %collective-permute-start.2 = (bf16[96,1536]{1,0:T(8,128)(2,1)S(1)}, bf16[96,1536]{1,0:T(8,128)(2,1)S(1)}, u32[]{:S(2)}, u32[]{:S(2)}) collective-permute-start(bf16[96,1536]{1,0:T(8,128)(2,1)S(1)} %pad_maximum_fusion.4), channel_id=1, source_target_pairs={{0,24},{4,28},{8,16},{12,20},{16,8},{20,12},{24,0},{28,4},{1,25},{... | collective-permute-start | bytes 884744 | tf_op jit(solution)/shard_map/ppermute | solution.py:573
  23.7 20.0 %copy-start.23 = (bf16[384,768]{1,0:T(8,128)(2,1)}, bf16[384,768]{1,0:T(8,128)(2,1)S(1)}, u32[]{:S(2)}) copy-start(bf16[384,768]{1,0:T(8,128)(2,1)S(1)} %pad_maximum_fusion.3.wa_ref) | copy-start | bytes 1769476
  29.5 14.0 %copy-start.25 = (f32[4,8,8,128]{3,1,2,0:T(8,128)}, f32[4,8,8,128]{3,1,2,0:T(8,128)S(1)}, u32[]{:S(2)}) copy-start(f32[4,8,8,128]{3,1,2,0:T(8,128)S(1)} %copy.116) | copy-start | bytes 393220
  30.7 20.6 %collective-permute-start.5 = (bf16[512,768]{1,0:T(8,128)(2,1)}, bf16[512,768]{1,0:T(8,128)(2,1)}, u32[]{:S(2)}, u32[]{:S(2)}) collective-permute-start(bf16[512,768]{1,0:T(8,128)(2,1)} %collective-permute-done.4.x2), channel_id=1, source_target_pairs={{0,1},{1,0},{2,3},{3,2},{4,5},{5,4},{6,7},{7,6},{8,9},{9,8},{10,11... | collective-permute-start | bytes 2359304 | tf_op jit(solution)/shard_map/ppermute | solution.py:599
  30.8 12.9 %copy-start.29 = (s32[4]{0:T(128)}, s32[4]{0:T(128)S(1)}, u32[]{:S(2)}) copy-start(s32[4]{0:T(128)S(1)} %and_select_fusion.1.refs_0_) | copy-start | bytes 52
  35.0 16.3 %collective-permute-start.9 = (bf16[384,768]{1,0:T(8,128)(2,1)S(1)}, bf16[384,768]{1,0:T(8,128)(2,1)}, u32[]{:S(2)}, u32[]{:S(2)}) collective-permute-start(bf16[384,768]{1,0:T(8,128)(2,1)S(1)} %pad_maximum_fusion.3.wa_ref), channel_id=1, source_target_pairs={{0,4},{4,0},{8,12},{12,8},{16,20},{20,16},{24,28},{28,24},{1,5},{5... | collective-permute-start | bytes 1769480 | tf_op jit(solution)/shard_map/ppermute | solution.py:573
  36.8 6.8 %copy-start.28 = (f32[192]{0:T(256)}, f32[192]{0:T(256)S(1)}, u32[]{:S(2)}) copy-start(f32[192]{0:T(256)S(1)} %dynamic_slice.11) | copy-start | bytes 2308
  38.5 5.1 %copy-start.27 = (s32[1,1,4,512]{3,1,2,0:T(1,128)}, s32[1,1,4,512]{3,1,2,0:T(1,128)S(1)}, u32[]{:S(2)}) copy-start(s32[1,1,4,512]{3,1,2,0:T(1,128)S(1)} %copy.111) | copy-start | bytes 24580
  43.7 3.0 %copy-start.5 = (bf16[384,1536]{1,0:T(8,128)(2,1)}, bf16[384,1536]{1,0:T(8,128)(2,1)S(1)}, u32[]{:S(2)}) copy-start(bf16[384,1536]{1,0:T(8,128)(2,1)S(1)} %pad_maximum_fusion.refs_1_.refs_0_) | copy-start | bytes 3538948
  43.7 34.1 %collective-permute-start.12 = (bf16[384,1536]{1,0:T(8,128)(2,1)S(1)}, bf16[384,1536]{1,0:T(8,128)(2,1)}, u32[]{:S(2)}, u32[]{:S(2)}) collective-permute-start(bf16[384,1536]{1,0:T(8,128)(2,1)S(1)} %pad_maximum_fusion.refs_1_.refs_0_), channel_id=1, source_target_pairs={{0,4},{4,0},{8,12},{12,8},{16,20},{20,16},{24,28},{28,24},{1,5},{5... | collective-permute-start | bytes 3538952 | tf_op jit(solution)/shard_map/ppermute | solution.py:573
  45.2 29.9 %collective-permute-start.13 = (bf16[384,1536]{1,0:T(8,128)(2,1)S(1)}, bf16[384,1536]{1,0:T(8,128)(2,1)S(1)}, u32[]{:S(2)}, u32[]{:S(2)}) collective-permute-start(bf16[384,1536]{1,0:T(8,128)(2,1)S(1)} %pad_maximum_fusion.refs_1_.refs_0_), channel_id=1, source_target_pairs={{0,2},{1,3},{2,0},{3,1},{4,6},{5,7},{6,4},{7,5},{8,10},{9,11},{10,... | collective-permute-start | bytes 3538952 | tf_op jit(solution)/shard_map/ppermute | solution.py:599
  51.3 28.7 %collective-permute-start.11 = (bf16[384,1536]{1,0:T(8,128)(2,1)}, bf16[384,1536]{1,0:T(8,128)(2,1)}, u32[]{:S(2)}, u32[]{:S(2)}) collective-permute-start(bf16[384,1536]{1,0:T(8,128)(2,1)} %copy-done.5), channel_id=1, source_target_pairs={{0,1},{1,0},{2,3},{3,2},{4,5},{5,4},{6,7},{7,6},{8,9},{9,8},{10,11... | collective-permute-start | bytes 3538952 | tf_op jit(solution)/shard_map/ppermute | solution.py:599
  74.5 3.8 %copy-start.20 = (bf16[512,768]{1,0:T(8,128)(2,1)S(1)}, bf16[512,768]{1,0:T(8,128)(2,1)}, u32[]{:S(2)}) copy-start(bf16[512,768]{1,0:T(8,128)(2,1)} %get-tuple-element.59) | copy-start | bytes 2359300
  74.5 3.7 %collective-permute-start.10 = (bf16[512,768]{1,0:T(8,128)(2,1)}, bf16[512,768]{1,0:T(8,128)(2,1)S(1)}, u32[]{:S(2)}, u32[]{:S(2)}) collective-permute-start(bf16[512,768]{1,0:T(8,128)(2,1)} %get-tuple-element.60), channel_id=1, source_target_pairs={{0,1},{1,0},{2,3},{3,2},{4,5},{5,4},{6,7},{7,6},{8,9},{9,8},{10,11... | collective-permute-start | bytes 2359304 | tf_op jit(solution)/shard_map/ppermute | solution.py:599
  75.1 3.4 %copy-start.8 = (bf16[384,1536]{1,0:T(8,128)(2,1)}, bf16[384,1536]{1,0:T(8,128)(2,1)S(1)}, u32[]{:S(2)}) copy-start(bf16[384,1536]{1,0:T(8,128)(2,1)S(1)} %collective-permute-done.13.refs_4_.refs_2_) | copy-start | bytes 3538948
  76.2 22.8 %collective-permute-start.17 = (bf16[288,1536]{1,0:T(8,128)(2,1)}, bf16[288,1536]{1,0:T(8,128)(2,1)}, u32[]{:S(2)}, u32[]{:S(2)}) collective-permute-start(bf16[288,1536]{1,0:T(8,128)(2,1)} %slice.220), channel_id=1, source_target_pairs={{0,4},{4,0},{8,12},{12,8},{16,20},{20,16},{24,28},{28,24},{1,5},{5... | collective-permute-start | bytes 2654216 | tf_op jit(solution)/shard_map/ppermute | solution.py:573
  77.8 35.3 %collective-permute-start.19 = (bf16[384,1536]{1,0:T(8,128)(2,1)S(1)}, bf16[384,1536]{1,0:T(8,128)(2,1)}, u32[]{:S(2)}, u32[]{:S(2)}) collective-permute-start(bf16[384,1536]{1,0:T(8,128)(2,1)S(1)} %collective-permute-done.13.refs_4_.refs_2_), channel_id=1, source_target_pairs={{0,1},{1,0},{2,3},{3,2},{4,5},{5,4},{6,7},{7,6},{8,9},{9,8},{10,11... | collective-permute-start | bytes 3538952 | tf_op jit(solution)/shard_map/ppermute | solution.py:599
  77.8 35.3 %collective-permute-start.18 = (bf16[384,1536]{1,0:T(8,128)(2,1)}, bf16[384,1536]{1,0:T(8,128)(2,1)}, u32[]{:S(2)}, u32[]{:S(2)}) collective-permute-start(bf16[384,1536]{1,0:T(8,128)(2,1)} %collective-permute-done.12.refs_3_.refs_1_), channel_id=1, source_target_pairs={{0,1},{1,0},{2,3},{3,2},{4,5},{5,4},{6,7},{7,6},{8,9},{9,8},{10,11... | collective-permute-start | bytes 3538952 | tf_op jit(solution)/shard_map/ppermute | solution.py:599
  78.5 1.6 copy-start.12
  78.5 19.5 %collective-permute-start.15 = (bf16[512,768]{1,0:T(8,128)(2,1)S(1)}, bf16[512,768]{1,0:T(8,128)(2,1)S(1)}, u32[]{:S(2)}, u32[]{:S(2)}) collective-permute-start(bf16[512,768]{1,0:T(8,128)(2,1)S(1)} %add_convert_fusion.4.refs_1_), channel_id=1, source_target_pairs={{0,2},{1,3},{2,0},{3,1},{4,6},{5,7},{6,4},{7,5},{8,10},{9,11},{10,... | collective-permute-start | bytes 2359304 | tf_op jit(solution)/shard_map/ppermute | solution.py:599
  98.9 14.2 %collective-permute-start.21 = (bf16[288,1536]{1,0:T(8,128)(2,1)}, bf16[288,1536]{1,0:T(8,128)(2,1)}, u32[]{:S(2)}, u32[]{:S(2)}) collective-permute-start(bf16[288,1536]{1,0:T(8,128)(2,1)} %later.26.refs_4_), channel_id=1, source_target_pairs={{0,1},{1,0},{2,3},{3,2},{4,5},{5,4},{6,7},{7,6},{8,9},{9,8},{10,11... | collective-permute-start | bytes 2654216 | tf_op jit(solution)/shard_map/ppermute | solution.py:599
  98.9 14.2 %collective-permute-start.14 = (bf16[512,768]{1,0:T(8,128)(2,1)}, bf16[512,768]{1,0:T(8,128)(2,1)}, u32[]{:S(2)}, u32[]{:S(2)}) collective-permute-start(bf16[512,768]{1,0:T(8,128)(2,1)} %get-tuple-element.62), channel_id=1, source_target_pairs={{0,1},{1,0},{2,3},{3,2},{4,5},{5,4},{6,7},{7,6},{8,9},{9,8},{10,11... | collective-permute-start | bytes 2359304 | tf_op jit(solution)/shard_map/ppermute | solution.py:599
  100.4 9.0 %collective-permute-start.16 = (bf16[96,1536]{1,0:T(8,128)(2,1)S(1)}, bf16[96,1536]{1,0:T(8,128)(2,1)S(1)}, u32[]{:S(2)}, u32[]{:S(2)}) collective-permute-start(bf16[96,1536]{1,0:T(8,128)(2,1)S(1)} %slice.219), channel_id=1, source_target_pairs={{0,2},{1,3},{2,0},{3,1},{4,6},{5,7},{6,4},{7,5},{8,10},{9,11},{10,... | collective-permute-start | bytes 884744 | tf_op jit(solution)/shard_map/ppermute | solution.py:599
  110.2 2.9 %collective-permute-start.20 = (bf16[96,1536]{1,0:T(8,128)(2,1)}, bf16[96,1536]{1,0:T(8,128)(2,1)S(1)}, u32[]{:S(2)}, u32[]{:S(2)}) collective-permute-start(bf16[96,1536]{1,0:T(8,128)(2,1)} %later.25.refs_3_), channel_id=1, source_target_pairs={{0,1},{1,0},{2,3},{3,2},{4,5},{5,4},{6,7},{7,6},{8,9},{9,8},{10,11... | collective-permute-start | bytes 884744 | tf_op jit(solution)/shard_map/ppermute | solution.py:599
  144.4 5.6 %collective-permute-start.22 = (bf16[384,1536]{1,0:T(8,128)(2,1)}, bf16[384,1536]{1,0:T(8,128)(2,1)S(1)}, u32[]{:S(2)}, u32[]{:S(2)}) collective-permute-start(bf16[384,1536]{1,0:T(8,128)(2,1)} %get-tuple-element.67), channel_id=1, source_target_pairs={{0,1},{1,0},{2,3},{3,2},{4,5},{5,4},{6,7},{7,6},{8,9},{9,8},{10,11... | collective-permute-start | bytes 3538952 | tf_op jit(solution)/shard_map/ppermute | solution.py:599
  145.0 32.3 %collective-permute-start.24 = (bf16[1152,1536]{1,0:T(8,128)(2,1)}, bf16[1152,1536]{1,0:T(8,128)(2,1)}, u32[]{:S(2)}, u32[]{:S(2)}) collective-permute-start(bf16[1152,1536]{1,0:T(8,128)(2,1)} %get-tuple-element.74), channel_id=1, source_target_pairs={{0,1},{1,0},{2,3},{3,2},{4,5},{5,4},{6,7},{7,6},{8,9},{9,8},{10,11... | collective-permute-start | bytes 10616840 | tf_op jit(solution)/shard_map/ppermute | solution.py:599
  145.2 9.5 %collective-permute-start.23 = (bf16[512,768]{1,0:T(8,128)(2,1)}, bf16[512,768]{1,0:T(8,128)(2,1)}, u32[]{:S(2)}, u32[]{:S(2)}) collective-permute-start(bf16[512,768]{1,0:T(8,128)(2,1)} %get-tuple-element.70.g0), channel_id=1, source_target_pairs={{0,1},{1,0},{2,3},{3,2},{4,5},{5,4},{6,7},{7,6},{8,9},{9,8},{10,11... | collective-permute-start | bytes 2359304 | tf_op jit(solution)/shard_map/ppermute | solution.py:599
  145.7 29.9 %collective-permute-start.27 = (bf16[512,768]{1,0:T(8,128)(2,1)}, bf16[512,768]{1,0:T(8,128)(2,1)}, u32[]{:S(2)}, u32[]{:S(2)}) collective-permute-start(bf16[512,768]{1,0:T(8,128)(2,1)} %get-tuple-element.70.g0), channel_id=1, source_target_pairs={{0,2},{1,3},{2,0},{3,1},{4,6},{5,7},{6,4},{7,5},{8,10},{9,11},{10,... | collective-permute-start | bytes 2359304 | tf_op jit(solution)/shard_map/ppermute | solution.py:599
  151.5 2.7 copy-start.11
  151.5 24.9 %collective-permute-start.29 = (bf16[288,1536]{1,0:T(8,128)(2,1)S(1)}, bf16[288,1536]{1,0:T(8,128)(2,1)S(1)}, u32[]{:S(2)}, u32[]{:S(2)}) collective-permute-start(bf16[288,1536]{1,0:T(8,128)(2,1)S(1)} %add_convert_fusion.1.refs_2_), channel_id=1, source_target_pairs={{0,4},{4,0},{8,12},{12,8},{16,20},{20,16},{24,28},{28,24},{1,5},{5... | collective-permute-start | bytes 2654216 | tf_op jit(solution)/shard_map/ppermute | solution.py:573
  154.1 21.5 %collective-permute-start.25 = (bf16[96,1536]{1,0:T(8,128)(2,1)}, bf16[96,1536]{1,0:T(8,128)(2,1)S(1)}, u32[]{:S(2)}, u32[]{:S(2)}) collective-permute-start(bf16[96,1536]{1,0:T(8,128)(2,1)} %add_convert_fusion.6.refs_1_), channel_id=1, source_target_pairs={{0,2},{1,3},{2,0},{3,1},{4,6},{5,7},{6,4},{7,5},{8,10},{9,11},{10,... | collective-permute-start | bytes 884744 | tf_op jit(solution)/shard_map/ppermute | solution.py:599
  175.6 10.7 %collective-permute-start.28 = (bf16[512,768]{1,0:T(8,128)(2,1)}, bf16[512,768]{1,0:T(8,128)(2,1)}, u32[]{:S(2)}, u32[]{:S(2)}) collective-permute-start(bf16[512,768]{1,0:T(8,128)(2,1)} %later.31.g0.g2), channel_id=1, source_target_pairs={{0,1},{1,0},{2,3},{3,2},{4,5},{5,4},{6,7},{7,6},{8,9},{9,8},{10,11... | collective-permute-start | bytes 2359304 | tf_op jit(solution)/shard_map/ppermute | solution.py:599
  177.3 3.2 %copy-start.10 = (bf16[288,1536]{1,0:T(8,128)(2,1)S(1)}, bf16[288,1536]{1,0:T(8,128)(2,1)}, u32[]{:S(2)}) copy-start(bf16[288,1536]{1,0:T(8,128)(2,1)} %later.32) | copy-start | bytes 2654212
  183.0 1.1 copy-start.7
  183.0 1.7 copy-start.6
  183.0 36.0 %collective-permute-start.26 = (bf16[384,1536]{1,0:T(8,128)(2,1)S(1)}, bf16[384,1536]{1,0:T(8,128)(2,1)}, u32[]{:S(2)}, u32[]{:S(2)}) collective-permute-start(bf16[384,1536]{1,0:T(8,128)(2,1)S(1)} %get-tuple-element.207.refs_1_), channel_id=1, source_target_pairs={{0,4},{4,0},{8,12},{12,8},{16,20},{20,16},{24,28},{28,24},{1,5},{5... | collective-permute-start | bytes 3538952 | tf_op jit(solution)/shard_map/ppermute | solution.py:573
  184.7 34.3 %collective-permute-start.30 = (bf16[384,1536]{1,0:T(8,128)(2,1)S(1)}, bf16[384,1536]{1,0:T(8,128)(2,1)}, u32[]{:S(2)}, u32[]{:S(2)}) collective-permute-start(bf16[384,1536]{1,0:T(8,128)(2,1)S(1)} %copy-done.6), channel_id=1, source_target_pairs={{0,2},{1,3},{2,0},{3,1},{4,6},{5,7},{6,4},{7,5},{8,10},{9,11},{10,... | collective-permute-start | bytes 3538952 | tf_op jit(solution)/shard_map/ppermute | solution.py:599
  217.8 22.1 %collective-permute-start.33 = (bf16[384,768]{1,0:T(8,128)(2,1)}, bf16[384,768]{1,0:T(8,128)(2,1)S(1)}, u32[]{:S(2)}, u32[]{:S(2)}) collective-permute-start(bf16[384,768]{1,0:T(8,128)(2,1)} %get-tuple-element.91), channel_id=1, source_target_pairs={{0,4},{4,0},{8,12},{12,8},{16,20},{20,16},{24,28},{28,24},{1,5},{5... | collective-permute-start | bytes 1769480 | tf_op jit(solution)/shard_map/ppermute | solution.py:573
  226.0 13.0 %all-to-all-start.1 = ((f32[32,8,128]{2,1,0:T(8,128)}), f32[32,8,128]{2,1,0:T(8,128)S(1)}, u32[]{:S(2)}, u32[]{:S(2)}) async-start(f32[32,8,128]{2,1,0:T(8,128)} %bitcast.33), calls=%async_computation.1 | async-start | bytes 262144 | tf_op jit(solution)/shard_map/all_to_all | solution.py:768
  239.7 1.1 copy-start.4
  239.7 23.2 %collective-permute-start.31 = (bf16[1024,768]{1,0:T(8,128)(2,1)}, bf16[1024,768]{1,0:T(8,128)(2,1)S(1)}, u32[]{:S(2)}, u32[]{:S(2)}) collective-permute-start(bf16[1024,768]{1,0:T(8,128)(2,1)} %later.40), channel_id=1, source_target_pairs={{0,1},{1,0},{2,3},{3,2},{4,5},{5,4},{6,7},{7,6},{8,9},{9,8},{10,11... | collective-permute-start | bytes 4718600 | tf_op jit(solution)/shard_map/ppermute | solution.py:599
  240.7 15.0 %copy-start.2 = (bf16[384,768]{1,0:T(8,128)(2,1)}, bf16[384,768]{1,0:T(8,128)(2,1)S(1)}, u32[]{:S(2)}) copy-start(bf16[384,768]{1,0:T(8,128)(2,1)S(1)} %collective-permute-done.33.refs_3_) | copy-start | bytes 1769476
  240.9 16.4 %copy-start = (bf16[384,1536]{1,0:T(8,128)(2,1)S(1)}, bf16[384,1536]{1,0:T(8,128)(2,1)}, u32[]{:S(2)}) copy-start(bf16[384,1536]{1,0:T(8,128)(2,1)} %add_convert_fusion) | copy-start | bytes 3538948
  240.9 8.4 %collective-permute-start.34 = (bf16[96,768]{1,0:T(8,128)(2,1)S(1)}, bf16[96,768]{1,0:T(8,128)(2,1)S(1)}, u32[]{:S(2)}, u32[]{:S(2)}) collective-permute-start(bf16[96,768]{1,0:T(8,128)(2,1)S(1)} %get-tuple-element.188), channel_id=1, source_target_pairs={{0,8},{4,12},{8,0},{12,4},{16,24},{20,28},{24,16},{28,20},{1,9},{5... | collective-permute-start | bytes 442376 | tf_op jit(solution)/shard_map/ppermute | solution.py:573
  241.7 14.0 %collective-permute-start.35 = (bf16[96,768]{1,0:T(8,128)(2,1)S(1)}, bf16[96,768]{1,0:T(8,128)(2,1)S(1)}, u32[]{:S(2)}, u32[]{:S(2)}) collective-permute-start(bf16[96,768]{1,0:T(8,128)(2,1)S(1)} %get-tuple-element.190), channel_id=1, source_target_pairs={{0,16},{4,20},{8,24},{12,28},{16,0},{20,4},{24,8},{28,12},{1,17},{... | collective-permute-start | bytes 442376 | tf_op jit(solution)/shard_map/ppermute | solution.py:573
  243.7 11.9 %collective-permute-start.36 = (bf16[96,768]{1,0:T(8,128)(2,1)S(1)}, bf16[96,768]{1,0:T(8,128)(2,1)S(1)}, u32[]{:S(2)}, u32[]{:S(2)}) collective-permute-start(bf16[96,768]{1,0:T(8,128)(2,1)S(1)} %get-tuple-element.189), channel_id=1, source_target_pairs={{0,24},{4,28},{8,16},{12,20},{16,8},{20,12},{24,0},{28,4},{1,25},{... | collective-permute-start | bytes 442376 | tf_op jit(solution)/shard_map/ppermute | solution.py:573
  258.1 8.4 %copy-start.26 = (f32[8,128]{1,0:T(8,128)S(1)}, f32[8,128]{1,0:T(8,128)}, u32[]{:S(2)}) copy-start(f32[8,128]{1,0:T(8,128)} %reduce_sum.71) | copy-start | bytes 12292
  258.1 13.4 %collective-permute-start.37 = (bf16[96,1536]{1,0:T(8,128)(2,1)S(1)}, bf16[96,1536]{1,0:T(8,128)(2,1)}, u32[]{:S(2)}, u32[]{:S(2)}) collective-permute-start(bf16[96,1536]{1,0:T(8,128)(2,1)S(1)} %get-tuple-element.183), channel_id=1, source_target_pairs={{0,8},{4,12},{8,0},{12,4},{16,24},{20,28},{24,16},{28,20},{1,9},{5... | collective-permute-start | bytes 884744 | tf_op jit(solution)/shard_map/ppermute | solution.py:573
  260.5 23.7 %collective-permute-start.38 = (bf16[96,1536]{1,0:T(8,128)(2,1)}, bf16[96,1536]{1,0:T(8,128)(2,1)S(1)}, u32[]{:S(2)}, u32[]{:S(2)}) collective-permute-start(bf16[96,1536]{1,0:T(8,128)(2,1)} %get-tuple-element.185), channel_id=1, source_target_pairs={{0,16},{4,20},{8,24},{12,28},{16,0},{20,4},{24,8},{28,12},{1,17},{... | collective-permute-start | bytes 884744 | tf_op jit(solution)/shard_map/ppermute | solution.py:573
  261.3 23.6 %collective-permute-start.39 = (bf16[96,1536]{1,0:T(8,128)(2,1)}, bf16[96,1536]{1,0:T(8,128)(2,1)S(1)}, u32[]{:S(2)}, u32[]{:S(2)}) collective-permute-start(bf16[96,1536]{1,0:T(8,128)(2,1)} %get-tuple-element.184), channel_id=1, source_target_pairs={{0,24},{4,28},{8,16},{12,20},{16,8},{20,12},{24,0},{28,4},{1,25},{... | collective-permute-start | bytes 884744 | tf_op jit(solution)/shard_map/ppermute | solution.py:573
  265.1 23.1 %collective-permute-start.32 = (bf16[512,768]{1,0:T(8,128)(2,1)}, bf16[512,768]{1,0:T(8,128)(2,1)}, u32[]{:S(2)}, u32[]{:S(2)}) collective-permute-start(bf16[512,768]{1,0:T(8,128)(2,1)} %add_convert_fusion.3), channel_id=1, source_target_pairs={{0,2},{1,3},{2,0},{3,1},{4,6},{5,7},{6,4},{7,5},{8,10},{9,11},{10,... | collective-permute-start | bytes 2359304 | tf_op jit(solution)/shard_map/ppermute | solution.py:599
  284.9 1.1 copy-start.17
  286.0 2.2 copy-start.1
  286.0 2.2 copy-start.14
  (9 other events, 7.3 us)
